TPU v7x, 32 devices: a whole 2x2x4 slice. The times are simulated.
32 devices in a mesh: groups: 2 (over y), chan: 4 (over z), tile: 2 (over x), rep: 2 (over core).
Axes of the slice: x: 2, y: 2, z: 4, core: 2. Of those that a mesh axis runs over, the one named last changes fastest.
Arguments:
- generator: float32 [8, 4, 512, 512], P(('groups', 'chan'), ('tile', 'rep')), parts along dimension 0, may hold values from -1.2 to 1.2
- hamiltonian: float32 [8, 4, 512, 512], P(('groups', 'chan'), ('tile', 'rep')), parts along dimension 0, may hold values from -1.2 to 1.2
- pair_weights: float32 [8, 4, 512], P(('groups', 'chan'), ('tile', 'rep')), parts along dimension 0, may hold values from -1 to 1
- cross_weights: float32 [8, 4, 3, 512], P(('groups', 'chan'), ('tile', 'rep')), parts along dimension 0, may hold values from -1 to 1
- recoupling: float32 [8, 16, 16], replicated, may hold values from -1.5 to 1.5
- cross_owner: int32 [8, 4], P('groups', ('tile', 'rep')), parts along dimension 0, may hold values from 0 to 3, as said below
- tile_order: int32 [8, 4, 16], P(('groups', 'chan'), ('tile', 'rep')), parts along dimension 0, may hold values from 0 to 15, each once within a row
- recoupling_index: int32 [8, 4], P('groups', ('tile', 'rep')), parts along dimension 0, may hold values from 0 to 7
Outputs:
- commutator: float32 [8, 4, 512, 512], P(('groups', 'chan'), ('tile', 'rep')), parts along dimension 0
There are 2 independent parts, one for each index of `groups`. A program takes and returns all parts, laid end to end along the dimension named above; an argument that names none is the same for every part. Nothing has to cross between parts.
Inputs may be any that keep to these rules, and one draw needn't show every extreme that they name: `cross_owner`: in every column no owner hosts more than 3 cross-coupled channels, and one owner hosts exactly 3. `tile_order`: each channel's list names every one of its tiles once.
All inputs are finite; a program needn't handle non-finite values.
Results may differ from a plain program's by a relative error of at most 0.0003.
Values sent between devices are 32-bit elements; how exact they have to be, the bound alone decides.
No kernel may reach another device: no remote copies, remote signals or barrier semaphores. Data moves between devices by JAX's collectives and lax.ppermute only.
A program may use at most 64 MiB of HBM per device.

v0:
```python
import math

import jax
import jax.numpy as jnp
from jax import lax
from jax.sharding import PartitionSpec as P

TS = 128


highest = lax.Precision.HIGHEST


def to_tiles(matrix, tile_size):
    leading = matrix.shape[:-2]
    blocks = matrix.shape[-1] // tile_size
    shaped = matrix.reshape(leading + (blocks, tile_size, blocks, tile_size))
    shaped = jnp.swapaxes(shaped, -3, -2)
    return shaped.reshape(leading + (blocks * blocks, tile_size, tile_size))


def from_tiles(pieces, tile_size):
    leading = pieces.shape[:-3]
    blocks = math.isqrt(pieces.shape[-3])
    shaped = pieces.reshape(leading + (blocks, blocks, tile_size, tile_size))
    shaped = jnp.swapaxes(shaped, -3, -2)
    return shaped.reshape(leading + (blocks * tile_size, blocks * tile_size))


def bracket(left_matrix, right_matrix, weights):
    scaled = weights[..., None, :]
    left_term = jnp.matmul(left_matrix * scaled, right_matrix, precision=highest)
    right_term = jnp.matmul(right_matrix * scaled, left_matrix, precision=highest)
    return left_term - right_term


def cross_term(generator_cross, hamilton_cross, mixers, weights):
    generator_mixed = jnp.einsum("csji,csixy->csjxy", mixers, generator_cross, precision=highest)
    hamilton_mixed = jnp.einsum("csji,csixy->csjxy", mixers, hamilton_cross, precision=highest)
    product = bracket(from_tiles(generator_mixed, TS), from_tiles(hamilton_mixed, TS), weights)
    return jnp.einsum("csji,csjxy->csixy", mixers, to_tiles(product, TS), precision=highest)


def body(
    generator,
    hamiltonian,
    pair_weights,
    cross_weights,
    recoupling,
    cross_owner,
    tile_order,
    recoupling_index,
):
    channels = cross_owner.shape[0]
    column_count = generator.shape[1]
    tile_count = tile_order.shape[-1]
    spread = tile_count // channels
    capacity = cross_weights.shape[2]
    my_index = lax.axis_index("chan")
    chan_range = jnp.arange(channels, dtype=jnp.int32)
    tile_range = jnp.arange(tile_count, dtype=jnp.int32)
    spread_range = jnp.arange(spread, dtype=jnp.int32)
    column_range = jnp.arange(column_count, dtype=jnp.int32)
    slot_range = jnp.arange(capacity, dtype=jnp.int32)
    generator_tiles = to_tiles(generator[0], TS)
    hamilton_tiles = to_tiles(hamiltonian[0], TS)
    orders = tile_order[0]
    owners = jnp.transpose(cross_owner)
    mixer_index = jnp.transpose(recoupling_index)
    same_owner = owners[:, :, None] == owners[:, None, :]
    earlier = chan_range[None, :] < chan_range[:, None]
    slot_of = jnp.sum((same_owner & earlier[None]).astype(jnp.int32), axis=2)
    inverse = jnp.sum(
        jnp.where(orders[:, :, None] == tile_range[None, None, :], tile_range[None, :, None], 0),
        axis=1,
    )
    target = inverse // spread
    target_rank = inverse % spread
    column_index = column_range[:, None, None, None]
    hosting = (owners[:, :, None, None] == chan_range[None, None, :, None]) & (
        slot_of[:, :, None, None] == slot_range[None, None, None, :]
    )
    hosted = jnp.sum(jnp.where(hosting, chan_range[None, :, None, None], 0), axis=1)
    filled = jnp.any(hosting, axis=1)
    ordinal = hosted[:, :, :, None] * spread + spread_range[None, None, None, :]
    chosen = jnp.take_along_axis(orders, ordinal.reshape(column_count, -1), axis=1).reshape(
        ordinal.shape
    )
    chosen = jnp.transpose(chosen, (0, 2, 3, 1))
    keeping = jnp.transpose(filled, (0, 2, 1))[:, :, None, :, None, None]
    generator_send = jnp.where(keeping, generator_tiles[column_index, chosen], 0.0)
    hamilton_send = jnp.where(keeping, hamilton_tiles[column_index, chosen], 0.0)
    generator_got, hamilton_got = (
        lax.all_to_all(generator_send, "chan", split_axis=3, concat_axis=3, tiled=True),
        lax.all_to_all(hamilton_send, "chan", split_axis=3, concat_axis=3, tiled=True),
    )
    hosted_here = jnp.take(hosted, my_index, axis=1)
    mixers = recoupling[jnp.take_along_axis(mixer_index, hosted_here, axis=1)]
    weights_cross = cross_weights[0]
    shape_back = (column_count, capacity, tile_count, TS, TS)
    returned = cross_term(
        generator_got.reshape(shape_back), hamilton_got.reshape(shape_back), mixers, weights_cross
    )
    returned_home = lax.all_to_all(
        returned.reshape(column_count, capacity, spread, channels, TS, TS),
        "chan",
        split_axis=3,
        concat_axis=3,
        tiled=True,
    )
    from_slot = jnp.take_along_axis(slot_of, target, axis=1)
    from_device = jnp.take_along_axis(owners, target, axis=1)
    back_tiles = returned_home[column_range[:, None], from_slot, target_rank, from_device]
    direct = bracket(generator[0], hamiltonian[0], pair_weights[0])
    summed = direct + from_tiles(back_tiles, TS)
    return (0.5 * (summed + jnp.swapaxes(summed, -1, -2)))[None]


def solution(mesh):
    placed = (
        P(("groups", "chan"), ("tile", "rep"), None, None),
        P(("groups", "chan"), ("tile", "rep"), None, None),
        P(("groups", "chan"), ("tile", "rep"), None),
        P(("groups", "chan"), ("tile", "rep"), None, None),
        P(),
        P("groups", ("tile", "rep")),
        P(("groups", "chan"), ("tile", "rep"), None),
        P("groups", ("tile", "rep")),
    )
    return jax.shard_map(
        body,
        mesh=mesh,
        in_specs=placed,
        out_specs=P(("groups", "chan"), ("tile", "rep"), None, None),
        check_vma=False,
    )
```

profile of v0, /device:TPU:28, one launch (start us, length us, event | category | flops | bytes accessed | tf_op | source)
XLA Modules:
  0.0 289.5 jit_solution(5570581685007703052)
XLA Ops:
  0.0 0.9 convert_reduce_fusion
  2.2 1.4 gather_fusion.2
  4.0 1.6 reshape_squeeze.6
  6.2 2.5 gather_fusion.3
  8.7 2.5 gather_fusion.4
  11.4 5.4 %broadcast_select_fusion = (f32[1,3,4,4,128,128]{5,4,3,2,1,0:T(8,128)}, f32[1,3,4,4,128,128]{5,4,3,2,1,0:T(8,128)S(1)}) fusion(f32[1,3,4,4,128,128]{5,4,3,2,1,0:T(8,128)} %bitcast.161, pred[3,4]{1,0:T(4,128)(4,1)S(1)} %bitcast.171, f32[1,3,4,4,128,128]{5,4,3,2,1,0:T(8,128)} %bitcast.160), kind=kLoop, calls=%fused_computation.15 | loop fusion | flops 1572864 | bytes 12582924 | tf_op jit(solution)/shard_map/jit(_where)/select_n | solution.py:92
  16.9 1.9 copy.87
  18.8 5.1 %all-to-all-start = ((f32[1,3,4,4,128,128]{5,4,2,1,0,3:T(8,128)}), f32[1,3,4,4,128,128]{5,4,2,1,0,3:T(8,128)S(1)}, u32[]{:S(2)}, u32[]{:S(2)}) async-start(f32[1,3,4,4,128,128]{5,4,2,1,0,3:T(8,128)} %copy.87), calls=%async_computation | async-start | bytes 6291456 | tf_op jit(solution)/shard_map/all_to_all | solution.py:94
  23.8 3.9 %copy.91 = f32[1,3,4,4,128,128]{5,4,2,1,0,3:T(8,128)} copy(f32[1,3,4,4,128,128]{5,4,3,2,1,0:T(8,128)} %get-tuple-element.19) | data formatting | bytes 6291456 | tf_op jit(solution)/shard_map/jit(_where)/select_n | solution.py:92
  27.7 64.4 %all-to-all-done = f32[1,3,4,4,128,128]{5,4,2,1,0,3:T(8,128)S(1)} async-done(((f32[1,3,4,4,128,128]{5,4,2,1,0,3:T(8,128)}), f32[1,3,4,4,128,128]{5,4,2,1,0,3:T(8,128)S(1)}, u32[]{:S(2)}, u32[]{:S(2)}) %all-to-all-start) | async-done | bytes 3145760 | tf_op jit(solution)/shard_map/all_to_all | solution.py:94
  92.2 7.0 %all-to-all-start.1 = ((f32[1,3,4,4,128,128]{5,4,2,1,0,3:T(8,128)}), f32[1,3,4,4,128,128]{5,4,2,1,0,3:T(8,128)}, u32[]{:S(2)}, u32[]{:S(2)}) async-start(f32[1,3,4,4,128,128]{5,4,2,1,0,3:T(8,128)} %copy.91), calls=%async_computation.1 | async-start | bytes 6291456 | tf_op jit(solution)/shard_map/all_to_all | solution.py:95
  100.6 2.0 copy.88
  102.6 2.9 %fusion.24 = f32[3,16,128,128]{3,1,2,0:T(8,128)S(1)} fusion(f32[3,16,128,128]{3,1,2,0:T(8,128)S(1)} %bitcast.155, f32[3,16,16]{2,1,0:T(8,128)S(1)} %gather_fusion.1), kind=kOutput, calls=%fused_computation.34 | convolution fusion | flops 150994944 | bytes 6294528 | tf_op jit(solution)/shard_map/csji,csixy->csjxy/dot_general | solution.py:38
  105.5 2.4 copy.89
  107.9 3.3 %reshape.759 = f32[3,512,512]{2,1,0:T(8,128)S(1)} reshape(f32[1,3,4,128,4,128]{5,4,3,2,1,0:T(4,128)} %copy.89) | data formatting | bytes 6291456 | tf_op jit(solution)/shard_map/reshape | solution.py:27
  111.3 55.8 %all-to-all-done.1 = f32[1,3,4,4,128,128]{5,4,2,1,0,3:T(8,128)} async-done(((f32[1,3,4,4,128,128]{5,4,2,1,0,3:T(8,128)}), f32[1,3,4,4,128,128]{5,4,2,1,0,3:T(8,128)}, u32[]{:S(2)}, u32[]{:S(2)}) %all-to-all-start.1) | async-done | bytes 3145760 | tf_op jit(solution)/shard_map/all_to_all | solution.py:95
  167.0 3.9 %copy.92 = f32[1,3,4,4,128,128]{5,3,2,4,1,0:T(4,128)S(1)} copy(f32[1,3,4,4,128,128]{5,4,2,1,0,3:T(8,128)} %all-to-all-done.1) | data formatting | bytes 6291456 | tf_op jit(solution)/shard_map/all_to_all | solution.py:95
  170.9 2.9 %fusion.22 = f32[3,16,128,128]{3,1,2,0:T(8,128)S(1)} fusion(f32[3,16,128,128]{3,1,2,0:T(8,128)S(1)} %bitcast.157, f32[3,16,16]{2,1,0:T(8,128)S(1)} %gather_fusion.1), kind=kOutput, calls=%fused_computation.32 | convolution fusion | flops 150994944 | bytes 6294528 | tf_op jit(solution)/shard_map/csji,csixy->csjxy/dot_general | solution.py:39
  173.9 2.4 copy.93
  176.2 5.1 %squeeze_reshape.4 = f32[3,512,512]{2,1,0:T(8,128)} reshape(f32[1,3,4,128,4,128]{5,4,3,2,1,0:T(4,128)} %copy.93) | data formatting | bytes 6291456 | tf_op jit(solution)/shard_map/squeeze;reshape | solution.py:32
  181.3 7.6 %fusion = f32[3,512,512]{2,1,0:T(8,128)S(1)} fusion(f32[3,512,512]{2,1,0:T(8,128)S(1)} %reshape.759, f32[3,512,512]{2,1,0:T(8,128)} %squeeze_reshape.4, f32[3,512]{1,0:T(4,128)S(1)} %bitcast.166), kind=kOutput, calls=%fused_computation.8 | convolution fusion | flops 4832624640 | bytes 9443328 | tf_op jit(solution)/shard_map/dot_general | solution.py:33
  188.9 7.1 %fusion.4 = f32[3,512,512]{2,1,0:T(8,128)} fusion(f32[3,512,512]{2,1,0:T(8,128)S(1)} %fusion, f32[3,512,512]{2,1,0:T(8,128)S(1)} %copy-done.5, f32[3,512,512]{2,1,0:T(8,128)S(1)} %reshape.759, f32[3,512]{1,0:T(4,128)S(1)} %bitcast.167), kind=kOutput, calls=%fused_computation.12 | convolution fusion | flops 4833411072 | bytes 12589056 | tf_op jit(solution)/shard_map/dot_general | solution.py:32
  196.0 3.4 %reshape.763 = f32[1,3,4,128,4,128]{5,4,3,2,1,0:T(4,128)S(1)} reshape(f32[3,512,512]{2,1,0:T(8,128)} %fusion.4) | data formatting | bytes 6291456 | tf_op jit(solution)/shard_map/reshape | solution.py:17
  200.0 3.0 %fusion.26 = f32[3,16,128,128]{3,1,2,0:T(8,128)S(1)} fusion(f32[3,16,128,128]{3,1,2,0:T(8,128)S(1)} %bitcast.153, f32[3,16,16]{2,1,0:T(8,128)S(1)} %gather_fusion.1), kind=kOutput, calls=%fused_computation.36 | convolution fusion | flops 150994944 | bytes 6294528 | tf_op jit(solution)/shard_map/csji,csjxy->csixy/dot_general | solution.py:41
  203.0 2.6 copy.96
  205.6 6.2 %all-to-all-start.2 = ((f32[1,3,4,4,128,128]{5,4,2,1,0,3:T(8,128)}), f32[1,3,4,4,128,128]{5,4,2,1,0,3:T(8,128)S(1)}, u32[]{:S(2)}, u32[]{:S(2)}) async-start(f32[1,3,4,4,128,128]{5,4,2,1,0,3:T(8,128)} %copy.96), calls=%async_computation.2 | async-start | bytes 6291456 | tf_op jit(solution)/shard_map/all_to_all | solution.py:104
  213.3 4.4 %fusion.15 = f32[512,512]{1,0:T(8,128)} fusion(f32[1,1,512,512]{3,2,1,0:T(8,128)} %param.11, f32[1,1,512,512]{3,2,1,0:T(8,128)} %param.10, f32[512]{0:T(512)S(1)} %bitcast.169), kind=kOutput, calls=%fused_computation.25 | convolution fusion | flops 1610874880 | bytes 3147776 | tf_op jit(solution)/shard_map/dot_general | solution.py:32
  217.7 61.9 %all-to-all-done.2 = f32[1,3,4,4,128,128]{5,4,2,1,0,3:T(8,128)S(1)} async-done(((f32[1,3,4,4,128,128]{5,4,2,1,0,3:T(8,128)}), f32[1,3,4,4,128,128]{5,4,2,1,0,3:T(8,128)S(1)}, u32[]{:S(2)}, u32[]{:S(2)}) %all-to-all-start.2) | async-done | bytes 3145760 | tf_op jit(solution)/shard_map/all_to_all | solution.py:104
  279.5 1.8 copy.97
  281.4 2.7 gather_fusion.5
  284.8 3.2 %fusion.10 = f32[1,512,512]{2,1,0:T(8,128)S(1)} fusion(f32[512,512]{1,0:T(8,128)} %fusion.15, f32[64,8,4,128]{3,2,1,0:T(4,128)S(1)} %bitcast.162, f32[1,1,512,512]{3,2,1,0:T(8,128)S(1)} %copy-done.8, f32[1,1,512,512]{3,2,1,0:T(8,128)S(1)} %copy-done.7, f32[512]{0:T(512)S(1)} %bitcast.170), kind=kOutput, calls=%fused_computation.19 | convolution fusion | flops 1611399168 | bytes 5244928 | tf_op jit(solution)/shard_map/dot_general | solution.py:33
  288.3 1.2 fusion.12
  (64 shorter events, 6.9 us)
Async XLA Ops:
  0.0 100.0 %copy-start = (f32[8,16,16]{2,1,0:T(8,128)S(1)}, f32[8,16,16]{2,1,0:T(8,128)}, u32[]{:S(2)}) copy-start(f32[8,16,16]{2,1,0:T(8,128)} %param.14) | copy-start | bytes 24580
  0.0 5.7 %copy-start.6 = (f32[1,1,512,512]{3,2,1,0:T(8,128)S(1)}, f32[1,1,512,512]{3,2,1,0:T(8,128)}, u32[]{:S(2)}) copy-start(f32[1,1,512,512]{3,2,1,0:T(8,128)} %param.11) | copy-start | bytes 3145732
  18.8 73.4 %all-to-all-start = ((f32[1,3,4,4,128,128]{5,4,2,1,0,3:T(8,128)}), f32[1,3,4,4,128,128]{5,4,2,1,0,3:T(8,128)S(1)}, u32[]{:S(2)}, u32[]{:S(2)}) async-start(f32[1,3,4,4,128,128]{5,4,2,1,0,3:T(8,128)} %copy.87), calls=%async_computation | async-start | bytes 6291456 | tf_op jit(solution)/shard_map/all_to_all | solution.py:94
  27.7 71.4 %copy-start.10 = (f32[1,1,3,512]{3,1,2,0:T(1,128)S(1)}, f32[1,1,3,512]{3,1,2,0:T(1,128)}, u32[]{:S(2)}) copy-start(f32[1,1,3,512]{3,1,2,0:T(1,128)} %param.13) | copy-start | bytes 18436
  27.7 71.6 %copy-start.2 = (s32[4,1]{0,1:T(1,128)S(1)}, s32[4,1]{0,1:T(1,128)}, u32[]{:S(2)}) copy-start(s32[4,1]{0,1:T(1,128)} %param.17) | copy-start | bytes 52
  92.2 74.9 %all-to-all-start.1 = ((f32[1,3,4,4,128,128]{5,4,2,1,0,3:T(8,128)}), f32[1,3,4,4,128,128]{5,4,2,1,0,3:T(8,128)}, u32[]{:S(2)}, u32[]{:S(2)}) async-start(f32[1,3,4,4,128,128]{5,4,2,1,0,3:T(8,128)} %copy.91), calls=%async_computation.1 | async-start | bytes 6291456 | tf_op jit(solution)/shard_map/all_to_all | solution.py:95
  181.3 7.6 %copy-start.5 = (f32[3,512,512]{2,1,0:T(8,128)S(1)}, f32[3,512,512]{2,1,0:T(8,128)}, u32[]{:S(2)}) copy-start(f32[3,512,512]{2,1,0:T(8,128)} %squeeze_reshape.4) | copy-start | bytes 9437188
  205.6 6.2 %copy-start.3 = (s32[1,1,16]{2,1,0:T(1,128)S(1)}, s32[1,1,16]{2,1,0:T(1,128)}, u32[]{:S(2)}) copy-start(s32[1,1,16]{2,1,0:T(1,128)} %param.16) | copy-start | bytes 196
  205.6 7.0 %copy-start.4 = (s32[4,1]{0,1:T(1,128)S(1)}, s32[4,1]{0,1:T(1,128)}, u32[]{:S(2)}) copy-start(s32[4,1]{0,1:T(1,128)} %param.15) | copy-start | bytes 52
  205.6 7.7 %copy-start.9 = (f32[1,1,512]{2,1,0:T(1,128)S(1)}, f32[1,1,512]{2,1,0:T(1,128)}, u32[]{:S(2)}) copy-start(f32[1,1,512]{2,1,0:T(1,128)} %param.12) | copy-start | bytes 6148
  205.6 74.0 %all-to-all-start.2 = ((f32[1,3,4,4,128,128]{5,4,2,1,0,3:T(8,128)}), f32[1,3,4,4,128,128]{5,4,2,1,0,3:T(8,128)S(1)}, u32[]{:S(2)}, u32[]{:S(2)}) async-start(f32[1,3,4,4,128,128]{5,4,2,1,0,3:T(8,128)} %copy.96), calls=%async_computation.2 | async-start | bytes 6291456 | tf_op jit(solution)/shard_map/all_to_all | solution.py:104
  281.4 3.4 %copy-start.7 = (f32[1,1,512,512]{3,2,1,0:T(8,128)S(1)}, f32[1,1,512,512]{3,2,1,0:T(8,128)}, u32[]{:S(2)}) copy-start(f32[1,1,512,512]{3,2,1,0:T(8,128)} %param.11) | copy-start | bytes 3145732
  281.4 3.4 %copy-start.8 = (f32[1,1,512,512]{3,2,1,0:T(8,128)S(1)}, f32[1,1,512,512]{3,2,1,0:T(8,128)}, u32[]{:S(2)}) copy-start(f32[1,1,512,512]{3,2,1,0:T(8,128)} %param.10) | copy-start | bytes 3145732
  284.8 4.8 %copy-start.1 = (f32[8,16,16]{2,1,0:T(8,128)S(1)}, f32[8,16,16]{2,1,0:T(8,128)}, u32[]{:S(2)}) copy-start(f32[8,16,16]{2,1,0:T(8,128)} %param.14) | copy-start | bytes 24580
where the time goes:
time: 294 us; the launch traced here: 290 us
  waiting for transfers between devices  182 us (62%)
  local copies, waits for them, and re-layouts  48.8 us (17%)
  matrix products  31.1 us (11%)
  starting transfers between devices  18.2 us (6%)
  other arithmetic  9.05 us (3%)
    all_to_all x1, waiting for transfers between devices, body(): lax.all_to_all(generator_send, 'chan', split_axis=3, concat_axis=3, tiled...  64.4 us
    all_to_all x1, waiting for transfers between devices, body(): lax.all_to_all(returned.reshape(column_count, capacity, spread, channels,...  61.9 us
    all_to_all x1, waiting for transfers between devices, body(): lax.all_to_all(hamilton_send, 'chan', split_axis=3, concat_axis=3, tiled=...  55.8 us
    dot_general x2, matrix products, bracket(): jnp.matmul(left_matrix * scaled, right_matrix, precision=highest)  11.5 us
    dot_general x2, matrix products, bracket(): jnp.matmul(right_matrix * scaled, left_matrix, precision=highest)  10.8 us
    all_to_all x1, starting transfers between devices, body(): lax.all_to_all(hamilton_send, 'chan', split_axis=3, concat_axis=3, tiled=...  6.96 us
    all_to_all x1, starting transfers between devices, body(): lax.all_to_all(returned.reshape(column_count, capacity, spread, channels,...  6.17 us
  transfers between devices with their start and end apart: 3, of which 3 were waited for; matrix products, arithmetic and copies ran while one was open for 8% of the time, Pallas kernels for 0%

commit v1 on v0

v1 whole, which is shorter than its diff:
```python
import math

import jax
import jax.numpy as jnp
from jax import lax
from jax.sharding import PartitionSpec as P

TS = 128


highest = lax.Precision.HIGHEST


def to_tiles(matrix, tile_size):
    leading = matrix.shape[:-2]
    blocks = matrix.shape[-1] // tile_size
    shaped = matrix.reshape(leading + (blocks, tile_size, blocks, tile_size))
    shaped = jnp.swapaxes(shaped, -3, -2)
    return shaped.reshape(leading + (blocks * blocks, tile_size, tile_size))


def from_tiles(pieces, tile_size):
    leading = pieces.shape[:-3]
    blocks = math.isqrt(pieces.shape[-3])
    shaped = pieces.reshape(leading + (blocks, blocks, tile_size, tile_size))
    shaped = jnp.swapaxes(shaped, -3, -2)
    return shaped.reshape(leading + (blocks * tile_size, blocks * tile_size))


def bracket(left_matrix, right_matrix, weights):
    scaled = weights[..., None, :]
    left_term = jnp.matmul(left_matrix * scaled, right_matrix, precision=highest)
    right_term = jnp.matmul(right_matrix * scaled, left_matrix, precision=highest)
    return left_term - right_term


def body(
    generator,
    hamiltonian,
    pair_weights,
    cross_weights,
    recoupling,
    cross_owner,
    tile_order,
    recoupling_index,
):
    channels = cross_owner.shape[0]
    tile_count = tile_order.shape[-1]
    spread = tile_count // channels
    capacity = cross_weights.shape[2]
    me = lax.axis_index("chan")
    chan_range = jnp.arange(channels, dtype=jnp.int32)
    tile_range = jnp.arange(tile_count, dtype=jnp.int32)

    order = tile_order[0, 0]
    owners = cross_owner[:, 0]
    earlier = chan_range[None, :] < chan_range[:, None]
    same_owner = owners[:, None] == owners[None, :]
    slot_of = jnp.sum((same_owner & earlier).astype(jnp.int32), axis=1)

    generator_tiles = to_tiles(generator[0, 0], TS)
    hamilton_tiles = to_tiles(hamiltonian[0, 0], TS)
    send = jnp.stack([generator_tiles[order], hamilton_tiles[order]], axis=1)
    send = send.reshape(channels, spread, 2, TS, TS)
    got = lax.all_to_all(send, "chan", 0, 0, tiled=True)

    weight_send = cross_weights[0, 0][jnp.clip(slot_of, 0, capacity - 1)]
    weight_got = lax.all_to_all(weight_send, "chan", 0, 0, tiled=True)
    weights_cross = weight_got[owners[me]]

    cross = jnp.swapaxes(got, 0, 1).reshape(tile_count, 2, TS, TS)
    mixer = recoupling[recoupling_index[me, 0]]
    generator_mixed = jnp.einsum("ji,ixy->jxy", mixer, cross[:, 0], precision=highest)
    hamilton_mixed = jnp.einsum("ji,ixy->jxy", mixer, cross[:, 1], precision=highest)
    product = bracket(
        from_tiles(generator_mixed, TS), from_tiles(hamilton_mixed, TS), weights_cross
    )
    back = jnp.einsum("ji,jxy->ixy", mixer, to_tiles(product, TS), precision=highest)
    back = jnp.swapaxes(back.reshape(spread, channels, TS, TS), 0, 1)
    home = lax.all_to_all(back, "chan", 0, 0, tiled=True)
    inverse = jnp.zeros((tile_count,), jnp.int32).at[order].set(tile_range)
    returned = home.reshape(tile_count, TS, TS)[inverse]

    direct = bracket(generator[0, 0], hamiltonian[0, 0], pair_weights[0, 0])
    summed = direct + from_tiles(returned, TS)
    return (0.5 * (summed + summed.T))[None, None]


def solution(mesh):
    placed = (
        P(("groups", "chan"), ("tile", "rep"), None, None),
        P(("groups", "chan"), ("tile", "rep"), None, None),
        P(("groups", "chan"), ("tile", "rep"), None),
        P(("groups", "chan"), ("tile", "rep"), None, None),
        P(),
        P("groups", ("tile", "rep")),
        P(("groups", "chan"), ("tile", "rep"), None),
        P("groups", ("tile", "rep")),
    )
    return jax.shard_map(
        body,
        mesh=mesh,
        in_specs=placed,
        out_specs=P(("groups", "chan"), ("tile", "rep"), None, None),
        check_vma=False,
    )
```

time: 294 us -> 120 us (0.41)
  the two profiles are of different devices: /device:TPU:28 before, /device:TPU:0 now
where the time goes in v1:
time: 120 us
  waiting for transfers between devices  64.3 us (54%)
  local copies, waits for them, and re-layouts  19.2 us (16%)
  starting transfers between devices  15.2 us (13%)
  matrix products  12.6 us (10%)
  between operations  4.22 us (4%)
  other arithmetic  4.18 us (3%)
    all_to_all x1, waiting for transfers between devices, body(): got = lax.all_to_all(send, 'chan', 0, 0, tiled=True)  42.9 us
    all_to_all x1, waiting for transfers between devices, body(): home = lax.all_to_all(back, 'chan', 0, 0, tiled=True)  21.5 us
    all_to_all x1, starting transfers between devices, body(): weight_got = lax.all_to_all(weight_send, 'chan', 0, 0, tiled=True)  6.32 us
    all_to_all x1, starting transfers between devices, body(): got = lax.all_to_all(send, 'chan', 0, 0, tiled=True)  5.22 us
    dot_general x2, matrix products, bracket(): jnp.matmul(left_matrix * scaled, right_matrix, precision=highest)  4.7 us
    dot_general x2, matrix products, bracket(): jnp.matmul(right_matrix * scaled, left_matrix, precision=highest)  3.8 us
    all_to_all x1, starting transfers between devices, body(): home = lax.all_to_all(back, 'chan', 0, 0, tiled=True)  3.7 us
    gather x2, local copies, waits for them, and re-layouts, body(): send = jnp.stack([generator_tiles[order], hamilton_tiles[order]], axis=1)  3.17 us
  transfers between devices with their start and end apart: 3, of which 2 were waited for; matrix products, arithmetic and copies ran while one was open for 13% of the time, Pallas kernels for 0%

profile of v1, /device:TPU:0, one launch (start us, length us, event | category | flops | bytes accessed | tf_op | source)
XLA Modules:
  0.0 119.8 jit_solution(7806554461178340481)
XLA Ops:
  0.0 0.7 copy.71
  0.7 0.9 convert_reduce_fusion
  1.7 0.6 gather_fusion.2
  2.2 0.6 copy.40
  2.8 6.3 %all-to-all-start.1 = ((f32[4,1,512]{2,1,0:T(1,128)}), f32[4,1,512]{2,1,0:T(1,128)S(1)}, u32[]{:S(2)}, u32[]{:S(2)}) async-start(f32[4,1,512]{2,1,0:T(1,128)} %copy.40), calls=%async_computation.1 | async-start | bytes 16384 | tf_op jit(solution)/shard_map/all_to_all | solution.py:68
  9.1 0.7 fusion.24
  9.8 1.7 %reshape_squeeze.6 = f32[4,128,4,128]{3,2,1,0:T(4,128)S(1)} reshape(f32[1,1,512,512]{3,2,1,0:T(8,128)} %param.8) | data formatting | bytes 2097152 | tf_op jit(solution)/shard_map/reshape;squeeze | solution.py:17
  11.6 1.3 %reshape_squeeze.7 = f32[4,128,4,128]{3,2,1,0:T(4,128)} reshape(f32[1,1,512,512]{3,2,1,0:T(8,128)S(1)} %copy-done.1) | data formatting | bytes 2097152 | tf_op jit(solution)/shard_map/reshape;squeeze | solution.py:17
  12.9 1.3 %copy.37 = f32[4,4,128,128]{3,2,1,0:T(8,128)S(1)} copy(f32[4,4,128,128]{3,1,2,0:T(4,128)} %bitcast.130) | data formatting | bytes 2097152 | tf_op jit(solution)/shard_map/transpose | solution.py:18
  14.3 1.6 %gather_fusion = f32[16,128,128]{2,1,0:T(8,128)} fusion(f32[16,128,128]{2,1,0:T(8,128)S(1)} %bitcast.123, s32[1024]{0:T(1024)S(1)} %pad_clamp_fusion.2), kind=kCustom, calls=%fused_computation | custom fusion | bytes 2097216 | tf_op jit(solution)/shard_map/gather | solution.py:63
  15.8 1.6 %gather_fusion.1 = f32[16,128,128]{2,1,0:T(8,128)} fusion(f32[16,128,128]{2,1,0:T(8,128)S(1)} %bitcast.124, s32[1024]{0:T(1024)S(1)} %pad_clamp_fusion.2), kind=kCustom, calls=%fused_computation.1 | custom fusion | bytes 2097216 | tf_op jit(solution)/shard_map/gather | solution.py:63
  17.4 1.4 %pad_maximum_fusion = f32[4,4,2,128,128]{4,3,1,0,2:T(8,128)S(1)} fusion(f32[4,4,1,128,128]{4,3,1,0,2:T(8,128)} %bitcast.132, f32[4,4,1,128,128]{4,3,1,0,2:T(8,128)S(1)} %bitcast.131), kind=kLoop, calls=%fused_computation.5 | loop fusion | flops 524288 | bytes 4194304 | tf_op jit(solution)/shard_map/stack | solution.py:63
  18.8 1.5 %copy.38 = f32[4,4,2,128,128]{4,3,1,2,0:T(8,128)} copy(f32[4,4,2,128,128]{4,3,1,0,2:T(8,128)S(1)} %pad_maximum_fusion) | data formatting | bytes 4194304 | tf_op jit(solution)/shard_map/stack | solution.py:63
  20.3 5.2 %all-to-all-start = ((f32[4,4,2,128,128]{4,3,1,2,0:T(8,128)}), f32[4,4,2,128,128]{4,3,1,2,0:T(8,128)S(1)}, u32[]{:S(2)}, u32[]{:S(2)}) async-start(f32[4,4,2,128,128]{4,3,1,2,0:T(8,128)} %copy.38), calls=%async_computation | async-start | bytes 4194304 | tf_op jit(solution)/shard_map/all_to_all | solution.py:65
  25.5 0.7 constant_dynamic-slice_fusion.1
  30.3 42.9 %all-to-all-done = f32[4,4,2,128,128]{4,3,1,2,0:T(8,128)S(1)} async-done(((f32[4,4,2,128,128]{4,3,1,2,0:T(8,128)}), f32[4,4,2,128,128]{4,3,1,2,0:T(8,128)S(1)}, u32[]{:S(2)}, u32[]{:S(2)}) %all-to-all-start) | async-done | bytes 2097184 | tf_op jit(solution)/shard_map/all_to_all | solution.py:65
  73.2 1.4 %copy.39 = f32[4,4,2,128,128]{4,1,0,3,2:T(4,128)S(1)} copy(f32[4,4,2,128,128]{4,3,0,2,1:T(8,128)S(1)} %bitcast.118) | data formatting | bytes 4194304 | tf_op jit(solution)/shard_map/transpose | solution.py:71
  74.5 1.3 %fusion.11 = f32[4,4,128,128]{3,1,2,0:T(4,128)S(1)} fusion(f32[4,4,16,1]{2,1,3,0:T(4,128)S(1)} %bitcast.134, f32[16,2,128,128]{3,0,2,1:T(8,128)S(1)} %bitcast.116), kind=kOutput, calls=%fused_computation.22 | convolution fusion | flops 50331648 | bytes 2105344 | tf_op jit(solution)/shard_map/ji,ixy->jxy/dot_general | solution.py:73
  75.8 1.6 %bitcast_multiply_fusion = (f32[4,128,4,128]{3,2,1,0:T(4,128)S(1)}, f32[4,128,4,128]{3,2,1,0:T(4,128)S(1)}, f32[4,4,128,128]{3,1,2,0:T(4,128)S(1)}) fusion(f32[4,128]{1,0:T(4,128)S(1)} %bitcast.138, f32[4,4,128,128]{3,1,2,0:T(4,128)S(1)} %fusion.11, f32[4,4,16,1]{2,1,3,0:T(4,128)S(1)} %bitcast.135, f32[16,2,128,128]{3,0,2,1:T(8,128)S(1)} %bitcast.117), kind=kOutput, calls=%fused_computation.26 | convolution fusion | flops 50855936 | bytes 5253120 | tf_op jit(solution)/shard_map/ji,ixy->jxy/dot_general | solution.py:74
  77.4 1.8 %fusion.5 = f32[512,512]{1,0:T(8,128)S(1)} fusion(f32[64,8,4,128]{3,2,1,0:T(4,128)S(1)} %bitcast.120, f32[64,8,4,128]{3,2,1,0:T(4,128)S(1)} %bitcast.119), kind=kOutput, calls=%fused_computation.14 | convolution fusion | flops 1610612736 | bytes 3145728 | tf_op jit(solution)/shard_map/dot_general | solution.py:32
  79.2 1.9 %convolution_subtract_fusion = f32[512,512]{1,0:T(8,128)S(1)} fusion(f32[512,512]{1,0:T(8,128)S(1)} %fusion.5, f32[64,8,4,128]{3,2,1,0:T(4,128)S(1)} %bitcast.115, f32[64,8,4,128]{3,2,1,0:T(4,128)S(1)} %bitcast.126), kind=kOutput, calls=%fused_computation.7 | convolution fusion | flops 1610874880 | bytes 4194304 | tf_op jit(solution)/shard_map/dot_general | solution.py:33
  81.1 0.4 reshape.129
  81.6 1.3 %convolution_bitcast_fusion = f32[4,4,128,128]{3,0,2,1:T(4,128)S(1)} fusion(f32[4,4,16,1]{2,1,3,0:T(4,128)S(1)} %bitcast.136, f32[16,128,128,1]{2,0,1,3:T(8,128)S(1)} %bitcast.127), kind=kOutput, calls=%fused_computation.6 | convolution fusion | flops 50331648 | bytes 2098176 | tf_op jit(solution)/shard_map/ji,jxy->ixy/dot_general | solution.py:78
  82.9 1.1 copy.42
  84.0 3.7 %all-to-all-start.2 = ((f32[4,4,128,128]{3,2,1,0:T(8,128)}), f32[4,4,128,128]{3,2,1,0:T(8,128)S(1)}, u32[]{:S(2)}, u32[]{:S(2)}) async-start(f32[4,4,128,128]{3,2,1,0:T(8,128)} %copy.42), calls=%async_computation.2 | async-start | bytes 2097152 | tf_op jit(solution)/shard_map/all_to_all | solution.py:80
  87.7 0.6 scatter_custom_fusion
  88.4 2.9 %fusion.16 = f32[512,512]{1,0:T(8,128)} fusion(f32[1,1,512,512]{3,2,1,0:T(8,128)S(1)} %copy-done.1, f32[1,1,512,512]{3,2,1,0:T(8,128)S(1)} %copy-done.2, f32[512]{0:T(512)S(1)} %bitcast.139), kind=kOutput, calls=%fused_computation.30 | convolution fusion | flops 1610874880 | bytes 3147776 | tf_op jit(solution)/shard_map/dot_general | solution.py:32
  91.3 21.5 %all-to-all-done.2 = f32[4,4,128,128]{3,2,1,0:T(8,128)S(1)} async-done(((f32[4,4,128,128]{3,2,1,0:T(8,128)}), f32[4,4,128,128]{3,2,1,0:T(8,128)S(1)}, u32[]{:S(2)}, u32[]{:S(2)}) %all-to-all-start.2) | async-done | bytes 1048608 | tf_op jit(solution)/shard_map/all_to_all | solution.py:80
  112.7 1.6 %gather_fusion.3 = f32[16,128,128]{2,1,0:T(8,128)} fusion(f32[16,128,128]{2,1,0:T(8,128)S(1)} %bitcast.122, s32[1024]{0:T(1024)S(1)} %pad_clamp_fusion), kind=kCustom, calls=%fused_computation.3 | custom fusion | bytes 2097216 | tf_op jit(solution)/shard_map/gather | solution.py:82
  114.3 2.0 %copy.43 = f32[4,128,4,128]{3,2,1,0:T(4,128)S(1)} copy(f32[4,128,4,128]{3,1,2,0:T(8,128)} %bitcast.125) | data formatting | bytes 2097152 | tf_op jit(solution)/shard_map/transpose | solution.py:26
  116.3 1.9 %fusion = f32[512,512]{1,0:T(8,128)S(1)} fusion(f32[512,512]{1,0:T(8,128)S(1)} %copy-done.3, f32[64,8,4,128]{3,2,1,0:T(4,128)S(1)} %bitcast.121, f32[1,1,512,512]{3,2,1,0:T(8,128)S(1)} %copy-done.2, f32[1,1,512,512]{3,2,1,0:T(8,128)S(1)} %copy-done.1, f32[512]{0:T(512)S(1)} %bitcast.140), kind=kOutput, calls=%fused_computation.9 | convolution fusion | flops 1611399168 | bytes 5244928 | tf_op jit(solution)/shard_map/dot_general | solution.py:33
  118.6 1.2 fusion.13
  (30 shorter events, 0.8 us)
Async XLA Ops:
  0.0 29.5 %copy-start = (f32[8,16,16]{2,1,0:T(8,128)S(1)}, f32[8,16,16]{2,1,0:T(8,128)}, u32[]{:S(2)}) copy-start(f32[8,16,16]{2,1,0:T(8,128)} %param.12) | copy-start | bytes 24580
  2.8 17.5 %all-to-all-start.1 = ((f32[4,1,512]{2,1,0:T(1,128)}), f32[4,1,512]{2,1,0:T(1,128)S(1)}, u32[]{:S(2)}, u32[]{:S(2)}) async-start(f32[4,1,512]{2,1,0:T(1,128)} %copy.40), calls=%async_computation.1 | async-start | bytes 16384 | tf_op jit(solution)/shard_map/all_to_all | solution.py:68
  9.8 1.8 %copy-start.1 = (f32[1,1,512,512]{3,2,1,0:T(8,128)S(1)}, f32[1,1,512,512]{3,2,1,0:T(8,128)}, u32[]{:S(2)}) copy-start(f32[1,1,512,512]{3,2,1,0:T(8,128)} %param.9) | copy-start | bytes 3145732
  15.8 1.6 %copy-start.4 = (f32[16,128,128]{2,1,0:T(8,128)S(1)}, f32[16,128,128]{2,1,0:T(8,128)}, u32[]{:S(2)}) copy-start(f32[16,128,128]{2,1,0:T(8,128)} %gather_fusion) | copy-start | bytes 3145732
  20.3 5.2 %copy-start.6 = (s32[4,1]{0,1:T(1,128)S(1)}, s32[4,1]{0,1:T(1,128)}, u32[]{:S(2)}) copy-start(s32[4,1]{0,1:T(1,128)} %param.13) | copy-start | bytes 52
  20.3 5.2 %copy-start.7 = (s32[4,1]{0,1:T(1,128)S(1)}, s32[4,1]{0,1:T(1,128)}, u32[]{:S(2)}) copy-start(s32[4,1]{0,1:T(1,128)} %param.15) | copy-start | bytes 52
  20.3 52.9 %all-to-all-start = ((f32[4,4,2,128,128]{4,3,1,2,0:T(8,128)}), f32[4,4,2,128,128]{4,3,1,2,0:T(8,128)S(1)}, u32[]{:S(2)}, u32[]{:S(2)}) async-start(f32[4,4,2,128,128]{4,3,1,2,0:T(8,128)} %copy.38), calls=%async_computation | async-start | bytes 4194304 | tf_op jit(solution)/shard_map/all_to_all | solution.py:65
  82.9 5.5 %copy-start.2 = (f32[1,1,512,512]{3,2,1,0:T(8,128)S(1)}, f32[1,1,512,512]{3,2,1,0:T(8,128)}, u32[]{:S(2)}) copy-start(f32[1,1,512,512]{3,2,1,0:T(8,128)} %param.8) | copy-start | bytes 3145732
  82.9 5.5 %copy-start.5 = (f32[1,1,512]{2,1,0:T(1,128)S(1)}, f32[1,1,512]{2,1,0:T(1,128)}, u32[]{:S(2)}) copy-start(f32[1,1,512]{2,1,0:T(1,128)} %param.10) | copy-start | bytes 6148
  84.0 28.7 %all-to-all-start.2 = ((f32[4,4,128,128]{3,2,1,0:T(8,128)}), f32[4,4,128,128]{3,2,1,0:T(8,128)S(1)}, u32[]{:S(2)}, u32[]{:S(2)}) async-start(f32[4,4,128,128]{3,2,1,0:T(8,128)} %copy.42), calls=%async_computation.2 | async-start | bytes 2097152 | tf_op jit(solution)/shard_map/all_to_all | solution.py:80
  114.3 2.0 %copy-start.3 = (f32[512,512]{1,0:T(8,128)S(1)}, f32[512,512]{1,0:T(8,128)}, u32[]{:S(2)}) copy-start(f32[512,512]{1,0:T(8,128)} %fusion.16) | copy-start | bytes 3145732

commit v2 on v1

--- a/solution.py
+++ b/solution.py
@@ -50,6 +50,7 @@
     capacity = cross_weights.shape[2]
     me = lax.axis_index("chan")
     chan_range = jnp.arange(channels, dtype=jnp.int32)
+    spread_range = jnp.arange(spread, dtype=jnp.int32)
     tile_range = jnp.arange(tile_count, dtype=jnp.int32)
 
     order = tile_order[0, 0]
@@ -58,28 +59,44 @@
     same_owner = owners[:, None] == owners[None, :]
     slot_of = jnp.sum((same_owner & earlier).astype(jnp.int32), axis=1)
 
+    dest = (me + chan_range) % channels
+    source = (me - chan_range) % channels
     generator_tiles = to_tiles(generator[0, 0], TS)
     hamilton_tiles = to_tiles(hamiltonian[0, 0], TS)
-    send = jnp.stack([generator_tiles[order], hamilton_tiles[order]], axis=1)
-    send = send.reshape(channels, spread, 2, TS, TS)
-    got = lax.all_to_all(send, "chan", 0, 0, tiled=True)
+    picked = order[dest[:, None] * spread + spread_range[None, :]]
+    send = jnp.stack([generator_tiles[picked], hamilton_tiles[picked]], axis=2)
+    weight_send = cross_weights[0, 0][jnp.clip(slot_of[dest], 0, capacity - 1)]
+    got = [send[0]]
+    weight_got = [weight_send[0]]
+    for shift in range(1, channels):
+        pairs = [(c, (c + shift) % channels) for c in range(channels)]
+        tiles_in, weights_in = lax.ppermute((send[shift], weight_send[shift]), "chan", pairs)
+        got.append(tiles_in)
+        weight_got.append(weights_in)
+    got = jnp.stack(got)
+    weights_cross = jnp.stack(weight_got)[(me - owners[me]) % channels]
 
-    weight_send = cross_weights[0, 0][jnp.clip(slot_of, 0, capacity - 1)]
-    weight_got = lax.all_to_all(weight_send, "chan", 0, 0, tiled=True)
-    weights_cross = weight_got[owners[me]]
-
-    cross = jnp.swapaxes(got, 0, 1).reshape(tile_count, 2, TS, TS)
     mixer = recoupling[recoupling_index[me, 0]]
-    generator_mixed = jnp.einsum("ji,ixy->jxy", mixer, cross[:, 0], precision=highest)
-    hamilton_mixed = jnp.einsum("ji,ixy->jxy", mixer, cross[:, 1], precision=highest)
+    column_of = (spread_range[None, :] * channels + source[:, None]).reshape(-1)
+    mixer_in = mixer[:, column_of]
+    cross = got.reshape(tile_count, 2, TS, TS)
+    generator_mixed = jnp.einsum("ji,ixy->jxy", mixer_in, cross[:, 0], precision=highest)
+    hamilton_mixed = jnp.einsum("ji,ixy->jxy", mixer_in, cross[:, 1], precision=highest)
     product = bracket(
         from_tiles(generator_mixed, TS), from_tiles(hamilton_mixed, TS), weights_cross
     )
-    back = jnp.einsum("ji,jxy->ixy", mixer, to_tiles(product, TS), precision=highest)
-    back = jnp.swapaxes(back.reshape(spread, channels, TS, TS), 0, 1)
-    home = lax.all_to_all(back, "chan", 0, 0, tiled=True)
+    mixer_out = mixer[:, (spread_range[None, :] * channels + dest[:, None]).reshape(-1)]
+    back = jnp.einsum("ji,jxy->ixy", mixer_out, to_tiles(product, TS), precision=highest)
+    back = back.reshape(channels, spread, TS, TS)
+    home = [back[0]]
+    for shift in range(1, channels):
+        pairs = [(c, (c + shift) % channels) for c in range(channels)]
+        home.append(lax.ppermute(back[shift], "chan", pairs))
+    home = jnp.stack(home)
     inverse = jnp.zeros((tile_count,), jnp.int32).at[order].set(tile_range)
-    returned = home.reshape(tile_count, TS, TS)[inverse]
+    from_g = inverse // spread
+    at_shift = (me - from_g) % channels
+    returned = home[at_shift, inverse % spread]
 
     direct = bracket(generator[0, 0], hamiltonian[0, 0], pair_weights[0, 0])
     summed = direct + from_tiles(returned, TS)

time: 120 us -> 115 us (0.958)
  the two profiles are of different devices: /device:TPU:0 before, /device:TPU:28 now
where the time goes in v2:
time: 115 us; the launch traced here: 114 us
  waiting for transfers between devices  52.9 us (46%)
  local copies, waits for them, and re-layouts  24.6 us (21%)
  matrix products  13.3 us (12%)
  starting transfers between devices  12.9 us (11%)
  other arithmetic  7.79 us (7%)
  between operations  2.82 us (2%)
    ppermute x6, waiting for transfers between devices, body(): lax.ppermute((send[shift], weight_send[shift]), 'chan', pairs)  33.1 us
    ppermute x3, waiting for transfers between devices, body(): home.append(lax.ppermute(back[shift], 'chan', pairs))  19.8 us
    ppermute x6, starting transfers between devices, body(): lax.ppermute((send[shift], weight_send[shift]), 'chan', pairs)  8.16 us
    dot_general x2, matrix products, bracket(): jnp.matmul(right_matrix * scaled, left_matrix, precision=highest)  4.79 us
    ppermute x3, starting transfers between devices, body(): home.append(lax.ppermute(back[shift], 'chan', pairs))  4.78 us
    dot_general x2, matrix products, bracket(): jnp.matmul(left_matrix * scaled, right_matrix, precision=highest)  4.7 us
    gather x2, local copies, waits for them, and re-layouts, body(): send = jnp.stack([generator_tiles[picked], hamilton_tiles[picked]], axis=2)  4.49 us
    transpose x3, local copies, waits for them, and re-layouts, to_tiles(): shaped = jnp.swapaxes(shaped, -3, -2)  3.84 us
  transfers between devices with their start and end apart: 9, of which 4 were waited for; matrix products, arithmetic and copies ran while one was open for 18% of the time, Pallas kernels for 0%

profile of v2, /device:TPU:28, one launch (start us, length us, event | category | flops | bytes accessed | tf_op | source)
XLA Modules:
  0.0 114.3 jit_solution(18321892358397157783)
XLA Ops:
  0.0 0.9 convert_reduce_fusion
  3.2 1.7 %collective-permute-start.4 = (f32[512]{0:T(512)S(1)}, f32[512]{0:T(512)S(1)}, u32[]{:S(2)}, u32[]{:S(2)}) collective-permute-start(f32[512]{0:T(512)S(1)} %bitcast.172), channel_id=1, source_target_pairs={{0,8},{4,12},{8,0},{12,4},{1,9},{5,13},{9,1},{13,5},{2,10},{6,14},... | collective-permute-start | bytes 6152 | tf_op jit(solution)/shard_map/ppermute | solution.py:73
  5.9 1.3 %reshape_squeeze.6 = f32[4,128,4,128]{3,2,1,0:T(4,128)} reshape(f32[1,1,512,512]{3,2,1,0:T(8,128)S(1)} %copy-done.3) | data formatting | bytes 2097152 | tf_op jit(solution)/shard_map/reshape;squeeze | solution.py:17
  7.3 1.3 %copy.42 = f32[4,4,128,128]{3,2,1,0:T(8,128)S(1)} copy(f32[4,4,128,128]{3,1,2,0:T(4,128)} %bitcast.152) | data formatting | bytes 2097152 | tf_op jit(solution)/shard_map/transpose | solution.py:18
  8.6 1.3 %reshape_squeeze.7 = f32[4,128,4,128]{3,2,1,0:T(4,128)} reshape(f32[1,1,512,512]{3,2,1,0:T(8,128)S(1)} %copy-done.2) | data formatting | bytes 2097152 | tf_op jit(solution)/shard_map/reshape;squeeze | solution.py:17
  9.9 2.3 %copy.43 = f32[4,4,128,128]{3,2,1,0:T(8,128)} copy(f32[4,4,128,128]{3,1,2,0:T(4,128)} %bitcast.153) | data formatting | bytes 2097152 | tf_op jit(solution)/shard_map/transpose | solution.py:18
  12.2 1.6 %gather_fusion.3 = f32[16,128,128]{2,1,0:T(8,128)} fusion(f32[16,128,128]{2,1,0:T(8,128)S(1)} %bitcast.146, s32[1024]{0:T(1024)S(1)} %pad_clamp_fusion.2), kind=kCustom, calls=%fused_computation.3 | custom fusion | bytes 2097216 | tf_op jit(solution)/shard_map/gather | solution.py:67
  13.8 2.9 %gather_fusion.4 = f32[16,128,128]{2,1,0:T(8,128)} fusion(f32[16,128,128]{2,1,0:T(8,128)} %bitcast.147, s32[1024]{0:T(1024)S(1)} %pad_clamp_fusion.2), kind=kCustom, calls=%fused_computation.4 | custom fusion | bytes 2097216 | tf_op jit(solution)/shard_map/gather | solution.py:67
  16.7 2.7 %fusion.24 = (f32[1,4,2,128,128]{4,3,1,2,0:T(8,128)}, f32[4,2,128,128]{3,2,0,1:T(8,128)}, f32[4,2,128,128]{3,2,0,1:T(8,128)}, f32[4,2,128,128]{3,2,0,1:T(8,128)}) fusion(f32[4,4,1,128,128]{4,3,1,0,2:T(8,128)S(1)} %bitcast.154, f32[4,4,1,128,128]{4,3,1,0,2:T(8,128)} %bitcast.155), kind=kLoop, calls=%fused_computation.48 | loop fusion | flops 524288 | bytes 4194304
  19.4 2.5 %collective-permute-start = (f32[4,2,128,128]{3,2,0,1:T(8,128)}, f32[4,2,128,128]{3,2,0,1:T(8,128)S(1)}, u32[]{:S(2)}, u32[]{:S(2)}) collective-permute-start(f32[4,2,128,128]{3,2,0,1:T(8,128)} %get-tuple-element.6), channel_id=1, source_target_pairs={{0,4},{4,8},{8,12},{12,0},{1,5},{5,9},{9,13},{13,1},{2,6},{6,10},{... | collective-permute-start | bytes 1572872 | tf_op jit(solution)/shard_map/ppermute | solution.py:73
  24.9 2.9 %fusion.16 = f32[512,512]{1,0:T(8,128)} fusion(f32[1,1,512,512]{3,2,1,0:T(8,128)S(1)} %copy-done.2, f32[1,1,512,512]{3,2,1,0:T(8,128)S(1)} %copy-done.3, f32[512]{0:T(512)S(1)} %bitcast.166), kind=kOutput, calls=%fused_computation.40 | convolution fusion | flops 1610874880 | bytes 3147776 | tf_op jit(solution)/shard_map/dot_general | solution.py:32
  28.4 2.9 %collective-permute-start.5 = (f32[512]{0:T(512)S(1)}, f32[512]{0:T(512)S(1)}, u32[]{:S(2)}, u32[]{:S(2)}) collective-permute-start(f32[512]{0:T(512)S(1)} %bitcast.171), channel_id=1, source_target_pairs={{0,12},{4,0},{8,4},{12,8},{1,13},{5,1},{9,5},{13,9},{2,14},{6,2},{... | collective-permute-start | bytes 6152 | tf_op jit(solution)/shard_map/ppermute | solution.py:73
  33.3 22.9 %collective-permute-done.5 = f32[512]{0:T(512)S(1)} collective-permute-done((f32[512]{0:T(512)S(1)}, f32[512]{0:T(512)S(1)}, u32[]{:S(2)}, u32[]{:S(2)}) %collective-permute-start.5) | collective-permute-done | bytes 2080 | tf_op jit(solution)/shard_map/ppermute | solution.py:73
  56.3 10.2 %collective-permute-done.1 = f32[4,2,128,128]{3,2,0,1:T(8,128)} collective-permute-done((f32[4,2,128,128]{3,2,0,1:T(8,128)}, f32[4,2,128,128]{3,2,0,1:T(8,128)}, u32[]{:S(2)}, u32[]{:S(2)}) %collective-permute-start.1) | collective-permute-done | bytes 524320 | tf_op jit(solution)/shard_map/ppermute | solution.py:73
  66.5 1.4 %pad_maximum_fusion = f32[4,4,2,128,128]{4,3,1,2,0:T(8,128)S(1)} fusion(f32[1,4,2,128,128]{4,3,1,2,0:T(8,128)} %bitcast.26, f32[1,4,2,128,128]{4,3,1,2,0:T(8,128)} %bitcast.24, f32[1,4,2,128,128]{4,3,1,2,0:T(8,128)S(1)} %bitcast.159, f32[1,4,2,128,128]{4,3,1,2,0:T(8,128)S(1)} %copy-done.6), kind=kLoop, calls=%fused_computation.15 | loop fusion | flops 1572864 | bytes 4194304 | tf_op jit(solution)/shard_map/stack | solution.py:76
  67.9 1.4 %copy.47 = f32[4,4,2,128,128]{4,1,0,3,2:T(4,128)S(1)} copy(f32[4,4,2,128,128]{4,3,1,2,0:T(8,128)S(1)} %pad_maximum_fusion) | data formatting | bytes 4194304 | tf_op jit(solution)/shard_map/stack | solution.py:76
  69.3 1.3 %fusion.11 = f32[4,4,128,128]{3,1,2,0:T(4,128)S(1)} fusion(f32[4,4,16,1]{2,1,3,0:T(4,128)S(1)} %bitcast.162, f32[16,2,128,128]{3,0,2,1:T(8,128)S(1)} %bitcast.141), kind=kOutput, calls=%fused_computation.31 | convolution fusion | flops 50331648 | bytes 2105344 | tf_op jit(solution)/shard_map/ji,ixy->jxy/dot_general | solution.py:83
  70.5 1.5 %bitcast_multiply_fusion = (f32[4,128,4,128]{3,2,1,0:T(4,128)S(1)}, f32[4,128,4,128]{3,2,1,0:T(4,128)S(1)}, f32[4,4,128,128]{3,1,2,0:T(4,128)S(1)}) fusion(f32[4,128]{1,0:T(4,128)S(1)} %bitcast.165, f32[4,4,128,128]{3,1,2,0:T(4,128)S(1)} %fusion.11, f32[4,4,16,1]{2,1,3,0:T(4,128)S(1)} %bitcast.163, f32[16,2,128,128]{3,0,2,1:T(8,128)S(1)} %bitcast.142), kind=kOutput, calls=%fused_computation.36 | convolution fusion | flops 50855936 | bytes 5253120 | tf_op jit(solution)/shard_map/ji,ixy->jxy/dot_general | solution.py:84
  72.1 1.8 %fusion.5 = f32[512,512]{1,0:T(8,128)S(1)} fusion(f32[64,8,4,128]{3,2,1,0:T(4,128)S(1)} %bitcast.144, f32[64,8,4,128]{3,2,1,0:T(4,128)S(1)} %bitcast.143), kind=kOutput, calls=%fused_computation.23 | convolution fusion | flops 1610612736 | bytes 3145728 | tf_op jit(solution)/shard_map/dot_general | solution.py:32
  73.9 2.8 %convolution_subtract_fusion = f32[512,512]{1,0:T(8,128)} fusion(f32[512,512]{1,0:T(8,128)S(1)} %fusion.5, f32[64,8,4,128]{3,2,1,0:T(4,128)S(1)} %bitcast.140, f32[64,8,4,128]{3,2,1,0:T(4,128)S(1)} %bitcast.148), kind=kOutput, calls=%fused_computation.16 | convolution fusion | flops 1610874880 | bytes 4194304 | tf_op jit(solution)/shard_map/dot_general | solution.py:33
  76.8 1.6 %reshape.308 = f32[4,128,4,128]{3,2,1,0:T(4,128)S(1)} reshape(f32[512,512]{1,0:T(8,128)} %convolution_subtract_fusion) | data formatting | bytes 2097152 | tf_op jit(solution)/shard_map/reshape | solution.py:17
  78.5 1.0 fusion.30
  79.5 0.9 slice_bitcast_fusion.4
  80.4 2.8 %collective-permute-start.7 = (f32[4,128,128]{2,0,1:T(4,128)S(1)}, f32[4,128,128]{2,0,1:T(4,128)S(1)}, u32[]{:S(2)}, u32[]{:S(2)}) collective-permute-start(f32[4,128,128]{2,0,1:T(4,128)S(1)} %get-tuple-element.11), channel_id=1, source_target_pairs={{0,8},{4,12},{8,0},{12,4},{1,9},{5,13},{9,1},{13,5},{2,10},{6,14},... | collective-permute-start | bytes 786440 | tf_op jit(solution)/shard_map/ppermute | solution.py:94
  83.1 2.0 %collective-permute-start.8 = (f32[4,128,128]{2,0,1:T(4,128)S(1)}, f32[4,128,128]{2,0,1:T(4,128)}, u32[]{:S(2)}, u32[]{:S(2)}) collective-permute-start(f32[4,128,128]{2,0,1:T(4,128)S(1)} %get-tuple-element.10), channel_id=1, source_target_pairs={{0,12},{4,0},{8,4},{12,8},{1,13},{5,1},{9,5},{13,9},{2,14},{6,2},{... | collective-permute-start | bytes 786440 | tf_op jit(solution)/shard_map/ppermute | solution.py:94
  86.0 1.5 %collective-permute-done.6 = f32[4,128,128]{2,0,1:T(4,128)S(1)} collective-permute-done((f32[4,128,128]{2,0,1:T(4,128)}, f32[4,128,128]{2,0,1:T(4,128)S(1)}, u32[]{:S(2)}, u32[]{:S(2)}) %collective-permute-start.6) | collective-permute-done | bytes 262176 | tf_op jit(solution)/shard_map/ppermute | solution.py:94
  87.5 18.3 %collective-permute-done.7 = f32[4,128,128]{2,0,1:T(4,128)S(1)} collective-permute-done((f32[4,128,128]{2,0,1:T(4,128)S(1)}, f32[4,128,128]{2,0,1:T(4,128)S(1)}, u32[]{:S(2)}, u32[]{:S(2)}) %collective-permute-start.7) | collective-permute-done | bytes 262176 | tf_op jit(solution)/shard_map/ppermute | solution.py:94
  105.8 1.3 %pad_maximum_fusion.1 = f32[4,4,128,128]{3,1,2,0:T(4,128)S(1)} fusion(f32[1,4,128,128]{3,1,2,0:T(4,128)} %bitcast.53, f32[1,4,128,128]{3,1,2,0:T(4,128)S(1)} %bitcast.161, f32[1,4,128,128]{3,1,2,0:T(4,128)S(1)} %bitcast.160, f32[1,4,128,128]{3,1,2,0:T(4,128)S(1)} %get-tuple-element.9), kind=kLoop, calls=%fused_computation.32 | loop fusion | flops 786432 | bytes 2097152 | tf_op jit(solution)/shard_map/stack | solution.py:95
  107.2 1.6 %gather_fusion.7 = f32[16,128,128]{2,1,0:T(8,128)} fusion(f32[4,4,128,128]{3,2,1,0:T(8,128)S(1)} %copy.49, s32[16]{0:T(128)S(1)} %fusion.47), kind=kCustom, calls=%fused_computation.7 | custom fusion | bytes 2097280 | tf_op jit(solution)/shard_map/gather | solution.py:99
  108.8 2.0 %copy.50 = f32[4,4,128,128]{3,1,2,0:T(4,128)S(1)} copy(f32[4,4,128,128]{3,2,1,0:T(8,128)} %bitcast.150) | data formatting | bytes 2097152 | tf_op jit(solution)/shard_map/reshape | solution.py:25
  110.8 2.0 %fusion = f32[512,512]{1,0:T(8,128)S(1)} fusion(f32[512,512]{1,0:T(8,128)S(1)} %copy-done.4, f32[64,8,4,128]{3,2,1,0:T(4,128)S(1)} %bitcast.145, f32[1,1,512,512]{3,2,1,0:T(8,128)S(1)} %copy-done.3, f32[1,1,512,512]{3,2,1,0:T(8,128)S(1)} %copy-done.2, f32[512]{0:T(512)S(1)} %bitcast.167), kind=kOutput, calls=%fused_computation.18 | convolution fusion | flops 1611399168 | bytes 5244928 | tf_op jit(solution)/shard_map/dot_general | solution.py:33
  113.1 1.2 %fusion.13 = f32[1,1,512,512]{3,2,1,0:T(8,128)} fusion(f32[512,512]{1,0:T(8,128)S(1)} %fusion, f32[512,512]{0,1:T(8,128)S(1)} %copy.51), kind=kLoop, calls=%fused_computation.35 | loop fusion | flops 524288 | bytes 3145728 | tf_op jit(solution)/shard_map/broadcast_in_dim | solution.py:103
  (69 shorter events, 7.8 us)
Async XLA Ops:
  0.0 28.4 %copy-start = (f32[8,16,16]{2,1,0:T(8,128)S(1)}, f32[8,16,16]{2,1,0:T(8,128)}, u32[]{:S(2)}) copy-start(f32[8,16,16]{2,1,0:T(8,128)} %param.12) | copy-start | bytes 24580
  0.0 5.1 %copy-start.1 = (s32[1,1,16]{2,1,0:T(1,128)S(1)}, s32[1,1,16]{2,1,0:T(1,128)}, u32[]{:S(2)}) copy-start(s32[1,1,16]{2,1,0:T(1,128)} %param.14) | copy-start | bytes 196
  0.0 5.9 %copy-start.3 = (f32[1,1,512,512]{3,2,1,0:T(8,128)S(1)}, f32[1,1,512,512]{3,2,1,0:T(8,128)}, u32[]{:S(2)}) copy-start(f32[1,1,512,512]{3,2,1,0:T(8,128)} %param.8) | copy-start | bytes 3145732
  2.9 25.5 %collective-permute-start.3 = (f32[512]{0:T(512)S(1)}, f32[512]{0:T(512)S(1)}, u32[]{:S(2)}, u32[]{:S(2)}) collective-permute-start(f32[512]{0:T(512)S(1)} %bitcast.173), channel_id=1, source_target_pairs={{0,4},{4,8},{8,12},{12,0},{1,5},{5,9},{9,13},{13,1},{2,6},{6,10},{... | collective-permute-start | bytes 6152 | tf_op jit(solution)/shard_map/ppermute | solution.py:73
  3.2 30.1 %collective-permute-start.4 = (f32[512]{0:T(512)S(1)}, f32[512]{0:T(512)S(1)}, u32[]{:S(2)}, u32[]{:S(2)}) collective-permute-start(f32[512]{0:T(512)S(1)} %bitcast.172), channel_id=1, source_target_pairs={{0,8},{4,12},{8,0},{12,4},{1,9},{5,13},{9,1},{13,5},{2,10},{6,14},... | collective-permute-start | bytes 6152 | tf_op jit(solution)/shard_map/ppermute | solution.py:73
  5.9 2.7 %copy-start.2 = (f32[1,1,512,512]{3,2,1,0:T(8,128)S(1)}, f32[1,1,512,512]{3,2,1,0:T(8,128)}, u32[]{:S(2)}) copy-start(f32[1,1,512,512]{3,2,1,0:T(8,128)} %param.9) | copy-start | bytes 3145732
  13.8 2.9 %copy-start.5 = (f32[16,128,128]{2,1,0:T(8,128)S(1)}, f32[16,128,128]{2,1,0:T(8,128)}, u32[]{:S(2)}) copy-start(f32[16,128,128]{2,1,0:T(8,128)} %gather_fusion.3) | copy-start | bytes 3145732
  16.7 6.0 %copy-start.8 = (s32[4,1]{0,1:T(1,128)S(1)}, s32[4,1]{0,1:T(1,128)}, u32[]{:S(2)}) copy-start(s32[4,1]{0,1:T(1,128)} %param.13) | copy-start | bytes 52
  16.7 6.0 %copy-start.9 = (s32[4,1]{0,1:T(1,128)S(1)}, s32[4,1]{0,1:T(1,128)}, u32[]{:S(2)}) copy-start(s32[4,1]{0,1:T(1,128)} %param.15) | copy-start | bytes 52
  16.7 8.1 %copy-start.7 = (f32[1,1,512]{2,1,0:T(1,128)S(1)}, f32[1,1,512]{2,1,0:T(1,128)}, u32[]{:S(2)}) copy-start(f32[1,1,512]{2,1,0:T(1,128)} %param.10) | copy-start | bytes 6148
  19.4 47.1 %copy-start.6 = (f32[1,4,2,128,128]{4,3,1,2,0:T(8,128)S(1)}, f32[1,4,2,128,128]{4,3,1,2,0:T(8,128)}, u32[]{:S(2)}) copy-start(f32[1,4,2,128,128]{4,3,1,2,0:T(8,128)} %get-tuple-element.5) | copy-start | bytes 1572868
  19.4 36.9 %collective-permute-start = (f32[4,2,128,128]{3,2,0,1:T(8,128)}, f32[4,2,128,128]{3,2,0,1:T(8,128)S(1)}, u32[]{:S(2)}, u32[]{:S(2)}) collective-permute-start(f32[4,2,128,128]{3,2,0,1:T(8,128)} %get-tuple-element.6), channel_id=1, source_target_pairs={{0,4},{4,8},{8,12},{12,0},{1,5},{5,9},{9,13},{13,1},{2,6},{6,10},{... | collective-permute-start | bytes 1572872 | tf_op jit(solution)/shard_map/ppermute | solution.py:73
  21.9 44.6 %collective-permute-start.1 = (f32[4,2,128,128]{3,2,0,1:T(8,128)}, f32[4,2,128,128]{3,2,0,1:T(8,128)}, u32[]{:S(2)}, u32[]{:S(2)}) collective-permute-start(f32[4,2,128,128]{3,2,0,1:T(8,128)} %get-tuple-element.8), channel_id=1, source_target_pairs={{0,8},{4,12},{8,0},{12,4},{1,9},{5,13},{9,1},{13,5},{2,10},{6,14},... | collective-permute-start | bytes 1572872 | tf_op jit(solution)/shard_map/ppermute | solution.py:73
  21.9 44.6 %collective-permute-start.2 = (f32[4,2,128,128]{3,2,0,1:T(8,128)}, f32[4,2,128,128]{3,2,0,1:T(8,128)}, u32[]{:S(2)}, u32[]{:S(2)}) collective-permute-start(f32[4,2,128,128]{3,2,0,1:T(8,128)} %get-tuple-element.7), channel_id=1, source_target_pairs={{0,12},{4,0},{8,4},{12,8},{1,13},{5,1},{9,5},{13,9},{2,14},{6,2},{... | collective-permute-start | bytes 1572872 | tf_op jit(solution)/shard_map/ppermute | solution.py:73
  28.4 27.8 %collective-permute-start.5 = (f32[512]{0:T(512)S(1)}, f32[512]{0:T(512)S(1)}, u32[]{:S(2)}, u32[]{:S(2)}) collective-permute-start(f32[512]{0:T(512)S(1)} %bitcast.171), channel_id=1, source_target_pairs={{0,12},{4,0},{8,4},{12,8},{1,13},{5,1},{9,5},{13,9},{2,14},{6,2},{... | collective-permute-start | bytes 6152 | tf_op jit(solution)/shard_map/ppermute | solution.py:73
  80.4 7.1 %collective-permute-start.6 = (f32[4,128,128]{2,0,1:T(4,128)}, f32[4,128,128]{2,0,1:T(4,128)S(1)}, u32[]{:S(2)}, u32[]{:S(2)}) collective-permute-start(f32[4,128,128]{2,0,1:T(4,128)} %get-tuple-element.12), channel_id=1, source_target_pairs={{0,4},{4,8},{8,12},{12,0},{1,5},{5,9},{9,13},{13,1},{2,6},{6,10},{... | collective-permute-start | bytes 786440 | tf_op jit(solution)/shard_map/ppermute | solution.py:94
  80.4 25.4 %collective-permute-start.7 = (f32[4,128,128]{2,0,1:T(4,128)S(1)}, f32[4,128,128]{2,0,1:T(4,128)S(1)}, u32[]{:S(2)}, u32[]{:S(2)}) collective-permute-start(f32[4,128,128]{2,0,1:T(4,128)S(1)} %get-tuple-element.11), channel_id=1, source_target_pairs={{0,8},{4,12},{8,0},{12,4},{1,9},{5,13},{9,1},{13,5},{2,10},{6,14},... | collective-permute-start | bytes 786440 | tf_op jit(solution)/shard_map/ppermute | solution.py:94
  83.1 22.7 %collective-permute-start.8 = (f32[4,128,128]{2,0,1:T(4,128)S(1)}, f32[4,128,128]{2,0,1:T(4,128)}, u32[]{:S(2)}, u32[]{:S(2)}) collective-permute-start(f32[4,128,128]{2,0,1:T(4,128)S(1)} %get-tuple-element.10), channel_id=1, source_target_pairs={{0,12},{4,0},{8,4},{12,8},{1,13},{5,1},{9,5},{13,9},{2,14},{6,2},{... | collective-permute-start | bytes 786440 | tf_op jit(solution)/shard_map/ppermute | solution.py:94
  108.8 2.0 %copy-start.4 = (f32[512,512]{1,0:T(8,128)S(1)}, f32[512,512]{1,0:T(8,128)}, u32[]{:S(2)}) copy-start(f32[512,512]{1,0:T(8,128)} %fusion.16) | copy-start | bytes 3145732

commit v3 on v2

--- a/solution.py
+++ b/solution.py
@@ -4,6 +4,8 @@
 import jax.numpy as jnp
 from jax import lax
 from jax.sharding import PartitionSpec as P
+from jax.experimental import pallas as pl
+from jax.experimental.pallas import tpu as pltpu
 
 TS = 128
 
@@ -34,6 +36,83 @@
     return left_term - right_term
 
 
+def build_sends(picked, weight_slot, generator, hamiltonian, weight_rows, channels, spread):
+    blocks = generator.shape[-1] // TS
+    rows = 2 * spread * TS + weight_rows.shape[1]
+
+    def kernel(picked_ref, slot_ref, gen_ref, ham_ref, weight_ref, *rest):
+        outs, sems = rest[:channels], rest[channels]
+        copies = []
+        for s in range(channels):
+            for r in range(spread):
+                tile = picked_ref[s * spread + r]
+                top = pl.multiple_of((tile // blocks) * TS, TS)
+                left = pl.multiple_of((tile % blocks) * TS, TS)
+                for m, src in enumerate((gen_ref, ham_ref)):
+                    copies.append(pltpu.make_async_copy(
+                        src.at[pl.ds(top, TS), pl.ds(left, TS)],
+                        outs[s].at[pl.ds((2 * r + m) * TS, TS), :],
+                        sems.at[len(copies)],
+                    ))
+            copies.append(pltpu.make_async_copy(
+                weight_ref.at[slot_ref[s]],
+                outs[s].at[pl.ds(2 * spread * TS, weight_rows.shape[1]), :],
+                sems.at[len(copies)],
+            ))
+        for copy in copies:
+            copy.start()
+        for copy in copies:
+            copy.wait()
+
+    count = channels * (2 * spread + 1)
+    return pl.pallas_call(
+        kernel,
+        grid_spec=pltpu.PrefetchScalarGridSpec(
+            num_scalar_prefetch=2,
+            grid=(1,),
+            in_specs=[pl.BlockSpec(memory_space=pl.ANY)] * 3,
+            out_specs=[pl.BlockSpec(memory_space=pl.ANY)] * channels,
+            scratch_shapes=[pltpu.SemaphoreType.DMA((count,))],
+        ),
+        out_shape=[jax.ShapeDtypeStruct((rows, TS), jnp.float32)] * channels,
+    )(picked, weight_slot, generator, hamiltonian, weight_rows)
+
+
+def finish(direct, home, place):
+    size = direct.shape[-1]
+    blocks = size // TS
+    spread = home[0].shape[0]
+
+    def kernel(place_ref, direct_ref, *rest):
+        pieces, out_ref = rest[:-1], rest[-1]
+        for a in range(blocks):
+            for b in range(blocks):
+                out_ref[a * TS:(a + 1) * TS, b * TS:(b + 1) * TS] = 0.5 * (
+                    direct_ref[a * TS:(a + 1) * TS, b * TS:(b + 1) * TS]
+                    + direct_ref[b * TS:(b + 1) * TS, a * TS:(a + 1) * TS].T
+                )
+        for s, piece in enumerate(pieces):
+            for r in range(spread):
+                tile = place_ref[s * spread + r]
+                top = pl.multiple_of((tile // blocks) * TS, TS)
+                left = pl.multiple_of((tile % blocks) * TS, TS)
+                value = 0.5 * piece[r]
+                out_ref[pl.ds(top, TS), pl.ds(left, TS)] += value
+                out_ref[pl.ds(left, TS), pl.ds(top, TS)] += value.T
+
+    whole = pl.BlockSpec(memory_space=pltpu.VMEM)
+    return pl.pallas_call(
+        kernel,
+        grid_spec=pltpu.PrefetchScalarGridSpec(
+            num_scalar_prefetch=1,
+            grid=(1,),
+            in_specs=[whole] * (1 + len(home)),
+            out_specs=whole,
+        ),
+        out_shape=jax.ShapeDtypeStruct((size, size), jnp.float32),
+    )(place, direct, *home)
+
+
 def body(
     generator,
     hamiltonian,
@@ -48,10 +127,10 @@
     tile_count = tile_order.shape[-1]
     spread = tile_count // channels
     capacity = cross_weights.shape[2]
+    size = generator.shape[-1]
     me = lax.axis_index("chan")
     chan_range = jnp.arange(channels, dtype=jnp.int32)
     spread_range = jnp.arange(spread, dtype=jnp.int32)
-    tile_range = jnp.arange(tile_count, dtype=jnp.int32)
 
     order = tile_order[0, 0]
     owners = cross_owner[:, 0]
@@ -61,25 +140,24 @@
 
     dest = (me + chan_range) % channels
     source = (me - chan_range) % channels
-    generator_tiles = to_tiles(generator[0, 0], TS)
-    hamilton_tiles = to_tiles(hamiltonian[0, 0], TS)
-    picked = order[dest[:, None] * spread + spread_range[None, :]]
-    send = jnp.stack([generator_tiles[picked], hamilton_tiles[picked]], axis=2)
-    weight_send = cross_weights[0, 0][jnp.clip(slot_of[dest], 0, capacity - 1)]
-    got = [send[0]]
-    weight_got = [weight_send[0]]
+    picked = order[(dest[:, None] * spread + spread_range[None, :]).reshape(-1)]
+    weight_slot = jnp.clip(slot_of[dest], 0, capacity - 1)
+    weight_rows = cross_weights[0, 0].reshape(capacity, size // TS, TS)
+    sends = build_sends(
+        picked, weight_slot, generator[0, 0], hamiltonian[0, 0], weight_rows, channels, spread
+    )
+    got = [sends[0]]
     for shift in range(1, channels):
         pairs = [(c, (c + shift) % channels) for c in range(channels)]
-        tiles_in, weights_in = lax.ppermute((send[shift], weight_send[shift]), "chan", pairs)
-        got.append(tiles_in)
-        weight_got.append(weights_in)
+        got.append(lax.ppermute(sends[shift], "chan", pairs))
     got = jnp.stack(got)
-    weights_cross = jnp.stack(weight_got)[(me - owners[me]) % channels]
+    tiles_got = got[:, : 2 * spread * TS].reshape(channels, spread, 2, TS, TS)
+    weights_cross = got[(me - owners[me]) % channels, 2 * spread * TS :].reshape(-1)
 
     mixer = recoupling[recoupling_index[me, 0]]
     column_of = (spread_range[None, :] * channels + source[:, None]).reshape(-1)
     mixer_in = mixer[:, column_of]
-    cross = got.reshape(tile_count, 2, TS, TS)
+    cross = tiles_got.reshape(tile_count, 2, TS, TS)
     generator_mixed = jnp.einsum("ji,ixy->jxy", mixer_in, cross[:, 0], precision=highest)
     hamilton_mixed = jnp.einsum("ji,ixy->jxy", mixer_in, cross[:, 1], precision=highest)
     product = bracket(
@@ -92,15 +170,10 @@
     for shift in range(1, channels):
         pairs = [(c, (c + shift) % channels) for c in range(channels)]
         home.append(lax.ppermute(back[shift], "chan", pairs))
-    home = jnp.stack(home)
-    inverse = jnp.zeros((tile_count,), jnp.int32).at[order].set(tile_range)
-    from_g = inverse // spread
-    at_shift = (me - from_g) % channels
-    returned = home[at_shift, inverse % spread]
+    place = order[(source[:, None] * spread + spread_range[None, :]).reshape(-1)]
 
     direct = bracket(generator[0, 0], hamiltonian[0, 0], pair_weights[0, 0])
-    summed = direct + from_tiles(returned, TS)
-    return (0.5 * (summed + summed.T))[None, None]
+    return finish(direct, home, place)[None, None]
 
 
 def solution(mesh):

time: 115 us -> 162 us (1.41)
  Pallas kernels: 0 us -> 69.8 us
  local copies, waits for them, and re-layouts: 24.6 us -> 10.2 us
  starting transfers between devices: 12.9 us -> 6.11 us
  other arithmetic: 7.79 us -> 3.34 us
  matrix products: 13.3 us -> 15.3 us
    pallas_call x0 -> x2, Pallas kernels: none -> 69.8 us  [the longest x1 65.9 us: build_sends(): pl.pallas_call(kernel, grid_spec=pltpu.PrefetchScalarGridSpec(num_scalar_...]
    ppermute x6 -> x3, starting transfers between devices: 8.16 us -> 2.41 us  [body(): got.append(lax.ppermute(sends[shift], 'chan', pairs))]
    gather x7 -> x3, local copies, waits for them, and re-layouts: 8.04 us -> 3.64 us  [the longest x1 1.82 us: body(): picked = order[(dest[:, None] * spread + spread_range[None, :]).reshape(-1)]]
    another operation x4 -> x0, local copies, waits for them, and re-layouts: 4.09 us -> none  [the longest x2 2.62 us: to_tiles(): shaped = matrix.reshape(leading + (blocks, tile_size, blocks, tile_size))]
    ppermute x6 -> x3, waiting for transfers between devices: 33.1 us -> 36.9 us  [body(): got.append(lax.ppermute(sends[shift], 'chan', pairs))]
    transpose x3 -> x1, local copies, waits for them, and re-layouts: 3.84 us -> 0.18 us  [to_tiles(): shaped = jnp.swapaxes(shaped, -3, -2)]
    unnamed x1 -> x0, other arithmetic: 2.66 us -> none
    ppermute x3, waiting for transfers between devices: 19.8 us -> 17.5 us  [body(): home.append(lax.ppermute(back[shift], 'chan', pairs))]
  transfers between devices with their start and end apart: 9 -> 6, of which waited for: 4 -> 3; matrix products, arithmetic and copies ran while one was open for 18% -> 6% of each run, Pallas kernels for 0% -> 0%
where the time goes in v3:
time: 162 us
  Pallas kernels  69.8 us (43%)
  waiting for transfers between devices  54.4 us (34%)
  matrix products  15.3 us (9%)
  local copies, waits for them, and re-layouts  10.2 us (6%)
  starting transfers between devices  6.11 us (4%)
  other arithmetic  3.34 us (2%)
  between operations  2.66 us (2%)
    pallas_call x1, Pallas kernels, build_sends(): pl.pallas_call(kernel, grid_spec=pltpu.PrefetchScalarGridSpec(num_scalar_...  65.9 us
    ppermute x3, waiting for transfers between devices, body(): got.append(lax.ppermute(sends[shift], 'chan', pairs))  36.9 us
    ppermute x3, waiting for transfers between devices, body(): home.append(lax.ppermute(back[shift], 'chan', pairs))  17.5 us
    dot_general x2, matrix products, bracket(): jnp.matmul(right_matrix * scaled, left_matrix, precision=highest)  5.79 us
    dot_general x2, matrix products, bracket(): jnp.matmul(left_matrix * scaled, right_matrix, precision=highest)  4.7 us
    pallas_call x1, Pallas kernels, finish(): pl.pallas_call(kernel, grid_spec=pltpu.PrefetchScalarGridSpec(num_scalar_...  3.95 us
    ppermute x3, starting transfers between devices, body(): home.append(lax.ppermute(back[shift], 'chan', pairs))  3.7 us
  transfers between devices with their start and end apart: 6, of which 3 were waited for; matrix products, arithmetic and copies ran while one was open for 6% of the time, Pallas kernels for 0%

profile of v3, /device:TPU:28, one launch (start us, length us, event | category | flops | bytes accessed | tf_op | source)
XLA Modules:
  0.0 161.9 jit_solution(9819725707557362061)
XLA Ops:
  0.5 1.1 convert_reduce_fusion
  1.6 0.6 gather_fusion.4
  2.2 0.6 broadcast_clamp_fusion.slot_ref
  2.8 1.8 %gather_fusion.3 = s32[16]{0:T(128)} fusion(s32[16]{0:T(128)} %bitcast.85, s32[1024]{0:T(1024)S(1)} %pad_clamp_fusion.1), kind=kCustom, calls=%fused_computation.3 | custom fusion | bytes 192 | tf_op jit(solution)/shard_map/gather | solution.py:143
  4.6 65.9 %shard_map.82 = (f32[1028,128]{1,0:T(8,128)}, f32[1028,128]{1,0:T(8,128)}, f32[1028,128]{1,0:T(8,128)}, f32[1028,128]{1,0:T(8,128)}) custom-call(s32[16]{0:T(128)} %gather_fusion.3, s32[4]{0:T(128)} %broadcast_clamp_fusion.slot_ref, f32[512,512]{1,0:T(8,128)} %bitcast.88, f32[512,512]{1,0:T(8,128)} %bitcast.89, f32[3,4,128]{2,1,0:T(4,128)} %bitcast.105), custom_call_target="tpu_custom_call" | custom-call | tf_op jit(solution)/shard_map/pallas_call | solution.py:68
  70.5 0.3 collective-permute-start
  70.8 1.7 %collective-permute-start.1 = (f32[1028,128]{1,0:T(8,128)}, f32[1028,128]{1,0:T(8,128)}, u32[]{:S(2)}, u32[]{:S(2)}) collective-permute-start(f32[1028,128]{1,0:T(8,128)} %get-tuple-element.11), channel_id=1, source_target_pairs={{0,8},{4,12},{8,0},{12,4},{1,9},{5,13},{9,1},{13,5},{2,10},{6,14},... | collective-permute-start | bytes 1579016 | tf_op jit(solution)/shard_map/ppermute | solution.py:152
  72.5 0.4 collective-permute-start.2
  73.0 0.6 constant_dynamic-slice_fusion
  76.2 0.6 gather_fusion.2
  76.9 0.6 gather_fusion.1
  77.5 1.2 gather_fusion
  78.7 2.9 %fusion.12 = f32[512,512]{1,0:T(8,128)} fusion(f32[1,1,512,512]{3,2,1,0:T(8,128)S(1)} %copy-done.2, f32[512]{0:T(512)S(1)} %bitcast.103, f32[1,1,512,512]{3,2,1,0:T(8,128)S(1)} %copy-done.3), kind=kOutput, calls=%fused_computation.24 | convolution fusion | flops 1610874880 | bytes 3147776 | tf_op jit(solution)/shard_map/dot_general | solution.py:34
  81.6 3.3 %collective-permute-done = f32[1028,128]{1,0:T(8,128)S(1)} collective-permute-done((f32[1028,128]{1,0:T(8,128)}, f32[1028,128]{1,0:T(8,128)S(1)}, u32[]{:S(2)}, u32[]{:S(2)}) %collective-permute-start) | collective-permute-done | bytes 526368 | tf_op jit(solution)/shard_map/ppermute | solution.py:152
  84.9 33.6 %collective-permute-done.1 = f32[1028,128]{1,0:T(8,128)} collective-permute-done((f32[1028,128]{1,0:T(8,128)}, f32[1028,128]{1,0:T(8,128)}, u32[]{:S(2)}, u32[]{:S(2)}) %collective-permute-start.1) | collective-permute-done | bytes 526368 | tf_op jit(solution)/shard_map/ppermute | solution.py:152
  118.5 1.3 pad_maximum_fusion
  120.1 1.8 %fusion.10 = f32[4,4,128,128]{3,1,2,0:T(4,128)S(1)} fusion(f32[4,4,16,1]{2,1,3,0:T(4,128)S(1)} %bitcast.100, f32[16,1,128,128]{3,2,1,0:T(8,128)S(1)} %get-tuple-element.13), kind=kOutput, calls=%fused_computation.20 | convolution fusion | flops 50331648 | bytes 2098176 | tf_op jit(solution)/shard_map/ji,ixy->jxy/dot_general | solution.py:161
  121.9 2.1 %bitcast_multiply_fusion = (f32[4,128,4,128]{3,2,1,0:T(4,128)S(1)}, f32[4,128,4,128]{3,2,1,0:T(4,128)S(1)}, f32[4,4,128,128]{3,1,2,0:T(4,128)S(1)}) fusion(f32[4,128]{1,0:T(4,128)S(1)} %dynamic-slice_bitcast_fusion, f32[4,4,128,128]{3,1,2,0:T(4,128)S(1)} %fusion.10, f32[4,4,16,1]{2,1,3,0:T(4,128)S(1)} %bitcast.101, ...), kind=kOutput, calls=%fused_computation.21 | convolution fusion | flops 50855936 | bytes 5245952 | tf_op jit(solution)/shard_map/ji,ixy->jxy/dot_general | solution.py:162
  124.0 1.8 %fusion.4 = f32[512,512]{1,0:T(8,128)S(1)} fusion(f32[64,8,4,128]{3,2,1,0:T(4,128)S(1)} %bitcast.92, f32[64,8,4,128]{3,2,1,0:T(4,128)S(1)} %bitcast.91), kind=kOutput, calls=%fused_computation.12 | convolution fusion | flops 1610612736 | bytes 3145728 | tf_op jit(solution)/shard_map/dot_general | solution.py:34
  125.8 2.9 %convolution_subtract_fusion = f32[512,512]{1,0:T(8,128)} fusion(f32[512,512]{1,0:T(8,128)S(1)} %fusion.4, f32[64,8,4,128]{3,2,1,0:T(4,128)S(1)} %bitcast.87, f32[64,8,4,128]{3,2,1,0:T(4,128)S(1)} %bitcast.93), kind=kOutput, calls=%fused_computation.6 | convolution fusion | flops 1610874880 | bytes 4194304 | tf_op jit(solution)/shard_map/dot_general | solution.py:35
  128.7 1.6 reshape.257
  130.3 0.2 copy.32
  130.5 1.0 fusion.18
  131.7 0.2 collective-permute-start.3
  132.0 1.4 collective-permute-start.4
  133.4 2.1 %collective-permute-start.5 = (f32[4,128,128]{2,1,0:T(8,128)S(1)}, f32[4,128,128]{2,1,0:T(8,128)S(1)}, u32[]{:S(2)}, u32[]{:S(2)}) collective-permute-start(f32[4,128,128]{2,1,0:T(8,128)S(1)} %copy.43), channel_id=1, source_target_pairs={{0,12},{4,0},{8,4},{12,8},{1,13},{5,1},{9,5},{13,9},{2,14},{6,2},{... | collective-permute-start | bytes 786440 | tf_op jit(solution)/shard_map/ppermute | solution.py:172
  135.4 2.9 %convolution_subtract_fusion.1.direct_ref = f32[512,512]{1,0:T(8,128)} fusion(f32[512,512]{1,0:T(8,128)S(1)} %copy-done.4, f32[1,1,512,512]{3,2,1,0:T(8,128)S(1)} %copy-done.3, f32[512]{0:T(512)S(1)} %bitcast.104, f32[1,1,512,512]{3,2,1,0:T(8,128)S(1)} %copy-done.2), kind=kOutput, calls=%fused_computation.7 | convolution fusion | flops 1611137024 | bytes 4196352 | tf_op jit(solution)/shard_map/dot_general | solution.py:35
  138.4 0.7 copy.40.rest_0_
  139.1 17.5 %collective-permute-done.4.rest_2_ = f32[4,128,128]{2,1,0:T(8,128)S(1)} collective-permute-done((f32[4,128,128]{2,1,0:T(8,128)S(1)}, f32[4,128,128]{2,1,0:T(8,128)S(1)}, u32[]{:S(2)}, u32[]{:S(2)}) %collective-permute-start.4) | collective-permute-done | bytes 262176 | tf_op jit(solution)/shard_map/ppermute | solution.py:172
  156.6 0.7 copy-done.7
  157.3 0.7 copy-done.8
  158.0 4.0 %shard_map.83 = f32[512,512]{1,0:T(8,128)} custom-call(s32[16]{0:T(128)} %gather_fusion, f32[512,512]{1,0:T(8,128)} %convolution_subtract_fusion.1.direct_ref, f32[4,128,128]{2,1,0:T(8,128)} %copy.40.rest_0_, f32[4,128,128]{2,1,0:T(8,128)} %copy-done.6, f32[4,128,128]{2,1,0:T(8,128)} %copy-done.7, f32[4,128,128]{2,1,0:T(8,128)} %copy-done.8), custom_call_target="tpu_custom_call" | custom-call | tf_op jit(solution)/shard_map/pallas_call | solution.py:104
  (55 shorter events, 1.4 us)
Async XLA Ops:
  0.0 75.9 %copy-start = (f32[8,16,16]{2,1,0:T(8,128)S(1)}, f32[8,16,16]{2,1,0:T(8,128)}, u32[]{:S(2)}) copy-start(f32[8,16,16]{2,1,0:T(8,128)} %param.12) | copy-start | bytes 24580
  0.0 72.9 %copy-start.10 = (s32[4,1]{0,1:T(1,128)S(1)}, s32[4,1]{0,1:T(1,128)}, u32[]{:S(2)}) copy-start(s32[4,1]{0,1:T(1,128)} %param.13) | copy-start | bytes 52
  0.0 77.5 %copy-start.1 = (s32[1,1,16]{2,1,0:T(1,128)S(1)}, s32[1,1,16]{2,1,0:T(1,128)}, u32[]{:S(2)}) copy-start(s32[1,1,16]{2,1,0:T(1,128)} %param.14) | copy-start | bytes 196
  0.0 78.7 %copy-start.3 = (f32[1,1,512,512]{3,2,1,0:T(8,128)S(1)}, f32[1,1,512,512]{3,2,1,0:T(8,128)}, u32[]{:S(2)}) copy-start(f32[1,1,512,512]{3,2,1,0:T(8,128)} %param.9) | copy-start | bytes 3145732
  0.0 78.7 %copy-start.2 = (f32[1,1,512,512]{3,2,1,0:T(8,128)S(1)}, f32[1,1,512,512]{3,2,1,0:T(8,128)}, u32[]{:S(2)}) copy-start(f32[1,1,512,512]{3,2,1,0:T(8,128)} %param.8) | copy-start | bytes 3145732
  0.0 72.9 %copy-start.11 = (s32[4,1]{0,1:T(1,128)S(1)}, s32[4,1]{0,1:T(1,128)}, u32[]{:S(2)}) copy-start(s32[4,1]{0,1:T(1,128)} %param.15) | copy-start | bytes 52
  0.0 78.7 %copy-start.9 = (f32[1,1,512]{2,1,0:T(1,128)S(1)}, f32[1,1,512]{2,1,0:T(1,128)}, u32[]{:S(2)}) copy-start(f32[1,1,512]{2,1,0:T(1,128)} %param.10) | copy-start | bytes 6148
  70.5 48.0 %copy-start.5 = (f32[1028,128]{1,0:T(8,128)S(1)}, f32[1028,128]{1,0:T(8,128)}, u32[]{:S(2)}) copy-start(f32[1028,128]{1,0:T(8,128)} %get-tuple-element.9) | copy-start | bytes 1579012
  70.5 14.4 %collective-permute-start = (f32[1028,128]{1,0:T(8,128)}, f32[1028,128]{1,0:T(8,128)S(1)}, u32[]{:S(2)}, u32[]{:S(2)}) collective-permute-start(f32[1028,128]{1,0:T(8,128)} %get-tuple-element.10), channel_id=1, source_target_pairs={{0,4},{4,8},{8,12},{12,0},{1,5},{5,9},{9,13},{13,1},{2,6},{6,10},{... | collective-permute-start | bytes 1579016 | tf_op jit(solution)/shard_map/ppermute | solution.py:152
  70.8 47.7 %collective-permute-start.1 = (f32[1028,128]{1,0:T(8,128)}, f32[1028,128]{1,0:T(8,128)}, u32[]{:S(2)}, u32[]{:S(2)}) collective-permute-start(f32[1028,128]{1,0:T(8,128)} %get-tuple-element.11), channel_id=1, source_target_pairs={{0,8},{4,12},{8,0},{12,4},{1,9},{5,13},{9,1},{13,5},{2,10},{6,14},... | collective-permute-start | bytes 1579016 | tf_op jit(solution)/shard_map/ppermute | solution.py:152
  72.5 46.0 %collective-permute-start.2 = (f32[1028,128]{1,0:T(8,128)}, f32[1028,128]{1,0:T(8,128)}, u32[]{:S(2)}, u32[]{:S(2)}) collective-permute-start(f32[1028,128]{1,0:T(8,128)} %get-tuple-element.12), channel_id=1, source_target_pairs={{0,12},{4,0},{8,4},{12,8},{1,13},{5,1},{9,5},{13,9},{2,14},{6,2},{... | collective-permute-start | bytes 1579016 | tf_op jit(solution)/shard_map/ppermute | solution.py:152
  131.5 4.0 %copy-start.4 = (f32[512,512]{1,0:T(8,128)S(1)}, f32[512,512]{1,0:T(8,128)}, u32[]{:S(2)}) copy-start(f32[512,512]{1,0:T(8,128)} %fusion.12) | copy-start | bytes 3145732
  131.7 7.4 %collective-permute-start.3 = (f32[4,128,128]{2,1,0:T(8,128)S(1)}, f32[4,128,128]{2,1,0:T(8,128)S(1)}, u32[]{:S(2)}, u32[]{:S(2)}) collective-permute-start(f32[4,128,128]{2,1,0:T(8,128)S(1)} %copy.41), channel_id=1, source_target_pairs={{0,4},{4,8},{8,12},{12,0},{1,5},{5,9},{9,13},{13,1},{2,6},{6,10},{... | collective-permute-start | bytes 786440 | tf_op jit(solution)/shard_map/ppermute | solution.py:172
  132.0 24.6 %collective-permute-start.4 = (f32[4,128,128]{2,1,0:T(8,128)S(1)}, f32[4,128,128]{2,1,0:T(8,128)S(1)}, u32[]{:S(2)}, u32[]{:S(2)}) collective-permute-start(f32[4,128,128]{2,1,0:T(8,128)S(1)} %copy.42), channel_id=1, source_target_pairs={{0,8},{4,12},{8,0},{12,4},{1,9},{5,13},{9,1},{13,5},{2,10},{6,14},... | collective-permute-start | bytes 786440 | tf_op jit(solution)/shard_map/ppermute | solution.py:172
  133.4 23.2 %collective-permute-start.5 = (f32[4,128,128]{2,1,0:T(8,128)S(1)}, f32[4,128,128]{2,1,0:T(8,128)S(1)}, u32[]{:S(2)}, u32[]{:S(2)}) collective-permute-start(f32[4,128,128]{2,1,0:T(8,128)S(1)} %copy.43), channel_id=1, source_target_pairs={{0,12},{4,0},{8,4},{12,8},{1,13},{5,1},{9,5},{13,9},{2,14},{6,2},{... | collective-permute-start | bytes 786440 | tf_op jit(solution)/shard_map/ppermute | solution.py:172
  139.1 17.5 %copy-start.6 = (f32[4,128,128]{2,1,0:T(8,128)}, f32[4,128,128]{2,1,0:T(8,128)S(1)}, u32[]{:S(2)}) copy-start(f32[4,128,128]{2,1,0:T(8,128)S(1)} %collective-permute-done.3.rest_1_) | copy-start | bytes 786436
  156.6 0.7 copy-start.7
  157.3 0.7 copy-start.8

commit v4 on v3

--- a/solution.py
+++ b/solution.py
@@ -40,39 +40,26 @@
     blocks = generator.shape[-1] // TS
     rows = 2 * spread * TS + weight_rows.shape[1]
 
-    def kernel(picked_ref, slot_ref, gen_ref, ham_ref, weight_ref, *rest):
-        outs, sems = rest[:channels], rest[channels]
-        copies = []
+    def kernel(picked_ref, slot_ref, gen_ref, ham_ref, weight_ref, *outs):
         for s in range(channels):
             for r in range(spread):
                 tile = picked_ref[s * spread + r]
                 top = pl.multiple_of((tile // blocks) * TS, TS)
                 left = pl.multiple_of((tile % blocks) * TS, TS)
                 for m, src in enumerate((gen_ref, ham_ref)):
-                    copies.append(pltpu.make_async_copy(
-                        src.at[pl.ds(top, TS), pl.ds(left, TS)],
-                        outs[s].at[pl.ds((2 * r + m) * TS, TS), :],
-                        sems.at[len(copies)],
-                    ))
-            copies.append(pltpu.make_async_copy(
-                weight_ref.at[slot_ref[s]],
-                outs[s].at[pl.ds(2 * spread * TS, weight_rows.shape[1]), :],
-                sems.at[len(copies)],
-            ))
-        for copy in copies:
-            copy.start()
-        for copy in copies:
-            copy.wait()
+                    outs[s][(2 * r + m) * TS:(2 * r + m + 1) * TS, :] = src[
+                        pl.ds(top, TS), pl.ds(left, TS)
+                    ]
+            outs[s][2 * spread * TS:, :] = weight_ref[slot_ref[s]]
 
-    count = channels * (2 * spread + 1)
+    whole = pl.BlockSpec(memory_space=pltpu.VMEM)
     return pl.pallas_call(
         kernel,
         grid_spec=pltpu.PrefetchScalarGridSpec(
             num_scalar_prefetch=2,
             grid=(1,),
-            in_specs=[pl.BlockSpec(memory_space=pl.ANY)] * 3,
-            out_specs=[pl.BlockSpec(memory_space=pl.ANY)] * channels,
-            scratch_shapes=[pltpu.SemaphoreType.DMA((count,))],
+            in_specs=[whole] * 3,
+            out_specs=[whole] * channels,
         ),
         out_shape=[jax.ShapeDtypeStruct((rows, TS), jnp.float32)] * channels,
     )(picked, weight_slot, generator, hamiltonian, weight_rows)

time: 162 us -> 100 us (0.62)
  Pallas kernels: 69.8 us -> 7.73 us
    pallas_call x1, Pallas kernels: 65.9 us -> 3.78 us  [build_sends(): pl.pallas_call(kernel, grid_spec=pltpu.PrefetchScalarGridSpec(num_scalar_...]
  transfers between devices with their start and end apart: 6 -> 6, of which waited for: 3 -> 3; matrix products, arithmetic and copies ran while one was open for 6% -> 10% of each run, Pallas kernels for 0% -> 0%
where the time goes in v4:
time: 100 us; the launch traced here: 99.8 us
  waiting for transfers between devices  54.4 us (54%)
  matrix products  15.3 us (15%)
  local copies, waits for them, and re-layouts  10.2 us (10%)
  Pallas kernels  7.73 us (8%)
  starting transfers between devices  6.06 us (6%)
  other arithmetic  3.34 us (3%)
  between operations  2.65 us (3%)
    ppermute x3, waiting for transfers between devices, body(): got.append(lax.ppermute(sends[shift], 'chan', pairs))  36.9 us
    ppermute x3, waiting for transfers between devices, body(): home.append(lax.ppermute(back[shift], 'chan', pairs))  17.5 us
    dot_general x2, matrix products, bracket(): jnp.matmul(right_matrix * scaled, left_matrix, precision=highest)  5.79 us
    dot_general x2, matrix products, bracket(): jnp.matmul(left_matrix * scaled, right_matrix, precision=highest)  4.7 us
    pallas_call x1, Pallas kernels, finish(): pl.pallas_call(kernel, grid_spec=pltpu.PrefetchScalarGridSpec(num_scalar_...  3.95 us
    pallas_call x1, Pallas kernels, build_sends(): pl.pallas_call(kernel, grid_spec=pltpu.PrefetchScalarGridSpec(num_scalar_...  3.78 us
    ppermute x3, starting transfers between devices, body(): home.append(lax.ppermute(back[shift], 'chan', pairs))  3.7 us
    ppermute x3, starting transfers between devices, body(): got.append(lax.ppermute(sends[shift], 'chan', pairs))  2.36 us
  transfers between devices with their start and end apart: 6, of which 3 were waited for; matrix products, arithmetic and copies ran while one was open for 10% of the time, Pallas kernels for 0%

profile of v4, /device:TPU:28, one launch (start us, length us, event | category | flops | bytes accessed | tf_op | source)
XLA Modules:
  0.0 99.8 jit_solution(8658415869693864719)
XLA Ops:
  0.5 1.1 %convert_reduce_fusion = s32[4]{0:T(128)S(1)} fusion(s32[4]{0:T(128)} %bitcast.106), kind=kLoop, calls=%fused_computation.49 | loop fusion | flops 76 | bytes 32 | tf_op jit(solution)/shard_map/reduce_sum | solution.py:126
  1.6 0.6 gather_fusion.4
  2.2 0.6 broadcast_clamp_fusion.slot_ref
  2.8 1.8 %gather_fusion.3 = s32[16]{0:T(128)} fusion(s32[16]{0:T(128)} %bitcast.85, s32[1024]{0:T(1024)S(1)} %pad_clamp_fusion.1), kind=kCustom, calls=%fused_computation.3 | custom fusion | bytes 192 | tf_op jit(solution)/shard_map/gather | solution.py:130
  4.6 3.8 %shard_map.82 = (f32[1028,128]{1,0:T(8,128)}, f32[1028,128]{1,0:T(8,128)}, f32[1028,128]{1,0:T(8,128)}, f32[1028,128]{1,0:T(8,128)}) custom-call(s32[16]{0:T(128)} %gather_fusion.3, s32[4]{0:T(128)} %broadcast_clamp_fusion.slot_ref, f32[512,512]{1,0:T(8,128)} %bitcast.88, f32[512,512]{1,0:T(8,128)} %bitcast.89, f32[3,4,128]{2,1,0:T(4,128)} %bitcast.105), custom_call_target="tpu_custom_call" | custom-call | tf_op jit(solution)/shard_map/pallas_call | solution.py:56
  8.4 0.2 collective-permute-start
  8.6 1.7 %collective-permute-start.1 = (f32[1028,128]{1,0:T(8,128)}, f32[1028,128]{1,0:T(8,128)}, u32[]{:S(2)}, u32[]{:S(2)}) collective-permute-start(f32[1028,128]{1,0:T(8,128)} %get-tuple-element.11), channel_id=1, source_target_pairs={{0,8},{4,12},{8,0},{12,4},{1,9},{5,13},{9,1},{13,5},{2,10},{6,14},... | collective-permute-start | bytes 1579016 | tf_op jit(solution)/shard_map/ppermute | solution.py:139
  10.3 0.4 collective-permute-start.2
  10.8 0.6 constant_dynamic-slice_fusion
  14.0 0.6 gather_fusion.2
  14.8 0.6 gather_fusion.1
  15.4 1.2 %gather_fusion = s32[16]{0:T(128)} fusion(s32[16]{0:T(128)S(1)} %bitcast.86, s32[1024]{0:T(1024)S(1)} %pad_clamp_fusion.4), kind=kCustom, calls=%fused_computation | custom fusion | bytes 192 | tf_op jit(solution)/shard_map/gather | solution.py:160
  16.5 2.9 %fusion.12 = f32[512,512]{1,0:T(8,128)} fusion(f32[1,1,512,512]{3,2,1,0:T(8,128)S(1)} %copy-done.2, f32[512]{0:T(512)S(1)} %bitcast.103, f32[1,1,512,512]{3,2,1,0:T(8,128)S(1)} %copy-done.3), kind=kOutput, calls=%fused_computation.24 | convolution fusion | flops 1610874880 | bytes 3147776 | tf_op jit(solution)/shard_map/dot_general | solution.py:34
  19.4 3.3 %collective-permute-done = f32[1028,128]{1,0:T(8,128)S(1)} collective-permute-done((f32[1028,128]{1,0:T(8,128)}, f32[1028,128]{1,0:T(8,128)S(1)}, u32[]{:S(2)}, u32[]{:S(2)}) %collective-permute-start) | collective-permute-done | bytes 526368 | tf_op jit(solution)/shard_map/ppermute | solution.py:139
  22.7 33.6 %collective-permute-done.1 = f32[1028,128]{1,0:T(8,128)} collective-permute-done((f32[1028,128]{1,0:T(8,128)}, f32[1028,128]{1,0:T(8,128)}, u32[]{:S(2)}, u32[]{:S(2)}) %collective-permute-start.1) | collective-permute-done | bytes 526368 | tf_op jit(solution)/shard_map/ppermute | solution.py:139
  56.3 1.3 %pad_maximum_fusion = f32[4,1028,128]{2,1,0:T(8,128)S(1)} fusion(f32[1,1028,128]{2,1,0:T(8,128)} %bitcast.23, f32[1,1028,128]{2,1,0:T(8,128)} %bitcast.22, f32[1,1028,128]{2,1,0:T(8,128)S(1)} %bitcast.99, f32[1,1028,128]{2,1,0:T(8,128)S(1)} %bitcast.98), kind=kLoop, calls=%fused_computation.5 | loop fusion | flops 1579008 | bytes 4210688 | tf_op jit(solution)/shard_map/stack | solution.py:140
  58.0 1.8 %fusion.10 = f32[4,4,128,128]{3,1,2,0:T(4,128)S(1)} fusion(f32[4,4,16,1]{2,1,3,0:T(4,128)S(1)} %bitcast.100, f32[16,1,128,128]{3,2,1,0:T(8,128)S(1)} %get-tuple-element.13), kind=kOutput, calls=%fused_computation.20 | convolution fusion | flops 50331648 | bytes 2098176 | tf_op jit(solution)/shard_map/ji,ixy->jxy/dot_general | solution.py:148
  59.7 2.1 %bitcast_multiply_fusion = (f32[4,128,4,128]{3,2,1,0:T(4,128)S(1)}, f32[4,128,4,128]{3,2,1,0:T(4,128)S(1)}, f32[4,4,128,128]{3,1,2,0:T(4,128)S(1)}) fusion(f32[4,128]{1,0:T(4,128)S(1)} %dynamic-slice_bitcast_fusion, f32[4,4,128,128]{3,1,2,0:T(4,128)S(1)} %fusion.10, f32[4,4,16,1]{2,1,3,0:T(4,128)S(1)} %bitcast.101, ...), kind=kOutput, calls=%fused_computation.21 | convolution fusion | flops 50855936 | bytes 5245952 | tf_op jit(solution)/shard_map/ji,ixy->jxy/dot_general | solution.py:149
  61.8 1.8 %fusion.4 = f32[512,512]{1,0:T(8,128)S(1)} fusion(f32[64,8,4,128]{3,2,1,0:T(4,128)S(1)} %bitcast.92, f32[64,8,4,128]{3,2,1,0:T(4,128)S(1)} %bitcast.91), kind=kOutput, calls=%fused_computation.12 | convolution fusion | flops 1610612736 | bytes 3145728 | tf_op jit(solution)/shard_map/dot_general | solution.py:34
  63.7 2.9 %convolution_subtract_fusion = f32[512,512]{1,0:T(8,128)} fusion(f32[512,512]{1,0:T(8,128)S(1)} %fusion.4, f32[64,8,4,128]{3,2,1,0:T(4,128)S(1)} %bitcast.87, f32[64,8,4,128]{3,2,1,0:T(4,128)S(1)} %bitcast.93), kind=kOutput, calls=%fused_computation.6 | convolution fusion | flops 1610874880 | bytes 4194304 | tf_op jit(solution)/shard_map/dot_general | solution.py:35
  66.5 1.6 %reshape.257 = f32[4,128,4,128]{3,2,1,0:T(4,128)S(1)} reshape(f32[512,512]{1,0:T(8,128)} %convolution_subtract_fusion) | data formatting | bytes 2097152 | tf_op jit(solution)/shard_map/reshape | solution.py:19
  68.1 0.2 copy.32
  68.3 1.0 %fusion.18 = f32[16,128,128]{2,0,1:T(8,128)S(1)} fusion(f32[16,128,128]{2,0,1:T(8,128)S(1)} %bitcast.94, f32[16,16]{1,0:T(8,128)S(1)} %gather_fusion.1), kind=kOutput, calls=%fused_computation.30 | convolution fusion | flops 50331648 | bytes 2098176 | tf_op jit(solution)/shard_map/ji,jxy->ixy/dot_general | solution.py:154
  69.5 0.2 collective-permute-start.3
  69.8 1.4 %collective-permute-start.4 = (f32[4,128,128]{2,1,0:T(8,128)S(1)}, f32[4,128,128]{2,1,0:T(8,128)S(1)}, u32[]{:S(2)}, u32[]{:S(2)}) collective-permute-start(f32[4,128,128]{2,1,0:T(8,128)S(1)} %copy.42), channel_id=1, source_target_pairs={{0,8},{4,12},{8,0},{12,4},{1,9},{5,13},{9,1},{13,5},{2,10},{6,14},... | collective-permute-start | bytes 786440 | tf_op jit(solution)/shard_map/ppermute | solution.py:159
  71.2 2.1 %collective-permute-start.5 = (f32[4,128,128]{2,1,0:T(8,128)S(1)}, f32[4,128,128]{2,1,0:T(8,128)S(1)}, u32[]{:S(2)}, u32[]{:S(2)}) collective-permute-start(f32[4,128,128]{2,1,0:T(8,128)S(1)} %copy.43), channel_id=1, source_target_pairs={{0,12},{4,0},{8,4},{12,8},{1,13},{5,1},{9,5},{13,9},{2,14},{6,2},{... | collective-permute-start | bytes 786440 | tf_op jit(solution)/shard_map/ppermute | solution.py:159
  73.3 2.9 %convolution_subtract_fusion.1.direct_ref = f32[512,512]{1,0:T(8,128)} fusion(f32[512,512]{1,0:T(8,128)S(1)} %copy-done.4, f32[1,1,512,512]{3,2,1,0:T(8,128)S(1)} %copy-done.3, f32[512]{0:T(512)S(1)} %bitcast.104, f32[1,1,512,512]{3,2,1,0:T(8,128)S(1)} %copy-done.2), kind=kOutput, calls=%fused_computation.7 | convolution fusion | flops 1611137024 | bytes 4196352 | tf_op jit(solution)/shard_map/dot_general | solution.py:35
  76.2 0.7 copy.40.rest_0_
  76.9 17.5 %collective-permute-done.4.rest_2_ = f32[4,128,128]{2,1,0:T(8,128)S(1)} collective-permute-done((f32[4,128,128]{2,1,0:T(8,128)S(1)}, f32[4,128,128]{2,1,0:T(8,128)S(1)}, u32[]{:S(2)}, u32[]{:S(2)}) %collective-permute-start.4) | collective-permute-done | bytes 262176 | tf_op jit(solution)/shard_map/ppermute | solution.py:159
  94.4 0.7 copy-done.7
  95.1 0.7 copy-done.8
  95.8 3.9 %shard_map.83 = f32[512,512]{1,0:T(8,128)} custom-call(s32[16]{0:T(128)} %gather_fusion, f32[512,512]{1,0:T(8,128)} %convolution_subtract_fusion.1.direct_ref, f32[4,128,128]{2,1,0:T(8,128)} %copy.40.rest_0_, f32[4,128,128]{2,1,0:T(8,128)} %copy-done.6, f32[4,128,128]{2,1,0:T(8,128)} %copy-done.7, f32[4,128,128]{2,1,0:T(8,128)} %copy-done.8), custom_call_target="tpu_custom_call" | custom-call | tf_op jit(solution)/shard_map/pallas_call | solution.py:91
  (55 shorter events, 1.4 us)
Async XLA Ops:
  0.0 13.8 %copy-start = (f32[8,16,16]{2,1,0:T(8,128)S(1)}, f32[8,16,16]{2,1,0:T(8,128)}, u32[]{:S(2)}) copy-start(f32[8,16,16]{2,1,0:T(8,128)} %param.12) | copy-start | bytes 24580
  0.0 10.8 %copy-start.10 = (s32[4,1]{0,1:T(1,128)S(1)}, s32[4,1]{0,1:T(1,128)}, u32[]{:S(2)}) copy-start(s32[4,1]{0,1:T(1,128)} %param.13) | copy-start | bytes 52
  0.0 15.3 %copy-start.1 = (s32[1,1,16]{2,1,0:T(1,128)S(1)}, s32[1,1,16]{2,1,0:T(1,128)}, u32[]{:S(2)}) copy-start(s32[1,1,16]{2,1,0:T(1,128)} %param.14) | copy-start | bytes 196
  0.0 16.5 %copy-start.3 = (f32[1,1,512,512]{3,2,1,0:T(8,128)S(1)}, f32[1,1,512,512]{3,2,1,0:T(8,128)}, u32[]{:S(2)}) copy-start(f32[1,1,512,512]{3,2,1,0:T(8,128)} %param.9) | copy-start | bytes 3145732
  0.0 16.5 %copy-start.2 = (f32[1,1,512,512]{3,2,1,0:T(8,128)S(1)}, f32[1,1,512,512]{3,2,1,0:T(8,128)}, u32[]{:S(2)}) copy-start(f32[1,1,512,512]{3,2,1,0:T(8,128)} %param.8) | copy-start | bytes 3145732
  0.0 10.7 %copy-start.11 = (s32[4,1]{0,1:T(1,128)S(1)}, s32[4,1]{0,1:T(1,128)}, u32[]{:S(2)}) copy-start(s32[4,1]{0,1:T(1,128)} %param.15) | copy-start | bytes 52
  0.0 16.5 %copy-start.9 = (f32[1,1,512]{2,1,0:T(1,128)S(1)}, f32[1,1,512]{2,1,0:T(1,128)}, u32[]{:S(2)}) copy-start(f32[1,1,512]{2,1,0:T(1,128)} %param.10) | copy-start | bytes 6148
  8.4 47.9 %copy-start.5 = (f32[1028,128]{1,0:T(8,128)S(1)}, f32[1028,128]{1,0:T(8,128)}, u32[]{:S(2)}) copy-start(f32[1028,128]{1,0:T(8,128)} %get-tuple-element.9) | copy-start | bytes 1579012
  8.4 14.3 %collective-permute-start = (f32[1028,128]{1,0:T(8,128)}, f32[1028,128]{1,0:T(8,128)S(1)}, u32[]{:S(2)}, u32[]{:S(2)}) collective-permute-start(f32[1028,128]{1,0:T(8,128)} %get-tuple-element.10), channel_id=1, source_target_pairs={{0,4},{4,8},{8,12},{12,0},{1,5},{5,9},{9,13},{13,1},{2,6},{6,10},{... | collective-permute-start | bytes 1579016 | tf_op jit(solution)/shard_map/ppermute | solution.py:139
  8.6 47.7 %collective-permute-start.1 = (f32[1028,128]{1,0:T(8,128)}, f32[1028,128]{1,0:T(8,128)}, u32[]{:S(2)}, u32[]{:S(2)}) collective-permute-start(f32[1028,128]{1,0:T(8,128)} %get-tuple-element.11), channel_id=1, source_target_pairs={{0,8},{4,12},{8,0},{12,4},{1,9},{5,13},{9,1},{13,5},{2,10},{6,14},... | collective-permute-start | bytes 1579016 | tf_op jit(solution)/shard_map/ppermute | solution.py:139
  10.3 46.0 %collective-permute-start.2 = (f32[1028,128]{1,0:T(8,128)}, f32[1028,128]{1,0:T(8,128)}, u32[]{:S(2)}, u32[]{:S(2)}) collective-permute-start(f32[1028,128]{1,0:T(8,128)} %get-tuple-element.12), channel_id=1, source_target_pairs={{0,12},{4,0},{8,4},{12,8},{1,13},{5,1},{9,5},{13,9},{2,14},{6,2},{... | collective-permute-start | bytes 1579016 | tf_op jit(solution)/shard_map/ppermute | solution.py:139
  69.3 4.0 %copy-start.4 = (f32[512,512]{1,0:T(8,128)S(1)}, f32[512,512]{1,0:T(8,128)}, u32[]{:S(2)}) copy-start(f32[512,512]{1,0:T(8,128)} %fusion.12) | copy-start | bytes 3145732
  69.5 7.4 %collective-permute-start.3 = (f32[4,128,128]{2,1,0:T(8,128)S(1)}, f32[4,128,128]{2,1,0:T(8,128)S(1)}, u32[]{:S(2)}, u32[]{:S(2)}) collective-permute-start(f32[4,128,128]{2,1,0:T(8,128)S(1)} %copy.41), channel_id=1, source_target_pairs={{0,4},{4,8},{8,12},{12,0},{1,5},{5,9},{9,13},{13,1},{2,6},{6,10},{... | collective-permute-start | bytes 786440 | tf_op jit(solution)/shard_map/ppermute | solution.py:159
  69.8 24.6 %collective-permute-start.4 = (f32[4,128,128]{2,1,0:T(8,128)S(1)}, f32[4,128,128]{2,1,0:T(8,128)S(1)}, u32[]{:S(2)}, u32[]{:S(2)}) collective-permute-start(f32[4,128,128]{2,1,0:T(8,128)S(1)} %copy.42), channel_id=1, source_target_pairs={{0,8},{4,12},{8,0},{12,4},{1,9},{5,13},{9,1},{13,5},{2,10},{6,14},... | collective-permute-start | bytes 786440 | tf_op jit(solution)/shard_map/ppermute | solution.py:159
  71.2 23.2 %collective-permute-start.5 = (f32[4,128,128]{2,1,0:T(8,128)S(1)}, f32[4,128,128]{2,1,0:T(8,128)S(1)}, u32[]{:S(2)}, u32[]{:S(2)}) collective-permute-start(f32[4,128,128]{2,1,0:T(8,128)S(1)} %copy.43), channel_id=1, source_target_pairs={{0,12},{4,0},{8,4},{12,8},{1,13},{5,1},{9,5},{13,9},{2,14},{6,2},{... | collective-permute-start | bytes 786440 | tf_op jit(solution)/shard_map/ppermute | solution.py:159
  76.9 17.5 %copy-start.6 = (f32[4,128,128]{2,1,0:T(8,128)}, f32[4,128,128]{2,1,0:T(8,128)S(1)}, u32[]{:S(2)}) copy-start(f32[4,128,128]{2,1,0:T(8,128)S(1)} %collective-permute-done.3.rest_1_) | copy-start | bytes 786436
  94.4 0.7 copy-start.7
  95.1 0.7 copy-start.8

commit v5 on v4

--- a/solution.py
+++ b/solution.py
@@ -10,7 +10,7 @@
 TS = 128
 
 
-highest = lax.Precision.HIGHEST
+highest = lax.Precision.HIGH
 
 
 def to_tiles(matrix, tile_size):
@@ -38,7 +38,7 @@
 
 def build_sends(picked, weight_slot, generator, hamiltonian, weight_rows, channels, spread):
     blocks = generator.shape[-1] // TS
-    rows = 2 * spread * TS + weight_rows.shape[1]
+    rows = 2 * spread * TS + weight_rows.shape[1] // TS
 
     def kernel(picked_ref, slot_ref, gen_ref, ham_ref, weight_ref, *outs):
         for s in range(channels):
@@ -50,7 +50,14 @@
                     outs[s][(2 * r + m) * TS:(2 * r + m + 1) * TS, :] = src[
                         pl.ds(top, TS), pl.ds(left, TS)
                     ]
-            outs[s][2 * spread * TS:, :] = weight_ref[slot_ref[s]]
+            slot = slot_ref[s]
+            for c in range(weight_ref.shape[1] // TS):
+                row = 2 * spread * TS + c
+                rows_here = weight_ref[:, c * TS:(c + 1) * TS]
+                value = rows_here[0:1]
+                for q in range(1, weight_ref.shape[0]):
+                    value = jnp.where(slot == q, rows_here[q:q + 1], value)
+                outs[s][row:row + 1, :] = value
 
     whole = pl.BlockSpec(memory_space=pltpu.VMEM)
     return pl.pallas_call(
@@ -72,12 +79,7 @@
 
     def kernel(place_ref, direct_ref, *rest):
         pieces, out_ref = rest[:-1], rest[-1]
-        for a in range(blocks):
-            for b in range(blocks):
-                out_ref[a * TS:(a + 1) * TS, b * TS:(b + 1) * TS] = 0.5 * (
-                    direct_ref[a * TS:(a + 1) * TS, b * TS:(b + 1) * TS]
-                    + direct_ref[b * TS:(b + 1) * TS, a * TS:(a + 1) * TS].T
-                )
+        out_ref[...] = direct_ref[...]
         for s, piece in enumerate(pieces):
             for r in range(spread):
                 tile = place_ref[s * spread + r]
@@ -129,7 +131,7 @@
     source = (me - chan_range) % channels
     picked = order[(dest[:, None] * spread + spread_range[None, :]).reshape(-1)]
     weight_slot = jnp.clip(slot_of[dest], 0, capacity - 1)
-    weight_rows = cross_weights[0, 0].reshape(capacity, size // TS, TS)
+    weight_rows = cross_weights[0, 0]
     sends = build_sends(
         picked, weight_slot, generator[0, 0], hamiltonian[0, 0], weight_rows, channels, spread
     )
@@ -160,7 +162,7 @@
     place = order[(source[:, None] * spread + spread_range[None, :]).reshape(-1)]
 
     direct = bracket(generator[0, 0], hamiltonian[0, 0], pair_weights[0, 0])
-    return finish(direct, home, place)[None, None]
+    return finish(0.5 * (direct + direct.T), home, place)[None, None]
 
 
 def solution(mesh):

time: 100 us -> 98.2 us (0.982)
  matrix products: 15.3 us -> 8.41 us
  waiting for transfers between devices: 54.4 us -> 56.5 us
  local copies, waits for them, and re-layouts: 10.2 us -> 12.1 us
  other arithmetic: 3.34 us -> 4.75 us
    dot_general x2, matrix products: 5.79 us -> 3.03 us  [bracket(): jnp.matmul(right_matrix * scaled, left_matrix, precision=highest)]
    dot_general x2, matrix products: 4.7 us -> 2.05 us  [bracket(): jnp.matmul(left_matrix * scaled, right_matrix, precision=highest)]
    ppermute x3, waiting for transfers between devices: 17.5 us -> 19.2 us  [body(): home.append(lax.ppermute(back[shift], 'chan', pairs))]
    unnamed x28 -> x27, local copies, waits for them, and re-layouts: 2.19 us -> 3.5 us
    mul x0 -> x1, other arithmetic: none -> 1.23 us  [body(): return finish(0.5 * (direct + direct.T), home, place)[None, None]]
  transfers between devices with their start and end apart: 6 -> 6, of which waited for: 3 -> 4; matrix products, arithmetic and copies ran while one was open for 10% -> 8% of each run, Pallas kernels for 0% -> 0%
where the time goes in v5:
time: 98.2 us; the launch traced here: 97.8 us
  waiting for transfers between devices  56.5 us (58%)
  local copies, waits for them, and re-layouts  12.1 us (12%)
  matrix products  8.41 us (9%)
  Pallas kernels  7.54 us (8%)
  starting transfers between devices  5.87 us (6%)
  other arithmetic  4.75 us (5%)
  between operations  2.65 us (3%)
    ppermute x3, waiting for transfers between devices, body(): got.append(lax.ppermute(sends[shift], 'chan', pairs))  37.2 us
    ppermute x3, waiting for transfers between devices, body(): home.append(lax.ppermute(back[shift], 'chan', pairs))  19.2 us
    pallas_call x1, Pallas kernels, build_sends(): pl.pallas_call(kernel, grid_spec=pltpu.PrefetchScalarGridSpec(num_scalar_...  3.8 us
    pallas_call x1, Pallas kernels, finish(): pl.pallas_call(kernel, grid_spec=pltpu.PrefetchScalarGridSpec(num_scalar_...  3.75 us
    ppermute x3, starting transfers between devices, body(): home.append(lax.ppermute(back[shift], 'chan', pairs))  3.51 us
    unnamed x27, local copies, waits for them, and re-layouts  3.5 us
    dot_general x2, matrix products, bracket(): jnp.matmul(right_matrix * scaled, left_matrix, precision=highest)  3.03 us
    ppermute x3, starting transfers between devices, body(): got.append(lax.ppermute(sends[shift], 'chan', pairs))  2.36 us
  transfers between devices with their start and end apart: 6, of which 4 were waited for; matrix products, arithmetic and copies ran while one was open for 8% of the time, Pallas kernels for 0%

profile of v5, /device:TPU:28, one launch (start us, length us, event | category | flops | bytes accessed | tf_op | source)
XLA Modules:
  0.0 97.8 jit_solution(9683839642328822154)
XLA Ops:
  0.5 1.1 %convert_reduce_fusion = s32[4]{0:T(128)S(1)} fusion(s32[4]{0:T(128)} %bitcast.111), kind=kLoop, calls=%fused_computation.52 | loop fusion | flops 76 | bytes 32 | tf_op jit(solution)/shard_map/reduce_sum | solution.py:128
  1.6 0.6 gather_fusion.4
  2.2 0.6 broadcast_clamp_fusion.slot_ref
  2.8 1.3 %copy.83 = f32[1,1,3,512]{3,2,1,0:T(4,128)} copy(f32[1,1,3,512]{3,1,2,0:T(1,128)} %param.11) | data formatting | bytes 12288
  4.1 1.9 %gather_fusion.3 = s32[16]{0:T(128)} fusion(s32[16]{0:T(128)} %bitcast.91, s32[1024]{0:T(1024)S(1)} %pad_clamp_fusion.1), kind=kCustom, calls=%fused_computation.3 | custom fusion | bytes 192 | tf_op jit(solution)/shard_map/gather | solution.py:132
  6.0 3.8 %shard_map.82 = (f32[1028,128]{1,0:T(8,128)}, f32[1028,128]{1,0:T(8,128)}, f32[1028,128]{1,0:T(8,128)}, f32[1028,128]{1,0:T(8,128)}) custom-call(s32[16]{0:T(128)} %gather_fusion.3, s32[4]{0:T(128)} %broadcast_clamp_fusion.slot_ref, f32[512,512]{1,0:T(8,128)} %bitcast.94, f32[512,512]{1,0:T(8,128)} %bitcast.95, f32[3,512]{1,0:T(4,128)} %bitcast.107), custom_call_target="tpu_custom_call" | custom-call | tf_op jit(solution)/shard_map/pallas_call | solution.py:63
  10.0 1.7 %collective-permute-start.1 = (f32[1028,128]{1,0:T(8,128)}, f32[1028,128]{1,0:T(8,128)}, u32[]{:S(2)}, u32[]{:S(2)}) collective-permute-start(f32[1028,128]{1,0:T(8,128)} %get-tuple-element.11), channel_id=1, source_target_pairs={{0,8},{4,12},{8,0},{12,4},{1,9},{5,13},{9,1},{13,5},{2,10},{6,14},... | collective-permute-start | bytes 1579016 | tf_op jit(solution)/shard_map/ppermute | solution.py:141
  11.7 0.4 collective-permute-start.2
  12.2 0.7 constant_dynamic-slice_fusion
  15.5 0.6 gather_fusion.2
  16.2 0.6 gather_fusion.1
  16.8 1.2 %gather_fusion = s32[16]{0:T(128)} fusion(s32[16]{0:T(128)S(1)} %bitcast.92, s32[1024]{0:T(1024)S(1)} %pad_clamp_fusion.4), kind=kCustom, calls=%fused_computation | custom fusion | bytes 192 | tf_op jit(solution)/shard_map/gather | solution.py:162
  18.0 1.0 %fusion.13 = f32[512,512]{0,1:T(8,128)S(1)} fusion(f32[1,1,512,512]{3,2,1,0:T(8,128)S(1)} %copy-done.2, f32[512]{0:T(512)S(1)} %bitcast.109, f32[1,1,512,512]{3,2,1,0:T(8,128)S(1)} %copy-done.3), kind=kOutput, calls=%fused_computation.26 | convolution fusion | flops 805568512 | bytes 3147776 | tf_op jit(solution)/shard_map/dot_general | solution.py:34
  19.1 1.0 %convolution_subtract_fusion.1 = f32[512,512]{0,1:T(8,128)S(1)} fusion(f32[512,512]{0,1:T(8,128)S(1)} %fusion.13, f32[1,1,512,512]{3,2,1,0:T(8,128)S(1)} %copy-done.3, f32[512]{0:T(512)S(1)} %bitcast.110, f32[1,1,512,512]{3,2,1,0:T(8,128)S(1)} %copy-done.2), kind=kOutput, calls=%fused_computation.7 | convolution fusion | flops 805830656 | bytes 4196352 | tf_op jit(solution)/shard_map/dot_general | solution.py:35
  20.5 3.8 %collective-permute-done = f32[1028,128]{1,0:T(8,128)} collective-permute-done((f32[1028,128]{1,0:T(8,128)}, f32[1028,128]{1,0:T(8,128)}, u32[]{:S(2)}, u32[]{:S(2)}) %collective-permute-start) | collective-permute-done | bytes 526368 | tf_op jit(solution)/shard_map/ppermute | solution.py:141
  24.2 33.5 %collective-permute-done.1 = f32[1028,128]{1,0:T(8,128)} collective-permute-done((f32[1028,128]{1,0:T(8,128)}, f32[1028,128]{1,0:T(8,128)}, u32[]{:S(2)}, u32[]{:S(2)}) %collective-permute-start.1) | collective-permute-done | bytes 526368 | tf_op jit(solution)/shard_map/ppermute | solution.py:141
  57.7 1.5 %pad_maximum_fusion = f32[4,1028,128]{2,1,0:T(8,128)S(1)} fusion(f32[1,1028,128]{2,1,0:T(8,128)} %bitcast.23, f32[1,1028,128]{2,1,0:T(8,128)} %bitcast.22, f32[1,1028,128]{2,1,0:T(8,128)} %bitcast.21, f32[1,1028,128]{2,1,0:T(8,128)S(1)} %bitcast.104), kind=kLoop, calls=%fused_computation.5 | loop fusion | flops 1579008 | bytes 4210688 | tf_op jit(solution)/shard_map/stack | solution.py:142
  59.6 1.2 %fusion.10 = f32[4,4,128,128]{3,1,2,0:T(4,128)S(1)} fusion(f32[4,4,16,1]{2,1,3,0:T(4,128)S(1)} %bitcast.105, f32[16,1,128,128]{3,2,1,0:T(8,128)S(1)} %get-tuple-element.13), kind=kOutput, calls=%fused_computation.20 | convolution fusion | flops 25165824 | bytes 2098176 | tf_op jit(solution)/shard_map/ji,ixy->jxy/dot_general | solution.py:150
  60.8 1.5 %bitcast_multiply_fusion = (f32[4,128,4,128]{3,2,1,0:T(4,128)S(1)}, f32[4,128,4,128]{3,2,1,0:T(4,128)S(1)}, f32[4,4,128,128]{3,1,2,0:T(4,128)S(1)}) fusion(f32[4,128]{1,0:T(4,128)S(1)} %dynamic-slice_bitcast_fusion, f32[4,4,128,128]{3,1,2,0:T(4,128)S(1)} %fusion.10, f32[4,4,16,1]{2,1,3,0:T(4,128)S(1)} %bitcast.106, ...), kind=kOutput, calls=%fused_computation.21 | convolution fusion | flops 25690112 | bytes 5245952 | tf_op jit(solution)/shard_map/ji,ixy->jxy/dot_general | solution.py:151
  62.4 1.0 %fusion.4 = f32[512,512]{1,0:T(8,128)S(1)} fusion(f32[64,8,4,128]{3,2,1,0:T(4,128)S(1)} %bitcast.98, f32[64,8,4,128]{3,2,1,0:T(4,128)S(1)} %bitcast.97), kind=kOutput, calls=%fused_computation.12 | convolution fusion | flops 805306368 | bytes 3145728 | tf_op jit(solution)/shard_map/dot_general | solution.py:34
  63.4 2.0 %convolution_subtract_fusion = f32[512,512]{1,0:T(8,128)} fusion(f32[512,512]{1,0:T(8,128)S(1)} %fusion.4, f32[64,8,4,128]{3,2,1,0:T(4,128)S(1)} %bitcast.93, f32[64,8,4,128]{3,2,1,0:T(4,128)S(1)} %bitcast.99), kind=kOutput, calls=%fused_computation.6 | convolution fusion | flops 805568512 | bytes 4194304 | tf_op jit(solution)/shard_map/dot_general | solution.py:35
  65.4 1.6 %reshape.257 = f32[4,128,4,128]{3,2,1,0:T(4,128)S(1)} reshape(f32[512,512]{1,0:T(8,128)} %convolution_subtract_fusion) | data formatting | bytes 2097152 | tf_op jit(solution)/shard_map/reshape | solution.py:19
  67.2 0.6 fusion.19
  68.0 1.4 %collective-permute-start.4 = (f32[4,128,128]{2,1,0:T(8,128)S(1)}, f32[4,128,128]{2,1,0:T(8,128)S(1)}, u32[]{:S(2)}, u32[]{:S(2)}) collective-permute-start(f32[4,128,128]{2,1,0:T(8,128)S(1)} %copy.54), channel_id=1, source_target_pairs={{0,8},{4,12},{8,0},{12,4},{1,9},{5,13},{9,1},{13,5},{2,10},{6,14},... | collective-permute-start | bytes 786440 | tf_op jit(solution)/shard_map/ppermute | solution.py:161
  69.4 2.1 %collective-permute-start.5 = (f32[4,128,128]{2,1,0:T(8,128)S(1)}, f32[4,128,128]{2,1,0:T(8,128)S(1)}, u32[]{:S(2)}, u32[]{:S(2)}) collective-permute-start(f32[4,128,128]{2,1,0:T(8,128)S(1)} %copy.55), channel_id=1, source_target_pairs={{0,12},{4,0},{8,4},{12,8},{1,13},{5,1},{9,5},{13,9},{2,14},{6,2},{... | collective-permute-start | bytes 786440 | tf_op jit(solution)/shard_map/ppermute | solution.py:161
  71.5 1.2 %fusion.11.direct_ref = f32[512,512]{1,0:T(8,128)} fusion(f32[512,512]{1,0:T(8,128)S(1)} %copy.36, f32[512,512]{0,1:T(8,128)S(1)} %convolution_subtract_fusion.1), kind=kLoop, calls=%fused_computation.24 | loop fusion | flops 524288 | bytes 3145728 | tf_op jit(solution)/shard_map/mul | solution.py:165
  72.7 0.7 copy.52.rest_0_
  73.4 1.7 %collective-permute-done.3.rest_1_ = f32[4,128,128]{2,1,0:T(8,128)S(1)} collective-permute-done((f32[4,128,128]{2,1,0:T(8,128)S(1)}, f32[4,128,128]{2,1,0:T(8,128)S(1)}, u32[]{:S(2)}, u32[]{:S(2)}) %collective-permute-start.3) | collective-permute-done | bytes 262176 | tf_op jit(solution)/shard_map/ppermute | solution.py:161
  75.2 17.5 %collective-permute-done.4.rest_2_ = f32[4,128,128]{2,1,0:T(8,128)S(1)} collective-permute-done((f32[4,128,128]{2,1,0:T(8,128)S(1)}, f32[4,128,128]{2,1,0:T(8,128)S(1)}, u32[]{:S(2)}, u32[]{:S(2)}) %collective-permute-start.4) | collective-permute-done | bytes 262176 | tf_op jit(solution)/shard_map/ppermute | solution.py:161
  92.7 0.7 copy-done.6
  93.4 0.7 copy-done.7
  94.1 3.7 %shard_map.83 = f32[512,512]{1,0:T(8,128)} custom-call(s32[16]{0:T(128)} %gather_fusion, f32[512,512]{1,0:T(8,128)} %fusion.11.direct_ref, f32[4,128,128]{2,1,0:T(8,128)} %copy.52.rest_0_, f32[4,128,128]{2,1,0:T(8,128)} %copy-done.5, f32[4,128,128]{2,1,0:T(8,128)} %copy-done.6, f32[4,128,128]{2,1,0:T(8,128)} %copy-done.7), custom_call_target="tpu_custom_call" | custom-call | tf_op jit(solution)/shard_map/pallas_call | solution.py:93
  (56 shorter events, 2.2 us)
Async XLA Ops:
  0.0 15.2 %copy-start = (f32[8,16,16]{2,1,0:T(8,128)S(1)}, f32[8,16,16]{2,1,0:T(8,128)}, u32[]{:S(2)}) copy-start(f32[8,16,16]{2,1,0:T(8,128)} %param.12) | copy-start | bytes 24580
  0.0 12.2 %copy-start.9 = (s32[4,1]{0,1:T(1,128)S(1)}, s32[4,1]{0,1:T(1,128)}, u32[]{:S(2)}) copy-start(s32[4,1]{0,1:T(1,128)} %param.13) | copy-start | bytes 52
  0.0 16.8 %copy-start.1 = (s32[1,1,16]{2,1,0:T(1,128)S(1)}, s32[1,1,16]{2,1,0:T(1,128)}, u32[]{:S(2)}) copy-start(s32[1,1,16]{2,1,0:T(1,128)} %param.14) | copy-start | bytes 196
  0.0 18.0 %copy-start.3 = (f32[1,1,512,512]{3,2,1,0:T(8,128)S(1)}, f32[1,1,512,512]{3,2,1,0:T(8,128)}, u32[]{:S(2)}) copy-start(f32[1,1,512,512]{3,2,1,0:T(8,128)} %param.9) | copy-start | bytes 3145732
  0.0 18.0 %copy-start.2 = (f32[1,1,512,512]{3,2,1,0:T(8,128)S(1)}, f32[1,1,512,512]{3,2,1,0:T(8,128)}, u32[]{:S(2)}) copy-start(f32[1,1,512,512]{3,2,1,0:T(8,128)} %param.8) | copy-start | bytes 3145732
  0.0 12.1 %copy-start.10 = (s32[4,1]{0,1:T(1,128)S(1)}, s32[4,1]{0,1:T(1,128)}, u32[]{:S(2)}) copy-start(s32[4,1]{0,1:T(1,128)} %param.15) | copy-start | bytes 52
  0.0 18.0 %copy-start.8 = (f32[1,1,512]{2,1,0:T(1,128)S(1)}, f32[1,1,512]{2,1,0:T(1,128)}, u32[]{:S(2)}) copy-start(f32[1,1,512]{2,1,0:T(1,128)} %param.10) | copy-start | bytes 6148
  9.8 14.4 %collective-permute-start = (f32[1028,128]{1,0:T(8,128)}, f32[1028,128]{1,0:T(8,128)}, u32[]{:S(2)}, u32[]{:S(2)}) collective-permute-start(f32[1028,128]{1,0:T(8,128)} %get-tuple-element.10), channel_id=1, source_target_pairs={{0,4},{4,8},{8,12},{12,0},{1,5},{5,9},{9,13},{13,1},{2,6},{6,10},{... | collective-permute-start | bytes 1579016 | tf_op jit(solution)/shard_map/ppermute | solution.py:141
  10.0 47.7 %collective-permute-start.1 = (f32[1028,128]{1,0:T(8,128)}, f32[1028,128]{1,0:T(8,128)}, u32[]{:S(2)}, u32[]{:S(2)}) collective-permute-start(f32[1028,128]{1,0:T(8,128)} %get-tuple-element.11), channel_id=1, source_target_pairs={{0,8},{4,12},{8,0},{12,4},{1,9},{5,13},{9,1},{13,5},{2,10},{6,14},... | collective-permute-start | bytes 1579016 | tf_op jit(solution)/shard_map/ppermute | solution.py:141
  11.7 46.0 %collective-permute-start.2 = (f32[1028,128]{1,0:T(8,128)}, f32[1028,128]{1,0:T(8,128)}, u32[]{:S(2)}, u32[]{:S(2)}) collective-permute-start(f32[1028,128]{1,0:T(8,128)} %get-tuple-element.12), channel_id=1, source_target_pairs={{0,12},{4,0},{8,4},{12,8},{1,13},{5,1},{9,5},{13,9},{2,14},{6,2},{... | collective-permute-start | bytes 1579016 | tf_op jit(solution)/shard_map/ppermute | solution.py:141
  20.1 37.6 %copy-start.4 = (f32[1028,128]{1,0:T(8,128)S(1)}, f32[1028,128]{1,0:T(8,128)}, u32[]{:S(2)}) copy-start(f32[1028,128]{1,0:T(8,128)} %get-tuple-element.9) | copy-start | bytes 1579012
  67.9 7.2 %collective-permute-start.3 = (f32[4,128,128]{2,1,0:T(8,128)S(1)}, f32[4,128,128]{2,1,0:T(8,128)S(1)}, u32[]{:S(2)}, u32[]{:S(2)}) collective-permute-start(f32[4,128,128]{2,1,0:T(8,128)S(1)} %copy.53), channel_id=1, source_target_pairs={{0,4},{4,8},{8,12},{12,0},{1,5},{5,9},{9,13},{13,1},{2,6},{6,10},{... | collective-permute-start | bytes 786440 | tf_op jit(solution)/shard_map/ppermute | solution.py:161
  68.0 24.6 %collective-permute-start.4 = (f32[4,128,128]{2,1,0:T(8,128)S(1)}, f32[4,128,128]{2,1,0:T(8,128)S(1)}, u32[]{:S(2)}, u32[]{:S(2)}) collective-permute-start(f32[4,128,128]{2,1,0:T(8,128)S(1)} %copy.54), channel_id=1, source_target_pairs={{0,8},{4,12},{8,0},{12,4},{1,9},{5,13},{9,1},{13,5},{2,10},{6,14},... | collective-permute-start | bytes 786440 | tf_op jit(solution)/shard_map/ppermute | solution.py:161
  69.4 23.2 %collective-permute-start.5 = (f32[4,128,128]{2,1,0:T(8,128)S(1)}, f32[4,128,128]{2,1,0:T(8,128)S(1)}, u32[]{:S(2)}, u32[]{:S(2)}) collective-permute-start(f32[4,128,128]{2,1,0:T(8,128)S(1)} %copy.55), channel_id=1, source_target_pairs={{0,12},{4,0},{8,4},{12,8},{1,13},{5,1},{9,5},{13,9},{2,14},{6,2},{... | collective-permute-start | bytes 786440 | tf_op jit(solution)/shard_map/ppermute | solution.py:161
  75.2 17.5 %copy-start.5 = (f32[4,128,128]{2,1,0:T(8,128)}, f32[4,128,128]{2,1,0:T(8,128)S(1)}, u32[]{:S(2)}) copy-start(f32[4,128,128]{2,1,0:T(8,128)S(1)} %collective-permute-done.3.rest_1_) | copy-start | bytes 786436
  92.7 0.7 copy-start.6
  93.4 0.7 copy-start.7

commit v6 on v5

--- a/solution.py
+++ b/solution.py
@@ -36,26 +36,33 @@
     return left_term - right_term
 
 
-def build_sends(picked, weight_slot, generator, hamiltonian, weight_rows, channels, spread):
+def build_sends(order, owners, generator, hamiltonian, cross_weights, channels, spread):
     blocks = generator.shape[-1] // TS
-    rows = 2 * spread * TS + weight_rows.shape[1] // TS
+    capacity, length = cross_weights.shape[-2:]
+    rows = 2 * spread * TS + length // TS
 
-    def kernel(picked_ref, slot_ref, gen_ref, ham_ref, weight_ref, *outs):
+    def kernel(order_ref, owner_ref, gen_ref, ham_ref, weight_ref, *outs):
+        me = lax.axis_index("chan")
         for s in range(channels):
+            g = (me + s) % channels
             for r in range(spread):
-                tile = picked_ref[s * spread + r]
+                tile = order_ref[g * spread + r]
                 top = pl.multiple_of((tile // blocks) * TS, TS)
                 left = pl.multiple_of((tile % blocks) * TS, TS)
                 for m, src in enumerate((gen_ref, ham_ref)):
                     outs[s][(2 * r + m) * TS:(2 * r + m + 1) * TS, :] = src[
                         pl.ds(top, TS), pl.ds(left, TS)
                     ]
-            slot = slot_ref[s]
-            for c in range(weight_ref.shape[1] // TS):
+            mine = owner_ref[g]
+            slot = 0
+            for other in range(channels - 1):
+                slot = slot + jnp.where((other < g) & (owner_ref[other] == mine), 1, 0)
+            slot = jnp.minimum(slot, capacity - 1)
+            for c in range(length // TS):
                 row = 2 * spread * TS + c
-                rows_here = weight_ref[:, c * TS:(c + 1) * TS]
+                rows_here = weight_ref[0, 0, :, c * TS:(c + 1) * TS]
                 value = rows_here[0:1]
-                for q in range(1, weight_ref.shape[0]):
+                for q in range(1, capacity):
                     value = jnp.where(slot == q, rows_here[q:q + 1], value)
                 outs[s][row:row + 1, :] = value
 
@@ -69,7 +76,7 @@
             out_specs=[whole] * channels,
         ),
         out_shape=[jax.ShapeDtypeStruct((rows, TS), jnp.float32)] * channels,
-    )(picked, weight_slot, generator, hamiltonian, weight_rows)
+    )(order, owners, generator, hamiltonian, cross_weights)
 
 
 def finish(direct, home, place):
@@ -123,17 +130,11 @@
 
     order = tile_order[0, 0]
     owners = cross_owner[:, 0]
-    earlier = chan_range[None, :] < chan_range[:, None]
-    same_owner = owners[:, None] == owners[None, :]
-    slot_of = jnp.sum((same_owner & earlier).astype(jnp.int32), axis=1)
 
     dest = (me + chan_range) % channels
     source = (me - chan_range) % channels
-    picked = order[(dest[:, None] * spread + spread_range[None, :]).reshape(-1)]
-    weight_slot = jnp.clip(slot_of[dest], 0, capacity - 1)
-    weight_rows = cross_weights[0, 0]
     sends = build_sends(
-        picked, weight_slot, generator[0, 0], hamiltonian[0, 0], weight_rows, channels, spread
+        order, owners, generator[0, 0], hamiltonian[0, 0], cross_weights, channels, spread
     )
     got = [sends[0]]
     for shift in range(1, channels):

time: 98.2 us -> 93.6 us (0.953)
  other arithmetic: 4.75 us -> 2.94 us
  local copies, waits for them, and re-layouts: 12.1 us -> 10.3 us
  waiting for transfers between devices: 56.5 us -> 55.5 us
    gather x2 -> x0, local copies, waits for them, and re-layouts: 2.53 us -> none  [the longest x1 1.89 us: body(): picked = order[(dest[:, None] * spread + spread_range[None, :]).reshape(-1)]]
    reduce_sum x1 -> x0, other arithmetic: 1.13 us -> none  [body(): slot_of = jnp.sum((same_owner & earlier).astype(jnp.int32), axis=1)]
    ppermute x3, waiting for transfers between devices: 37.2 us -> 36.3 us  [body(): got.append(lax.ppermute(sends[shift], 'chan', pairs))]
  transfers between devices with their start and end apart: 6 -> 6, of which waited for: 4 -> 4; matrix products, arithmetic and copies ran while one was open for 8% -> 9% of each run, Pallas kernels for 0% -> 0%
where the time goes in v6:
time: 93.6 us; the launch traced here: 93.3 us
  waiting for transfers between devices  55.5 us (59%)
  local copies, waits for them, and re-layouts  10.3 us (11%)
  matrix products  8.43 us (9%)
  Pallas kernels  7.55 us (8%)
  starting transfers between devices  5.87 us (6%)
  other arithmetic  2.94 us (3%)
  between operations  2.78 us (3%)
    ppermute x3, waiting for transfers between devices, body(): got.append(lax.ppermute(sends[shift], 'chan', pairs))  36.3 us
    ppermute x3, waiting for transfers between devices, body(): home.append(lax.ppermute(back[shift], 'chan', pairs))  19.2 us
    pallas_call x1, Pallas kernels, build_sends(): pl.pallas_call(kernel, grid_spec=pltpu.PrefetchScalarGridSpec(num_scalar_...  3.8 us
    pallas_call x1, Pallas kernels, finish(): pl.pallas_call(kernel, grid_spec=pltpu.PrefetchScalarGridSpec(num_scalar_...  3.76 us
    unnamed x27, local copies, waits for them, and re-layouts  3.65 us
    ppermute x3, starting transfers between devices, body(): home.append(lax.ppermute(back[shift], 'chan', pairs))  3.51 us
    dot_general x2, matrix products, bracket(): jnp.matmul(right_matrix * scaled, left_matrix, precision=highest)  3.03 us
    ppermute x3, starting transfers between devices, body(): got.append(lax.ppermute(sends[shift], 'chan', pairs))  2.36 us
  transfers between devices with their start and end apart: 6, of which 4 were waited for; matrix products, arithmetic and copies ran while one was open for 9% of the time, Pallas kernels for 0%

profile of v6, /device:TPU:28, one launch (start us, length us, event | category | flops | bytes accessed | tf_op | source)
XLA Modules:
  0.0 93.3 jit_solution(926556182323340703)
XLA Ops:
  0.0 1.4 %copy.28.weight_ref = f32[1,1,3,512]{3,2,1,0:T(4,128)} copy(f32[1,1,3,512]{3,1,2,0:T(1,128)} %param.11) | data formatting | bytes 12288 | tf_op args[3]
  1.5 3.8 %shard_map.82 = (f32[1028,128]{1,0:T(8,128)}, f32[1028,128]{1,0:T(8,128)}, f32[1028,128]{1,0:T(8,128)}, f32[1028,128]{1,0:T(8,128)}) custom-call(s32[16]{0:T(128)} %bitcast.84, s32[4]{0:T(128)} %bitcast.103, f32[512,512]{1,0:T(8,128)} %bitcast.87, f32[512,512]{1,0:T(8,128)} %bitcast.88, f32[1,1,3,512]{3,2,1,0:T(4,128)} %copy.28.weight_ref), custom_call_target="tpu_custom_call" | custom-call | tf_op jit(solution)/shard_map/pallas_call | solution.py:70
  5.3 0.2 collective-permute-start
  5.5 1.7 %collective-permute-start.1 = (f32[1028,128]{1,0:T(8,128)}, f32[1028,128]{1,0:T(8,128)}, u32[]{:S(2)}, u32[]{:S(2)}) collective-permute-start(f32[1028,128]{1,0:T(8,128)} %get-tuple-element.11), channel_id=1, source_target_pairs={{0,8},{4,12},{8,0},{12,4},{1,9},{5,13},{9,1},{13,5},{2,10},{6,14},... | collective-permute-start | bytes 1579016 | tf_op jit(solution)/shard_map/ppermute | solution.py:142
  7.2 0.5 collective-permute-start.2
  7.7 0.6 constant_dynamic-slice_fusion
  9.0 0.6 constant_dynamic-slice_fusion.2
  11.8 0.6 gather_fusion.2
  12.5 0.6 gather_fusion.1
  13.1 1.0 %fusion.13 = f32[512,512]{0,1:T(8,128)S(1)} fusion(f32[1,1,512,512]{3,2,1,0:T(8,128)S(1)} %copy-done.2, f32[512]{0:T(512)S(1)} %bitcast.101, f32[1,1,512,512]{3,2,1,0:T(8,128)S(1)} %copy-done.3), kind=kOutput, calls=%fused_computation.24 | convolution fusion | flops 805568512 | bytes 3147776 | tf_op jit(solution)/shard_map/dot_general | solution.py:34
  14.2 1.0 %convolution_subtract_fusion.1 = f32[512,512]{0,1:T(8,128)S(1)} fusion(f32[512,512]{0,1:T(8,128)S(1)} %fusion.13, f32[1,1,512,512]{3,2,1,0:T(8,128)S(1)} %copy-done.3, f32[512]{0:T(512)S(1)} %bitcast.102, f32[1,1,512,512]{3,2,1,0:T(8,128)S(1)} %copy-done.2), kind=kOutput, calls=%fused_computation.5 | convolution fusion | flops 805830656 | bytes 4196352 | tf_op jit(solution)/shard_map/dot_general | solution.py:35
  15.2 0.3 copy.25
  15.7 1.2 %gather_fusion = s32[16]{0:T(128)} fusion(s32[16]{0:T(128)S(1)} %bitcast.85, s32[1024]{0:T(1024)S(1)} %pad_clamp_fusion.2), kind=kCustom, calls=%fused_computation | custom fusion | bytes 192 | tf_op jit(solution)/shard_map/gather | solution.py:163
  17.0 2.8 %collective-permute-done = f32[1028,128]{1,0:T(8,128)} collective-permute-done((f32[1028,128]{1,0:T(8,128)}, f32[1028,128]{1,0:T(8,128)}, u32[]{:S(2)}, u32[]{:S(2)}) %collective-permute-start) | collective-permute-done | bytes 526368 | tf_op jit(solution)/shard_map/ppermute | solution.py:142
  19.7 33.5 %collective-permute-done.1 = f32[1028,128]{1,0:T(8,128)} collective-permute-done((f32[1028,128]{1,0:T(8,128)}, f32[1028,128]{1,0:T(8,128)}, u32[]{:S(2)}, u32[]{:S(2)}) %collective-permute-start.1) | collective-permute-done | bytes 526368 | tf_op jit(solution)/shard_map/ppermute | solution.py:142
  53.2 1.5 %pad_maximum_fusion = f32[4,1028,128]{2,1,0:T(8,128)S(1)} fusion(f32[1,1028,128]{2,1,0:T(8,128)} %bitcast.21, f32[1,1028,128]{2,1,0:T(8,128)} %bitcast.20, f32[1,1028,128]{2,1,0:T(8,128)} %bitcast.19, f32[1,1028,128]{2,1,0:T(8,128)S(1)} %bitcast.97), kind=kLoop, calls=%fused_computation.3 | loop fusion | flops 1579008 | bytes 4210688 | tf_op jit(solution)/shard_map/stack | solution.py:143
  54.9 0.2 fusion.28
  55.1 1.2 %fusion.10 = f32[4,4,128,128]{3,1,2,0:T(4,128)S(1)} fusion(f32[4,4,16,1]{2,1,3,0:T(4,128)S(1)} %bitcast.98, f32[16,1,128,128]{3,2,1,0:T(8,128)S(1)} %get-tuple-element.13), kind=kOutput, calls=%fused_computation.18 | convolution fusion | flops 25165824 | bytes 2098176 | tf_op jit(solution)/shard_map/ji,ixy->jxy/dot_general | solution.py:151
  56.4 1.5 %bitcast_multiply_fusion = (f32[4,128,4,128]{3,2,1,0:T(4,128)S(1)}, f32[4,128,4,128]{3,2,1,0:T(4,128)S(1)}, f32[4,4,128,128]{3,1,2,0:T(4,128)S(1)}) fusion(f32[4,128]{1,0:T(4,128)S(1)} %dynamic-slice_bitcast_fusion, f32[4,4,128,128]{3,1,2,0:T(4,128)S(1)} %fusion.10, f32[4,4,16,1]{2,1,3,0:T(4,128)S(1)} %bitcast.99, f32[16,1,128,128]{3,2,1,0:T(8,128)S(1)} %get-tuple-element.14), kind=kOutput, calls=%fused_computation.19 | convolution fusion | flops 25690112 | bytes 5245952 | tf_op jit(solution)/shard_map/ji,ixy->jxy/dot_general | solution.py:152
  57.9 1.0 %fusion.4 = f32[512,512]{1,0:T(8,128)S(1)} fusion(f32[64,8,4,128]{3,2,1,0:T(4,128)S(1)} %bitcast.91, f32[64,8,4,128]{3,2,1,0:T(4,128)S(1)} %bitcast.90), kind=kOutput, calls=%fused_computation.10 | convolution fusion | flops 805306368 | bytes 3145728 | tf_op jit(solution)/shard_map/dot_general | solution.py:34
  58.9 2.0 %convolution_subtract_fusion = f32[512,512]{1,0:T(8,128)} fusion(f32[512,512]{1,0:T(8,128)S(1)} %fusion.4, f32[64,8,4,128]{3,2,1,0:T(4,128)S(1)} %bitcast.86, f32[64,8,4,128]{3,2,1,0:T(4,128)S(1)} %bitcast.92), kind=kOutput, calls=%fused_computation.4 | convolution fusion | flops 805568512 | bytes 4194304 | tf_op jit(solution)/shard_map/dot_general | solution.py:35
  60.9 1.6 %reshape.186 = f32[4,128,4,128]{3,2,1,0:T(4,128)S(1)} reshape(f32[512,512]{1,0:T(8,128)} %convolution_subtract_fusion) | data formatting | bytes 2097152 | tf_op jit(solution)/shard_map/reshape | solution.py:19
  62.7 0.6 fusion.19
  63.5 1.4 %collective-permute-start.4 = (f32[4,128,128]{2,1,0:T(8,128)S(1)}, f32[4,128,128]{2,1,0:T(8,128)S(1)}, u32[]{:S(2)}, u32[]{:S(2)}) collective-permute-start(f32[4,128,128]{2,1,0:T(8,128)S(1)} %copy.43), channel_id=1, source_target_pairs={{0,8},{4,12},{8,0},{12,4},{1,9},{5,13},{9,1},{13,5},{2,10},{6,14},... | collective-permute-start | bytes 786440 | tf_op jit(solution)/shard_map/ppermute | solution.py:162
  65.0 2.1 %collective-permute-start.5 = (f32[4,128,128]{2,1,0:T(8,128)S(1)}, f32[4,128,128]{2,1,0:T(8,128)S(1)}, u32[]{:S(2)}, u32[]{:S(2)}) collective-permute-start(f32[4,128,128]{2,1,0:T(8,128)S(1)} %copy.44), channel_id=1, source_target_pairs={{0,12},{4,0},{8,4},{12,8},{1,13},{5,1},{9,5},{13,9},{2,14},{6,2},{... | collective-permute-start | bytes 786440 | tf_op jit(solution)/shard_map/ppermute | solution.py:162
  67.0 1.2 %fusion.11.direct_ref = f32[512,512]{1,0:T(8,128)} fusion(f32[512,512]{1,0:T(8,128)S(1)} %copy.25, f32[512,512]{0,1:T(8,128)S(1)} %convolution_subtract_fusion.1), kind=kLoop, calls=%fused_computation.22 | loop fusion | flops 524288 | bytes 3145728 | tf_op jit(solution)/shard_map/mul | solution.py:166
  68.2 0.7 copy.41.rest_0_
  69.0 1.7 %collective-permute-done.3.rest_1_ = f32[4,128,128]{2,1,0:T(8,128)S(1)} collective-permute-done((f32[4,128,128]{2,1,0:T(8,128)S(1)}, f32[4,128,128]{2,1,0:T(8,128)S(1)}, u32[]{:S(2)}, u32[]{:S(2)}) %collective-permute-start.3) | collective-permute-done | bytes 262176 | tf_op jit(solution)/shard_map/ppermute | solution.py:162
  70.7 17.5 %collective-permute-done.4.rest_2_ = f32[4,128,128]{2,1,0:T(8,128)S(1)} collective-permute-done((f32[4,128,128]{2,1,0:T(8,128)S(1)}, f32[4,128,128]{2,1,0:T(8,128)S(1)}, u32[]{:S(2)}, u32[]{:S(2)}) %collective-permute-start.4) | collective-permute-done | bytes 262176 | tf_op jit(solution)/shard_map/ppermute | solution.py:162
  88.2 0.7 copy-done.6
  88.9 0.7 copy-done.7
  89.6 3.8 %shard_map.83 = f32[512,512]{1,0:T(8,128)} custom-call(s32[16]{0:T(128)} %gather_fusion, f32[512,512]{1,0:T(8,128)} %fusion.11.direct_ref, f32[4,128,128]{2,1,0:T(8,128)} %copy.41.rest_0_, f32[4,128,128]{2,1,0:T(8,128)} %copy-done.5, f32[4,128,128]{2,1,0:T(8,128)} %copy-done.6, f32[4,128,128]{2,1,0:T(8,128)} %copy-done.7), custom_call_target="tpu_custom_call" | custom-call | tf_op jit(solution)/shard_map/pallas_call | solution.py:100
  (47 shorter events, 1.3 us)
Async XLA Ops:
  0.0 11.5 %copy-start = (f32[8,16,16]{2,1,0:T(8,128)S(1)}, f32[8,16,16]{2,1,0:T(8,128)}, u32[]{:S(2)}) copy-start(f32[8,16,16]{2,1,0:T(8,128)} %param.12) | copy-start | bytes 24580
  0.0 7.6 %copy-start.9 = (s32[4,1]{0,1:T(1,128)S(1)}, s32[4,1]{0,1:T(1,128)}, u32[]{:S(2)}) copy-start(s32[4,1]{0,1:T(1,128)} %param.13) | copy-start | bytes 52
  0.0 13.1 %copy-start.3 = (f32[1,1,512,512]{3,2,1,0:T(8,128)S(1)}, f32[1,1,512,512]{3,2,1,0:T(8,128)}, u32[]{:S(2)}) copy-start(f32[1,1,512,512]{3,2,1,0:T(8,128)} %param.9) | copy-start | bytes 3145732
  0.0 13.1 %copy-start.2 = (f32[1,1,512,512]{3,2,1,0:T(8,128)S(1)}, f32[1,1,512,512]{3,2,1,0:T(8,128)}, u32[]{:S(2)}) copy-start(f32[1,1,512,512]{3,2,1,0:T(8,128)} %param.8) | copy-start | bytes 3145732
  0.0 9.0 %copy-start.10 = (s32[4,1]{0,1:T(1,128)S(1)}, s32[4,1]{0,1:T(1,128)}, u32[]{:S(2)}) copy-start(s32[4,1]{0,1:T(1,128)} %param.15) | copy-start | bytes 52
  0.0 13.1 %copy-start.8 = (f32[1,1,512]{2,1,0:T(1,128)S(1)}, f32[1,1,512]{2,1,0:T(1,128)}, u32[]{:S(2)}) copy-start(f32[1,1,512]{2,1,0:T(1,128)} %param.10) | copy-start | bytes 6148
  5.3 14.4 %collective-permute-start = (f32[1028,128]{1,0:T(8,128)}, f32[1028,128]{1,0:T(8,128)}, u32[]{:S(2)}, u32[]{:S(2)}) collective-permute-start(f32[1028,128]{1,0:T(8,128)} %get-tuple-element.10), channel_id=1, source_target_pairs={{0,4},{4,8},{8,12},{12,0},{1,5},{5,9},{9,13},{13,1},{2,6},{6,10},{... | collective-permute-start | bytes 1579016 | tf_op jit(solution)/shard_map/ppermute | solution.py:142
  5.5 47.7 %collective-permute-start.1 = (f32[1028,128]{1,0:T(8,128)}, f32[1028,128]{1,0:T(8,128)}, u32[]{:S(2)}, u32[]{:S(2)}) collective-permute-start(f32[1028,128]{1,0:T(8,128)} %get-tuple-element.11), channel_id=1, source_target_pairs={{0,8},{4,12},{8,0},{12,4},{1,9},{5,13},{9,1},{13,5},{2,10},{6,14},... | collective-permute-start | bytes 1579016 | tf_op jit(solution)/shard_map/ppermute | solution.py:142
  7.2 46.0 %collective-permute-start.2 = (f32[1028,128]{1,0:T(8,128)}, f32[1028,128]{1,0:T(8,128)}, u32[]{:S(2)}, u32[]{:S(2)}) collective-permute-start(f32[1028,128]{1,0:T(8,128)} %get-tuple-element.12), channel_id=1, source_target_pairs={{0,12},{4,0},{8,4},{12,8},{1,13},{5,1},{9,5},{13,9},{2,14},{6,2},{... | collective-permute-start | bytes 1579016 | tf_op jit(solution)/shard_map/ppermute | solution.py:142
  14.1 1.6 %copy-start.1 = (s32[1,1,16]{2,1,0:T(1,128)S(1)}, s32[1,1,16]{2,1,0:T(1,128)}, u32[]{:S(2)}) copy-start(s32[1,1,16]{2,1,0:T(1,128)} %param.14) | copy-start | bytes 196
  15.2 38.0 %copy-start.4 = (f32[1028,128]{1,0:T(8,128)S(1)}, f32[1028,128]{1,0:T(8,128)}, u32[]{:S(2)}) copy-start(f32[1028,128]{1,0:T(8,128)} %get-tuple-element.9) | copy-start | bytes 1579012
  63.5 7.2 %collective-permute-start.3 = (f32[4,128,128]{2,1,0:T(8,128)S(1)}, f32[4,128,128]{2,1,0:T(8,128)S(1)}, u32[]{:S(2)}, u32[]{:S(2)}) collective-permute-start(f32[4,128,128]{2,1,0:T(8,128)S(1)} %copy.42), channel_id=1, source_target_pairs={{0,4},{4,8},{8,12},{12,0},{1,5},{5,9},{9,13},{13,1},{2,6},{6,10},{... | collective-permute-start | bytes 786440 | tf_op jit(solution)/shard_map/ppermute | solution.py:162
  63.5 24.6 %collective-permute-start.4 = (f32[4,128,128]{2,1,0:T(8,128)S(1)}, f32[4,128,128]{2,1,0:T(8,128)S(1)}, u32[]{:S(2)}, u32[]{:S(2)}) collective-permute-start(f32[4,128,128]{2,1,0:T(8,128)S(1)} %copy.43), channel_id=1, source_target_pairs={{0,8},{4,12},{8,0},{12,4},{1,9},{5,13},{9,1},{13,5},{2,10},{6,14},... | collective-permute-start | bytes 786440 | tf_op jit(solution)/shard_map/ppermute | solution.py:162
  65.0 23.2 %collective-permute-start.5 = (f32[4,128,128]{2,1,0:T(8,128)S(1)}, f32[4,128,128]{2,1,0:T(8,128)S(1)}, u32[]{:S(2)}, u32[]{:S(2)}) collective-permute-start(f32[4,128,128]{2,1,0:T(8,128)S(1)} %copy.44), channel_id=1, source_target_pairs={{0,12},{4,0},{8,4},{12,8},{1,13},{5,1},{9,5},{13,9},{2,14},{6,2},{... | collective-permute-start | bytes 786440 | tf_op jit(solution)/shard_map/ppermute | solution.py:162
  70.7 17.5 %copy-start.5 = (f32[4,128,128]{2,1,0:T(8,128)}, f32[4,128,128]{2,1,0:T(8,128)S(1)}, u32[]{:S(2)}) copy-start(f32[4,128,128]{2,1,0:T(8,128)S(1)} %collective-permute-done.3.rest_1_) | copy-start | bytes 786436
  88.2 0.7 copy-start.6
  88.9 0.7 copy-start.7

commit v7 on v6

--- a/solution.py
+++ b/solution.py
@@ -86,24 +86,32 @@
 
     def kernel(place_ref, direct_ref, *rest):
         pieces, out_ref = rest[:-1], rest[-1]
+        a = pl.program_id(0)
         out_ref[...] = direct_ref[...]
         for s, piece in enumerate(pieces):
             for r in range(spread):
                 tile = place_ref[s * spread + r]
-                top = pl.multiple_of((tile // blocks) * TS, TS)
-                left = pl.multiple_of((tile % blocks) * TS, TS)
-                value = 0.5 * piece[r]
-                out_ref[pl.ds(top, TS), pl.ds(left, TS)] += value
-                out_ref[pl.ds(left, TS), pl.ds(top, TS)] += value.T
+                row, col = tile // blocks, tile % blocks
 
-    whole = pl.BlockSpec(memory_space=pltpu.VMEM)
+                @pl.when(row == a)
+                def _():
+                    left = pl.multiple_of(col * TS, TS)
+                    out_ref[:, pl.ds(left, TS)] += 0.5 * piece[r]
+
+                @pl.when(col == a)
+                def _():
+                    left = pl.multiple_of(row * TS, TS)
+                    out_ref[:, pl.ds(left, TS)] += 0.5 * piece[r].T
+
+    band = pl.BlockSpec((TS, size), lambda a, place: (a, 0))
+    whole = pl.BlockSpec((spread, TS, TS), lambda a, place: (0, 0, 0))
     return pl.pallas_call(
         kernel,
         grid_spec=pltpu.PrefetchScalarGridSpec(
             num_scalar_prefetch=1,
-            grid=(1,),
-            in_specs=[whole] * (1 + len(home)),
-            out_specs=whole,
+            grid=(blocks,),
+            in_specs=[band] + [whole] * len(home),
+            out_specs=band,
         ),
         out_shape=jax.ShapeDtypeStruct((size, size), jnp.float32),
     )(place, direct, *home)

time: 93.6 us -> 95.9 us (1.025)
  Pallas kernels: 7.55 us -> 9.72 us
    pallas_call x1, Pallas kernels: 3.76 us -> 5.92 us  [finish(): pl.pallas_call(kernel, grid_spec=pltpu.PrefetchScalarGridSpec(num_scalar_...]
where the time goes in v7:
time: 95.9 us; the launch traced here: 95.5 us
  waiting for transfers between devices  55.5 us (58%)
  local copies, waits for them, and re-layouts  10.3 us (11%)
  Pallas kernels  9.72 us (10%)
  matrix products  8.43 us (9%)
  starting transfers between devices  5.86 us (6%)
  other arithmetic  2.94 us (3%)
  between operations  2.78 us (3%)
    ppermute x3, waiting for transfers between devices, body(): got.append(lax.ppermute(sends[shift], 'chan', pairs))  36.3 us
    ppermute x3, waiting for transfers between devices, body(): home.append(lax.ppermute(back[shift], 'chan', pairs))  19.2 us
    pallas_call x1, Pallas kernels, finish(): pl.pallas_call(kernel, grid_spec=pltpu.PrefetchScalarGridSpec(num_scalar_...  5.92 us
    pallas_call x1, Pallas kernels, build_sends(): pl.pallas_call(kernel, grid_spec=pltpu.PrefetchScalarGridSpec(num_scalar_...  3.8 us
    unnamed x27, local copies, waits for them, and re-layouts  3.65 us
    ppermute x3, starting transfers between devices, body(): home.append(lax.ppermute(back[shift], 'chan', pairs))  3.5 us
    dot_general x2, matrix products, bracket(): jnp.matmul(right_matrix * scaled, left_matrix, precision=highest)  3.03 us
    ppermute x3, starting transfers between devices, body(): got.append(lax.ppermute(sends[shift], 'chan', pairs))  2.36 us
  transfers between devices with their start and end apart: 6, of which 4 were waited for; matrix products, arithmetic and copies ran while one was open for 9% of the time, Pallas kernels for 0%

profile of v7, /device:TPU:28, one launch (start us, length us, event | category | flops | bytes accessed | tf_op | source)
XLA Modules:
  0.0 95.5 jit_solution(9687126268234972788)
XLA Ops:
  0.0 1.4 %copy.28.weight_ref = f32[1,1,3,512]{3,2,1,0:T(4,128)} copy(f32[1,1,3,512]{3,1,2,0:T(1,128)} %param.11) | data formatting | bytes 12288 | tf_op args[3]
  1.5 3.8 %shard_map.82 = (f32[1028,128]{1,0:T(8,128)}, f32[1028,128]{1,0:T(8,128)}, f32[1028,128]{1,0:T(8,128)}, f32[1028,128]{1,0:T(8,128)}) custom-call(s32[16]{0:T(128)} %bitcast.84, s32[4]{0:T(128)} %bitcast.103, f32[512,512]{1,0:T(8,128)} %bitcast.87, f32[512,512]{1,0:T(8,128)} %bitcast.88, f32[1,1,3,512]{3,2,1,0:T(4,128)} %copy.28.weight_ref), custom_call_target="tpu_custom_call" | custom-call | tf_op jit(solution)/shard_map/pallas_call | solution.py:70
  5.3 0.2 collective-permute-start
  5.5 1.7 %collective-permute-start.1 = (f32[1028,128]{1,0:T(8,128)}, f32[1028,128]{1,0:T(8,128)}, u32[]{:S(2)}, u32[]{:S(2)}) collective-permute-start(f32[1028,128]{1,0:T(8,128)} %get-tuple-element.11), channel_id=1, source_target_pairs={{0,8},{4,12},{8,0},{12,4},{1,9},{5,13},{9,1},{13,5},{2,10},{6,14},... | collective-permute-start | bytes 1579016 | tf_op jit(solution)/shard_map/ppermute | solution.py:150
  7.2 0.4 collective-permute-start.2
  7.7 0.6 constant_dynamic-slice_fusion
  9.0 0.6 constant_dynamic-slice_fusion.2
  11.8 0.6 gather_fusion.2
  12.5 0.6 gather_fusion.1
  13.1 1.0 %fusion.13 = f32[512,512]{0,1:T(8,128)S(1)} fusion(f32[1,1,512,512]{3,2,1,0:T(8,128)S(1)} %copy-done.2, f32[512]{0:T(512)S(1)} %bitcast.101, f32[1,1,512,512]{3,2,1,0:T(8,128)S(1)} %copy-done.3), kind=kOutput, calls=%fused_computation.24 | convolution fusion | flops 805568512 | bytes 3147776 | tf_op jit(solution)/shard_map/dot_general | solution.py:34
  14.2 1.0 %convolution_subtract_fusion.1 = f32[512,512]{0,1:T(8,128)S(1)} fusion(f32[512,512]{0,1:T(8,128)S(1)} %fusion.13, f32[1,1,512,512]{3,2,1,0:T(8,128)S(1)} %copy-done.3, f32[512]{0:T(512)S(1)} %bitcast.102, f32[1,1,512,512]{3,2,1,0:T(8,128)S(1)} %copy-done.2), kind=kOutput, calls=%fused_computation.5 | convolution fusion | flops 805830656 | bytes 4196352 | tf_op jit(solution)/shard_map/dot_general | solution.py:35
  15.2 0.3 copy.25
  15.7 1.2 %gather_fusion = s32[16]{0:T(128)} fusion(s32[16]{0:T(128)S(1)} %bitcast.85, s32[1024]{0:T(1024)S(1)} %pad_clamp_fusion.2), kind=kCustom, calls=%fused_computation | custom fusion | bytes 192 | tf_op jit(solution)/shard_map/gather | solution.py:171
  17.0 2.8 %collective-permute-done = f32[1028,128]{1,0:T(8,128)} collective-permute-done((f32[1028,128]{1,0:T(8,128)}, f32[1028,128]{1,0:T(8,128)}, u32[]{:S(2)}, u32[]{:S(2)}) %collective-permute-start) | collective-permute-done | bytes 526368 | tf_op jit(solution)/shard_map/ppermute | solution.py:150
  19.7 33.5 %collective-permute-done.1 = f32[1028,128]{1,0:T(8,128)} collective-permute-done((f32[1028,128]{1,0:T(8,128)}, f32[1028,128]{1,0:T(8,128)}, u32[]{:S(2)}, u32[]{:S(2)}) %collective-permute-start.1) | collective-permute-done | bytes 526368 | tf_op jit(solution)/shard_map/ppermute | solution.py:150
  53.2 1.5 %pad_maximum_fusion = f32[4,1028,128]{2,1,0:T(8,128)S(1)} fusion(f32[1,1028,128]{2,1,0:T(8,128)} %bitcast.21, f32[1,1028,128]{2,1,0:T(8,128)} %bitcast.20, f32[1,1028,128]{2,1,0:T(8,128)} %bitcast.19, f32[1,1028,128]{2,1,0:T(8,128)S(1)} %bitcast.97), kind=kLoop, calls=%fused_computation.3 | loop fusion | flops 1579008 | bytes 4210688 | tf_op jit(solution)/shard_map/stack | solution.py:151
  54.9 0.2 fusion.28
  55.1 1.2 %fusion.10 = f32[4,4,128,128]{3,1,2,0:T(4,128)S(1)} fusion(f32[4,4,16,1]{2,1,3,0:T(4,128)S(1)} %bitcast.98, f32[16,1,128,128]{3,2,1,0:T(8,128)S(1)} %get-tuple-element.13), kind=kOutput, calls=%fused_computation.18 | convolution fusion | flops 25165824 | bytes 2098176 | tf_op jit(solution)/shard_map/ji,ixy->jxy/dot_general | solution.py:159
  56.4 1.5 %bitcast_multiply_fusion = (f32[4,128,4,128]{3,2,1,0:T(4,128)S(1)}, f32[4,128,4,128]{3,2,1,0:T(4,128)S(1)}, f32[4,4,128,128]{3,1,2,0:T(4,128)S(1)}) fusion(f32[4,128]{1,0:T(4,128)S(1)} %dynamic-slice_bitcast_fusion, f32[4,4,128,128]{3,1,2,0:T(4,128)S(1)} %fusion.10, f32[4,4,16,1]{2,1,3,0:T(4,128)S(1)} %bitcast.99, f32[16,1,128,128]{3,2,1,0:T(8,128)S(1)} %get-tuple-element.14), kind=kOutput, calls=%fused_computation.19 | convolution fusion | flops 25690112 | bytes 5245952 | tf_op jit(solution)/shard_map/ji,ixy->jxy/dot_general | solution.py:160
  57.9 1.0 %fusion.4 = f32[512,512]{1,0:T(8,128)S(1)} fusion(f32[64,8,4,128]{3,2,1,0:T(4,128)S(1)} %bitcast.91, f32[64,8,4,128]{3,2,1,0:T(4,128)S(1)} %bitcast.90), kind=kOutput, calls=%fused_computation.10 | convolution fusion | flops 805306368 | bytes 3145728 | tf_op jit(solution)/shard_map/dot_general | solution.py:34
  58.9 2.0 %convolution_subtract_fusion = f32[512,512]{1,0:T(8,128)} fusion(f32[512,512]{1,0:T(8,128)S(1)} %fusion.4, f32[64,8,4,128]{3,2,1,0:T(4,128)S(1)} %bitcast.86, f32[64,8,4,128]{3,2,1,0:T(4,128)S(1)} %bitcast.92), kind=kOutput, calls=%fused_computation.4 | convolution fusion | flops 805568512 | bytes 4194304 | tf_op jit(solution)/shard_map/dot_general | solution.py:35
  60.9 1.6 %reshape.186 = f32[4,128,4,128]{3,2,1,0:T(4,128)S(1)} reshape(f32[512,512]{1,0:T(8,128)} %convolution_subtract_fusion) | data formatting | bytes 2097152 | tf_op jit(solution)/shard_map/reshape | solution.py:19
  62.7 0.6 fusion.19
  63.5 1.4 %collective-permute-start.4 = (f32[4,128,128]{2,1,0:T(8,128)S(1)}, f32[4,128,128]{2,1,0:T(8,128)S(1)}, u32[]{:S(2)}, u32[]{:S(2)}) collective-permute-start(f32[4,128,128]{2,1,0:T(8,128)S(1)} %copy.43), channel_id=1, source_target_pairs={{0,8},{4,12},{8,0},{12,4},{1,9},{5,13},{9,1},{13,5},{2,10},{6,14},... | collective-permute-start | bytes 786440 | tf_op jit(solution)/shard_map/ppermute | solution.py:170
  65.0 2.1 %collective-permute-start.5 = (f32[4,128,128]{2,1,0:T(8,128)S(1)}, f32[4,128,128]{2,1,0:T(8,128)S(1)}, u32[]{:S(2)}, u32[]{:S(2)}) collective-permute-start(f32[4,128,128]{2,1,0:T(8,128)S(1)} %copy.44), channel_id=1, source_target_pairs={{0,12},{4,0},{8,4},{12,8},{1,13},{5,1},{9,5},{13,9},{2,14},{6,2},{... | collective-permute-start | bytes 786440 | tf_op jit(solution)/shard_map/ppermute | solution.py:170
  67.0 1.2 %fusion.11.direct_ref = f32[512,512]{1,0:T(8,128)} fusion(f32[512,512]{1,0:T(8,128)S(1)} %copy.25, f32[512,512]{0,1:T(8,128)S(1)} %convolution_subtract_fusion.1), kind=kLoop, calls=%fused_computation.22 | loop fusion | flops 524288 | bytes 3145728 | tf_op jit(solution)/shard_map/mul | solution.py:174
  68.2 0.7 copy.41.rest_0_
  69.0 1.7 %collective-permute-done.3.rest_1_ = f32[4,128,128]{2,1,0:T(8,128)S(1)} collective-permute-done((f32[4,128,128]{2,1,0:T(8,128)S(1)}, f32[4,128,128]{2,1,0:T(8,128)S(1)}, u32[]{:S(2)}, u32[]{:S(2)}) %collective-permute-start.3) | collective-permute-done | bytes 262176 | tf_op jit(solution)/shard_map/ppermute | solution.py:170
  70.7 17.5 %collective-permute-done.4.rest_2_ = f32[4,128,128]{2,1,0:T(8,128)S(1)} collective-permute-done((f32[4,128,128]{2,1,0:T(8,128)S(1)}, f32[4,128,128]{2,1,0:T(8,128)S(1)}, u32[]{:S(2)}, u32[]{:S(2)}) %collective-permute-start.4) | collective-permute-done | bytes 262176 | tf_op jit(solution)/shard_map/ppermute | solution.py:170
  88.2 0.7 copy-done.6
  88.9 0.7 copy-done.7
  89.6 5.9 %shard_map.83 = f32[512,512]{1,0:T(8,128)} custom-call(s32[16]{0:T(128)} %gather_fusion, f32[512,512]{1,0:T(8,128)} %fusion.11.direct_ref, f32[4,128,128]{2,1,0:T(8,128)} %copy.41.rest_0_, f32[4,128,128]{2,1,0:T(8,128)} %copy-done.5, f32[4,128,128]{2,1,0:T(8,128)} %copy-done.6, f32[4,128,128]{2,1,0:T(8,128)} %copy-done.7), custom_call_target="tpu_custom_call" | custom-call | tf_op jit(solution)/shard_map/pallas_call | solution.py:108
  (47 shorter events, 1.3 us)
Async XLA Ops:
  0.0 11.5 %copy-start = (f32[8,16,16]{2,1,0:T(8,128)S(1)}, f32[8,16,16]{2,1,0:T(8,128)}, u32[]{:S(2)}) copy-start(f32[8,16,16]{2,1,0:T(8,128)} %param.12) | copy-start | bytes 24580
  0.0 7.6 %copy-start.9 = (s32[4,1]{0,1:T(1,128)S(1)}, s32[4,1]{0,1:T(1,128)}, u32[]{:S(2)}) copy-start(s32[4,1]{0,1:T(1,128)} %param.13) | copy-start | bytes 52
  0.0 13.1 %copy-start.3 = (f32[1,1,512,512]{3,2,1,0:T(8,128)S(1)}, f32[1,1,512,512]{3,2,1,0:T(8,128)}, u32[]{:S(2)}) copy-start(f32[1,1,512,512]{3,2,1,0:T(8,128)} %param.9) | copy-start | bytes 3145732
  0.0 13.1 %copy-start.2 = (f32[1,1,512,512]{3,2,1,0:T(8,128)S(1)}, f32[1,1,512,512]{3,2,1,0:T(8,128)}, u32[]{:S(2)}) copy-start(f32[1,1,512,512]{3,2,1,0:T(8,128)} %param.8) | copy-start | bytes 3145732
  0.0 9.0 %copy-start.10 = (s32[4,1]{0,1:T(1,128)S(1)}, s32[4,1]{0,1:T(1,128)}, u32[]{:S(2)}) copy-start(s32[4,1]{0,1:T(1,128)} %param.15) | copy-start | bytes 52
  0.0 13.1 %copy-start.8 = (f32[1,1,512]{2,1,0:T(1,128)S(1)}, f32[1,1,512]{2,1,0:T(1,128)}, u32[]{:S(2)}) copy-start(f32[1,1,512]{2,1,0:T(1,128)} %param.10) | copy-start | bytes 6148
  5.3 14.5 %collective-permute-start = (f32[1028,128]{1,0:T(8,128)}, f32[1028,128]{1,0:T(8,128)}, u32[]{:S(2)}, u32[]{:S(2)}) collective-permute-start(f32[1028,128]{1,0:T(8,128)} %get-tuple-element.10), channel_id=1, source_target_pairs={{0,4},{4,8},{8,12},{12,0},{1,5},{5,9},{9,13},{13,1},{2,6},{6,10},{... | collective-permute-start | bytes 1579016 | tf_op jit(solution)/shard_map/ppermute | solution.py:150
  5.5 47.7 %collective-permute-start.1 = (f32[1028,128]{1,0:T(8,128)}, f32[1028,128]{1,0:T(8,128)}, u32[]{:S(2)}, u32[]{:S(2)}) collective-permute-start(f32[1028,128]{1,0:T(8,128)} %get-tuple-element.11), channel_id=1, source_target_pairs={{0,8},{4,12},{8,0},{12,4},{1,9},{5,13},{9,1},{13,5},{2,10},{6,14},... | collective-permute-start | bytes 1579016 | tf_op jit(solution)/shard_map/ppermute | solution.py:150
  7.2 46.0 %collective-permute-start.2 = (f32[1028,128]{1,0:T(8,128)}, f32[1028,128]{1,0:T(8,128)}, u32[]{:S(2)}, u32[]{:S(2)}) collective-permute-start(f32[1028,128]{1,0:T(8,128)} %get-tuple-element.12), channel_id=1, source_target_pairs={{0,12},{4,0},{8,4},{12,8},{1,13},{5,1},{9,5},{13,9},{2,14},{6,2},{... | collective-permute-start | bytes 1579016 | tf_op jit(solution)/shard_map/ppermute | solution.py:150
  14.1 1.6 %copy-start.1 = (s32[1,1,16]{2,1,0:T(1,128)S(1)}, s32[1,1,16]{2,1,0:T(1,128)}, u32[]{:S(2)}) copy-start(s32[1,1,16]{2,1,0:T(1,128)} %param.14) | copy-start | bytes 196
  15.2 38.0 %copy-start.4 = (f32[1028,128]{1,0:T(8,128)S(1)}, f32[1028,128]{1,0:T(8,128)}, u32[]{:S(2)}) copy-start(f32[1028,128]{1,0:T(8,128)} %get-tuple-element.9) | copy-start | bytes 1579012
  63.5 7.2 %collective-permute-start.3 = (f32[4,128,128]{2,1,0:T(8,128)S(1)}, f32[4,128,128]{2,1,0:T(8,128)S(1)}, u32[]{:S(2)}, u32[]{:S(2)}) collective-permute-start(f32[4,128,128]{2,1,0:T(8,128)S(1)} %copy.42), channel_id=1, source_target_pairs={{0,4},{4,8},{8,12},{12,0},{1,5},{5,9},{9,13},{13,1},{2,6},{6,10},{... | collective-permute-start | bytes 786440 | tf_op jit(solution)/shard_map/ppermute | solution.py:170
  63.5 24.6 %collective-permute-start.4 = (f32[4,128,128]{2,1,0:T(8,128)S(1)}, f32[4,128,128]{2,1,0:T(8,128)S(1)}, u32[]{:S(2)}, u32[]{:S(2)}) collective-permute-start(f32[4,128,128]{2,1,0:T(8,128)S(1)} %copy.43), channel_id=1, source_target_pairs={{0,8},{4,12},{8,0},{12,4},{1,9},{5,13},{9,1},{13,5},{2,10},{6,14},... | collective-permute-start | bytes 786440 | tf_op jit(solution)/shard_map/ppermute | solution.py:170
  65.0 23.2 %collective-permute-start.5 = (f32[4,128,128]{2,1,0:T(8,128)S(1)}, f32[4,128,128]{2,1,0:T(8,128)S(1)}, u32[]{:S(2)}, u32[]{:S(2)}) collective-permute-start(f32[4,128,128]{2,1,0:T(8,128)S(1)} %copy.44), channel_id=1, source_target_pairs={{0,12},{4,0},{8,4},{12,8},{1,13},{5,1},{9,5},{13,9},{2,14},{6,2},{... | collective-permute-start | bytes 786440 | tf_op jit(solution)/shard_map/ppermute | solution.py:170
  70.7 17.5 %copy-start.5 = (f32[4,128,128]{2,1,0:T(8,128)}, f32[4,128,128]{2,1,0:T(8,128)S(1)}, u32[]{:S(2)}) copy-start(f32[4,128,128]{2,1,0:T(8,128)S(1)} %collective-permute-done.3.rest_1_) | copy-start | bytes 786436
  88.2 0.7 copy-start.6
  88.9 0.7 copy-start.7

commit v8 on v6

--- a/solution.py
+++ b/solution.py
@@ -140,21 +140,28 @@
     for shift in range(1, channels):
         pairs = [(c, (c + shift) % channels) for c in range(channels)]
         got.append(lax.ppermute(sends[shift], "chan", pairs))
-    got = jnp.stack(got)
-    tiles_got = got[:, : 2 * spread * TS].reshape(channels, spread, 2, TS, TS)
-    weights_cross = got[(me - owners[me]) % channels, 2 * spread * TS :].reshape(-1)
+    owner_shift = (me - owners[me]) % channels
+    weights_cross = sum(
+        jnp.where(owner_shift == shift, piece[2 * spread * TS :], 0.0)
+        for shift, piece in enumerate(got)
+    ).reshape(-1)
 
+    blocks = size // TS
     mixer = recoupling[recoupling_index[me, 0]]
-    column_of = (spread_range[None, :] * channels + source[:, None]).reshape(-1)
-    mixer_in = mixer[:, column_of]
-    cross = tiles_got.reshape(tile_count, 2, TS, TS)
-    generator_mixed = jnp.einsum("ji,ixy->jxy", mixer_in, cross[:, 0], precision=highest)
-    hamilton_mixed = jnp.einsum("ji,ixy->jxy", mixer_in, cross[:, 1], precision=highest)
-    product = bracket(
-        from_tiles(generator_mixed, TS), from_tiles(hamilton_mixed, TS), weights_cross
+    mixed = []
+    for m in range(2):
+        total = 0.0
+        for shift, piece in enumerate(got):
+            columns = spread_range * channels + source[shift]
+            weights_in = mixer[:, columns].reshape(blocks, blocks, spread)
+            tiles_in = piece[: 2 * spread * TS].reshape(spread, 2, TS, TS)[:, m]
+            total = total + jnp.einsum("abr,rxy->axby", weights_in, tiles_in, precision=highest)
+        mixed.append(total.reshape(size, size))
+    product = bracket(mixed[0], mixed[1], weights_cross).reshape(blocks, TS, blocks, TS)
+    mixer_out = mixer[:, (spread_range[None, :] * channels + dest[:, None]).reshape(-1)]
+    back = jnp.einsum(
+        "abi,axby->ixy", mixer_out.reshape(blocks, blocks, -1), product, precision=highest
     )
-    mixer_out = mixer[:, (spread_range[None, :] * channels + dest[:, None]).reshape(-1)]
-    back = jnp.einsum("ji,jxy->ixy", mixer_out, to_tiles(product, TS), precision=highest)
     back = back.reshape(channels, spread, TS, TS)
     home = [back[0]]
     for shift in range(1, channels):

time: 93.6 us -> 100 us (1.068); the launches traced: 93.3 us -> 98.7 us
  waiting for transfers between devices: 55.5 us -> 39.6 us
  local copies, waits for them, and re-layouts: 10.3 us -> 21 us
  matrix products: 8.43 us -> 18.2 us
  other arithmetic: 2.94 us -> 4.78 us
  starting transfers between devices: 5.87 us -> 4.55 us
    ppermute x3, waiting for transfers between devices: 36.3 us -> 20.5 us  [body(): got.append(lax.ppermute(sends[shift], 'chan', pairs))]
    dot_general x3 -> x9, matrix products: 3.34 us -> 10.9 us  [the longest x8 10.2 us: body(): jnp.einsum('abr,rxy->axby', weights_in, tiles_in, precision=highest)]
    slice x2 -> x9, local copies, waits for them, and re-layouts: 0.35 us -> 5.19 us  [the longest x8 4.54 us: body(): tiles_in = piece[:2 * spread * TS].reshape(spread, 2, TS, TS)[:, m]]
    unnamed x27 -> x29, local copies, waits for them, and re-layouts: 3.65 us -> 6.99 us
    select_n x1 -> x4, other arithmetic: 0.01 us -> 2.6 us  [body(): weights_in = mixer[:, columns].reshape(blocks, blocks, spread)]
    gather x2 -> x4, local copies, waits for them, and re-layouts: 0.64 us -> 2.23 us  [body(): weights_in = mixer[:, columns].reshape(blocks, blocks, spread)]
    another operation x1 -> x0, other arithmetic: 1.5 us -> none  [body(): got = jnp.stack(got)]
    ppermute x3, starting transfers between devices: 3.51 us -> 2.19 us  [body(): home.append(lax.ppermute(back[shift], 'chan', pairs))]
  transfers between devices with their start and end apart: 6 -> 6, of which waited for: 4 -> 3; matrix products, arithmetic and copies ran while one was open for 9% -> 23% of each run, Pallas kernels for 0% -> 0%
where the time goes in v8:
time: 100 us; the launch traced here: 98.7 us
  waiting for transfers between devices  39.6 us (40%)
  local copies, waits for them, and re-layouts  21 us (21%)
  matrix products  18.2 us (18%)
  Pallas kernels  7.59 us (8%)
  other arithmetic  4.78 us (5%)
  starting transfers between devices  4.55 us (5%)
  between operations  3 us (3%)
    ppermute x3, waiting for transfers between devices, body(): got.append(lax.ppermute(sends[shift], 'chan', pairs))  20.5 us
    ppermute x3, waiting for transfers between devices, body(): home.append(lax.ppermute(back[shift], 'chan', pairs))  19.1 us
    dot_general x8, matrix products, body(): jnp.einsum('abr,rxy->axby', weights_in, tiles_in, precision=highest)  10.2 us
    unnamed x29, local copies, waits for them, and re-layouts  6.99 us
    slice x8, local copies, waits for them, and re-layouts, body(): tiles_in = piece[:2 * spread * TS].reshape(spread, 2, TS, TS)[:, m]  4.54 us
    dot_general x2, matrix products, bracket(): jnp.matmul(right_matrix * scaled, left_matrix, precision=highest)  4.27 us
    pallas_call x1, Pallas kernels, build_sends(): pl.pallas_call(kernel, grid_spec=pltpu.PrefetchScalarGridSpec(num_scalar_...  3.84 us
    pallas_call x1, Pallas kernels, finish(): pl.pallas_call(kernel, grid_spec=pltpu.PrefetchScalarGridSpec(num_scalar_...  3.75 us
  transfers between devices with their start and end apart: 6, of which 3 were waited for; matrix products, arithmetic and copies ran while one was open for 23% of the time, Pallas kernels for 0%

profile of v8, /device:TPU:28, one launch (start us, length us, event | category | flops | bytes accessed | tf_op | source)
XLA Modules:
  0.0 98.7 jit_solution(8496796543146325352)
XLA Ops:
  0.0 1.3 %copy.41.weight_ref = f32[1,1,3,512]{3,2,1,0:T(4,128)} copy(f32[1,1,3,512]{3,1,2,0:T(1,128)} %param.11) | data formatting | bytes 12288 | tf_op args[3]
  1.3 3.8 %shard_map.82 = (f32[1028,128]{1,0:T(8,128)}, f32[1028,128]{1,0:T(8,128)}, f32[1028,128]{1,0:T(8,128)}, f32[1028,128]{1,0:T(8,128)}) custom-call(s32[16]{0:T(128)} %bitcast.158, s32[4]{0:T(128)} %bitcast.191, f32[512,512]{1,0:T(8,128)} %bitcast.165, f32[512,512]{1,0:T(8,128)} %bitcast.166, f32[1,1,3,512]{3,2,1,0:T(4,128)} %copy.41.weight_ref), custom_call_target="tpu_custom_call" | custom-call | tf_op jit(solution)/shard_map/pallas_call | solution.py:70
  5.4 1.7 %collective-permute-start.1 = (f32[1028,128]{1,0:T(8,128)}, f32[1028,128]{1,0:T(8,128)}, u32[]{:S(2)}, u32[]{:S(2)}) collective-permute-start(f32[1028,128]{1,0:T(8,128)} %get-tuple-element.11), channel_id=1, source_target_pairs={{0,8},{4,12},{8,0},{12,4},{1,9},{5,13},{9,1},{13,5},{2,10},{6,14},... | collective-permute-start | bytes 1579016 | tf_op jit(solution)/shard_map/ppermute | solution.py:142
  12.8 1.1 %slice.84 = f32[1024,128]{1,0:T(8,128)S(1)} slice(f32[1028,128]{1,0:T(8,128)} %get-tuple-element.9), slice={[0:1024], [0:128]} | slice | bytes 1048576 | tf_op jit(solution)/shard_map/slice | solution.py:157
  16.0 2.0 %fusion.20 = f32[128,128,4,4]{1,3,2,0:T(4,128)} fusion(f32[4,4,4,1]{2,1,0,3:T(4,128)S(1)} %bitcast.181, f32[4,1,128,128]{3,2,1,0:T(8,128)S(1)} %get-tuple-element.23), kind=kOutput, calls=%fused_computation.46 | convolution fusion | flops 6291456 | bytes 1310976 | tf_op jit(solution)/shard_map/abr,rxy->axby/dot_general | solution.py:158
  17.9 1.9 %fusion.19 = f32[128,128,4,4]{1,3,2,0:T(4,128)} fusion(f32[4,4,4,1]{2,1,0,3:T(4,128)S(1)} %bitcast.182, f32[4,1,128,128]{3,2,1,0:T(8,128)S(1)} %get-tuple-element.24), kind=kOutput, calls=%fused_computation.41 | convolution fusion | flops 6291456 | bytes 1310976 | tf_op jit(solution)/shard_map/abr,rxy->axby/dot_general | solution.py:158
  20.7 2.0 %fusion.13 = f32[512,512]{0,1:T(8,128)} fusion(f32[1,1,512,512]{3,2,1,0:T(8,128)S(1)} %copy-done.2, f32[512]{0:T(512)S(1)} %bitcast.189, f32[1,1,512,512]{3,2,1,0:T(8,128)S(1)} %copy-done.3), kind=kOutput, calls=%fused_computation.29 | convolution fusion | flops 805568512 | bytes 3147776 | tf_op jit(solution)/shard_map/dot_general | solution.py:34
  22.9 2.3 %convolution_subtract_fusion.1 = f32[512,512]{0,1:T(8,128)S(1)} fusion(f32[512,512]{0,1:T(8,128)} %fusion.13, f32[1,1,512,512]{3,2,1,0:T(8,128)S(1)} %copy-done.3, f32[512]{0:T(512)S(1)} %bitcast.190, f32[1,1,512,512]{3,2,1,0:T(8,128)S(1)} %copy-done.2), kind=kOutput, calls=%fused_computation.8 | convolution fusion | flops 805830656 | bytes 4196352 | tf_op jit(solution)/shard_map/dot_general | solution.py:35
  30.3 1.2 %gather_fusion = s32[16]{0:T(128)} fusion(s32[16]{0:T(128)S(1)} %bitcast.159, s32[1024]{0:T(1024)S(1)} %pad_clamp_fusion.5), kind=kCustom, calls=%fused_computation | custom fusion | bytes 192 | tf_op jit(solution)/shard_map/gather | solution.py:170
  31.5 1.1 %slice.121 = f32[1024,128]{1,0:T(8,128)S(1)} slice(f32[1028,128]{1,0:T(8,128)} %collective-permute-done), slice={[0:1024], [0:128]} | slice | bytes 1048576 | tf_op jit(solution)/shard_map/slice | solution.py:157
  32.6 20.5 %collective-permute-done.1 = f32[1028,128]{1,0:T(8,128)} collective-permute-done((f32[1028,128]{1,0:T(8,128)}, f32[1028,128]{1,0:T(8,128)}, u32[]{:S(2)}, u32[]{:S(2)}) %collective-permute-start.1) | collective-permute-done | bytes 526368 | tf_op jit(solution)/shard_map/ppermute | solution.py:142
  53.1 1.1 %slice.123 = f32[1024,128]{1,0:T(8,128)S(1)} slice(f32[1028,128]{1,0:T(8,128)} %collective-permute-done.1), slice={[0:1024], [0:128]} | slice | bytes 1048576 | tf_op jit(solution)/shard_map/slice | solution.py:157
  54.3 1.2 %slice.125 = f32[1024,128]{1,0:T(8,128)S(1)} slice(f32[1028,128]{1,0:T(8,128)} %collective-permute-done.2), slice={[0:1024], [0:128]} | slice | bytes 1048576 | tf_op jit(solution)/shard_map/slice | solution.py:157
  55.6 1.0 convolution_add_fusion.5
  56.6 1.0 convolution_add_fusion.4
  57.6 1.0 fusion.1
  58.8 1.0 %copy-done.4 = f32[128,128,4,4]{1,3,2,0:T(4,128)S(1)} copy-done((f32[128,128,4,4]{1,3,2,0:T(4,128)S(1)}, f32[128,128,4,4]{1,3,2,0:T(4,128)}, u32[]{:S(2)}) %copy-start.4) | copy-done | bytes 1048600
  59.8 1.0 convolution_add_fusion.2
  60.8 1.0 %convolution_add_fusion.1 = f32[128,128,4,4]{1,3,2,0:T(4,128)S(1)} fusion(f32[128,128,4,4]{1,3,2,0:T(4,128)S(1)} %convolution_add_fusion.2, f32[4,4,4,1]{2,1,0,3:T(4,128)S(1)} %bitcast.180, f32[4,1,128,128]{3,2,1,0:T(8,128)S(1)} %get-tuple-element.20), kind=kOutput, calls=%fused_computation.11 | convolution fusion | flops 6553600 | bytes 2359552 | tf_op jit(solution)/shard_map/abr,rxy->axby/dot_general | solution.py:158
  61.9 0.7 fusion.21
  62.6 1.3 %broadcast_multiply_fusion = (f32[4,128,4,128]{3,2,0,1:T(4,128)S(1)}, f32[4,128,4,128]{3,2,0,1:T(4,128)S(1)}, f32[4,128,4,128]{3,2,0,1:T(4,128)S(1)}) fusion(f32[4,128]{1,0:T(4,128)S(1)} %fusion.21, f32[4,128,4,128]{3,2,0,1:T(4,128)S(1)} %fusion.1, f32[128,128,4,4]{1,3,2,0:T(4,128)S(1)} %convolution_add_fusion.1, f32[4,4,4,1]{2,1,0,3:T(4,128)S(1)} %bitcast.176, ...), kind=kOutput, calls=%fused_computation.33 | convolution fusion | flops 7077888 | bytes 5507328 | tf_op jit(solution)/shard_map/abr,rxy->axby/dot_general | solution.py:158
  64.7 1.0 %fusion.6 = f32[512,512]{1,0:T(8,128)S(1)} fusion(f32[64,8,4,128]{3,2,1,0:T(4,128)S(1)} %bitcast.168, f32[64,8,4,128]{3,2,1,0:T(4,128)S(1)} %bitcast.167), kind=kOutput, calls=%fused_computation.21 | convolution fusion | flops 805306368 | bytes 3145728 | tf_op jit(solution)/shard_map/dot_general | solution.py:34
  65.7 2.0 %convolution_subtract_fusion = f32[512,512]{1,0:T(8,128)} fusion(f32[512,512]{1,0:T(8,128)S(1)} %fusion.6, f32[64,8,4,128]{3,2,1,0:T(4,128)S(1)} %bitcast.169, f32[64,8,4,128]{3,2,1,0:T(4,128)S(1)} %bitcast.170), kind=kOutput, calls=%fused_computation.7 | convolution fusion | flops 805568512 | bytes 4194304 | tf_op jit(solution)/shard_map/dot_general | solution.py:35
  67.7 1.6 %reshape.249 = f32[4,128,4,128]{3,2,1,0:T(4,128)S(1)} reshape(f32[512,512]{1,0:T(8,128)} %convolution_subtract_fusion) | data formatting | bytes 2097152 | tf_op jit(solution)/shard_map/reshape | solution.py:160
  69.3 0.7 convolution_bitcast_fusion
  70.4 2.1 %collective-permute-start.5 = (f32[4,128,128]{2,1,0:T(8,128)S(1)}, f32[4,128,128]{2,1,0:T(8,128)S(1)}, u32[]{:S(2)}, u32[]{:S(2)}) collective-permute-start(f32[4,128,128]{2,1,0:T(8,128)S(1)} %copy.93), channel_id=1, source_target_pairs={{0,12},{4,0},{8,4},{12,8},{1,13},{5,1},{9,5},{13,9},{2,14},{6,2},{... | collective-permute-start | bytes 786440 | tf_op jit(solution)/shard_map/ppermute | solution.py:169
  72.4 1.2 %fusion.11.direct_ref = f32[512,512]{1,0:T(8,128)} fusion(f32[512,512]{1,0:T(8,128)S(1)} %copy.38, f32[512,512]{0,1:T(8,128)S(1)} %convolution_subtract_fusion.1), kind=kLoop, calls=%fused_computation.27 | loop fusion | flops 524288 | bytes 3145728 | tf_op jit(solution)/shard_map/mul | solution.py:173
  73.7 0.7 copy.90.rest_0_
  74.4 4.0 %collective-permute-done.3.rest_1_ = f32[4,128,128]{2,1,0:T(8,128)S(1)} collective-permute-done((f32[4,128,128]{2,1,0:T(8,128)S(1)}, f32[4,128,128]{2,1,0:T(8,128)S(1)}, u32[]{:S(2)}, u32[]{:S(2)}) %collective-permute-start.3) | collective-permute-done | bytes 262176 | tf_op jit(solution)/shard_map/ppermute | solution.py:169
  78.4 15.1 %collective-permute-done.4.rest_2_ = f32[4,128,128]{2,1,0:T(8,128)S(1)} collective-permute-done((f32[4,128,128]{2,1,0:T(8,128)S(1)}, f32[4,128,128]{2,1,0:T(8,128)S(1)}, u32[]{:S(2)}, u32[]{:S(2)}) %collective-permute-start.4) | collective-permute-done | bytes 262176 | tf_op jit(solution)/shard_map/ppermute | solution.py:169
  93.5 0.7 copy-done.7
  94.9 3.8 %shard_map.83 = f32[512,512]{1,0:T(8,128)} custom-call(s32[16]{0:T(128)} %gather_fusion, f32[512,512]{1,0:T(8,128)} %fusion.11.direct_ref, f32[4,128,128]{2,1,0:T(8,128)} %copy.90.rest_0_, f32[4,128,128]{2,1,0:T(8,128)} %copy-done.6, f32[4,128,128]{2,1,0:T(8,128)} %copy-done.7, f32[4,128,128]{2,1,0:T(8,128)} %copy-done.8), custom_call_target="tpu_custom_call" | custom-call | tf_op jit(solution)/shard_map/pallas_call | solution.py:100
  (76 shorter events, 13.6 us)
Async XLA Ops:
  0.0 10.7 %copy-start = (f32[8,16,16]{2,1,0:T(8,128)S(1)}, f32[8,16,16]{2,1,0:T(8,128)}, u32[]{:S(2)}) copy-start(f32[8,16,16]{2,1,0:T(8,128)} %param.12) | copy-start | bytes 24580
  5.2 26.4 %collective-permute-start = (f32[1028,128]{1,0:T(8,128)}, f32[1028,128]{1,0:T(8,128)}, u32[]{:S(2)}, u32[]{:S(2)}) collective-permute-start(f32[1028,128]{1,0:T(8,128)} %get-tuple-element.10), channel_id=1, source_target_pairs={{0,4},{4,8},{8,12},{12,0},{1,5},{5,9},{9,13},{13,1},{2,6},{6,10},{... | collective-permute-start | bytes 1579016 | tf_op jit(solution)/shard_map/ppermute | solution.py:142
  5.4 47.7 %collective-permute-start.1 = (f32[1028,128]{1,0:T(8,128)}, f32[1028,128]{1,0:T(8,128)}, u32[]{:S(2)}, u32[]{:S(2)}) collective-permute-start(f32[1028,128]{1,0:T(8,128)} %get-tuple-element.11), channel_id=1, source_target_pairs={{0,8},{4,12},{8,0},{12,4},{1,9},{5,13},{9,1},{13,5},{2,10},{6,14},... | collective-permute-start | bytes 1579016 | tf_op jit(solution)/shard_map/ppermute | solution.py:142
  7.1 47.2 %collective-permute-start.2 = (f32[1028,128]{1,0:T(8,128)}, f32[1028,128]{1,0:T(8,128)}, u32[]{:S(2)}, u32[]{:S(2)}) collective-permute-start(f32[1028,128]{1,0:T(8,128)} %get-tuple-element.12), channel_id=1, source_target_pairs={{0,12},{4,0},{8,4},{12,8},{1,13},{5,1},{9,5},{13,9},{2,14},{6,2},{... | collective-permute-start | bytes 1579016 | tf_op jit(solution)/shard_map/ppermute | solution.py:142
  7.6 0.7 copy-start.11
  15.9 4.1 %copy-start.2 = (f32[1,1,512,512]{3,2,1,0:T(8,128)S(1)}, f32[1,1,512,512]{3,2,1,0:T(8,128)}, u32[]{:S(2)}) copy-start(f32[1,1,512,512]{3,2,1,0:T(8,128)} %param.8) | copy-start | bytes 3145732
  16.0 4.1 %copy-start.3 = (f32[1,1,512,512]{3,2,1,0:T(8,128)S(1)}, f32[1,1,512,512]{3,2,1,0:T(8,128)}, u32[]{:S(2)}) copy-start(f32[1,1,512,512]{3,2,1,0:T(8,128)} %param.9) | copy-start | bytes 3145732
  20.0 0.7 copy-start.9
  25.2 0.7 copy-start.10
  29.6 0.7 copy-start.1
  54.3 1.4 %copy-start.5 = (f32[128,128,4,4]{1,3,2,0:T(4,128)S(1)}, f32[128,128,4,4]{1,3,2,0:T(4,128)}, u32[]{:S(2)}) copy-start(f32[128,128,4,4]{1,3,2,0:T(4,128)} %fusion.20) | copy-start | bytes 3145732
  58.6 1.2 %copy-start.4 = (f32[128,128,4,4]{1,3,2,0:T(4,128)S(1)}, f32[128,128,4,4]{1,3,2,0:T(4,128)}, u32[]{:S(2)}) copy-start(f32[128,128,4,4]{1,3,2,0:T(4,128)} %fusion.19) | copy-start | bytes 3145732
  70.2 8.2 %collective-permute-start.3 = (f32[4,128,128]{2,1,0:T(8,128)S(1)}, f32[4,128,128]{2,1,0:T(8,128)S(1)}, u32[]{:S(2)}, u32[]{:S(2)}) collective-permute-start(f32[4,128,128]{2,1,0:T(8,128)S(1)} %copy.91), channel_id=1, source_target_pairs={{0,4},{4,8},{8,12},{12,0},{1,5},{5,9},{9,13},{13,1},{2,6},{6,10},{... | collective-permute-start | bytes 786440 | tf_op jit(solution)/shard_map/ppermute | solution.py:169
  70.3 23.2 %collective-permute-start.4 = (f32[4,128,128]{2,1,0:T(8,128)S(1)}, f32[4,128,128]{2,1,0:T(8,128)S(1)}, u32[]{:S(2)}, u32[]{:S(2)}) collective-permute-start(f32[4,128,128]{2,1,0:T(8,128)S(1)} %copy.92), channel_id=1, source_target_pairs={{0,8},{4,12},{8,0},{12,4},{1,9},{5,13},{9,1},{13,5},{2,10},{6,14},... | collective-permute-start | bytes 786440 | tf_op jit(solution)/shard_map/ppermute | solution.py:169
  70.4 23.1 %collective-permute-start.5 = (f32[4,128,128]{2,1,0:T(8,128)S(1)}, f32[4,128,128]{2,1,0:T(8,128)S(1)}, u32[]{:S(2)}, u32[]{:S(2)}) collective-permute-start(f32[4,128,128]{2,1,0:T(8,128)S(1)} %copy.93), channel_id=1, source_target_pairs={{0,12},{4,0},{8,4},{12,8},{1,13},{5,1},{9,5},{13,9},{2,14},{6,2},{... | collective-permute-start | bytes 786440 | tf_op jit(solution)/shard_map/ppermute | solution.py:169
  78.4 15.1 %copy-start.6 = (f32[4,128,128]{2,1,0:T(8,128)}, f32[4,128,128]{2,1,0:T(8,128)S(1)}, u32[]{:S(2)}) copy-start(f32[4,128,128]{2,1,0:T(8,128)S(1)} %collective-permute-done.3.rest_1_) | copy-start | bytes 786436
  93.5 0.7 copy-start.7
  94.2 0.7 copy-start.8

commit v9 on v6

--- a/solution.py
+++ b/solution.py
@@ -41,16 +41,15 @@
     capacity, length = cross_weights.shape[-2:]
     rows = 2 * spread * TS + length // TS
 
-    def kernel(order_ref, owner_ref, gen_ref, ham_ref, weight_ref, *outs):
-        me = lax.axis_index("chan")
-        for s in range(channels):
-            g = (me + s) % channels
+    def kernel(order_ref, owner_ref, gen_ref, ham_ref, weight_ref, out_ref):
+        for g in range(channels):
+            s = g
             for r in range(spread):
                 tile = order_ref[g * spread + r]
                 top = pl.multiple_of((tile // blocks) * TS, TS)
                 left = pl.multiple_of((tile % blocks) * TS, TS)
                 for m, src in enumerate((gen_ref, ham_ref)):
-                    outs[s][(2 * r + m) * TS:(2 * r + m + 1) * TS, :] = src[
+                    out_ref[s, (2 * r + m) * TS:(2 * r + m + 1) * TS, :] = src[
                         pl.ds(top, TS), pl.ds(left, TS)
                     ]
             mine = owner_ref[g]
@@ -64,7 +63,7 @@
                 value = rows_here[0:1]
                 for q in range(1, capacity):
                     value = jnp.where(slot == q, rows_here[q:q + 1], value)
-                outs[s][row:row + 1, :] = value
+                out_ref[s, row:row + 1, :] = value
 
     whole = pl.BlockSpec(memory_space=pltpu.VMEM)
     return pl.pallas_call(
@@ -73,19 +72,19 @@
             num_scalar_prefetch=2,
             grid=(1,),
             in_specs=[whole] * 3,
-            out_specs=[whole] * channels,
+            out_specs=whole,
         ),
-        out_shape=[jax.ShapeDtypeStruct((rows, TS), jnp.float32)] * channels,
+        out_shape=jax.ShapeDtypeStruct((channels, rows, TS), jnp.float32),
     )(order, owners, generator, hamiltonian, cross_weights)
 
 
 def finish(direct, home, place):
     size = direct.shape[-1]
     blocks = size // TS
-    spread = home[0].shape[0]
+    channels, spread = home.shape[:2]
 
-    def kernel(place_ref, direct_ref, *rest):
-        pieces, out_ref = rest[:-1], rest[-1]
+    def kernel(place_ref, direct_ref, home_ref, out_ref):
+        pieces = [home_ref.at[s] for s in range(channels)]
         out_ref[...] = direct_ref[...]
         for s, piece in enumerate(pieces):
             for r in range(spread):
@@ -102,11 +101,11 @@
         grid_spec=pltpu.PrefetchScalarGridSpec(
             num_scalar_prefetch=1,
             grid=(1,),
-            in_specs=[whole] * (1 + len(home)),
+            in_specs=[whole] * 2,
             out_specs=whole,
         ),
         out_shape=jax.ShapeDtypeStruct((size, size), jnp.float32),
-    )(place, direct, *home)
+    )(place, direct, home)
 
 
 def body(
@@ -131,39 +130,26 @@
     order = tile_order[0, 0]
     owners = cross_owner[:, 0]
 
-    dest = (me + chan_range) % channels
-    source = (me - chan_range) % channels
     sends = build_sends(
         order, owners, generator[0, 0], hamiltonian[0, 0], cross_weights, channels, spread
     )
-    got = [sends[0]]
-    for shift in range(1, channels):
-        pairs = [(c, (c + shift) % channels) for c in range(channels)]
-        got.append(lax.ppermute(sends[shift], "chan", pairs))
-    got = jnp.stack(got)
+    got = lax.all_to_all(sends, "chan", 0, 0, tiled=True)
     tiles_got = got[:, : 2 * spread * TS].reshape(channels, spread, 2, TS, TS)
-    weights_cross = got[(me - owners[me]) % channels, 2 * spread * TS :].reshape(-1)
+    weights_cross = got[owners[me], 2 * spread * TS :].reshape(-1)
 
     mixer = recoupling[recoupling_index[me, 0]]
-    column_of = (spread_range[None, :] * channels + source[:, None]).reshape(-1)
-    mixer_in = mixer[:, column_of]
-    cross = tiles_got.reshape(tile_count, 2, TS, TS)
-    generator_mixed = jnp.einsum("ji,ixy->jxy", mixer_in, cross[:, 0], precision=highest)
-    hamilton_mixed = jnp.einsum("ji,ixy->jxy", mixer_in, cross[:, 1], precision=highest)
+    cross = jnp.swapaxes(tiles_got, 0, 1).reshape(tile_count, 2, TS, TS)
+    generator_mixed = jnp.einsum("ji,ixy->jxy", mixer, cross[:, 0], precision=highest)
+    hamilton_mixed = jnp.einsum("ji,ixy->jxy", mixer, cross[:, 1], precision=highest)
     product = bracket(
         from_tiles(generator_mixed, TS), from_tiles(hamilton_mixed, TS), weights_cross
     )
-    mixer_out = mixer[:, (spread_range[None, :] * channels + dest[:, None]).reshape(-1)]
-    back = jnp.einsum("ji,jxy->ixy", mixer_out, to_tiles(product, TS), precision=highest)
-    back = back.reshape(channels, spread, TS, TS)
-    home = [back[0]]
-    for shift in range(1, channels):
-        pairs = [(c, (c + shift) % channels) for c in range(channels)]
-        home.append(lax.ppermute(back[shift], "chan", pairs))
-    place = order[(source[:, None] * spread + spread_range[None, :]).reshape(-1)]
+    back = jnp.einsum("ji,jxy->ixy", mixer, to_tiles(product, TS), precision=highest)
+    back = jnp.swapaxes(back.reshape(spread, channels, TS, TS), 0, 1)
+    home = lax.all_to_all(back, "chan", 0, 0, tiled=True)
 
     direct = bracket(generator[0, 0], hamiltonian[0, 0], pair_weights[0, 0])
-    return finish(0.5 * (direct + direct.T), home, place)[None, None]
+    return finish(0.5 * (direct + direct.T), home, order)[None, None]
 
 
 def solution(mesh):

time: 93.6 us -> 102 us (1.090)
  the two profiles are of different devices: /device:TPU:28 before, /device:TPU:0 now
where the time goes in v9:
time: 102 us; the launch traced here: 101 us
  waiting for transfers between devices  64.8 us (64%)
  starting transfers between devices  10.7 us (10%)
  Pallas kernels  7.6 us (7%)
  matrix products  6.63 us (6%)
  local copies, waits for them, and re-layouts  6.13 us (6%)
  between operations  4.18 us (4%)
  other arithmetic  1.24 us (1%)
    all_to_all x1, waiting for transfers between devices, body(): got = lax.all_to_all(sends, 'chan', 0, 0, tiled=True)  43.2 us
    all_to_all x1, waiting for transfers between devices, body(): home = lax.all_to_all(back, 'chan', 0, 0, tiled=True)  21.6 us
    all_to_all x1, starting transfers between devices, body(): got = lax.all_to_all(sends, 'chan', 0, 0, tiled=True)  6.45 us
    all_to_all x1, starting transfers between devices, body(): home = lax.all_to_all(back, 'chan', 0, 0, tiled=True)  4.26 us
    pallas_call x1, Pallas kernels, build_sends(): pl.pallas_call(kernel, grid_spec=pltpu.PrefetchScalarGridSpec(num_scalar_...  3.82 us
    pallas_call x1, Pallas kernels, finish(): pl.pallas_call(kernel, grid_spec=pltpu.PrefetchScalarGridSpec(num_scalar_...  3.78 us
    dot_general x2, matrix products, bracket(): jnp.matmul(right_matrix * scaled, left_matrix, precision=highest)  2.06 us
    dot_general x2, matrix products, bracket(): jnp.matmul(left_matrix * scaled, right_matrix, precision=highest)  2.05 us
  transfers between devices with their start and end apart: 2, of which 2 were waited for; matrix products, arithmetic and copies ran while one was open for 5% of the time, Pallas kernels for 0%

profile of v9, /device:TPU:0, one launch (start us, length us, event | category | flops | bytes accessed | tf_op | source)
XLA Modules:
  0.0 101.3 jit_solution(9505418060052555445)
XLA Ops:
  0.0 0.0 copy-start
  0.0 1.3 %copy.20.weight_ref = f32[1,1,3,512]{3,2,1,0:T(4,128)} copy(f32[1,1,3,512]{3,1,2,0:T(1,128)} %param.11) | data formatting | bytes 12288 | tf_op args[3]
  1.3 3.8 %shard_map.82 = f32[4,1028,128]{2,1,0:T(8,128)} custom-call(s32[16]{0:T(128)} %bitcast.103, s32[4]{0:T(128)} %bitcast.105, f32[512,512]{1,0:T(8,128)} %bitcast.88, f32[512,512]{1,0:T(8,128)} %bitcast.89, f32[1,1,3,512]{3,2,1,0:T(4,128)} %copy.20.weight_ref), custom_call_target="tpu_custom_call" | custom-call | tf_op jit(solution)/shard_map/pallas_call | solution.py:69
  5.2 6.4 %all-to-all-start = ((f32[4,1028,128]{2,1,0:T(8,128)}), f32[4,1028,128]{2,1,0:T(8,128)S(1)}, u32[]{:S(2)}, u32[]{:S(2)}) async-start(f32[4,1028,128]{2,1,0:T(8,128)} %shard_map.82), calls=%async_computation | async-start | bytes 4227072 | tf_op jit(solution)/shard_map/all_to_all | solution.py:136
  11.6 0.0 copy-done.4
  11.6 0.6 constant_dynamic-slice_fusion
  13.6 0.0 copy-done.5
  13.6 0.6 constant_dynamic-slice_fusion.2
  16.2 0.0 copy-done
  16.2 0.1 copy.19
  16.9 43.2 %all-to-all-done = f32[4,1028,128]{2,1,0:T(8,128)S(1)} async-done(((f32[4,1028,128]{2,1,0:T(8,128)}), f32[4,1028,128]{2,1,0:T(8,128)S(1)}, u32[]{:S(2)}, u32[]{:S(2)}) %all-to-all-start) | async-done | bytes 2105376 | tf_op jit(solution)/shard_map/all_to_all | solution.py:136
  60.1 0.1 slice.12
  60.3 1.4 %copy.21 = f32[4,4,2,128,128]{4,1,0,3,2:T(4,128)S(1)} copy(f32[4,4,2,128,128]{4,3,2,0,1:T(8,128)S(1)} %bitcast.92) | data formatting | bytes 4194304 | tf_op jit(solution)/shard_map/transpose | solution.py:141
  61.6 0.8 fusion.10
  62.4 1.0 %bitcast_multiply_fusion = (f32[4,128,4,128]{3,2,1,0:T(4,128)S(1)}, f32[4,128,4,128]{3,2,1,0:T(4,128)S(1)}, f32[4,4,128,128]{3,1,2,0:T(4,128)S(1)}) fusion(f32[4,128]{1,0:T(4,128)S(1)} %dynamic-slice_bitcast_fusion, f32[4,4,128,128]{3,1,2,0:T(4,128)S(1)} %fusion.10, f32[4,4,16,1]{2,1,3,0:T(4,128)S(1)} %bitcast.99, f32[16,2,128,128]{3,0,2,1:T(8,128)S(1)} %bitcast.91), kind=kOutput, calls=%fused_computation.15 | convolution fusion | flops 25690112 | bytes 5253120 | tf_op jit(solution)/shard_map/ji,ixy->jxy/dot_general | solution.py:143
  63.5 1.0 %fusion.4 = f32[512,512]{1,0:T(8,128)S(1)} fusion(f32[64,8,4,128]{3,2,1,0:T(4,128)S(1)} %bitcast.94, f32[64,8,4,128]{3,2,1,0:T(4,128)S(1)} %bitcast.93), kind=kOutput, calls=%fused_computation.6 | convolution fusion | flops 805306368 | bytes 3145728 | tf_op jit(solution)/shard_map/dot_general | solution.py:34
  64.5 1.0 %convolution_subtract_fusion = f32[512,512]{1,0:T(8,128)S(1)} fusion(f32[512,512]{1,0:T(8,128)S(1)} %fusion.4, f32[64,8,4,128]{3,2,1,0:T(4,128)S(1)} %bitcast.87, f32[64,8,4,128]{3,2,1,0:T(4,128)S(1)} %bitcast.95), kind=kOutput, calls=%fused_computation | convolution fusion | flops 805568512 | bytes 4194304 | tf_op jit(solution)/shard_map/dot_general | solution.py:35
  65.5 0.4 reshape.60
  65.9 0.2 copy.22
  66.1 0.7 fusion.21
  66.8 0.0 copy-start.1
  66.9 0.0 copy-start.2
  66.9 0.0 copy-start.3
  66.9 1.1 %copy.49 = f32[4,4,128,128]{3,2,0,1:T(8,128)} copy(f32[4,4,128,128]{3,1,2,0:T(4,128)S(1)} %fusion.21) | data formatting | bytes 2097152 | tf_op jit(solution)/shard_map/ji,jxy->ixy/dot_general | solution.py:147
  68.0 4.3 %all-to-all-start.1 = ((f32[4,4,128,128]{3,2,1,0:T(8,128)}), f32[4,4,128,128]{3,2,1,0:T(8,128)}, u32[]{:S(2)}, u32[]{:S(2)}) async-start(f32[4,4,128,128]{3,2,1,0:T(8,128)} %bitcast.86), calls=%async_computation.1 | async-start | bytes 2097152 | tf_op jit(solution)/shard_map/all_to_all | solution.py:149
  72.2 0.0 copy-done.1
  72.3 1.0 %fusion.13 = f32[512,512]{0,1:T(8,128)S(1)} fusion(f32[1,1,512,512]{3,2,1,0:T(8,128)S(1)} %copy-done.1, f32[512]{0:T(512)S(1)} %bitcast.101, f32[1,1,512,512]{3,2,1,0:T(8,128)S(1)} %copy-done.2), kind=kOutput, calls=%fused_computation.20 | convolution fusion | flops 805568512 | bytes 3147776 | tf_op jit(solution)/shard_map/dot_general | solution.py:34
  73.3 1.0 %convolution_subtract_fusion.1 = f32[512,512]{0,1:T(8,128)S(1)} fusion(f32[512,512]{0,1:T(8,128)S(1)} %fusion.13, f32[1,1,512,512]{3,2,1,0:T(8,128)S(1)} %copy-done.2, f32[512]{0:T(512)S(1)} %bitcast.102, f32[1,1,512,512]{3,2,1,0:T(8,128)S(1)} %copy-done.1), kind=kOutput, calls=%fused_computation.1 | convolution fusion | flops 805830656 | bytes 4196352 | tf_op jit(solution)/shard_map/dot_general | solution.py:35
  74.3 0.3 copy.18
  74.7 1.2 %fusion.11.direct_ref = f32[512,512]{1,0:T(8,128)} fusion(f32[512,512]{1,0:T(8,128)S(1)} %copy.18, f32[512,512]{0,1:T(8,128)S(1)} %convolution_subtract_fusion.1), kind=kLoop, calls=%fused_computation.18 | loop fusion | flops 524288 | bytes 3145728 | tf_op jit(solution)/shard_map/mul | solution.py:152
  75.9 21.6 %all-to-all-done.1.home_ref = f32[4,4,128,128]{3,2,1,0:T(8,128)} async-done(((f32[4,4,128,128]{3,2,1,0:T(8,128)}), f32[4,4,128,128]{3,2,1,0:T(8,128)}, u32[]{:S(2)}, u32[]{:S(2)}) %all-to-all-start.1) | async-done | bytes 1048608 | tf_op jit(solution)/shard_map/all_to_all | solution.py:149
  97.5 3.8 %shard_map.83 = f32[512,512]{1,0:T(8,128)} custom-call(s32[16]{0:T(128)} %bitcast.104, f32[512,512]{1,0:T(8,128)} %fusion.11.direct_ref, f32[4,4,128,128]{3,2,1,0:T(8,128)} %all-to-all-done.1.home_ref), custom_call_target="tpu_custom_call" | custom-call | tf_op jit(solution)/shard_map/pallas_call | solution.py:99
  (7 shorter events, 0.0 us)
Async XLA Ops:
  0.0 16.2 %copy-start = (f32[8,16,16]{2,1,0:T(8,128)S(1)}, f32[8,16,16]{2,1,0:T(8,128)}, u32[]{:S(2)}) copy-start(f32[8,16,16]{2,1,0:T(8,128)} %param.12) | copy-start | bytes 24580
  5.1 6.5 %copy-start.4 = (s32[4,1]{0,1:T(1,128)S(1)}, s32[4,1]{0,1:T(1,128)}, u32[]{:S(2)}) copy-start(s32[4,1]{0,1:T(1,128)} %param.13) | copy-start | bytes 52
  5.1 8.5 %copy-start.5 = (s32[4,1]{0,1:T(1,128)S(1)}, s32[4,1]{0,1:T(1,128)}, u32[]{:S(2)}) copy-start(s32[4,1]{0,1:T(1,128)} %param.15) | copy-start | bytes 52
  5.2 55.0 %all-to-all-start = ((f32[4,1028,128]{2,1,0:T(8,128)}), f32[4,1028,128]{2,1,0:T(8,128)S(1)}, u32[]{:S(2)}, u32[]{:S(2)}) async-start(f32[4,1028,128]{2,1,0:T(8,128)} %shard_map.82), calls=%async_computation | async-start | bytes 4227072 | tf_op jit(solution)/shard_map/all_to_all | solution.py:136
  66.8 5.4 %copy-start.1 = (f32[1,1,512,512]{3,2,1,0:T(8,128)S(1)}, f32[1,1,512,512]{3,2,1,0:T(8,128)}, u32[]{:S(2)}) copy-start(f32[1,1,512,512]{3,2,1,0:T(8,128)} %param.8) | copy-start | bytes 3145732
  66.9 5.4 %copy-start.2 = (f32[1,1,512,512]{3,2,1,0:T(8,128)S(1)}, f32[1,1,512,512]{3,2,1,0:T(8,128)}, u32[]{:S(2)}) copy-start(f32[1,1,512,512]{3,2,1,0:T(8,128)} %param.9) | copy-start | bytes 3145732
  66.9 5.4 %copy-start.3 = (f32[1,1,512]{2,1,0:T(1,128)S(1)}, f32[1,1,512]{2,1,0:T(1,128)}, u32[]{:S(2)}) copy-start(f32[1,1,512]{2,1,0:T(1,128)} %param.10) | copy-start | bytes 6148
  68.0 29.6 %all-to-all-start.1 = ((f32[4,4,128,128]{3,2,1,0:T(8,128)}), f32[4,4,128,128]{3,2,1,0:T(8,128)}, u32[]{:S(2)}, u32[]{:S(2)}) async-start(f32[4,4,128,128]{3,2,1,0:T(8,128)} %bitcast.86), calls=%async_computation.1 | async-start | bytes 2097152 | tf_op jit(solution)/shard_map/all_to_all | solution.py:149

commit v10 on v9

--- a/solution.py
+++ b/solution.py
@@ -41,15 +41,16 @@
     capacity, length = cross_weights.shape[-2:]
     rows = 2 * spread * TS + length // TS
 
-    def kernel(order_ref, owner_ref, gen_ref, ham_ref, weight_ref, out_ref):
-        for g in range(channels):
-            s = g
+    def kernel(order_ref, owner_ref, gen_ref, ham_ref, weight_ref, *outs):
+        me = lax.axis_index("chan")
+        for s in range(channels):
+            g = (me + s) % channels
             for r in range(spread):
                 tile = order_ref[g * spread + r]
                 top = pl.multiple_of((tile // blocks) * TS, TS)
                 left = pl.multiple_of((tile % blocks) * TS, TS)
                 for m, src in enumerate((gen_ref, ham_ref)):
-                    out_ref[s, (2 * r + m) * TS:(2 * r + m + 1) * TS, :] = src[
+                    outs[s][(2 * r + m) * TS:(2 * r + m + 1) * TS, :] = src[
                         pl.ds(top, TS), pl.ds(left, TS)
                     ]
             mine = owner_ref[g]
@@ -63,7 +64,7 @@
                 value = rows_here[0:1]
                 for q in range(1, capacity):
                     value = jnp.where(slot == q, rows_here[q:q + 1], value)
-                out_ref[s, row:row + 1, :] = value
+                outs[s][row:row + 1, :] = value
 
     whole = pl.BlockSpec(memory_space=pltpu.VMEM)
     return pl.pallas_call(
@@ -72,9 +73,9 @@
             num_scalar_prefetch=2,
             grid=(1,),
             in_specs=[whole] * 3,
-            out_specs=whole,
+            out_specs=[whole] * channels,
         ),
-        out_shape=jax.ShapeDtypeStruct((channels, rows, TS), jnp.float32),
+        out_shape=[jax.ShapeDtypeStruct((rows, TS), jnp.float32)] * channels,
     )(order, owners, generator, hamiltonian, cross_weights)
 
 
@@ -133,7 +134,11 @@
     sends = build_sends(
         order, owners, generator[0, 0], hamiltonian[0, 0], cross_weights, channels, spread
     )
-    got = lax.all_to_all(sends, "chan", 0, 0, tiled=True)
+    got = [sends[0]]
+    for shift in range(1, channels):
+        pairs = [(c, (c + shift) % channels) for c in range(channels)]
+        got.append(lax.ppermute(sends[shift], "chan", pairs))
+    got = jnp.stack(got)[(me - chan_range) % channels]
     tiles_got = got[:, : 2 * spread * TS].reshape(channels, spread, 2, TS, TS)
     weights_cross = got[owners[me], 2 * spread * TS :].reshape(-1)
 

time: 102 us -> 102 us (level)
  waiting for transfers between devices: 64.8 us -> 49.4 us
  starting transfers between devices: 10.7 us -> 21.1 us
  local copies, waits for them, and re-layouts: 6.13 us -> 10.4 us
  other arithmetic: 1.24 us -> 2.57 us
    all_to_all x1 -> x0, waiting for transfers between devices: 43.2 us -> none  [body(): got = lax.all_to_all(sends, 'chan', 0, 0, tiled=True)]
    ppermute x0 -> x3, waiting for transfers between devices: none -> 28 us  [body(): got.append(lax.ppermute(sends[shift], 'chan', pairs))]
    all_to_all x1, starting transfers between devices: 4.26 us -> 14.1 us  [body(): home = lax.all_to_all(back, 'chan', 0, 0, tiled=True)]
    ppermute x0 -> x3, starting transfers between devices: none -> 6.97 us  [body(): got.append(lax.ppermute(sends[shift], 'chan', pairs))]
    all_to_all x1 -> x0, starting transfers between devices: 6.45 us -> none  [body(): got = lax.all_to_all(sends, 'chan', 0, 0, tiled=True)]
    gather x0 -> x1, local copies, waits for them, and re-layouts: none -> 2.03 us  [body(): got = jnp.stack(got)[(me - chan_range) % channels]]
    slice x1 -> x2, local copies, waits for them, and re-layouts: 0.14 us -> 1.59 us  [body(): tiles_got = got[:, :2 * spread * TS].reshape(channels, spread, 2, TS, TS)]
    another operation x0 -> x1, other arithmetic: none -> 1.34 us  [body(): got = jnp.stack(got)[(me - chan_range) % channels]]
  transfers between devices with their start and end apart: 2 -> 4, of which waited for: 2 -> 3; matrix products, arithmetic and copies ran while one was open for 5% -> 5% of each run, Pallas kernels for 0% -> 0%
where the time goes in v10:
time: 102 us
  waiting for transfers between devices  49.4 us (48%)
  starting transfers between devices  21.1 us (21%)
  local copies, waits for them, and re-layouts  10.4 us (10%)
  Pallas kernels  7.61 us (7%)
  matrix products  6.63 us (6%)
  between operations  3.87 us (4%)
  other arithmetic  2.57 us (3%)
    ppermute x3, waiting for transfers between devices, body(): got.append(lax.ppermute(sends[shift], 'chan', pairs))  28 us
    all_to_all x1, waiting for transfers between devices, body(): home = lax.all_to_all(back, 'chan', 0, 0, tiled=True)  21.4 us
    all_to_all x1, starting transfers between devices, body(): home = lax.all_to_all(back, 'chan', 0, 0, tiled=True)  14.1 us
    ppermute x3, starting transfers between devices, body(): got.append(lax.ppermute(sends[shift], 'chan', pairs))  6.97 us
    pallas_call x1, Pallas kernels, build_sends(): pl.pallas_call(kernel, grid_spec=pltpu.PrefetchScalarGridSpec(num_scalar_...  3.83 us
    pallas_call x1, Pallas kernels, finish(): pl.pallas_call(kernel, grid_spec=pltpu.PrefetchScalarGridSpec(num_scalar_...  3.79 us
    unnamed x17, local copies, waits for them, and re-layouts  2.15 us
    dot_general x2, matrix products, bracket(): jnp.matmul(right_matrix * scaled, left_matrix, precision=highest)  2.06 us
  transfers between devices with their start and end apart: 4, of which 3 were waited for; matrix products, arithmetic and copies ran while one was open for 5% of the time, Pallas kernels for 0%

profile of v10, /device:TPU:0, one launch (start us, length us, event | category | flops | bytes accessed | tf_op | source)
XLA Modules:
  0.0 101.5 jit_solution(6121618859188076514)
XLA Ops:
  0.0 1.3 %copy.20.weight_ref = f32[1,1,3,512]{3,2,1,0:T(4,128)} copy(f32[1,1,3,512]{3,1,2,0:T(1,128)} %param.11) | data formatting | bytes 12288 | tf_op args[3]
  1.3 3.8 %shard_map.82 = (f32[1028,128]{1,0:T(8,128)}, f32[1028,128]{1,0:T(8,128)}, f32[1028,128]{1,0:T(8,128)}, f32[1028,128]{1,0:T(8,128)}) custom-call(s32[16]{0:T(128)} %bitcast.113, s32[4]{0:T(128)} %bitcast.115, f32[512,512]{1,0:T(8,128)} %bitcast.94, f32[512,512]{1,0:T(8,128)} %bitcast.95, f32[1,1,3,512]{3,2,1,0:T(4,128)} %copy.20.weight_ref), custom_call_target="tpu_custom_call" | custom-call | tf_op jit(solution)/shard_map/pallas_call | solution.py:70
  5.2 3.0 %collective-permute-start = (f32[1028,128]{1,0:T(8,128)}, f32[1028,128]{1,0:T(8,128)S(1)}, u32[]{:S(2)}, u32[]{:S(2)}) collective-permute-start(f32[1028,128]{1,0:T(8,128)} %get-tuple-element.10), channel_id=1, source_target_pairs={{0,4},{4,8},{8,12},{12,0},{1,5},{5,9},{9,13},{13,1},{2,6},{6,10},{... | collective-permute-start | bytes 1579016 | tf_op jit(solution)/shard_map/ppermute | solution.py:140
  8.2 2.6 %collective-permute-start.1 = (f32[1028,128]{1,0:T(8,128)}, f32[1028,128]{1,0:T(8,128)S(1)}, u32[]{:S(2)}, u32[]{:S(2)}) collective-permute-start(f32[1028,128]{1,0:T(8,128)} %get-tuple-element.11), channel_id=1, source_target_pairs={{0,8},{4,12},{8,0},{12,4},{1,9},{5,13},{9,1},{13,5},{2,10},{6,14},... | collective-permute-start | bytes 1579016 | tf_op jit(solution)/shard_map/ppermute | solution.py:140
  10.8 1.3 %collective-permute-start.2 = (f32[1028,128]{1,0:T(8,128)}, f32[1028,128]{1,0:T(8,128)S(1)}, u32[]{:S(2)}, u32[]{:S(2)}) collective-permute-start(f32[1028,128]{1,0:T(8,128)} %get-tuple-element.12), channel_id=1, source_target_pairs={{0,12},{4,0},{8,4},{12,8},{1,13},{5,1},{9,5},{13,9},{2,14},{6,2},{... | collective-permute-start | bytes 1579016 | tf_op jit(solution)/shard_map/ppermute | solution.py:140
  12.1 0.6 constant_dynamic-slice_fusion
  14.2 0.6 constant_dynamic-slice_fusion.2
  16.4 0.1 copy.19
  17.2 6.2 %collective-permute-done = f32[1028,128]{1,0:T(8,128)S(1)} collective-permute-done((f32[1028,128]{1,0:T(8,128)}, f32[1028,128]{1,0:T(8,128)S(1)}, u32[]{:S(2)}, u32[]{:S(2)}) %collective-permute-start) | collective-permute-done | bytes 526368 | tf_op jit(solution)/shard_map/ppermute | solution.py:140
  23.4 21.8 %collective-permute-done.1 = f32[1028,128]{1,0:T(8,128)S(1)} collective-permute-done((f32[1028,128]{1,0:T(8,128)}, f32[1028,128]{1,0:T(8,128)S(1)}, u32[]{:S(2)}, u32[]{:S(2)}) %collective-permute-start.1) | collective-permute-done | bytes 526368 | tf_op jit(solution)/shard_map/ppermute | solution.py:140
  45.2 0.8 copy-done.4
  46.0 1.3 %pad_maximum_fusion = f32[4,1028,128]{2,1,0:T(8,128)S(1)} fusion(f32[1,1028,128]{2,1,0:T(8,128)} %bitcast.107, f32[1,1028,128]{2,1,0:T(8,128)S(1)} %bitcast.106, f32[1,1028,128]{2,1,0:T(8,128)S(1)} %bitcast.105, f32[1,1028,128]{2,1,0:T(8,128)} %bitcast.104), kind=kLoop, calls=%fused_computation.1 | loop fusion | flops 1579008 | bytes 4210688 | tf_op jit(solution)/shard_map/stack | solution.py:141
  47.4 2.0 %gather_fusion = f32[4,1028,128]{2,1,0:T(8,128)} fusion(f32[4,1028,128]{2,1,0:T(8,128)S(1)} %pad_maximum_fusion, s32[1024]{0:T(1024)S(1)} %pad_clamp_fusion), kind=kCustom, calls=%fused_computation | custom fusion | bytes 4210704 | tf_op jit(solution)/shard_map/gather | solution.py:141
  49.4 1.6 %slice-done = f32[4,1024,128]{2,1,0:T(8,128)S(1)} async-done(((f32[4,1028,128]{2,1,0:T(8,128)}), f32[4,1024,128]{2,1,0:T(8,128)S(1)}, s32[]{:S(2)}) %slice-start) | async-done | bytes 2097176 | tf_op jit(solution)/shard_map/slice | solution.py:142
  51.0 1.4 %copy.21 = f32[4,4,2,128,128]{4,1,0,3,2:T(4,128)S(1)} copy(f32[4,4,2,128,128]{4,3,2,0,1:T(8,128)S(1)} %bitcast.96) | data formatting | bytes 4194304 | tf_op jit(solution)/shard_map/transpose | solution.py:146
  52.4 0.8 fusion.10
  53.1 1.0 %bitcast_multiply_fusion = (f32[4,128,4,128]{3,2,1,0:T(4,128)S(1)}, f32[4,128,4,128]{3,2,1,0:T(4,128)S(1)}, f32[4,4,128,128]{3,1,2,0:T(4,128)S(1)}) fusion(f32[4,128]{1,0:T(4,128)S(1)} %dynamic-slice_bitcast_fusion, f32[4,4,128,128]{3,1,2,0:T(4,128)S(1)} %fusion.10, f32[4,4,16,1]{2,1,3,0:T(4,128)S(1)} %bitcast.109, f32[16,2,128,128]{3,0,2,1:T(8,128)S(1)} %bitcast.98), kind=kOutput, calls=%fused_computation.17 | convolution fusion | flops 25690112 | bytes 5253120 | tf_op jit(solution)/shard_map/ji,ixy->jxy/dot_general | solution.py:148
  54.2 1.0 %fusion.4 = f32[512,512]{1,0:T(8,128)S(1)} fusion(f32[64,8,4,128]{3,2,1,0:T(4,128)S(1)} %bitcast.100, f32[64,8,4,128]{3,2,1,0:T(4,128)S(1)} %bitcast.99), kind=kOutput, calls=%fused_computation.8 | convolution fusion | flops 805306368 | bytes 3145728 | tf_op jit(solution)/shard_map/dot_general | solution.py:34
  55.2 1.0 %convolution_subtract_fusion = f32[512,512]{1,0:T(8,128)S(1)} fusion(f32[512,512]{1,0:T(8,128)S(1)} %fusion.4, f32[64,8,4,128]{3,2,1,0:T(4,128)S(1)} %bitcast.93, f32[64,8,4,128]{3,2,1,0:T(4,128)S(1)} %bitcast.101), kind=kOutput, calls=%fused_computation.2 | convolution fusion | flops 805568512 | bytes 4194304 | tf_op jit(solution)/shard_map/dot_general | solution.py:35
  56.2 0.4 reshape.109
  56.6 0.2 copy.22
  56.8 0.7 fusion.23
  57.5 0.0 copy-start.2
  57.6 0.0 copy-start.5
  57.6 1.1 %copy.49 = f32[4,4,128,128]{3,2,0,1:T(8,128)} copy(f32[4,4,128,128]{3,1,2,0:T(4,128)S(1)} %fusion.23) | data formatting | bytes 2097152 | tf_op jit(solution)/shard_map/ji,jxy->ixy/dot_general | solution.py:152
  58.7 14.1 %all-to-all-start = ((f32[4,4,128,128]{3,2,1,0:T(8,128)}), f32[4,4,128,128]{3,2,1,0:T(8,128)}, u32[]{:S(2)}, u32[]{:S(2)}) async-start(f32[4,4,128,128]{3,2,1,0:T(8,128)} %bitcast.92), calls=%async_computation | async-start | bytes 2097152 | tf_op jit(solution)/shard_map/all_to_all | solution.py:154
  72.7 1.0 %fusion.13 = f32[512,512]{0,1:T(8,128)S(1)} fusion(f32[1,1,512,512]{3,2,1,0:T(8,128)S(1)} %copy-done.1, f32[512]{0:T(512)S(1)} %bitcast.111, f32[1,1,512,512]{3,2,1,0:T(8,128)S(1)} %copy-done.2), kind=kOutput, calls=%fused_computation.22 | convolution fusion | flops 805568512 | bytes 3147776 | tf_op jit(solution)/shard_map/dot_general | solution.py:34
  73.8 1.0 %convolution_subtract_fusion.1 = f32[512,512]{0,1:T(8,128)S(1)} fusion(f32[512,512]{0,1:T(8,128)S(1)} %fusion.13, f32[1,1,512,512]{3,2,1,0:T(8,128)S(1)} %copy-done.2, f32[512]{0:T(512)S(1)} %bitcast.112, f32[1,1,512,512]{3,2,1,0:T(8,128)S(1)} %copy-done.1), kind=kOutput, calls=%fused_computation.3 | convolution fusion | flops 805830656 | bytes 4196352 | tf_op jit(solution)/shard_map/dot_general | solution.py:35
  74.8 0.3 copy.18
  75.2 1.2 %fusion.11.direct_ref = f32[512,512]{1,0:T(8,128)} fusion(f32[512,512]{1,0:T(8,128)S(1)} %copy.18, f32[512,512]{0,1:T(8,128)S(1)} %convolution_subtract_fusion.1), kind=kLoop, calls=%fused_computation.20 | loop fusion | flops 524288 | bytes 3145728 | tf_op jit(solution)/shard_map/mul | solution.py:157
  76.4 21.4 %all-to-all-done.home_ref = f32[4,4,128,128]{3,2,1,0:T(8,128)} async-done(((f32[4,4,128,128]{3,2,1,0:T(8,128)}), f32[4,4,128,128]{3,2,1,0:T(8,128)}, u32[]{:S(2)}, u32[]{:S(2)}) %all-to-all-start) | async-done | bytes 1048608 | tf_op jit(solution)/shard_map/all_to_all | solution.py:154
  97.7 3.8 %shard_map.83 = f32[512,512]{1,0:T(8,128)} custom-call(s32[16]{0:T(128)} %bitcast.114, f32[512,512]{1,0:T(8,128)} %fusion.11.direct_ref, f32[4,4,128,128]{3,2,1,0:T(8,128)} %all-to-all-done.home_ref), custom_call_target="tpu_custom_call" | custom-call | tf_op jit(solution)/shard_map/pallas_call | solution.py:100
  (20 shorter events, 0.1 us)
Async XLA Ops:
  0.0 16.3 %copy-start = (f32[8,16,16]{2,1,0:T(8,128)S(1)}, f32[8,16,16]{2,1,0:T(8,128)}, u32[]{:S(2)}) copy-start(f32[8,16,16]{2,1,0:T(8,128)} %param.12) | copy-start | bytes 24580
  0.0 12.1 %copy-start.6 = (s32[4,1]{0,1:T(1,128)S(1)}, s32[4,1]{0,1:T(1,128)}, u32[]{:S(2)}) copy-start(s32[4,1]{0,1:T(1,128)} %param.13) | copy-start | bytes 52
  0.0 14.1 %copy-start.7 = (s32[4,1]{0,1:T(1,128)S(1)}, s32[4,1]{0,1:T(1,128)}, u32[]{:S(2)}) copy-start(s32[4,1]{0,1:T(1,128)} %param.15) | copy-start | bytes 52
  5.2 18.2 %collective-permute-start = (f32[1028,128]{1,0:T(8,128)}, f32[1028,128]{1,0:T(8,128)S(1)}, u32[]{:S(2)}, u32[]{:S(2)}) collective-permute-start(f32[1028,128]{1,0:T(8,128)} %get-tuple-element.10), channel_id=1, source_target_pairs={{0,4},{4,8},{8,12},{12,0},{1,5},{5,9},{9,13},{13,1},{2,6},{6,10},{... | collective-permute-start | bytes 1579016 | tf_op jit(solution)/shard_map/ppermute | solution.py:140
  8.2 37.0 %collective-permute-start.1 = (f32[1028,128]{1,0:T(8,128)}, f32[1028,128]{1,0:T(8,128)S(1)}, u32[]{:S(2)}, u32[]{:S(2)}) collective-permute-start(f32[1028,128]{1,0:T(8,128)} %get-tuple-element.11), channel_id=1, source_target_pairs={{0,8},{4,12},{8,0},{12,4},{1,9},{5,13},{9,1},{13,5},{2,10},{6,14},... | collective-permute-start | bytes 1579016 | tf_op jit(solution)/shard_map/ppermute | solution.py:140
  10.8 34.4 %collective-permute-start.2 = (f32[1028,128]{1,0:T(8,128)}, f32[1028,128]{1,0:T(8,128)S(1)}, u32[]{:S(2)}, u32[]{:S(2)}) collective-permute-start(f32[1028,128]{1,0:T(8,128)} %get-tuple-element.12), channel_id=1, source_target_pairs={{0,12},{4,0},{8,4},{12,8},{1,13},{5,1},{9,5},{13,9},{2,14},{6,2},{... | collective-permute-start | bytes 1579016 | tf_op jit(solution)/shard_map/ppermute | solution.py:140
  45.2 0.8 copy-start.4
  49.4 1.6 %slice-start = ((f32[4,1028,128]{2,1,0:T(8,128)}), f32[4,1024,128]{2,1,0:T(8,128)S(1)}, s32[]{:S(2)}) async-start(f32[4,1028,128]{2,1,0:T(8,128)} %gather_fusion), calls=%async_computation.1 | async-start | bytes 4194304 | tf_op jit(solution)/shard_map/slice | solution.py:142
  49.4 2.9 %copy-start.3 = (f32[4,1028,128]{2,1,0:T(8,128)S(1)}, f32[4,1028,128]{2,1,0:T(8,128)}, u32[]{:S(2)}) copy-start(f32[4,1028,128]{2,1,0:T(8,128)} %gather_fusion) | copy-start | bytes 6316036
  57.5 15.2 %copy-start.1 = (f32[1,1,512,512]{3,2,1,0:T(8,128)S(1)}, f32[1,1,512,512]{3,2,1,0:T(8,128)}, u32[]{:S(2)}) copy-start(f32[1,1,512,512]{3,2,1,0:T(8,128)} %param.8) | copy-start | bytes 3145732
  57.5 15.2 %copy-start.2 = (f32[1,1,512,512]{3,2,1,0:T(8,128)S(1)}, f32[1,1,512,512]{3,2,1,0:T(8,128)}, u32[]{:S(2)}) copy-start(f32[1,1,512,512]{3,2,1,0:T(8,128)} %param.9) | copy-start | bytes 3145732
  57.6 15.2 %copy-start.5 = (f32[1,1,512]{2,1,0:T(1,128)S(1)}, f32[1,1,512]{2,1,0:T(1,128)}, u32[]{:S(2)}) copy-start(f32[1,1,512]{2,1,0:T(1,128)} %param.10) | copy-start | bytes 6148
  58.7 39.1 %all-to-all-start = ((f32[4,4,128,128]{3,2,1,0:T(8,128)}), f32[4,4,128,128]{3,2,1,0:T(8,128)}, u32[]{:S(2)}, u32[]{:S(2)}) async-start(f32[4,4,128,128]{3,2,1,0:T(8,128)} %bitcast.92), calls=%async_computation | async-start | bytes 2097152 | tf_op jit(solution)/shard_map/all_to_all | solution.py:154

commit v11 on v6

--- a/solution.py
+++ b/solution.py
@@ -109,6 +109,74 @@
     )(place, direct, *home)
 
 
+def three_pass_dot(left, right):
+    left_high = left.astype(jnp.bfloat16)
+    left_low = (left - left_high.astype(jnp.float32)).astype(jnp.bfloat16)
+    right_high = right.astype(jnp.bfloat16)
+    right_low = (right - right_high.astype(jnp.float32)).astype(jnp.bfloat16)
+    product = jnp.dot(left_high, right_high, preferred_element_type=jnp.float32)
+    product = product + jnp.dot(left_high, right_low, preferred_element_type=jnp.float32)
+    return product + jnp.dot(left_low, right_high, preferred_element_type=jnp.float32)
+
+
+def cross_term(pieces, mixer_in, mixer_out, owner_shift, size):
+    channels = len(pieces)
+    tile_count = mixer_in.shape[0]
+    spread = tile_count // channels
+    blocks = size // TS
+    weight_at = 2 * spread * TS
+    weight_rows = pieces[0].shape[0] - weight_at
+
+    def kernel(in_ref, out_ref, shift_ref, *refs):
+        got = refs[:channels]
+        outs = refs[channels:2 * channels]
+        left_ref, right_ref, product_ref = refs[2 * channels:]
+        shift = shift_ref[0]
+        weights = got[0][weight_at:weight_at + weight_rows, :]
+        for s in range(1, channels):
+            weights = jnp.where(shift == s, got[s][weight_at:weight_at + weight_rows, :], weights)
+
+        for m, mixed_ref in ((0, left_ref), (1, right_ref)):
+            def mix(j, carry, m=m, mixed_ref=mixed_ref):
+                total = jnp.zeros((TS, TS), jnp.float32)
+                for s in range(channels):
+                    for r in range(spread):
+                        tile = got[s][(2 * r + m) * TS:(2 * r + m + 1) * TS, :]
+                        total = total + in_ref[j, s * spread + r] * tile
+                top = pl.multiple_of((j // blocks) * TS, TS)
+                left = pl.multiple_of((j % blocks) * TS, TS)
+                mixed_ref[pl.ds(top, TS), pl.ds(left, TS)] = total
+                return carry
+
+            lax.fori_loop(0, tile_count, mix, 0)
+
+        left = left_ref[...]
+        right = right_ref[...]
+        scale = jnp.concatenate([weights[b:b + 1, :] for b in range(blocks)], axis=1)
+        product_ref[...] = three_pass_dot(left * scale, right) - three_pass_dot(right * scale, left)
+
+        for s in range(channels):
+            for r in range(spread):
+                t = s * spread + r
+
+                def back(j, total, t=t):
+                    top = pl.multiple_of((j // blocks) * TS, TS)
+                    left = pl.multiple_of((j % blocks) * TS, TS)
+                    return total + out_ref[j, t] * product_ref[pl.ds(top, TS), pl.ds(left, TS)]
+
+                outs[s][r] = lax.fori_loop(0, tile_count, back, jnp.zeros((TS, TS), jnp.float32))
+
+    smem = pl.BlockSpec(memory_space=pltpu.SMEM)
+    whole = pl.BlockSpec(memory_space=pltpu.VMEM)
+    return pl.pallas_call(
+        kernel,
+        in_specs=[smem] * 3 + [whole] * channels,
+        out_specs=[whole] * channels,
+        out_shape=[jax.ShapeDtypeStruct((spread, TS, TS), jnp.float32)] * channels,
+        scratch_shapes=[pltpu.VMEM((size, size), jnp.float32)] * 3,
+    )(mixer_in, mixer_out, owner_shift, *pieces)
+
+
 def body(
     generator,
     hamiltonian,
@@ -140,22 +208,12 @@
     for shift in range(1, channels):
         pairs = [(c, (c + shift) % channels) for c in range(channels)]
         got.append(lax.ppermute(sends[shift], "chan", pairs))
-    got = jnp.stack(got)
-    tiles_got = got[:, : 2 * spread * TS].reshape(channels, spread, 2, TS, TS)
-    weights_cross = got[(me - owners[me]) % channels, 2 * spread * TS :].reshape(-1)
 
     mixer = recoupling[recoupling_index[me, 0]]
-    column_of = (spread_range[None, :] * channels + source[:, None]).reshape(-1)
-    mixer_in = mixer[:, column_of]
-    cross = tiles_got.reshape(tile_count, 2, TS, TS)
-    generator_mixed = jnp.einsum("ji,ixy->jxy", mixer_in, cross[:, 0], precision=highest)
-    hamilton_mixed = jnp.einsum("ji,ixy->jxy", mixer_in, cross[:, 1], precision=highest)
-    product = bracket(
-        from_tiles(generator_mixed, TS), from_tiles(hamilton_mixed, TS), weights_cross
-    )
+    mixer_in = mixer[:, (spread_range[None, :] * channels + source[:, None]).reshape(-1)]
     mixer_out = mixer[:, (spread_range[None, :] * channels + dest[:, None]).reshape(-1)]
-    back = jnp.einsum("ji,jxy->ixy", mixer_out, to_tiles(product, TS), precision=highest)
-    back = back.reshape(channels, spread, TS, TS)
+    owner_shift = ((me - owners[me]) % channels).reshape(1)
+    back = cross_term(got, mixer_in, mixer_out, owner_shift, size)
     home = [back[0]]
     for shift in range(1, channels):
         pairs = [(c, (c + shift) % channels) for c in range(channels)]

time: 93.6 us -> 95.6 us (1.021)
  Pallas kernels: 7.55 us -> 20 us
  matrix products: 8.43 us -> 2.12 us
  other arithmetic: 2.94 us -> 1.41 us
  local copies, waits for them, and re-layouts: 10.3 us -> 8.97 us
  waiting for transfers between devices: 55.5 us -> 54.4 us
    pallas_call x0 -> x1, Pallas kernels: none -> 12.3 us  [cross_term(): pl.pallas_call(kernel, in_specs=[smem] * 3 + [whole] * channels, out_spec...]
    dot_general x3 -> x0, matrix products: 3.34 us -> none  [the longest x1 1.53 us: body(): jnp.einsum('ji,ixy->jxy', mixer_in, cross[:, 1], precision=highest)]
    ppermute x3, waiting for transfers between devices: 36.3 us -> 34.1 us  [body(): got.append(lax.ppermute(sends[shift], 'chan', pairs))]
    dot_general x2 -> x1, matrix products: 3.03 us -> 1.08 us  [bracket(): jnp.matmul(right_matrix * scaled, left_matrix, precision=highest)]
    reshape x1 -> x0, local copies, waits for them, and re-layouts: 1.56 us -> none  [to_tiles(): shaped = matrix.reshape(leading + (blocks, tile_size, blocks, tile_size))]
    another operation x1 -> x0, other arithmetic: 1.5 us -> none  [body(): got = jnp.stack(got)]
    ppermute x3, waiting for transfers between devices: 19.2 us -> 20.3 us  [body(): home.append(lax.ppermute(back[shift], 'chan', pairs))]
    dot_general x2 -> x1, matrix products: 2.06 us -> 1.05 us  [bracket(): jnp.matmul(left_matrix * scaled, right_matrix, precision=highest)]
where the time goes in v11:
time: 95.6 us; the launch traced here: 94.9 us
  waiting for transfers between devices  54.4 us (57%)
  Pallas kernels  20 us (21%)
  local copies, waits for them, and re-layouts  8.97 us (9%)
  starting transfers between devices  5.73 us (6%)
  between operations  2.31 us (2%)
  matrix products  2.12 us (2%)
  other arithmetic  1.41 us (1%)
    ppermute x3, waiting for transfers between devices, body(): got.append(lax.ppermute(sends[shift], 'chan', pairs))  34.1 us
    ppermute x3, waiting for transfers between devices, body(): home.append(lax.ppermute(back[shift], 'chan', pairs))  20.3 us
    pallas_call x1, Pallas kernels, cross_term(): pl.pallas_call(kernel, in_specs=[smem] * 3 + [whole] * channels, out_spec...  12.3 us
    pallas_call x1, Pallas kernels, build_sends(): pl.pallas_call(kernel, grid_spec=pltpu.PrefetchScalarGridSpec(num_scalar_...  3.94 us
    pallas_call x1, Pallas kernels, finish(): pl.pallas_call(kernel, grid_spec=pltpu.PrefetchScalarGridSpec(num_scalar_...  3.74 us
    unnamed x21, local copies, waits for them, and re-layouts  3.57 us
    ppermute x3, starting transfers between devices, body(): home.append(lax.ppermute(back[shift], 'chan', pairs))  3.36 us
    ppermute x3, starting transfers between devices, body(): got.append(lax.ppermute(sends[shift], 'chan', pairs))  2.36 us
  transfers between devices with their start and end apart: 6, of which 4 were waited for; matrix products, arithmetic and copies ran while one was open for 9% of the time, Pallas kernels for 0%

profile of v11, /device:TPU:28, one launch (start us, length us, event | category | flops | bytes accessed | tf_op | source)
XLA Modules:
  0.0 94.9 jit_solution(7966246749071739210)
XLA Ops:
  0.0 1.3 %copy.22.weight_ref = f32[1,1,3,512]{3,2,1,0:T(4,128)} copy(f32[1,1,3,512]{3,1,2,0:T(1,128)} %param.11) | data formatting | bytes 12288 | tf_op args[3]
  1.3 3.9 %shard_map.82 = (f32[1028,128]{1,0:T(8,128)}, f32[1028,128]{1,0:T(8,128)}, f32[1028,128]{1,0:T(8,128)}, f32[1028,128]{1,0:T(8,128)}) custom-call(s32[16]{0:T(128)} %bitcast.32, s32[4]{0:T(128)} %bitcast.42, f32[512,512]{1,0:T(8,128)} %bitcast.34, f32[512,512]{1,0:T(8,128)} %bitcast.35, f32[1,1,3,512]{3,2,1,0:T(4,128)} %copy.22.weight_ref), custom_call_target="tpu_custom_call" | custom-call | tf_op jit(solution)/shard_map/pallas_call | solution.py:70
  5.3 0.2 collective-permute-start
  5.5 1.7 %collective-permute-start.1 = (f32[1028,128]{1,0:T(8,128)}, f32[1028,128]{1,0:T(8,128)}, u32[]{:S(2)}, u32[]{:S(2)}) collective-permute-start(f32[1028,128]{1,0:T(8,128)} %get-tuple-element.15), channel_id=1, source_target_pairs={{0,8},{4,12},{8,0},{12,4},{1,9},{5,13},{9,1},{13,5},{2,10},{6,14},... | collective-permute-start | bytes 1579016 | tf_op jit(solution)/shard_map/ppermute | solution.py:210
  7.2 0.4 collective-permute-start.2
  7.6 0.7 copy-done.8
  8.3 0.5 constant_dynamic-slice_fusion
  9.4 0.6 copy-done.9
  10.1 0.5 constant_dynamic-slice_fusion.2
  12.4 0.1 add.157
  12.5 0.6 gather_fusion.1
  13.1 0.7 copy.20
  13.8 0.1 add.163
  13.9 0.6 gather_fusion.2
  14.4 0.7 copy.21
  15.1 1.0 %fusion.2 = f32[512,512]{0,1:T(8,128)S(1)} fusion(f32[1,1,512,512]{3,2,1,0:T(8,128)S(1)} %copy-done.2, f32[512]{0:T(512)S(1)} %bitcast.40, f32[1,1,512,512]{3,2,1,0:T(8,128)S(1)} %copy-done.3), kind=kOutput, calls=%fused_computation.7 | convolution fusion | flops 805568512 | bytes 3147776 | tf_op jit(solution)/shard_map/dot_general | solution.py:34
  16.2 1.1 %convolution_subtract_fusion = f32[512,512]{0,1:T(8,128)S(1)} fusion(f32[512,512]{0,1:T(8,128)S(1)} %fusion.2, f32[1,1,512,512]{3,2,1,0:T(8,128)S(1)} %copy-done.3, f32[512]{0:T(512)S(1)} %bitcast.41, f32[1,1,512,512]{3,2,1,0:T(8,128)S(1)} %copy-done.2), kind=kOutput, calls=%fused_computation.3 | convolution fusion | flops 805830656 | bytes 4196352 | tf_op jit(solution)/shard_map/dot_general | solution.py:35
  17.3 0.3 copy.18
  17.7 0.1 add.149
  17.8 0.1 copy-done.1
  17.9 1.2 %gather_fusion = s32[16]{0:T(128)} fusion(s32[16]{0:T(128)S(1)} %bitcast.33, s32[1024]{0:T(1024)S(1)} %pad_clamp_fusion.2), kind=kCustom, calls=%fused_computation | custom fusion | bytes 192 | tf_op jit(solution)/shard_map/gather | solution.py:221
  19.1 0.6 collective-permute-done.refs_1_
  19.7 33.5 %collective-permute-done.1.refs_2_ = f32[1028,128]{1,0:T(8,128)} collective-permute-done((f32[1028,128]{1,0:T(8,128)}, f32[1028,128]{1,0:T(8,128)}, u32[]{:S(2)}, u32[]{:S(2)}) %collective-permute-start.1) | collective-permute-done | bytes 526368 | tf_op jit(solution)/shard_map/ppermute | solution.py:210
  53.2 12.3 %shard_map.83 = (f32[4,128,128]{2,1,0:T(8,128)}, f32[4,128,128]{2,1,0:T(8,128)}, f32[4,128,128]{2,1,0:T(8,128)}, f32[4,128,128]{2,1,0:T(8,128)}) custom-call(f32[16,16]{1,0:T(8,128)} %bitcast.38, f32[16,16]{1,0:T(8,128)} %bitcast.39, s32[1]{0:T(128)} %bitcast.15.shift_ref, f32[1028,128]{1,0:T(8,128)} %get-tuple-element.13.refs_0_, ...), custom_call_target="tpu_custom_call" | custom-call | tf_op jit(solution)/shard_map/pallas_call | solution.py:171
  65.5 1.4 %collective-permute-start.4 = (f32[4,128,128]{2,1,0:T(8,128)}, f32[4,128,128]{2,1,0:T(8,128)S(1)}, u32[]{:S(2)}, u32[]{:S(2)}) collective-permute-start(f32[4,128,128]{2,1,0:T(8,128)} %get-tuple-element.19), channel_id=1, source_target_pairs={{0,8},{4,12},{8,0},{12,4},{1,9},{5,13},{9,1},{13,5},{2,10},{6,14},... | collective-permute-start | bytes 786440 | tf_op jit(solution)/shard_map/ppermute | solution.py:220
  66.8 2.0 %collective-permute-start.5 = (f32[4,128,128]{2,1,0:T(8,128)}, f32[4,128,128]{2,1,0:T(8,128)S(1)}, u32[]{:S(2)}, u32[]{:S(2)}) collective-permute-start(f32[4,128,128]{2,1,0:T(8,128)} %get-tuple-element.20), channel_id=1, source_target_pairs={{0,12},{4,0},{8,4},{12,8},{1,13},{5,1},{9,5},{13,9},{2,14},{6,2},{... | collective-permute-start | bytes 786440 | tf_op jit(solution)/shard_map/ppermute | solution.py:220
  68.8 1.2 %fusion.direct_ref = f32[512,512]{1,0:T(8,128)} fusion(f32[512,512]{1,0:T(8,128)S(1)} %copy.18, f32[512,512]{0,1:T(8,128)S(1)} %convolution_subtract_fusion), kind=kLoop, calls=%fused_computation.5 | loop fusion | flops 524288 | bytes 3145728 | tf_op jit(solution)/shard_map/mul | solution.py:224
  70.0 2.8 %collective-permute-done.3.rest_1_ = f32[4,128,128]{2,1,0:T(8,128)S(1)} collective-permute-done((f32[4,128,128]{2,1,0:T(8,128)}, f32[4,128,128]{2,1,0:T(8,128)S(1)}, u32[]{:S(2)}, u32[]{:S(2)}) %collective-permute-start.3) | collective-permute-done | bytes 262176 | tf_op jit(solution)/shard_map/ppermute | solution.py:220
  72.9 17.5 %collective-permute-done.4.rest_2_ = f32[4,128,128]{2,1,0:T(8,128)S(1)} collective-permute-done((f32[4,128,128]{2,1,0:T(8,128)}, f32[4,128,128]{2,1,0:T(8,128)S(1)}, u32[]{:S(2)}, u32[]{:S(2)}) %collective-permute-start.4) | collective-permute-done | bytes 262176 | tf_op jit(solution)/shard_map/ppermute | solution.py:220
  90.4 0.7 copy-done.5
  91.1 0.1 copy-done.6
  91.2 3.7 %shard_map.84 = f32[512,512]{1,0:T(8,128)} custom-call(s32[16]{0:T(128)} %gather_fusion, f32[512,512]{1,0:T(8,128)} %fusion.direct_ref, f32[4,128,128]{2,1,0:T(8,128)} %get-tuple-element.17.rest_0_, f32[4,128,128]{2,1,0:T(8,128)} %copy-done.4, f32[4,128,128]{2,1,0:T(8,128)} %copy-done.5, f32[4,128,128]{2,1,0:T(8,128)} %copy-done.6), custom_call_target="tpu_custom_call" | custom-call | tf_op jit(solution)/shard_map/pallas_call | solution.py:100
  (31 shorter events, 0.3 us)
Async XLA Ops:
  0.0 12.3 %copy-start = (f32[8,16,16]{2,1,0:T(8,128)S(1)}, f32[8,16,16]{2,1,0:T(8,128)}, u32[]{:S(2)}) copy-start(f32[8,16,16]{2,1,0:T(8,128)} %param.12) | copy-start | bytes 24580
  1.3 13.8 %copy-start.2 = (f32[1,1,512,512]{3,2,1,0:T(8,128)S(1)}, f32[1,1,512,512]{3,2,1,0:T(8,128)}, u32[]{:S(2)}) copy-start(f32[1,1,512,512]{3,2,1,0:T(8,128)} %param.8) | copy-start | bytes 3145732
  1.3 13.8 %copy-start.3 = (f32[1,1,512,512]{3,2,1,0:T(8,128)S(1)}, f32[1,1,512,512]{3,2,1,0:T(8,128)}, u32[]{:S(2)}) copy-start(f32[1,1,512,512]{3,2,1,0:T(8,128)} %param.9) | copy-start | bytes 3145732
  5.3 14.5 %collective-permute-start = (f32[1028,128]{1,0:T(8,128)}, f32[1028,128]{1,0:T(8,128)}, u32[]{:S(2)}, u32[]{:S(2)}) collective-permute-start(f32[1028,128]{1,0:T(8,128)} %get-tuple-element.14), channel_id=1, source_target_pairs={{0,4},{4,8},{8,12},{12,0},{1,5},{5,9},{9,13},{13,1},{2,6},{6,10},{... | collective-permute-start | bytes 1579016 | tf_op jit(solution)/shard_map/ppermute | solution.py:210
  5.5 47.7 %collective-permute-start.1 = (f32[1028,128]{1,0:T(8,128)}, f32[1028,128]{1,0:T(8,128)}, u32[]{:S(2)}, u32[]{:S(2)}) collective-permute-start(f32[1028,128]{1,0:T(8,128)} %get-tuple-element.15), channel_id=1, source_target_pairs={{0,8},{4,12},{8,0},{12,4},{1,9},{5,13},{9,1},{13,5},{2,10},{6,14},... | collective-permute-start | bytes 1579016 | tf_op jit(solution)/shard_map/ppermute | solution.py:210
  7.2 46.0 %collective-permute-start.2 = (f32[1028,128]{1,0:T(8,128)}, f32[1028,128]{1,0:T(8,128)}, u32[]{:S(2)}, u32[]{:S(2)}) collective-permute-start(f32[1028,128]{1,0:T(8,128)} %get-tuple-element.16), channel_id=1, source_target_pairs={{0,12},{4,0},{8,4},{12,8},{1,13},{5,1},{9,5},{13,9},{2,14},{6,2},{... | collective-permute-start | bytes 1579016 | tf_op jit(solution)/shard_map/ppermute | solution.py:210
  7.6 0.7 copy-start.8
  9.4 0.7 copy-start.9
  13.9 1.2 %copy-start.7 = (f32[1,1,512]{2,1,0:T(1,128)S(1)}, f32[1,1,512]{2,1,0:T(1,128)}, u32[]{:S(2)}) copy-start(f32[1,1,512]{2,1,0:T(1,128)} %param.10) | copy-start | bytes 6148
  17.2 0.7 copy-start.1
  65.5 7.4 %collective-permute-start.3 = (f32[4,128,128]{2,1,0:T(8,128)}, f32[4,128,128]{2,1,0:T(8,128)S(1)}, u32[]{:S(2)}, u32[]{:S(2)}) collective-permute-start(f32[4,128,128]{2,1,0:T(8,128)} %get-tuple-element.18), channel_id=1, source_target_pairs={{0,4},{4,8},{8,12},{12,0},{1,5},{5,9},{9,13},{13,1},{2,6},{6,10},{... | collective-permute-start | bytes 786440 | tf_op jit(solution)/shard_map/ppermute | solution.py:220
  65.5 24.9 %collective-permute-start.4 = (f32[4,128,128]{2,1,0:T(8,128)}, f32[4,128,128]{2,1,0:T(8,128)S(1)}, u32[]{:S(2)}, u32[]{:S(2)}) collective-permute-start(f32[4,128,128]{2,1,0:T(8,128)} %get-tuple-element.19), channel_id=1, source_target_pairs={{0,8},{4,12},{8,0},{12,4},{1,9},{5,13},{9,1},{13,5},{2,10},{6,14},... | collective-permute-start | bytes 786440 | tf_op jit(solution)/shard_map/ppermute | solution.py:220
  66.8 23.5 %collective-permute-start.5 = (f32[4,128,128]{2,1,0:T(8,128)}, f32[4,128,128]{2,1,0:T(8,128)S(1)}, u32[]{:S(2)}, u32[]{:S(2)}) collective-permute-start(f32[4,128,128]{2,1,0:T(8,128)} %get-tuple-element.20), channel_id=1, source_target_pairs={{0,12},{4,0},{8,4},{12,8},{1,13},{5,1},{9,5},{13,9},{2,14},{6,2},{... | collective-permute-start | bytes 786440 | tf_op jit(solution)/shard_map/ppermute | solution.py:220
  72.9 17.5 %copy-start.4 = (f32[4,128,128]{2,1,0:T(8,128)}, f32[4,128,128]{2,1,0:T(8,128)S(1)}, u32[]{:S(2)}) copy-start(f32[4,128,128]{2,1,0:T(8,128)S(1)} %collective-permute-done.3.rest_1_) | copy-start | bytes 786436
  90.4 0.7 copy-start.5
  90.4 0.8 copy-start.6

commit v12 on v6

--- a/solution.py
+++ b/solution.py
@@ -37,12 +37,26 @@
 
 
 def build_sends(order, owners, generator, hamiltonian, cross_weights, channels, spread):
-    blocks = generator.shape[-1] // TS
+    size = generator.shape[-1]
+    blocks = size // TS
     capacity, length = cross_weights.shape[-2:]
     rows = 2 * spread * TS + length // TS
 
-    def kernel(order_ref, owner_ref, gen_ref, ham_ref, weight_ref, *outs):
+    def kernel(order_ref, owner_ref, gen_hbm, ham_hbm, weight_ref, *refs):
+        outs = refs[:channels]
+        gen_ref, ham_ref, bufs, in_sems, out_sems = refs[channels:]
+        loads = []
+        for m, (src, dst) in enumerate(((gen_hbm, gen_ref), (ham_hbm, ham_ref))):
+            for b in range(blocks):
+                loads.append(pltpu.make_async_copy(
+                    src.at[b * TS:(b + 1) * TS, :], dst.at[b * TS:(b + 1) * TS, :], in_sems.at[m * blocks + b]
+                ))
+        for load in loads:
+            load.start()
+        for load in loads:
+            load.wait()
         me = lax.axis_index("chan")
+        stores = []
         for s in range(channels):
             g = (me + s) % channels
             for r in range(spread):
@@ -50,7 +64,7 @@
                 top = pl.multiple_of((tile // blocks) * TS, TS)
                 left = pl.multiple_of((tile % blocks) * TS, TS)
                 for m, src in enumerate((gen_ref, ham_ref)):
-                    outs[s][(2 * r + m) * TS:(2 * r + m + 1) * TS, :] = src[
+                    bufs[s, (2 * r + m) * TS:(2 * r + m + 1) * TS, :] = src[
                         pl.ds(top, TS), pl.ds(left, TS)
                     ]
             mine = owner_ref[g]
@@ -64,16 +78,28 @@
                 value = rows_here[0:1]
                 for q in range(1, capacity):
                     value = jnp.where(slot == q, rows_here[q:q + 1], value)
-                outs[s][row:row + 1, :] = value
-
-    whole = pl.BlockSpec(memory_space=pltpu.VMEM)
+                bufs[s, row:row + 1, :] = value
+            store = pltpu.make_async_copy(bufs.at[s], outs[s], out_sems.at[s])
+            store.start()
+            stores.append(store)
+        for store in stores:
+            store.wait()
+
+    hbm = pl.BlockSpec(memory_space=pl.ANY)
     return pl.pallas_call(
         kernel,
         grid_spec=pltpu.PrefetchScalarGridSpec(
             num_scalar_prefetch=2,
             grid=(1,),
-            in_specs=[whole] * 3,
-            out_specs=[whole] * channels,
+            in_specs=[hbm, hbm, pl.BlockSpec(memory_space=pltpu.VMEM)],
+            out_specs=[hbm] * channels,
+            scratch_shapes=[
+                pltpu.VMEM((size, size), jnp.float32),
+                pltpu.VMEM((size, size), jnp.float32),
+                pltpu.VMEM((channels, rows, TS), jnp.float32),
+                pltpu.SemaphoreType.DMA((2 * blocks,)),
+                pltpu.SemaphoreType.DMA((channels,)),
+            ],
         ),
         out_shape=[jax.ShapeDtypeStruct((rows, TS), jnp.float32)] * channels,
     )(order, owners, generator, hamiltonian, cross_weights)
@@ -82,28 +108,61 @@
 def finish(direct, home, place):
     size = direct.shape[-1]
     blocks = size // TS
+    channels = len(home)
     spread = home[0].shape[0]
 
-    def kernel(place_ref, direct_ref, *rest):
-        pieces, out_ref = rest[:-1], rest[-1]
-        out_ref[...] = direct_ref[...]
-        for s, piece in enumerate(pieces):
+    def kernel(place_ref, direct_hbm, *refs):
+        pieces_hbm = refs[:channels]
+        out_hbm = refs[channels]
+        work, pieces, in_sems, piece_sems, out_sems = refs[channels + 1:]
+        loads = [
+            pltpu.make_async_copy(
+                direct_hbm.at[b * TS:(b + 1) * TS, :], work.at[b * TS:(b + 1) * TS, :], in_sems.at[b]
+            )
+            for b in range(blocks)
+        ]
+        loads += [
+            pltpu.make_async_copy(pieces_hbm[s], pieces.at[s], piece_sems.at[s])
+            for s in range(channels)
+        ]
+        for load in loads:
+            load.start()
+        for load in loads:
+            load.wait()
+        for s in range(channels):
             for r in range(spread):
                 tile = place_ref[s * spread + r]
                 top = pl.multiple_of((tile // blocks) * TS, TS)
                 left = pl.multiple_of((tile % blocks) * TS, TS)
-                value = 0.5 * piece[r]
-                out_ref[pl.ds(top, TS), pl.ds(left, TS)] += value
-                out_ref[pl.ds(left, TS), pl.ds(top, TS)] += value.T
-
-    whole = pl.BlockSpec(memory_space=pltpu.VMEM)
+                value = 0.5 * pieces[s, r]
+                work[pl.ds(top, TS), pl.ds(left, TS)] += value
+                work[pl.ds(left, TS), pl.ds(top, TS)] += value.T
+        stores = [
+            pltpu.make_async_copy(
+                work.at[b * TS:(b + 1) * TS, :], out_hbm.at[b * TS:(b + 1) * TS, :], out_sems.at[b]
+            )
+            for b in range(blocks)
+        ]
+        for store in stores:
+            store.start()
+        for store in stores:
+            store.wait()
+
+    hbm = pl.BlockSpec(memory_space=pl.ANY)
     return pl.pallas_call(
         kernel,
         grid_spec=pltpu.PrefetchScalarGridSpec(
             num_scalar_prefetch=1,
             grid=(1,),
-            in_specs=[whole] * (1 + len(home)),
-            out_specs=whole,
+            in_specs=[hbm] * (1 + channels),
+            out_specs=hbm,
+            scratch_shapes=[
+                pltpu.VMEM((size, size), jnp.float32),
+                pltpu.VMEM((channels, spread, TS, TS), jnp.float32),
+                pltpu.SemaphoreType.DMA((blocks,)),
+                pltpu.SemaphoreType.DMA((channels,)),
+                pltpu.SemaphoreType.DMA((blocks,)),
+            ],
         ),
         out_shape=jax.ShapeDtypeStruct((size, size), jnp.float32),
     )(place, direct, *home)

time: 93.6 us -> 94.3 us (level)
  no operation moved by 1% of the time
where the time goes in v12:
time: 94.3 us; the launch traced here: 94 us
  waiting for transfers between devices  55.5 us (59%)
  local copies, waits for them, and re-layouts  10.3 us (11%)
  matrix products  8.42 us (9%)
  Pallas kernels  8.1 us (9%)
  starting transfers between devices  5.93 us (6%)
  other arithmetic  2.94 us (3%)
  between operations  2.79 us (3%)
    ppermute x3, waiting for transfers between devices, body(): got.append(lax.ppermute(sends[shift], 'chan', pairs))  36.3 us
    ppermute x3, waiting for transfers between devices, body(): home.append(lax.ppermute(back[shift], 'chan', pairs))  19.2 us
    pallas_call x1, Pallas kernels, build_sends(): pl.pallas_call(kernel, grid_spec=pltpu.PrefetchScalarGridSpec(num_scalar_...  4.35 us
    pallas_call x1, Pallas kernels, finish(): pl.pallas_call(kernel, grid_spec=pltpu.PrefetchScalarGridSpec(num_scalar_...  3.76 us
    unnamed x27, local copies, waits for them, and re-layouts  3.65 us
    ppermute x3, starting transfers between devices, body(): home.append(lax.ppermute(back[shift], 'chan', pairs))  3.52 us
    dot_general x2, matrix products, bracket(): jnp.matmul(right_matrix * scaled, left_matrix, precision=highest)  3.03 us
    ppermute x3, starting transfers between devices, body(): got.append(lax.ppermute(sends[shift], 'chan', pairs))  2.41 us
  transfers between devices with their start and end apart: 6, of which 4 were waited for; matrix products, arithmetic and copies ran while one was open for 9% of the time, Pallas kernels for 0%

profile of v12, /device:TPU:28, one launch (start us, length us, event | category | flops | bytes accessed | tf_op | source)
XLA Modules:
  0.0 94.0 jit_solution(10002796318238422758)
XLA Ops:
  0.0 1.4 %copy.28.weight_ref = f32[1,1,3,512]{3,2,1,0:T(4,128)} copy(f32[1,1,3,512]{3,1,2,0:T(1,128)} %param.11) | data formatting | bytes 12288 | tf_op args[3]
  1.5 4.3 %shard_map.82 = (f32[1028,128]{1,0:T(8,128)}, f32[1028,128]{1,0:T(8,128)}, f32[1028,128]{1,0:T(8,128)}, f32[1028,128]{1,0:T(8,128)}) custom-call(s32[16]{0:T(128)} %bitcast.84, s32[4]{0:T(128)} %bitcast.103, f32[512,512]{1,0:T(8,128)} %bitcast.87, f32[512,512]{1,0:T(8,128)} %bitcast.88, f32[1,1,3,512]{3,2,1,0:T(4,128)} %copy.28.weight_ref), custom_call_target="tpu_custom_call" | custom-call | tf_op jit(solution)/shard_map/pallas_call | solution.py:89
  5.8 0.3 collective-permute-start
  6.1 1.7 %collective-permute-start.1 = (f32[1028,128]{1,0:T(8,128)}, f32[1028,128]{1,0:T(8,128)}, u32[]{:S(2)}, u32[]{:S(2)}) collective-permute-start(f32[1028,128]{1,0:T(8,128)} %get-tuple-element.11), channel_id=1, source_target_pairs={{0,8},{4,12},{8,0},{12,4},{1,9},{5,13},{9,1},{13,5},{2,10},{6,14},... | collective-permute-start | bytes 1579016 | tf_op jit(solution)/shard_map/ppermute | solution.py:201
  7.8 0.4 collective-permute-start.2
  8.3 0.6 constant_dynamic-slice_fusion
  9.6 0.6 constant_dynamic-slice_fusion.2
  12.4 0.6 gather_fusion.2
  13.1 0.6 gather_fusion.1
  13.7 1.0 %fusion.13 = f32[512,512]{0,1:T(8,128)S(1)} fusion(f32[1,1,512,512]{3,2,1,0:T(8,128)S(1)} %copy-done.2, f32[512]{0:T(512)S(1)} %bitcast.101, f32[1,1,512,512]{3,2,1,0:T(8,128)S(1)} %copy-done.3), kind=kOutput, calls=%fused_computation.24 | convolution fusion | flops 805568512 | bytes 3147776 | tf_op jit(solution)/shard_map/dot_general | solution.py:34
  14.8 1.0 %convolution_subtract_fusion.1 = f32[512,512]{0,1:T(8,128)S(1)} fusion(f32[512,512]{0,1:T(8,128)S(1)} %fusion.13, f32[1,1,512,512]{3,2,1,0:T(8,128)S(1)} %copy-done.3, f32[512]{0:T(512)S(1)} %bitcast.102, f32[1,1,512,512]{3,2,1,0:T(8,128)S(1)} %copy-done.2), kind=kOutput, calls=%fused_computation.5 | convolution fusion | flops 805830656 | bytes 4196352 | tf_op jit(solution)/shard_map/dot_general | solution.py:35
  15.8 0.3 copy.25
  16.3 1.2 %gather_fusion = s32[16]{0:T(128)} fusion(s32[16]{0:T(128)S(1)} %bitcast.85, s32[1024]{0:T(1024)S(1)} %pad_clamp_fusion.2), kind=kCustom, calls=%fused_computation | custom fusion | bytes 192 | tf_op jit(solution)/shard_map/gather | solution.py:222
  17.6 2.8 %collective-permute-done = f32[1028,128]{1,0:T(8,128)} collective-permute-done((f32[1028,128]{1,0:T(8,128)}, f32[1028,128]{1,0:T(8,128)}, u32[]{:S(2)}, u32[]{:S(2)}) %collective-permute-start) | collective-permute-done | bytes 526368 | tf_op jit(solution)/shard_map/ppermute | solution.py:201
  20.3 33.5 %collective-permute-done.1 = f32[1028,128]{1,0:T(8,128)} collective-permute-done((f32[1028,128]{1,0:T(8,128)}, f32[1028,128]{1,0:T(8,128)}, u32[]{:S(2)}, u32[]{:S(2)}) %collective-permute-start.1) | collective-permute-done | bytes 526368 | tf_op jit(solution)/shard_map/ppermute | solution.py:201
  53.8 1.5 %pad_maximum_fusion = f32[4,1028,128]{2,1,0:T(8,128)S(1)} fusion(f32[1,1028,128]{2,1,0:T(8,128)} %bitcast.21, f32[1,1028,128]{2,1,0:T(8,128)} %bitcast.20, f32[1,1028,128]{2,1,0:T(8,128)} %bitcast.19, f32[1,1028,128]{2,1,0:T(8,128)S(1)} %bitcast.97), kind=kLoop, calls=%fused_computation.3 | loop fusion | flops 1579008 | bytes 4210688 | tf_op jit(solution)/shard_map/stack | solution.py:202
  55.5 0.2 fusion.28
  55.7 1.2 %fusion.10 = f32[4,4,128,128]{3,1,2,0:T(4,128)S(1)} fusion(f32[4,4,16,1]{2,1,3,0:T(4,128)S(1)} %bitcast.98, f32[16,1,128,128]{3,2,1,0:T(8,128)S(1)} %get-tuple-element.13), kind=kOutput, calls=%fused_computation.18 | convolution fusion | flops 25165824 | bytes 2098176 | tf_op jit(solution)/shard_map/ji,ixy->jxy/dot_general | solution.py:210
  57.0 1.5 %bitcast_multiply_fusion = (f32[4,128,4,128]{3,2,1,0:T(4,128)S(1)}, f32[4,128,4,128]{3,2,1,0:T(4,128)S(1)}, f32[4,4,128,128]{3,1,2,0:T(4,128)S(1)}) fusion(f32[4,128]{1,0:T(4,128)S(1)} %dynamic-slice_bitcast_fusion, f32[4,4,128,128]{3,1,2,0:T(4,128)S(1)} %fusion.10, f32[4,4,16,1]{2,1,3,0:T(4,128)S(1)} %bitcast.99, f32[16,1,128,128]{3,2,1,0:T(8,128)S(1)} %get-tuple-element.14), kind=kOutput, calls=%fused_computation.19 | convolution fusion | flops 25690112 | bytes 5245952 | tf_op jit(solution)/shard_map/ji,ixy->jxy/dot_general | solution.py:211
  58.5 1.0 %fusion.4 = f32[512,512]{1,0:T(8,128)S(1)} fusion(f32[64,8,4,128]{3,2,1,0:T(4,128)S(1)} %bitcast.91, f32[64,8,4,128]{3,2,1,0:T(4,128)S(1)} %bitcast.90), kind=kOutput, calls=%fused_computation.10 | convolution fusion | flops 805306368 | bytes 3145728 | tf_op jit(solution)/shard_map/dot_general | solution.py:34
  59.5 2.0 %convolution_subtract_fusion = f32[512,512]{1,0:T(8,128)} fusion(f32[512,512]{1,0:T(8,128)S(1)} %fusion.4, f32[64,8,4,128]{3,2,1,0:T(4,128)S(1)} %bitcast.86, f32[64,8,4,128]{3,2,1,0:T(4,128)S(1)} %bitcast.92), kind=kOutput, calls=%fused_computation.4 | convolution fusion | flops 805568512 | bytes 4194304 | tf_op jit(solution)/shard_map/dot_general | solution.py:35
  61.5 1.6 %reshape.186 = f32[4,128,4,128]{3,2,1,0:T(4,128)S(1)} reshape(f32[512,512]{1,0:T(8,128)} %convolution_subtract_fusion) | data formatting | bytes 2097152 | tf_op jit(solution)/shard_map/reshape | solution.py:19
  63.3 0.6 fusion.19
  64.1 1.4 %collective-permute-start.4 = (f32[4,128,128]{2,1,0:T(8,128)S(1)}, f32[4,128,128]{2,1,0:T(8,128)S(1)}, u32[]{:S(2)}, u32[]{:S(2)}) collective-permute-start(f32[4,128,128]{2,1,0:T(8,128)S(1)} %copy.43), channel_id=1, source_target_pairs={{0,8},{4,12},{8,0},{12,4},{1,9},{5,13},{9,1},{13,5},{2,10},{6,14},... | collective-permute-start | bytes 786440 | tf_op jit(solution)/shard_map/ppermute | solution.py:221
  65.6 2.1 %collective-permute-start.5 = (f32[4,128,128]{2,1,0:T(8,128)S(1)}, f32[4,128,128]{2,1,0:T(8,128)S(1)}, u32[]{:S(2)}, u32[]{:S(2)}) collective-permute-start(f32[4,128,128]{2,1,0:T(8,128)S(1)} %copy.44), channel_id=1, source_target_pairs={{0,12},{4,0},{8,4},{12,8},{1,13},{5,1},{9,5},{13,9},{2,14},{6,2},{... | collective-permute-start | bytes 786440 | tf_op jit(solution)/shard_map/ppermute | solution.py:221
  67.6 1.2 %fusion.11.direct_hbm = f32[512,512]{1,0:T(8,128)} fusion(f32[512,512]{1,0:T(8,128)S(1)} %copy.25, f32[512,512]{0,1:T(8,128)S(1)} %convolution_subtract_fusion.1), kind=kLoop, calls=%fused_computation.22 | loop fusion | flops 524288 | bytes 3145728 | tf_op jit(solution)/shard_map/mul | solution.py:225
  68.9 0.7 copy.41.refs_0_
  69.6 1.7 %collective-permute-done.3.refs_1_ = f32[4,128,128]{2,1,0:T(8,128)S(1)} collective-permute-done((f32[4,128,128]{2,1,0:T(8,128)S(1)}, f32[4,128,128]{2,1,0:T(8,128)S(1)}, u32[]{:S(2)}, u32[]{:S(2)}) %collective-permute-start.3) | collective-permute-done | bytes 262176 | tf_op jit(solution)/shard_map/ppermute | solution.py:221
  71.3 17.5 %collective-permute-done.4.refs_2_ = f32[4,128,128]{2,1,0:T(8,128)S(1)} collective-permute-done((f32[4,128,128]{2,1,0:T(8,128)S(1)}, f32[4,128,128]{2,1,0:T(8,128)S(1)}, u32[]{:S(2)}, u32[]{:S(2)}) %collective-permute-start.4) | collective-permute-done | bytes 262176 | tf_op jit(solution)/shard_map/ppermute | solution.py:221
  88.8 0.7 copy-done.6
  89.5 0.7 copy-done.7
  90.2 3.8 %shard_map.83 = f32[512,512]{1,0:T(8,128)} custom-call(s32[16]{0:T(128)} %gather_fusion, f32[512,512]{1,0:T(8,128)} %fusion.11.direct_hbm, f32[4,128,128]{2,1,0:T(8,128)} %copy.41.refs_0_, f32[4,128,128]{2,1,0:T(8,128)} %copy-done.5, f32[4,128,128]{2,1,0:T(8,128)} %copy-done.6, f32[4,128,128]{2,1,0:T(8,128)} %copy-done.7), custom_call_target="tpu_custom_call" | custom-call | tf_op jit(solution)/shard_map/pallas_call | solution.py:152
  (47 shorter events, 1.3 us)
Async XLA Ops:
  0.0 12.1 %copy-start = (f32[8,16,16]{2,1,0:T(8,128)S(1)}, f32[8,16,16]{2,1,0:T(8,128)}, u32[]{:S(2)}) copy-start(f32[8,16,16]{2,1,0:T(8,128)} %param.12) | copy-start | bytes 24580
  0.0 8.3 %copy-start.9 = (s32[4,1]{0,1:T(1,128)S(1)}, s32[4,1]{0,1:T(1,128)}, u32[]{:S(2)}) copy-start(s32[4,1]{0,1:T(1,128)} %param.13) | copy-start | bytes 52
  0.0 13.7 %copy-start.3 = (f32[1,1,512,512]{3,2,1,0:T(8,128)S(1)}, f32[1,1,512,512]{3,2,1,0:T(8,128)}, u32[]{:S(2)}) copy-start(f32[1,1,512,512]{3,2,1,0:T(8,128)} %param.9) | copy-start | bytes 3145732
  0.0 13.7 %copy-start.2 = (f32[1,1,512,512]{3,2,1,0:T(8,128)S(1)}, f32[1,1,512,512]{3,2,1,0:T(8,128)}, u32[]{:S(2)}) copy-start(f32[1,1,512,512]{3,2,1,0:T(8,128)} %param.8) | copy-start | bytes 3145732
  0.0 9.6 %copy-start.10 = (s32[4,1]{0,1:T(1,128)S(1)}, s32[4,1]{0,1:T(1,128)}, u32[]{:S(2)}) copy-start(s32[4,1]{0,1:T(1,128)} %param.15) | copy-start | bytes 52
  0.0 13.7 %copy-start.8 = (f32[1,1,512]{2,1,0:T(1,128)S(1)}, f32[1,1,512]{2,1,0:T(1,128)}, u32[]{:S(2)}) copy-start(f32[1,1,512]{2,1,0:T(1,128)} %param.10) | copy-start | bytes 6148
  5.8 14.5 %collective-permute-start = (f32[1028,128]{1,0:T(8,128)}, f32[1028,128]{1,0:T(8,128)}, u32[]{:S(2)}, u32[]{:S(2)}) collective-permute-start(f32[1028,128]{1,0:T(8,128)} %get-tuple-element.10), channel_id=1, source_target_pairs={{0,4},{4,8},{8,12},{12,0},{1,5},{5,9},{9,13},{13,1},{2,6},{6,10},{... | collective-permute-start | bytes 1579016 | tf_op jit(solution)/shard_map/ppermute | solution.py:201
  6.1 47.7 %collective-permute-start.1 = (f32[1028,128]{1,0:T(8,128)}, f32[1028,128]{1,0:T(8,128)}, u32[]{:S(2)}, u32[]{:S(2)}) collective-permute-start(f32[1028,128]{1,0:T(8,128)} %get-tuple-element.11), channel_id=1, source_target_pairs={{0,8},{4,12},{8,0},{12,4},{1,9},{5,13},{9,1},{13,5},{2,10},{6,14},... | collective-permute-start | bytes 1579016 | tf_op jit(solution)/shard_map/ppermute | solution.py:201
  7.8 46.0 %collective-permute-start.2 = (f32[1028,128]{1,0:T(8,128)}, f32[1028,128]{1,0:T(8,128)}, u32[]{:S(2)}, u32[]{:S(2)}) collective-permute-start(f32[1028,128]{1,0:T(8,128)} %get-tuple-element.12), channel_id=1, source_target_pairs={{0,12},{4,0},{8,4},{12,8},{1,13},{5,1},{9,5},{13,9},{2,14},{6,2},{... | collective-permute-start | bytes 1579016 | tf_op jit(solution)/shard_map/ppermute | solution.py:201
  14.8 1.6 %copy-start.1 = (s32[1,1,16]{2,1,0:T(1,128)S(1)}, s32[1,1,16]{2,1,0:T(1,128)}, u32[]{:S(2)}) copy-start(s32[1,1,16]{2,1,0:T(1,128)} %param.14) | copy-start | bytes 196
  15.8 38.0 %copy-start.4 = (f32[1028,128]{1,0:T(8,128)S(1)}, f32[1028,128]{1,0:T(8,128)}, u32[]{:S(2)}) copy-start(f32[1028,128]{1,0:T(8,128)} %get-tuple-element.9) | copy-start | bytes 1579012
  64.1 7.2 %collective-permute-start.3 = (f32[4,128,128]{2,1,0:T(8,128)S(1)}, f32[4,128,128]{2,1,0:T(8,128)S(1)}, u32[]{:S(2)}, u32[]{:S(2)}) collective-permute-start(f32[4,128,128]{2,1,0:T(8,128)S(1)} %copy.42), channel_id=1, source_target_pairs={{0,4},{4,8},{8,12},{12,0},{1,5},{5,9},{9,13},{13,1},{2,6},{6,10},{... | collective-permute-start | bytes 786440 | tf_op jit(solution)/shard_map/ppermute | solution.py:221
  64.1 24.6 %collective-permute-start.4 = (f32[4,128,128]{2,1,0:T(8,128)S(1)}, f32[4,128,128]{2,1,0:T(8,128)S(1)}, u32[]{:S(2)}, u32[]{:S(2)}) collective-permute-start(f32[4,128,128]{2,1,0:T(8,128)S(1)} %copy.43), channel_id=1, source_target_pairs={{0,8},{4,12},{8,0},{12,4},{1,9},{5,13},{9,1},{13,5},{2,10},{6,14},... | collective-permute-start | bytes 786440 | tf_op jit(solution)/shard_map/ppermute | solution.py:221
  65.6 23.2 %collective-permute-start.5 = (f32[4,128,128]{2,1,0:T(8,128)S(1)}, f32[4,128,128]{2,1,0:T(8,128)S(1)}, u32[]{:S(2)}, u32[]{:S(2)}) collective-permute-start(f32[4,128,128]{2,1,0:T(8,128)S(1)} %copy.44), channel_id=1, source_target_pairs={{0,12},{4,0},{8,4},{12,8},{1,13},{5,1},{9,5},{13,9},{2,14},{6,2},{... | collective-permute-start | bytes 786440 | tf_op jit(solution)/shard_map/ppermute | solution.py:221
  71.3 17.5 %copy-start.5 = (f32[4,128,128]{2,1,0:T(8,128)}, f32[4,128,128]{2,1,0:T(8,128)S(1)}, u32[]{:S(2)}) copy-start(f32[4,128,128]{2,1,0:T(8,128)S(1)} %collective-permute-done.3.refs_1_) | copy-start | bytes 786436
  88.8 0.7 copy-start.6
  89.5 0.7 copy-start.7

commit v13 on v6

--- a/solution.py
+++ b/solution.py
@@ -31,9 +31,9 @@
 
 def bracket(left_matrix, right_matrix, weights):
     scaled = weights[..., None, :]
-    left_term = jnp.matmul(left_matrix * scaled, right_matrix, precision=highest)
-    right_term = jnp.matmul(right_matrix * scaled, left_matrix, precision=highest)
-    return left_term - right_term
+    both_scaled = jnp.concatenate([left_matrix * scaled, right_matrix * scaled], axis=-1)
+    both = jnp.concatenate([right_matrix, -left_matrix], axis=-2)
+    return jnp.matmul(both_scaled, both, precision=highest)
 
 
 def build_sends(order, owners, generator, hamiltonian, cross_weights, channels, spread):

time: 93.6 us -> 93.6 us (level)
  matrix products: 8.43 us -> 6.89 us
  local copies, waits for them, and re-layouts: 10.3 us -> 11.4 us
    dot_general x4 -> x2, matrix products: 5.09 us -> 3.85 us  [bracket(): return jnp.matmul(both_scaled, both, precision=highest)]
    transpose x1, local copies, waits for them, and re-layouts: 0.18 us -> 1.4 us  [to_tiles(): shaped = jnp.swapaxes(shaped, -3, -2)]
    unnamed x27 -> x28, local copies, waits for them, and re-layouts: 3.65 us -> 3.82 us
  transfers between devices with their start and end apart: 6 -> 6, of which waited for: 4 -> 4; matrix products, arithmetic and copies ran while one was open for 9% -> 10% of each run, Pallas kernels for 0% -> 0%
where the time goes in v13:
time: 93.6 us; the launch traced here: 93.3 us
  waiting for transfers between devices  54.9 us (59%)
  local copies, waits for them, and re-layouts  11.4 us (12%)
  Pallas kernels  7.57 us (8%)
  matrix products  6.89 us (7%)
  starting transfers between devices  5.87 us (6%)
  other arithmetic  3.67 us (4%)
  between operations  3.01 us (3%)
    ppermute x3, waiting for transfers between devices, body(): got.append(lax.ppermute(sends[shift], 'chan', pairs))  35.6 us
    ppermute x3, waiting for transfers between devices, body(): home.append(lax.ppermute(back[shift], 'chan', pairs))  19.2 us
    dot_general x2, matrix products, bracket(): return jnp.matmul(both_scaled, both, precision=highest)  3.85 us
    unnamed x28, local copies, waits for them, and re-layouts  3.82 us
    pallas_call x1, Pallas kernels, build_sends(): pl.pallas_call(kernel, grid_spec=pltpu.PrefetchScalarGridSpec(num_scalar_...  3.81 us
    pallas_call x1, Pallas kernels, finish(): pl.pallas_call(kernel, grid_spec=pltpu.PrefetchScalarGridSpec(num_scalar_...  3.76 us
    ppermute x3, starting transfers between devices, body(): home.append(lax.ppermute(back[shift], 'chan', pairs))  3.51 us
    ppermute x3, starting transfers between devices, body(): got.append(lax.ppermute(sends[shift], 'chan', pairs))  2.36 us
  transfers between devices with their start and end apart: 6, of which 4 were waited for; matrix products, arithmetic and copies ran while one was open for 10% of the time, Pallas kernels for 0%

profile of v13, /device:TPU:28, one launch (start us, length us, event | category | flops | bytes accessed | tf_op | source)
XLA Modules:
  0.0 93.3 jit_solution(17885477296107629579)
XLA Ops:
  0.0 1.4 %copy.24.weight_ref = f32[1,1,3,512]{3,2,1,0:T(4,128)} copy(f32[1,1,3,512]{3,1,2,0:T(1,128)} %param.11) | data formatting | bytes 12288 | tf_op args[3]
  1.5 3.8 %shard_map.82 = (f32[1028,128]{1,0:T(8,128)}, f32[1028,128]{1,0:T(8,128)}, f32[1028,128]{1,0:T(8,128)}, f32[1028,128]{1,0:T(8,128)}) custom-call(s32[16]{0:T(128)} %bitcast.65, s32[4]{0:T(128)} %bitcast.85, f32[512,512]{1,0:T(8,128)} %bitcast.74, f32[512,512]{1,0:T(8,128)} %bitcast.67, f32[1,1,3,512]{3,2,1,0:T(4,128)} %copy.24.weight_ref), custom_call_target="tpu_custom_call" | custom-call | tf_op jit(solution)/shard_map/pallas_call | solution.py:70
  5.3 0.2 collective-permute-start
  5.5 1.7 %collective-permute-start.1 = (f32[1028,128]{1,0:T(8,128)}, f32[1028,128]{1,0:T(8,128)}, u32[]{:S(2)}, u32[]{:S(2)}) collective-permute-start(f32[1028,128]{1,0:T(8,128)} %get-tuple-element.11), channel_id=1, source_target_pairs={{0,8},{4,12},{8,0},{12,4},{1,9},{5,13},{9,1},{13,5},{2,10},{6,14},... | collective-permute-start | bytes 1579016 | tf_op jit(solution)/shard_map/ppermute | solution.py:142
  7.2 0.4 collective-permute-start.2
  7.7 0.7 constant_dynamic-slice_fusion
  9.1 0.7 constant_dynamic-slice_fusion.2
  12.0 0.6 gather_fusion.2
  12.8 0.6 gather_fusion.1
  13.4 0.4 bitcast_negate_fusion.1
  13.8 1.9 %fusion = f32[512,512]{1,0:T(8,128)S(1)} fusion(f32[512,512]{1,0:T(8,128)S(1)} %get-tuple-element.23, f32[512,512]{1,0:T(8,128)S(1)} %get-tuple-element.22, f32[512,512]{1,0:T(8,128)S(1)} %get-tuple-element.21, f32[512,512]{1,0:T(8,128)S(1)} %bitcast.68), kind=kOutput, calls=%fused_computation.4 | convolution fusion | flops 1611661312 | bytes 5242880 | tf_op jit(solution)/shard_map/dot_general | solution.py:36
  15.7 0.3 copy.21
  16.3 1.2 %gather_fusion = s32[16]{0:T(128)} fusion(s32[16]{0:T(128)S(1)} %bitcast.66, s32[1024]{0:T(1024)S(1)} %pad_clamp_fusion.2), kind=kCustom, calls=%fused_computation | custom fusion | bytes 192 | tf_op jit(solution)/shard_map/gather | solution.py:163
  17.6 2.1 %collective-permute-done = f32[1028,128]{1,0:T(8,128)S(1)} collective-permute-done((f32[1028,128]{1,0:T(8,128)}, f32[1028,128]{1,0:T(8,128)S(1)}, u32[]{:S(2)}, u32[]{:S(2)}) %collective-permute-start) | collective-permute-done | bytes 526368 | tf_op jit(solution)/shard_map/ppermute | solution.py:142
  19.6 33.6 %collective-permute-done.1 = f32[1028,128]{1,0:T(8,128)} collective-permute-done((f32[1028,128]{1,0:T(8,128)}, f32[1028,128]{1,0:T(8,128)}, u32[]{:S(2)}, u32[]{:S(2)}) %collective-permute-start.1) | collective-permute-done | bytes 526368 | tf_op jit(solution)/shard_map/ppermute | solution.py:142
  53.2 1.3 %pad_maximum_fusion = f32[4,1028,128]{2,1,0:T(8,128)S(1)} fusion(f32[1,1028,128]{2,1,0:T(8,128)} %bitcast.19, f32[1,1028,128]{2,1,0:T(8,128)} %bitcast.18, f32[1,1028,128]{2,1,0:T(8,128)S(1)} %bitcast.80, f32[1,1028,128]{2,1,0:T(8,128)S(1)} %bitcast.79), kind=kLoop, calls=%fused_computation.3 | loop fusion | flops 1579008 | bytes 4210688 | tf_op jit(solution)/shard_map/stack | solution.py:143
  54.9 1.2 %fusion.14 = f32[4,4,128,128]{3,1,2,0:T(4,128)S(1)} fusion(f32[4,4,16,1]{2,1,3,0:T(4,128)S(1)} %bitcast.81, f32[16,1,128,128]{3,2,1,0:T(8,128)S(1)} %get-tuple-element.14), kind=kOutput, calls=%fused_computation.22 | convolution fusion | flops 25165824 | bytes 2098176 | tf_op jit(solution)/shard_map/ji,ixy->jxy/dot_general | solution.py:152
  56.1 1.2 %fusion.15 = f32[4,4,128,128]{3,1,2,0:T(4,128)S(1)} fusion(f32[4,4,16,1]{2,1,3,0:T(4,128)S(1)} %bitcast.82, f32[16,1,128,128]{3,2,1,0:T(8,128)S(1)} %get-tuple-element.13), kind=kOutput, calls=%fused_computation.24 | convolution fusion | flops 25165824 | bytes 2098176 | tf_op jit(solution)/shard_map/ji,ixy->jxy/dot_general | solution.py:151
  57.5 0.5 bitcast_negate_fusion
  58.0 1.9 %fusion.7 = f32[512,512]{1,0:T(8,128)S(1)} fusion(f32[512,512]{1,0:T(8,128)S(1)} %get-tuple-element.24, f32[512,512]{1,0:T(8,128)S(1)} %get-tuple-element.20, f32[512,512]{1,0:T(8,128)S(1)} %get-tuple-element.19, f32[512,512]{1,0:T(8,128)S(1)} %bitcast.73), kind=kOutput, calls=%fused_computation.11 | convolution fusion | flops 1611661312 | bytes 5242880 | tf_op jit(solution)/shard_map/dot_general | solution.py:36
  59.9 1.3 %reshape.160 = f32[4,128,4,128]{3,2,1,0:T(4,128)} reshape(f32[512,512]{1,0:T(8,128)S(1)} %fusion.7) | data formatting | bytes 2097152 | tf_op jit(solution)/shard_map/reshape | solution.py:19
  61.2 1.4 %copy.27 = f32[4,4,128,128]{3,1,0,2:T(4,128)S(1)} copy(f32[4,4,128,128]{3,1,2,0:T(4,128)} %bitcast.76) | data formatting | bytes 2097152 | tf_op jit(solution)/shard_map/transpose | solution.py:20
  62.6 0.6 fusion.17
  63.5 1.4 %collective-permute-start.4 = (f32[4,128,128]{2,1,0:T(8,128)S(1)}, f32[4,128,128]{2,1,0:T(8,128)S(1)}, u32[]{:S(2)}, u32[]{:S(2)}) collective-permute-start(f32[4,128,128]{2,1,0:T(8,128)S(1)} %copy.37), channel_id=1, source_target_pairs={{0,8},{4,12},{8,0},{12,4},{1,9},{5,13},{9,1},{13,5},{2,10},{6,14},... | collective-permute-start | bytes 786440 | tf_op jit(solution)/shard_map/ppermute | solution.py:162
  64.9 2.1 %collective-permute-start.5 = (f32[4,128,128]{2,1,0:T(8,128)S(1)}, f32[4,128,128]{2,1,0:T(8,128)S(1)}, u32[]{:S(2)}, u32[]{:S(2)}) collective-permute-start(f32[4,128,128]{2,1,0:T(8,128)S(1)} %copy.38), channel_id=1, source_target_pairs={{0,12},{4,0},{8,4},{12,8},{1,13},{5,1},{9,5},{13,9},{2,14},{6,2},{... | collective-permute-start | bytes 786440 | tf_op jit(solution)/shard_map/ppermute | solution.py:162
  66.9 1.2 %fusion.16.direct_ref = f32[512,512]{1,0:T(8,128)} fusion(f32[512,512]{1,0:T(8,128)S(1)} %fusion, f32[512,512]{0,1:T(8,128)S(1)} %copy.21), kind=kLoop, calls=%fused_computation.26 | loop fusion | flops 524288 | bytes 3145728 | tf_op jit(solution)/shard_map/mul | solution.py:166
  68.2 0.7 copy.35.rest_0_
  68.9 1.7 %collective-permute-done.3.rest_1_ = f32[4,128,128]{2,1,0:T(8,128)S(1)} collective-permute-done((f32[4,128,128]{2,1,0:T(8,128)S(1)}, f32[4,128,128]{2,1,0:T(8,128)S(1)}, u32[]{:S(2)}, u32[]{:S(2)}) %collective-permute-start.3) | collective-permute-done | bytes 262176 | tf_op jit(solution)/shard_map/ppermute | solution.py:162
  70.6 17.5 %collective-permute-done.4.rest_2_ = f32[4,128,128]{2,1,0:T(8,128)S(1)} collective-permute-done((f32[4,128,128]{2,1,0:T(8,128)S(1)}, f32[4,128,128]{2,1,0:T(8,128)S(1)}, u32[]{:S(2)}, u32[]{:S(2)}) %collective-permute-start.4) | collective-permute-done | bytes 262176 | tf_op jit(solution)/shard_map/ppermute | solution.py:162
  88.1 0.7 copy-done.6
  88.8 0.7 copy-done.7
  89.5 3.8 %shard_map.83 = f32[512,512]{1,0:T(8,128)} custom-call(s32[16]{0:T(128)} %gather_fusion, f32[512,512]{1,0:T(8,128)} %fusion.16.direct_ref, f32[4,128,128]{2,1,0:T(8,128)} %copy.35.rest_0_, f32[4,128,128]{2,1,0:T(8,128)} %copy-done.5, f32[4,128,128]{2,1,0:T(8,128)} %copy-done.6, f32[4,128,128]{2,1,0:T(8,128)} %copy-done.7), custom_call_target="tpu_custom_call" | custom-call | tf_op jit(solution)/shard_map/pallas_call | solution.py:100
  (48 shorter events, 1.4 us)
Async XLA Ops:
  0.0 11.8 %copy-start = (f32[8,16,16]{2,1,0:T(8,128)S(1)}, f32[8,16,16]{2,1,0:T(8,128)}, u32[]{:S(2)}) copy-start(f32[8,16,16]{2,1,0:T(8,128)} %param.12) | copy-start | bytes 24580
  0.0 13.3 %copy-start.2 = (f32[1,1,512,512]{3,2,1,0:T(8,128)S(1)}, f32[1,1,512,512]{3,2,1,0:T(8,128)}, u32[]{:S(2)}) copy-start(f32[1,1,512,512]{3,2,1,0:T(8,128)} %param.9) | copy-start | bytes 3145732
  0.0 7.7 %copy-start.9 = (s32[4,1]{0,1:T(1,128)S(1)}, s32[4,1]{0,1:T(1,128)}, u32[]{:S(2)}) copy-start(s32[4,1]{0,1:T(1,128)} %param.13) | copy-start | bytes 52
  0.0 13.3 %copy-start.3 = (f32[1,1,512,512]{3,2,1,0:T(8,128)S(1)}, f32[1,1,512,512]{3,2,1,0:T(8,128)}, u32[]{:S(2)}) copy-start(f32[1,1,512,512]{3,2,1,0:T(8,128)} %param.8) | copy-start | bytes 3145732
  0.0 9.0 %copy-start.10 = (s32[4,1]{0,1:T(1,128)S(1)}, s32[4,1]{0,1:T(1,128)}, u32[]{:S(2)}) copy-start(s32[4,1]{0,1:T(1,128)} %param.15) | copy-start | bytes 52
  0.0 13.3 %copy-start.8 = (f32[1,1,512]{2,1,0:T(1,128)S(1)}, f32[1,1,512]{2,1,0:T(1,128)}, u32[]{:S(2)}) copy-start(f32[1,1,512]{2,1,0:T(1,128)} %param.10) | copy-start | bytes 6148
  5.3 14.3 %collective-permute-start = (f32[1028,128]{1,0:T(8,128)}, f32[1028,128]{1,0:T(8,128)S(1)}, u32[]{:S(2)}, u32[]{:S(2)}) collective-permute-start(f32[1028,128]{1,0:T(8,128)} %get-tuple-element.10), channel_id=1, source_target_pairs={{0,4},{4,8},{8,12},{12,0},{1,5},{5,9},{9,13},{13,1},{2,6},{6,10},{... | collective-permute-start | bytes 1579016 | tf_op jit(solution)/shard_map/ppermute | solution.py:142
  5.5 47.7 %collective-permute-start.1 = (f32[1028,128]{1,0:T(8,128)}, f32[1028,128]{1,0:T(8,128)}, u32[]{:S(2)}, u32[]{:S(2)}) collective-permute-start(f32[1028,128]{1,0:T(8,128)} %get-tuple-element.11), channel_id=1, source_target_pairs={{0,8},{4,12},{8,0},{12,4},{1,9},{5,13},{9,1},{13,5},{2,10},{6,14},... | collective-permute-start | bytes 1579016 | tf_op jit(solution)/shard_map/ppermute | solution.py:142
  7.2 46.0 %collective-permute-start.2 = (f32[1028,128]{1,0:T(8,128)}, f32[1028,128]{1,0:T(8,128)}, u32[]{:S(2)}, u32[]{:S(2)}) collective-permute-start(f32[1028,128]{1,0:T(8,128)} %get-tuple-element.12), channel_id=1, source_target_pairs={{0,12},{4,0},{8,4},{12,8},{1,13},{5,1},{9,5},{13,9},{2,14},{6,2},{... | collective-permute-start | bytes 1579016 | tf_op jit(solution)/shard_map/ppermute | solution.py:142
  15.7 0.7 copy-start.1
  15.7 37.5 %copy-start.4 = (f32[1028,128]{1,0:T(8,128)S(1)}, f32[1028,128]{1,0:T(8,128)}, u32[]{:S(2)}) copy-start(f32[1028,128]{1,0:T(8,128)} %get-tuple-element.9) | copy-start | bytes 1579012
  63.4 7.2 %collective-permute-start.3 = (f32[4,128,128]{2,1,0:T(8,128)S(1)}, f32[4,128,128]{2,1,0:T(8,128)S(1)}, u32[]{:S(2)}, u32[]{:S(2)}) collective-permute-start(f32[4,128,128]{2,1,0:T(8,128)S(1)} %copy.36), channel_id=1, source_target_pairs={{0,4},{4,8},{8,12},{12,0},{1,5},{5,9},{9,13},{13,1},{2,6},{6,10},{... | collective-permute-start | bytes 786440 | tf_op jit(solution)/shard_map/ppermute | solution.py:162
  63.5 24.6 %collective-permute-start.4 = (f32[4,128,128]{2,1,0:T(8,128)S(1)}, f32[4,128,128]{2,1,0:T(8,128)S(1)}, u32[]{:S(2)}, u32[]{:S(2)}) collective-permute-start(f32[4,128,128]{2,1,0:T(8,128)S(1)} %copy.37), channel_id=1, source_target_pairs={{0,8},{4,12},{8,0},{12,4},{1,9},{5,13},{9,1},{13,5},{2,10},{6,14},... | collective-permute-start | bytes 786440 | tf_op jit(solution)/shard_map/ppermute | solution.py:162
  64.9 23.2 %collective-permute-start.5 = (f32[4,128,128]{2,1,0:T(8,128)S(1)}, f32[4,128,128]{2,1,0:T(8,128)S(1)}, u32[]{:S(2)}, u32[]{:S(2)}) collective-permute-start(f32[4,128,128]{2,1,0:T(8,128)S(1)} %copy.38), channel_id=1, source_target_pairs={{0,12},{4,0},{8,4},{12,8},{1,13},{5,1},{9,5},{13,9},{2,14},{6,2},{... | collective-permute-start | bytes 786440 | tf_op jit(solution)/shard_map/ppermute | solution.py:162
  70.6 17.5 %copy-start.5 = (f32[4,128,128]{2,1,0:T(8,128)}, f32[4,128,128]{2,1,0:T(8,128)S(1)}, u32[]{:S(2)}) copy-start(f32[4,128,128]{2,1,0:T(8,128)S(1)} %collective-permute-done.3.rest_1_) | copy-start | bytes 786436
  88.1 0.7 copy-start.6
  88.8 0.7 copy-start.7

commit v14 on v6

--- a/solution.py
+++ b/solution.py
@@ -48,11 +48,14 @@
             for r in range(spread):
                 tile = order_ref[g * spread + r]
                 top = pl.multiple_of((tile // blocks) * TS, TS)
-                left = pl.multiple_of((tile % blocks) * TS, TS)
-                for m, src in enumerate((gen_ref, ham_ref)):
-                    outs[s][(2 * r + m) * TS:(2 * r + m + 1) * TS, :] = src[
-                        pl.ds(top, TS), pl.ds(left, TS)
-                    ]
+                for b in range(blocks):
+
+                    @pl.when(tile % blocks == b)
+                    def _(s=s, r=r, b=b, top=top):
+                        for m, src in enumerate((gen_ref, ham_ref)):
+                            outs[s][(2 * r + m) * TS:(2 * r + m + 1) * TS, :] = src[
+                                pl.ds(top, TS), b * TS:(b + 1) * TS
+                            ]
             mine = owner_ref[g]
             slot = 0
             for other in range(channels - 1):
@@ -90,11 +93,18 @@
         for s, piece in enumerate(pieces):
             for r in range(spread):
                 tile = place_ref[s * spread + r]
-                top = pl.multiple_of((tile // blocks) * TS, TS)
-                left = pl.multiple_of((tile % blocks) * TS, TS)
-                value = 0.5 * piece[r]
-                out_ref[pl.ds(top, TS), pl.ds(left, TS)] += value
-                out_ref[pl.ds(left, TS), pl.ds(top, TS)] += value.T
+                row, col = tile // blocks, tile % blocks
+                top = pl.multiple_of(row * TS, TS)
+                left = pl.multiple_of(col * TS, TS)
+                for b in range(blocks):
+
+                    @pl.when(col == b)
+                    def _(piece=piece, r=r, b=b, top=top):
+                        out_ref[pl.ds(top, TS), b * TS:(b + 1) * TS] += 0.5 * piece[r]
+
+                    @pl.when(row == b)
+                    def _(piece=piece, r=r, b=b, left=left):
+                        out_ref[pl.ds(left, TS), b * TS:(b + 1) * TS] += 0.5 * piece[r].T
 
     whole = pl.BlockSpec(memory_space=pltpu.VMEM)
     return pl.pallas_call(

time: 93.6 us -> 96.1 us (1.027)
  Pallas kernels: 7.55 us -> 10 us
    pallas_call x1, Pallas kernels: 3.76 us -> 5.77 us  [finish(): pl.pallas_call(kernel, grid_spec=pltpu.PrefetchScalarGridSpec(num_scalar_...]
where the time goes in v14:
time: 96.1 us; the launch traced here: 95.8 us
  waiting for transfers between devices  55.5 us (58%)
  local copies, waits for them, and re-layouts  10.3 us (11%)
  Pallas kernels  10 us (10%)
  matrix products  8.42 us (9%)
  starting transfers between devices  5.88 us (6%)
  other arithmetic  2.94 us (3%)
  between operations  2.78 us (3%)
    ppermute x3, waiting for transfers between devices, body(): got.append(lax.ppermute(sends[shift], 'chan', pairs))  36.3 us
    ppermute x3, waiting for transfers between devices, body(): home.append(lax.ppermute(back[shift], 'chan', pairs))  19.2 us
    pallas_call x1, Pallas kernels, finish(): pl.pallas_call(kernel, grid_spec=pltpu.PrefetchScalarGridSpec(num_scalar_...  5.77 us
    pallas_call x1, Pallas kernels, build_sends(): pl.pallas_call(kernel, grid_spec=pltpu.PrefetchScalarGridSpec(num_scalar_...  4.25 us
    unnamed x27, local copies, waits for them, and re-layouts  3.65 us
    ppermute x3, starting transfers between devices, body(): home.append(lax.ppermute(back[shift], 'chan', pairs))  3.53 us
    dot_general x2, matrix products, bracket(): jnp.matmul(right_matrix * scaled, left_matrix, precision=highest)  3.03 us
    ppermute x3, starting transfers between devices, body(): got.append(lax.ppermute(sends[shift], 'chan', pairs))  2.35 us
  transfers between devices with their start and end apart: 6, of which 4 were waited for; matrix products, arithmetic and copies ran while one was open for 9% of the time, Pallas kernels for 0%

profile of v14, /device:TPU:28, one launch (start us, length us, event | category | flops | bytes accessed | tf_op | source)
XLA Modules:
  0.0 95.8 jit_solution(9190285477780727244)
XLA Ops:
  0.0 1.4 %copy.28.weight_ref = f32[1,1,3,512]{3,2,1,0:T(4,128)} copy(f32[1,1,3,512]{3,1,2,0:T(1,128)} %param.11) | data formatting | bytes 12288 | tf_op args[3]
  1.5 4.2 %shard_map.82 = (f32[1028,128]{1,0:T(8,128)}, f32[1028,128]{1,0:T(8,128)}, f32[1028,128]{1,0:T(8,128)}, f32[1028,128]{1,0:T(8,128)}) custom-call(s32[16]{0:T(128)} %bitcast.84, s32[4]{0:T(128)} %bitcast.103, f32[512,512]{1,0:T(8,128)} %bitcast.87, f32[512,512]{1,0:T(8,128)} %bitcast.88, f32[1,1,3,512]{3,2,1,0:T(4,128)} %copy.28.weight_ref), custom_call_target="tpu_custom_call" | custom-call | tf_op jit(solution)/shard_map/pallas_call | solution.py:73
  5.7 0.2 collective-permute-start
  5.9 1.7 %collective-permute-start.1 = (f32[1028,128]{1,0:T(8,128)}, f32[1028,128]{1,0:T(8,128)}, u32[]{:S(2)}, u32[]{:S(2)}) collective-permute-start(f32[1028,128]{1,0:T(8,128)} %get-tuple-element.11), channel_id=1, source_target_pairs={{0,8},{4,12},{8,0},{12,4},{1,9},{5,13},{9,1},{13,5},{2,10},{6,14},... | collective-permute-start | bytes 1579016 | tf_op jit(solution)/shard_map/ppermute | solution.py:152
  7.6 0.4 collective-permute-start.2
  8.1 0.6 constant_dynamic-slice_fusion
  9.4 0.6 constant_dynamic-slice_fusion.2
  12.2 0.6 gather_fusion.2
  13.0 0.6 gather_fusion.1
  13.5 1.0 %fusion.13 = f32[512,512]{0,1:T(8,128)S(1)} fusion(f32[1,1,512,512]{3,2,1,0:T(8,128)S(1)} %copy-done.2, f32[512]{0:T(512)S(1)} %bitcast.101, f32[1,1,512,512]{3,2,1,0:T(8,128)S(1)} %copy-done.3), kind=kOutput, calls=%fused_computation.24 | convolution fusion | flops 805568512 | bytes 3147776 | tf_op jit(solution)/shard_map/dot_general | solution.py:34
  14.6 1.0 %convolution_subtract_fusion.1 = f32[512,512]{0,1:T(8,128)S(1)} fusion(f32[512,512]{0,1:T(8,128)S(1)} %fusion.13, f32[1,1,512,512]{3,2,1,0:T(8,128)S(1)} %copy-done.3, f32[512]{0:T(512)S(1)} %bitcast.102, f32[1,1,512,512]{3,2,1,0:T(8,128)S(1)} %copy-done.2), kind=kOutput, calls=%fused_computation.5 | convolution fusion | flops 805830656 | bytes 4196352 | tf_op jit(solution)/shard_map/dot_general | solution.py:35
  15.6 0.3 copy.25
  16.2 1.2 %gather_fusion = s32[16]{0:T(128)} fusion(s32[16]{0:T(128)S(1)} %bitcast.85, s32[1024]{0:T(1024)S(1)} %pad_clamp_fusion.2), kind=kCustom, calls=%fused_computation | custom fusion | bytes 192 | tf_op jit(solution)/shard_map/gather | solution.py:173
  17.4 2.8 %collective-permute-done = f32[1028,128]{1,0:T(8,128)} collective-permute-done((f32[1028,128]{1,0:T(8,128)}, f32[1028,128]{1,0:T(8,128)}, u32[]{:S(2)}, u32[]{:S(2)}) %collective-permute-start) | collective-permute-done | bytes 526368 | tf_op jit(solution)/shard_map/ppermute | solution.py:152
  20.2 33.5 %collective-permute-done.1 = f32[1028,128]{1,0:T(8,128)} collective-permute-done((f32[1028,128]{1,0:T(8,128)}, f32[1028,128]{1,0:T(8,128)}, u32[]{:S(2)}, u32[]{:S(2)}) %collective-permute-start.1) | collective-permute-done | bytes 526368 | tf_op jit(solution)/shard_map/ppermute | solution.py:152
  53.7 1.5 %pad_maximum_fusion = f32[4,1028,128]{2,1,0:T(8,128)S(1)} fusion(f32[1,1028,128]{2,1,0:T(8,128)} %bitcast.21, f32[1,1028,128]{2,1,0:T(8,128)} %bitcast.20, f32[1,1028,128]{2,1,0:T(8,128)} %bitcast.19, f32[1,1028,128]{2,1,0:T(8,128)S(1)} %bitcast.97), kind=kLoop, calls=%fused_computation.3 | loop fusion | flops 1579008 | bytes 4210688 | tf_op jit(solution)/shard_map/stack | solution.py:153
  55.3 0.2 fusion.28
  55.5 1.2 %fusion.10 = f32[4,4,128,128]{3,1,2,0:T(4,128)S(1)} fusion(f32[4,4,16,1]{2,1,3,0:T(4,128)S(1)} %bitcast.98, f32[16,1,128,128]{3,2,1,0:T(8,128)S(1)} %get-tuple-element.13), kind=kOutput, calls=%fused_computation.18 | convolution fusion | flops 25165824 | bytes 2098176 | tf_op jit(solution)/shard_map/ji,ixy->jxy/dot_general | solution.py:161
  56.8 1.5 %bitcast_multiply_fusion = (f32[4,128,4,128]{3,2,1,0:T(4,128)S(1)}, f32[4,128,4,128]{3,2,1,0:T(4,128)S(1)}, f32[4,4,128,128]{3,1,2,0:T(4,128)S(1)}) fusion(f32[4,128]{1,0:T(4,128)S(1)} %dynamic-slice_bitcast_fusion, f32[4,4,128,128]{3,1,2,0:T(4,128)S(1)} %fusion.10, f32[4,4,16,1]{2,1,3,0:T(4,128)S(1)} %bitcast.99, f32[16,1,128,128]{3,2,1,0:T(8,128)S(1)} %get-tuple-element.14), kind=kOutput, calls=%fused_computation.19 | convolution fusion | flops 25690112 | bytes 5245952 | tf_op jit(solution)/shard_map/ji,ixy->jxy/dot_general | solution.py:162
  58.3 1.0 %fusion.4 = f32[512,512]{1,0:T(8,128)S(1)} fusion(f32[64,8,4,128]{3,2,1,0:T(4,128)S(1)} %bitcast.91, f32[64,8,4,128]{3,2,1,0:T(4,128)S(1)} %bitcast.90), kind=kOutput, calls=%fused_computation.10 | convolution fusion | flops 805306368 | bytes 3145728 | tf_op jit(solution)/shard_map/dot_general | solution.py:34
  59.4 2.0 %convolution_subtract_fusion = f32[512,512]{1,0:T(8,128)} fusion(f32[512,512]{1,0:T(8,128)S(1)} %fusion.4, f32[64,8,4,128]{3,2,1,0:T(4,128)S(1)} %bitcast.86, f32[64,8,4,128]{3,2,1,0:T(4,128)S(1)} %bitcast.92), kind=kOutput, calls=%fused_computation.4 | convolution fusion | flops 805568512 | bytes 4194304 | tf_op jit(solution)/shard_map/dot_general | solution.py:35
  61.4 1.6 %reshape.186 = f32[4,128,4,128]{3,2,1,0:T(4,128)S(1)} reshape(f32[512,512]{1,0:T(8,128)} %convolution_subtract_fusion) | data formatting | bytes 2097152 | tf_op jit(solution)/shard_map/reshape | solution.py:19
  63.1 0.6 fusion.19
  64.0 1.4 %collective-permute-start.4 = (f32[4,128,128]{2,1,0:T(8,128)S(1)}, f32[4,128,128]{2,1,0:T(8,128)S(1)}, u32[]{:S(2)}, u32[]{:S(2)}) collective-permute-start(f32[4,128,128]{2,1,0:T(8,128)S(1)} %copy.43), channel_id=1, source_target_pairs={{0,8},{4,12},{8,0},{12,4},{1,9},{5,13},{9,1},{13,5},{2,10},{6,14},... | collective-permute-start | bytes 786440 | tf_op jit(solution)/shard_map/ppermute | solution.py:172
  65.4 2.1 %collective-permute-start.5 = (f32[4,128,128]{2,1,0:T(8,128)S(1)}, f32[4,128,128]{2,1,0:T(8,128)S(1)}, u32[]{:S(2)}, u32[]{:S(2)}) collective-permute-start(f32[4,128,128]{2,1,0:T(8,128)S(1)} %copy.44), channel_id=1, source_target_pairs={{0,12},{4,0},{8,4},{12,8},{1,13},{5,1},{9,5},{13,9},{2,14},{6,2},{... | collective-permute-start | bytes 786440 | tf_op jit(solution)/shard_map/ppermute | solution.py:172
  67.5 1.2 %fusion.11.direct_ref = f32[512,512]{1,0:T(8,128)} fusion(f32[512,512]{1,0:T(8,128)S(1)} %copy.25, f32[512,512]{0,1:T(8,128)S(1)} %convolution_subtract_fusion.1), kind=kLoop, calls=%fused_computation.22 | loop fusion | flops 524288 | bytes 3145728 | tf_op jit(solution)/shard_map/mul | solution.py:176
  68.7 0.7 copy.41.rest_0_
  69.4 1.7 %collective-permute-done.3.rest_1_ = f32[4,128,128]{2,1,0:T(8,128)S(1)} collective-permute-done((f32[4,128,128]{2,1,0:T(8,128)S(1)}, f32[4,128,128]{2,1,0:T(8,128)S(1)}, u32[]{:S(2)}, u32[]{:S(2)}) %collective-permute-start.3) | collective-permute-done | bytes 262176 | tf_op jit(solution)/shard_map/ppermute | solution.py:172
  71.1 17.5 %collective-permute-done.4.rest_2_ = f32[4,128,128]{2,1,0:T(8,128)S(1)} collective-permute-done((f32[4,128,128]{2,1,0:T(8,128)S(1)}, f32[4,128,128]{2,1,0:T(8,128)S(1)}, u32[]{:S(2)}, u32[]{:S(2)}) %collective-permute-start.4) | collective-permute-done | bytes 262176 | tf_op jit(solution)/shard_map/ppermute | solution.py:172
  88.6 0.7 copy-done.6
  89.3 0.7 copy-done.7
  90.0 5.8 %shard_map.83 = f32[512,512]{1,0:T(8,128)} custom-call(s32[16]{0:T(128)} %gather_fusion, f32[512,512]{1,0:T(8,128)} %fusion.11.direct_ref, f32[4,128,128]{2,1,0:T(8,128)} %copy.41.rest_0_, f32[4,128,128]{2,1,0:T(8,128)} %copy-done.5, f32[4,128,128]{2,1,0:T(8,128)} %copy-done.6, f32[4,128,128]{2,1,0:T(8,128)} %copy-done.7), custom_call_target="tpu_custom_call" | custom-call | tf_op jit(solution)/shard_map/pallas_call | solution.py:110
  (47 shorter events, 1.3 us)
Async XLA Ops:
  0.0 11.9 %copy-start = (f32[8,16,16]{2,1,0:T(8,128)S(1)}, f32[8,16,16]{2,1,0:T(8,128)}, u32[]{:S(2)}) copy-start(f32[8,16,16]{2,1,0:T(8,128)} %param.12) | copy-start | bytes 24580
  0.0 8.1 %copy-start.9 = (s32[4,1]{0,1:T(1,128)S(1)}, s32[4,1]{0,1:T(1,128)}, u32[]{:S(2)}) copy-start(s32[4,1]{0,1:T(1,128)} %param.13) | copy-start | bytes 52
  0.0 13.5 %copy-start.3 = (f32[1,1,512,512]{3,2,1,0:T(8,128)S(1)}, f32[1,1,512,512]{3,2,1,0:T(8,128)}, u32[]{:S(2)}) copy-start(f32[1,1,512,512]{3,2,1,0:T(8,128)} %param.9) | copy-start | bytes 3145732
  0.0 13.5 %copy-start.2 = (f32[1,1,512,512]{3,2,1,0:T(8,128)S(1)}, f32[1,1,512,512]{3,2,1,0:T(8,128)}, u32[]{:S(2)}) copy-start(f32[1,1,512,512]{3,2,1,0:T(8,128)} %param.8) | copy-start | bytes 3145732
  0.0 9.4 %copy-start.10 = (s32[4,1]{0,1:T(1,128)S(1)}, s32[4,1]{0,1:T(1,128)}, u32[]{:S(2)}) copy-start(s32[4,1]{0,1:T(1,128)} %param.15) | copy-start | bytes 52
  0.0 13.5 %copy-start.8 = (f32[1,1,512]{2,1,0:T(1,128)S(1)}, f32[1,1,512]{2,1,0:T(1,128)}, u32[]{:S(2)}) copy-start(f32[1,1,512]{2,1,0:T(1,128)} %param.10) | copy-start | bytes 6148
  5.7 14.5 %collective-permute-start = (f32[1028,128]{1,0:T(8,128)}, f32[1028,128]{1,0:T(8,128)}, u32[]{:S(2)}, u32[]{:S(2)}) collective-permute-start(f32[1028,128]{1,0:T(8,128)} %get-tuple-element.10), channel_id=1, source_target_pairs={{0,4},{4,8},{8,12},{12,0},{1,5},{5,9},{9,13},{13,1},{2,6},{6,10},{... | collective-permute-start | bytes 1579016 | tf_op jit(solution)/shard_map/ppermute | solution.py:152
  5.9 47.7 %collective-permute-start.1 = (f32[1028,128]{1,0:T(8,128)}, f32[1028,128]{1,0:T(8,128)}, u32[]{:S(2)}, u32[]{:S(2)}) collective-permute-start(f32[1028,128]{1,0:T(8,128)} %get-tuple-element.11), channel_id=1, source_target_pairs={{0,8},{4,12},{8,0},{12,4},{1,9},{5,13},{9,1},{13,5},{2,10},{6,14},... | collective-permute-start | bytes 1579016 | tf_op jit(solution)/shard_map/ppermute | solution.py:152
  7.6 46.0 %collective-permute-start.2 = (f32[1028,128]{1,0:T(8,128)}, f32[1028,128]{1,0:T(8,128)}, u32[]{:S(2)}, u32[]{:S(2)}) collective-permute-start(f32[1028,128]{1,0:T(8,128)} %get-tuple-element.12), channel_id=1, source_target_pairs={{0,12},{4,0},{8,4},{12,8},{1,13},{5,1},{9,5},{13,9},{2,14},{6,2},{... | collective-permute-start | bytes 1579016 | tf_op jit(solution)/shard_map/ppermute | solution.py:152
  14.6 1.6 %copy-start.1 = (s32[1,1,16]{2,1,0:T(1,128)S(1)}, s32[1,1,16]{2,1,0:T(1,128)}, u32[]{:S(2)}) copy-start(s32[1,1,16]{2,1,0:T(1,128)} %param.14) | copy-start | bytes 196
  15.6 38.0 %copy-start.4 = (f32[1028,128]{1,0:T(8,128)S(1)}, f32[1028,128]{1,0:T(8,128)}, u32[]{:S(2)}) copy-start(f32[1028,128]{1,0:T(8,128)} %get-tuple-element.9) | copy-start | bytes 1579012
  63.9 7.2 %collective-permute-start.3 = (f32[4,128,128]{2,1,0:T(8,128)S(1)}, f32[4,128,128]{2,1,0:T(8,128)S(1)}, u32[]{:S(2)}, u32[]{:S(2)}) collective-permute-start(f32[4,128,128]{2,1,0:T(8,128)S(1)} %copy.42), channel_id=1, source_target_pairs={{0,4},{4,8},{8,12},{12,0},{1,5},{5,9},{9,13},{13,1},{2,6},{6,10},{... | collective-permute-start | bytes 786440 | tf_op jit(solution)/shard_map/ppermute | solution.py:172
  64.0 24.6 %collective-permute-start.4 = (f32[4,128,128]{2,1,0:T(8,128)S(1)}, f32[4,128,128]{2,1,0:T(8,128)S(1)}, u32[]{:S(2)}, u32[]{:S(2)}) collective-permute-start(f32[4,128,128]{2,1,0:T(8,128)S(1)} %copy.43), channel_id=1, source_target_pairs={{0,8},{4,12},{8,0},{12,4},{1,9},{5,13},{9,1},{13,5},{2,10},{6,14},... | collective-permute-start | bytes 786440 | tf_op jit(solution)/shard_map/ppermute | solution.py:172
  65.4 23.2 %collective-permute-start.5 = (f32[4,128,128]{2,1,0:T(8,128)S(1)}, f32[4,128,128]{2,1,0:T(8,128)S(1)}, u32[]{:S(2)}, u32[]{:S(2)}) collective-permute-start(f32[4,128,128]{2,1,0:T(8,128)S(1)} %copy.44), channel_id=1, source_target_pairs={{0,12},{4,0},{8,4},{12,8},{1,13},{5,1},{9,5},{13,9},{2,14},{6,2},{... | collective-permute-start | bytes 786440 | tf_op jit(solution)/shard_map/ppermute | solution.py:172
  71.1 17.5 %copy-start.5 = (f32[4,128,128]{2,1,0:T(8,128)}, f32[4,128,128]{2,1,0:T(8,128)S(1)}, u32[]{:S(2)}) copy-start(f32[4,128,128]{2,1,0:T(8,128)S(1)} %collective-permute-done.3.rest_1_) | copy-start | bytes 786436
  88.6 0.7 copy-start.6
  89.3 0.7 copy-start.7

commit v15 on v10

--- a/solution.py
+++ b/solution.py
@@ -131,6 +131,8 @@
     order = tile_order[0, 0]
     owners = cross_owner[:, 0]
 
+    dest = (me + chan_range) % channels
+    source = (me - chan_range) % channels
     sends = build_sends(
         order, owners, generator[0, 0], hamiltonian[0, 0], cross_weights, channels, spread
     )
@@ -138,14 +140,16 @@
     for shift in range(1, channels):
         pairs = [(c, (c + shift) % channels) for c in range(channels)]
         got.append(lax.ppermute(sends[shift], "chan", pairs))
-    got = jnp.stack(got)[(me - chan_range) % channels]
+    got = jnp.stack(got)
     tiles_got = got[:, : 2 * spread * TS].reshape(channels, spread, 2, TS, TS)
-    weights_cross = got[owners[me], 2 * spread * TS :].reshape(-1)
+    weights_cross = got[(me - owners[me]) % channels, 2 * spread * TS :].reshape(-1)
 
     mixer = recoupling[recoupling_index[me, 0]]
-    cross = jnp.swapaxes(tiles_got, 0, 1).reshape(tile_count, 2, TS, TS)
-    generator_mixed = jnp.einsum("ji,ixy->jxy", mixer, cross[:, 0], precision=highest)
-    hamilton_mixed = jnp.einsum("ji,ixy->jxy", mixer, cross[:, 1], precision=highest)
+    column_of = (spread_range[None, :] * channels + source[:, None]).reshape(-1)
+    mixer_in = mixer[:, column_of]
+    cross = tiles_got.reshape(tile_count, 2, TS, TS)
+    generator_mixed = jnp.einsum("ji,ixy->jxy", mixer_in, cross[:, 0], precision=highest)
+    hamilton_mixed = jnp.einsum("ji,ixy->jxy", mixer_in, cross[:, 1], precision=highest)
     product = bracket(
         from_tiles(generator_mixed, TS), from_tiles(hamilton_mixed, TS), weights_cross
     )

time: 102 us -> 97.3 us (0.954)
  local copies, waits for them, and re-layouts: 10.4 us -> 5.75 us
    slice x2 -> x1, local copies, waits for them, and re-layouts: 1.59 us -> 0.14 us  [body(): tiles_got = got[:, :2 * spread * TS].reshape(channels, spread, 2, TS, TS)]
    gather x1 -> x2, local copies, waits for them, and re-layouts: 2.03 us -> 0.64 us  [body(): mixer_in = mixer[:, column_of]]
    transpose x1 -> x0, local copies, waits for them, and re-layouts: 1.35 us -> none  [body(): cross = jnp.swapaxes(tiles_got, 0, 1).reshape(tile_count, 2, TS, TS)]
    unnamed x17 -> x13, local copies, waits for them, and re-layouts: 2.15 us -> 1.35 us
  transfers between devices with their start and end apart: 4 -> 4, of which waited for: 3 -> 3; matrix products, arithmetic and copies ran while one was open for 5% -> 6% of each run, Pallas kernels for 0% -> 0%
where the time goes in v15:
time: 97.3 us; the launch traced here: 97 us
  waiting for transfers between devices  49.4 us (51%)
  starting transfers between devices  21 us (22%)
  Pallas kernels  7.62 us (8%)
  matrix products  7.62 us (8%)
  local copies, waits for them, and re-layouts  5.75 us (6%)
  between operations  2.95 us (3%)
  other arithmetic  2.57 us (3%)
    ppermute x3, waiting for transfers between devices, body(): got.append(lax.ppermute(sends[shift], 'chan', pairs))  28.1 us
    all_to_all x1, waiting for transfers between devices, body(): home = lax.all_to_all(back, 'chan', 0, 0, tiled=True)  21.3 us
    all_to_all x1, starting transfers between devices, body(): home = lax.all_to_all(back, 'chan', 0, 0, tiled=True)  14.1 us
    ppermute x3, starting transfers between devices, body(): got.append(lax.ppermute(sends[shift], 'chan', pairs))  6.96 us
    pallas_call x1, Pallas kernels, build_sends(): pl.pallas_call(kernel, grid_spec=pltpu.PrefetchScalarGridSpec(num_scalar_...  3.83 us
    pallas_call x1, Pallas kernels, finish(): pl.pallas_call(kernel, grid_spec=pltpu.PrefetchScalarGridSpec(num_scalar_...  3.79 us
    dot_general x2, matrix products, bracket(): jnp.matmul(right_matrix * scaled, left_matrix, precision=highest)  2.06 us
    dot_general x2, matrix products, bracket(): jnp.matmul(left_matrix * scaled, right_matrix, precision=highest)  2.05 us
  transfers between devices with their start and end apart: 4, of which 3 were waited for; matrix products, arithmetic and copies ran while one was open for 6% of the time, Pallas kernels for 0%

profile of v15, /device:TPU:0, one launch (start us, length us, event | category | flops | bytes accessed | tf_op | source)
XLA Modules:
  0.0 97.0 jit_solution(16183689382669386567)
XLA Ops:
  0.0 1.3 %copy.25.weight_ref = f32[1,1,3,512]{3,2,1,0:T(4,128)} copy(f32[1,1,3,512]{3,1,2,0:T(1,128)} %param.11) | data formatting | bytes 12288 | tf_op args[3]
  1.3 3.8 %shard_map.82 = (f32[1028,128]{1,0:T(8,128)}, f32[1028,128]{1,0:T(8,128)}, f32[1028,128]{1,0:T(8,128)}, f32[1028,128]{1,0:T(8,128)}) custom-call(s32[16]{0:T(128)} %bitcast.111, s32[4]{0:T(128)} %bitcast.113, f32[512,512]{1,0:T(8,128)} %bitcast.92, f32[512,512]{1,0:T(8,128)} %bitcast.93, f32[1,1,3,512]{3,2,1,0:T(4,128)} %copy.25.weight_ref), custom_call_target="tpu_custom_call" | custom-call | tf_op jit(solution)/shard_map/pallas_call | solution.py:70
  5.2 3.0 %collective-permute-start = (f32[1028,128]{1,0:T(8,128)}, f32[1028,128]{1,0:T(8,128)S(1)}, u32[]{:S(2)}, u32[]{:S(2)}) collective-permute-start(f32[1028,128]{1,0:T(8,128)} %get-tuple-element.10), channel_id=1, source_target_pairs={{0,4},{4,8},{8,12},{12,0},{1,5},{5,9},{9,13},{13,1},{2,6},{6,10},{... | collective-permute-start | bytes 1579016 | tf_op jit(solution)/shard_map/ppermute | solution.py:142
  8.2 2.6 %collective-permute-start.1 = (f32[1028,128]{1,0:T(8,128)}, f32[1028,128]{1,0:T(8,128)S(1)}, u32[]{:S(2)}, u32[]{:S(2)}) collective-permute-start(f32[1028,128]{1,0:T(8,128)} %get-tuple-element.11), channel_id=1, source_target_pairs={{0,8},{4,12},{8,0},{12,4},{1,9},{5,13},{9,1},{13,5},{2,10},{6,14},... | collective-permute-start | bytes 1579016 | tf_op jit(solution)/shard_map/ppermute | solution.py:142
  10.8 1.3 %collective-permute-start.2 = (f32[1028,128]{1,0:T(8,128)}, f32[1028,128]{1,0:T(8,128)S(1)}, u32[]{:S(2)}, u32[]{:S(2)}) collective-permute-start(f32[1028,128]{1,0:T(8,128)} %get-tuple-element.12), channel_id=1, source_target_pairs={{0,12},{4,0},{8,4},{12,8},{1,13},{5,1},{9,5},{13,9},{2,14},{6,2},{... | collective-permute-start | bytes 1579016 | tf_op jit(solution)/shard_map/ppermute | solution.py:142
  12.1 0.7 constant_dynamic-slice_fusion
  13.5 0.7 constant_dynamic-slice_fusion.2
  16.3 0.1 copy.23
  16.4 0.1 broadcast_add_fusion
  16.4 0.1 add.68
  16.5 0.6 gather_fusion
  17.1 0.1 copy.24
  17.2 6.2 %collective-permute-done = f32[1028,128]{1,0:T(8,128)S(1)} collective-permute-done((f32[1028,128]{1,0:T(8,128)}, f32[1028,128]{1,0:T(8,128)S(1)}, u32[]{:S(2)}, u32[]{:S(2)}) %collective-permute-start) | collective-permute-done | bytes 526368 | tf_op jit(solution)/shard_map/ppermute | solution.py:142
  23.4 21.8 %collective-permute-done.1 = f32[1028,128]{1,0:T(8,128)S(1)} collective-permute-done((f32[1028,128]{1,0:T(8,128)}, f32[1028,128]{1,0:T(8,128)S(1)}, u32[]{:S(2)}, u32[]{:S(2)}) %collective-permute-start.1) | collective-permute-done | bytes 526368 | tf_op jit(solution)/shard_map/ppermute | solution.py:142
  45.2 1.2 %pad_maximum_fusion = f32[4,1028,128]{2,1,0:T(8,128)S(1)} fusion(f32[1,1028,128]{2,1,0:T(8,128)S(1)} %bitcast.105, f32[1,1028,128]{2,1,0:T(8,128)S(1)} %bitcast.104, f32[1,1028,128]{2,1,0:T(8,128)S(1)} %bitcast.103, f32[1,1028,128]{2,1,0:T(8,128)} %bitcast.102), kind=kLoop, calls=%fused_computation.1 | loop fusion | flops 1579008 | bytes 4210688 | tf_op jit(solution)/shard_map/stack | solution.py:143
  46.5 0.1 slice.14
  46.6 0.2 fusion.23
  46.8 1.2 %fusion.10 = f32[4,4,128,128]{3,1,2,0:T(4,128)S(1)} fusion(f32[4,4,16,1]{2,1,3,0:T(4,128)S(1)} %bitcast.106, f32[16,1,128,128]{3,2,1,0:T(8,128)S(1)} %get-tuple-element.13), kind=kOutput, calls=%fused_computation.16 | convolution fusion | flops 25165824 | bytes 2098176 | tf_op jit(solution)/shard_map/ji,ixy->jxy/dot_general | solution.py:151
  48.1 1.5 %bitcast_multiply_fusion = (f32[4,128,4,128]{3,2,1,0:T(4,128)S(1)}, f32[4,128,4,128]{3,2,1,0:T(4,128)S(1)}, f32[4,4,128,128]{3,1,2,0:T(4,128)S(1)}) fusion(f32[4,128]{1,0:T(4,128)S(1)} %dynamic-slice_bitcast_fusion, f32[4,4,128,128]{3,1,2,0:T(4,128)S(1)} %fusion.10, f32[4,4,16,1]{2,1,3,0:T(4,128)S(1)} %bitcast.107, ...), kind=kOutput, calls=%fused_computation.17 | convolution fusion | flops 25690112 | bytes 5245952 | tf_op jit(solution)/shard_map/ji,ixy->jxy/dot_general | solution.py:152
  49.6 1.0 %fusion.4 = f32[512,512]{1,0:T(8,128)S(1)} fusion(f32[64,8,4,128]{3,2,1,0:T(4,128)S(1)} %bitcast.96, f32[64,8,4,128]{3,2,1,0:T(4,128)S(1)} %bitcast.95), kind=kOutput, calls=%fused_computation.8 | convolution fusion | flops 805306368 | bytes 3145728 | tf_op jit(solution)/shard_map/dot_general | solution.py:34
  50.6 1.0 %convolution_subtract_fusion = f32[512,512]{1,0:T(8,128)S(1)} fusion(f32[512,512]{1,0:T(8,128)S(1)} %fusion.4, f32[64,8,4,128]{3,2,1,0:T(4,128)S(1)} %bitcast.91, f32[64,8,4,128]{3,2,1,0:T(4,128)S(1)} %bitcast.97), kind=kOutput, calls=%fused_computation.2 | convolution fusion | flops 805568512 | bytes 4194304 | tf_op jit(solution)/shard_map/dot_general | solution.py:35
  51.7 0.4 reshape.100
  52.0 0.2 copy.28
  52.2 0.7 fusion.24
  53.0 1.1 %copy.63 = f32[4,4,128,128]{3,2,0,1:T(8,128)} copy(f32[4,4,128,128]{3,1,2,0:T(4,128)S(1)} %fusion.24) | data formatting | bytes 2097152 | tf_op jit(solution)/shard_map/ji,jxy->ixy/dot_general | solution.py:156
  54.1 14.1 %all-to-all-start = ((f32[4,4,128,128]{3,2,1,0:T(8,128)}), f32[4,4,128,128]{3,2,1,0:T(8,128)}, u32[]{:S(2)}, u32[]{:S(2)}) async-start(f32[4,4,128,128]{3,2,1,0:T(8,128)} %bitcast.90), calls=%async_computation | async-start | bytes 2097152 | tf_op jit(solution)/shard_map/all_to_all | solution.py:158
  68.2 1.0 %fusion.13 = f32[512,512]{0,1:T(8,128)S(1)} fusion(f32[1,1,512,512]{3,2,1,0:T(8,128)S(1)} %copy-done.1, f32[512]{0:T(512)S(1)} %bitcast.109, f32[1,1,512,512]{3,2,1,0:T(8,128)S(1)} %copy-done.2), kind=kOutput, calls=%fused_computation.22 | convolution fusion | flops 805568512 | bytes 3147776 | tf_op jit(solution)/shard_map/dot_general | solution.py:34
  69.2 1.0 %convolution_subtract_fusion.1 = f32[512,512]{0,1:T(8,128)S(1)} fusion(f32[512,512]{0,1:T(8,128)S(1)} %fusion.13, f32[1,1,512,512]{3,2,1,0:T(8,128)S(1)} %copy-done.2, f32[512]{0:T(512)S(1)} %bitcast.110, f32[1,1,512,512]{3,2,1,0:T(8,128)S(1)} %copy-done.1), kind=kOutput, calls=%fused_computation.3 | convolution fusion | flops 805830656 | bytes 4196352 | tf_op jit(solution)/shard_map/dot_general | solution.py:35
  70.3 0.3 copy.22
  70.6 1.2 %fusion.11.direct_ref = f32[512,512]{1,0:T(8,128)} fusion(f32[512,512]{1,0:T(8,128)S(1)} %copy.22, f32[512,512]{0,1:T(8,128)S(1)} %convolution_subtract_fusion.1), kind=kLoop, calls=%fused_computation.20 | loop fusion | flops 524288 | bytes 3145728 | tf_op jit(solution)/shard_map/mul | solution.py:161
  71.8 21.3 %all-to-all-done.home_ref = f32[4,4,128,128]{3,2,1,0:T(8,128)} async-done(((f32[4,4,128,128]{3,2,1,0:T(8,128)}), f32[4,4,128,128]{3,2,1,0:T(8,128)}, u32[]{:S(2)}, u32[]{:S(2)}) %all-to-all-start) | async-done | bytes 1048608 | tf_op jit(solution)/shard_map/all_to_all | solution.py:158
  93.2 3.8 %shard_map.83 = f32[512,512]{1,0:T(8,128)} custom-call(s32[16]{0:T(128)} %bitcast.112, f32[512,512]{1,0:T(8,128)} %fusion.11.direct_ref, f32[4,4,128,128]{3,2,1,0:T(8,128)} %all-to-all-done.home_ref), custom_call_target="tpu_custom_call" | custom-call | tf_op jit(solution)/shard_map/pallas_call | solution.py:100
  (18 shorter events, 0.1 us)
Async XLA Ops:
  0.0 16.3 %copy-start = (f32[8,16,16]{2,1,0:T(8,128)S(1)}, f32[8,16,16]{2,1,0:T(8,128)}, u32[]{:S(2)}) copy-start(f32[8,16,16]{2,1,0:T(8,128)} %param.12) | copy-start | bytes 24580
  0.0 12.1 %copy-start.4 = (s32[4,1]{0,1:T(1,128)S(1)}, s32[4,1]{0,1:T(1,128)}, u32[]{:S(2)}) copy-start(s32[4,1]{0,1:T(1,128)} %param.13) | copy-start | bytes 52
  0.0 13.5 %copy-start.5 = (s32[4,1]{0,1:T(1,128)S(1)}, s32[4,1]{0,1:T(1,128)}, u32[]{:S(2)}) copy-start(s32[4,1]{0,1:T(1,128)} %param.15) | copy-start | bytes 52
  5.2 18.2 %collective-permute-start = (f32[1028,128]{1,0:T(8,128)}, f32[1028,128]{1,0:T(8,128)S(1)}, u32[]{:S(2)}, u32[]{:S(2)}) collective-permute-start(f32[1028,128]{1,0:T(8,128)} %get-tuple-element.10), channel_id=1, source_target_pairs={{0,4},{4,8},{8,12},{12,0},{1,5},{5,9},{9,13},{13,1},{2,6},{6,10},{... | collective-permute-start | bytes 1579016 | tf_op jit(solution)/shard_map/ppermute | solution.py:142
  8.2 37.0 %collective-permute-start.1 = (f32[1028,128]{1,0:T(8,128)}, f32[1028,128]{1,0:T(8,128)S(1)}, u32[]{:S(2)}, u32[]{:S(2)}) collective-permute-start(f32[1028,128]{1,0:T(8,128)} %get-tuple-element.11), channel_id=1, source_target_pairs={{0,8},{4,12},{8,0},{12,4},{1,9},{5,13},{9,1},{13,5},{2,10},{6,14},... | collective-permute-start | bytes 1579016 | tf_op jit(solution)/shard_map/ppermute | solution.py:142
  10.8 34.4 %collective-permute-start.2 = (f32[1028,128]{1,0:T(8,128)}, f32[1028,128]{1,0:T(8,128)S(1)}, u32[]{:S(2)}, u32[]{:S(2)}) collective-permute-start(f32[1028,128]{1,0:T(8,128)} %get-tuple-element.12), channel_id=1, source_target_pairs={{0,12},{4,0},{8,4},{12,8},{1,13},{5,1},{9,5},{13,9},{2,14},{6,2},{... | collective-permute-start | bytes 1579016 | tf_op jit(solution)/shard_map/ppermute | solution.py:142
  53.0 15.2 %copy-start.1 = (f32[1,1,512,512]{3,2,1,0:T(8,128)S(1)}, f32[1,1,512,512]{3,2,1,0:T(8,128)}, u32[]{:S(2)}) copy-start(f32[1,1,512,512]{3,2,1,0:T(8,128)} %param.8) | copy-start | bytes 3145732
  53.0 15.2 %copy-start.2 = (f32[1,1,512,512]{3,2,1,0:T(8,128)S(1)}, f32[1,1,512,512]{3,2,1,0:T(8,128)}, u32[]{:S(2)}) copy-start(f32[1,1,512,512]{3,2,1,0:T(8,128)} %param.9) | copy-start | bytes 3145732
  53.0 15.2 %copy-start.3 = (f32[1,1,512]{2,1,0:T(1,128)S(1)}, f32[1,1,512]{2,1,0:T(1,128)}, u32[]{:S(2)}) copy-start(f32[1,1,512]{2,1,0:T(1,128)} %param.10) | copy-start | bytes 6148
  54.1 39.1 %all-to-all-start = ((f32[4,4,128,128]{3,2,1,0:T(8,128)}), f32[4,4,128,128]{3,2,1,0:T(8,128)}, u32[]{:S(2)}, u32[]{:S(2)}) async-start(f32[4,4,128,128]{3,2,1,0:T(8,128)} %bitcast.90), calls=%async_computation | async-start | bytes 2097152 | tf_op jit(solution)/shard_map/all_to_all | solution.py:158

commit v16 on v6

--- a/solution.py
+++ b/solution.py
@@ -148,11 +148,10 @@
     column_of = (spread_range[None, :] * channels + source[:, None]).reshape(-1)
     mixer_in = mixer[:, column_of]
     cross = tiles_got.reshape(tile_count, 2, TS, TS)
-    generator_mixed = jnp.einsum("ji,ixy->jxy", mixer_in, cross[:, 0], precision=highest)
-    hamilton_mixed = jnp.einsum("ji,ixy->jxy", mixer_in, cross[:, 1], precision=highest)
-    product = bracket(
-        from_tiles(generator_mixed, TS), from_tiles(hamilton_mixed, TS), weights_cross
-    )
+    mixed = from_tiles(jnp.einsum("ji,imxy->mjxy", mixer_in, cross, precision=highest), TS)
+    scaled = mixed * weights_cross[None, None, :]
+    terms = jnp.einsum("kij,kjl->kil", scaled, mixed[::-1], precision=highest)
+    product = terms[0] - terms[1]
     mixer_out = mixer[:, (spread_range[None, :] * channels + dest[:, None]).reshape(-1)]
     back = jnp.einsum("ji,jxy->ixy", mixer_out, to_tiles(product, TS), precision=highest)
     back = back.reshape(channels, spread, TS, TS)

time: 93.6 us -> 94.9 us (1.014)
  local copies, waits for them, and re-layouts: 10.3 us -> 11.9 us
    dot_general x2, matrix products: 2.78 us -> 6.11 us  [the longest x1 4.18 us: body(): terms = jnp.einsum('kij,kjl->kil', scaled, mixed[::-1], precision=highest)]
    dot_general x2 -> x1, matrix products: 3.03 us -> 1.03 us  [bracket(): jnp.matmul(right_matrix * scaled, left_matrix, precision=highest)]
    dot_general x2 -> x1, matrix products: 2.06 us -> 1.02 us  [bracket(): jnp.matmul(left_matrix * scaled, right_matrix, precision=highest)]
    sub x1, local copies, waits for them, and re-layouts: 0.33 us -> 1.31 us  [bracket(): return left_term - right_term]
    unnamed x27 -> x29, local copies, waits for them, and re-layouts: 3.65 us -> 3.65 us
  transfers between devices with their start and end apart: 6 -> 6, of which waited for: 4 -> 4; matrix products, arithmetic and copies ran while one was open for 9% -> 10% of each run, Pallas kernels for 0% -> 0%
where the time goes in v16:
time: 94.9 us; the launch traced here: 94.6 us
  waiting for transfers between devices  54.6 us (58%)
  local copies, waits for them, and re-layouts  11.9 us (13%)
  matrix products  8.72 us (9%)
  Pallas kernels  7.54 us (8%)
  starting transfers between devices  5.88 us (6%)
  other arithmetic  3.14 us (3%)
  between operations  2.89 us (3%)
    ppermute x3, waiting for transfers between devices, body(): got.append(lax.ppermute(sends[shift], 'chan', pairs))  35.4 us
    ppermute x3, waiting for transfers between devices, body(): home.append(lax.ppermute(back[shift], 'chan', pairs))  19.2 us
    dot_general x1, matrix products, body(): terms = jnp.einsum('kij,kjl->kil', scaled, mixed[::-1], precision=highest)  4.18 us
    pallas_call x1, Pallas kernels, build_sends(): pl.pallas_call(kernel, grid_spec=pltpu.PrefetchScalarGridSpec(num_scalar_...  3.79 us
    pallas_call x1, Pallas kernels, finish(): pl.pallas_call(kernel, grid_spec=pltpu.PrefetchScalarGridSpec(num_scalar_...  3.74 us
    unnamed x29, local copies, waits for them, and re-layouts  3.65 us
    ppermute x3, starting transfers between devices, body(): home.append(lax.ppermute(back[shift], 'chan', pairs))  3.52 us
    ppermute x3, starting transfers between devices, body(): got.append(lax.ppermute(sends[shift], 'chan', pairs))  2.36 us
  transfers between devices with their start and end apart: 6, of which 4 were waited for; matrix products, arithmetic and copies ran while one was open for 10% of the time, Pallas kernels for 0%

profile of v16, /device:TPU:28, one launch (start us, length us, event | category | flops | bytes accessed | tf_op | source)
XLA Modules:
  0.0 94.6 jit_solution(13376270332332354034)
XLA Ops:
  0.0 1.4 %copy.26.weight_ref = f32[1,1,3,512]{3,2,1,0:T(4,128)} copy(f32[1,1,3,512]{3,1,2,0:T(1,128)} %param.11) | data formatting | bytes 12288 | tf_op args[3]
  1.5 3.8 %shard_map.82 = (f32[1028,128]{1,0:T(8,128)}, f32[1028,128]{1,0:T(8,128)}, f32[1028,128]{1,0:T(8,128)}, f32[1028,128]{1,0:T(8,128)}) custom-call(s32[16]{0:T(128)} %bitcast.51, s32[4]{0:T(128)} %bitcast.64, f32[512,512]{1,0:T(8,128)} %bitcast.53, f32[512,512]{1,0:T(8,128)} %bitcast.54, f32[1,1,3,512]{3,2,1,0:T(4,128)} %copy.26.weight_ref), custom_call_target="tpu_custom_call" | custom-call | tf_op jit(solution)/shard_map/pallas_call | solution.py:70
  5.3 0.2 collective-permute-start
  5.5 1.7 %collective-permute-start.1 = (f32[1028,128]{1,0:T(8,128)}, f32[1028,128]{1,0:T(8,128)}, u32[]{:S(2)}, u32[]{:S(2)}) collective-permute-start(f32[1028,128]{1,0:T(8,128)} %get-tuple-element.11), channel_id=1, source_target_pairs={{0,8},{4,12},{8,0},{12,4},{1,9},{5,13},{9,1},{13,5},{2,10},{6,14},... | collective-permute-start | bytes 1579016 | tf_op jit(solution)/shard_map/ppermute | solution.py:142
  7.2 0.4 collective-permute-start.2
  7.6 0.6 constant_dynamic-slice_fusion
  9.0 0.6 constant_dynamic-slice_fusion.2
  11.9 0.6 gather_fusion.2
  12.4 0.6 gather_fusion.1
  13.0 1.0 %fusion.6 = f32[512,512]{0,1:T(8,128)S(1)} fusion(f32[1,1,512,512]{3,2,1,0:T(8,128)S(1)} %copy-done.2, f32[512]{0:T(512)S(1)} %bitcast.62, f32[1,1,512,512]{3,2,1,0:T(8,128)S(1)} %copy-done.3), kind=kOutput, calls=%fused_computation.13 | convolution fusion | flops 805568512 | bytes 3147776 | tf_op jit(solution)/shard_map/dot_general | solution.py:34
  14.0 1.0 %convolution_subtract_fusion = f32[512,512]{0,1:T(8,128)S(1)} fusion(f32[512,512]{0,1:T(8,128)S(1)} %fusion.6, f32[1,1,512,512]{3,2,1,0:T(8,128)S(1)} %copy-done.3, f32[512]{0:T(512)S(1)} %bitcast.63, f32[1,1,512,512]{3,2,1,0:T(8,128)S(1)} %copy-done.2), kind=kOutput, calls=%fused_computation.8 | convolution fusion | flops 805830656 | bytes 4196352 | tf_op jit(solution)/shard_map/dot_general | solution.py:35
  15.1 1.3 %copy.24 = f32[512,512]{1,0:T(8,128)} copy(f32[512,512]{0,1:T(8,128)S(1)} %convolution_subtract_fusion) | data formatting | bytes 2097152 | tf_op jit(solution)/shard_map/sub | solution.py:36
  16.6 1.2 %gather_fusion = s32[16]{0:T(128)} fusion(s32[16]{0:T(128)S(1)} %bitcast.52, s32[1024]{0:T(1024)S(1)} %pad_clamp_fusion.2), kind=kCustom, calls=%fused_computation | custom fusion | bytes 192 | tf_op jit(solution)/shard_map/gather | solution.py:162
  17.8 1.9 %collective-permute-done = f32[1028,128]{1,0:T(8,128)} collective-permute-done((f32[1028,128]{1,0:T(8,128)}, f32[1028,128]{1,0:T(8,128)}, u32[]{:S(2)}, u32[]{:S(2)}) %collective-permute-start) | collective-permute-done | bytes 526368 | tf_op jit(solution)/shard_map/ppermute | solution.py:142
  19.7 33.5 %collective-permute-done.1 = f32[1028,128]{1,0:T(8,128)} collective-permute-done((f32[1028,128]{1,0:T(8,128)}, f32[1028,128]{1,0:T(8,128)}, u32[]{:S(2)}, u32[]{:S(2)}) %collective-permute-start.1) | collective-permute-done | bytes 526368 | tf_op jit(solution)/shard_map/ppermute | solution.py:142
  53.2 1.5 %pad_maximum_fusion = f32[4,1028,128]{2,1,0:T(8,128)S(1)} fusion(f32[1,1028,128]{2,1,0:T(8,128)} %bitcast.16, f32[1,1028,128]{2,1,0:T(8,128)} %bitcast.15, f32[1,1028,128]{2,1,0:T(8,128)} %bitcast.14, f32[1,1028,128]{2,1,0:T(8,128)S(1)} %bitcast.61), kind=kLoop, calls=%fused_computation.5 | loop fusion | flops 1579008 | bytes 4210688 | tf_op jit(solution)/shard_map/stack | solution.py:143
  54.9 1.9 %fusion.2 = f32[2,128,128,16]{2,3,1,0:T(8,128)S(1)} fusion(f32[16,2,128,128]{3,2,1,0:T(8,128)S(1)} %bitcast.55, f32[16,16]{1,0:T(8,128)S(1)} %gather_fusion.2), kind=kOutput, calls=%fused_computation.6 | convolution fusion | flops 50331648 | bytes 4195328 | tf_op jit(solution)/shard_map/ji,imxy->mjxy/dot_general | solution.py:151
  56.8 0.4 copy.29
  57.2 1.8 %reshape.170 = f32[2,512,512]{2,1,0:T(8,128)} reshape(f32[2,4,128,4,128]{4,3,2,1,0:T(4,128)S(1)} %copy.29) | data formatting | bytes 4194304 | tf_op jit(solution)/shard_map/reshape | solution.py:29
  59.0 4.2 %fusion = f32[2,512,512]{2,1,0:T(8,128)S(1)} fusion(f32[2,512,512]{2,1,0:T(8,128)} %reshape.170, f32[512]{0:T(512)S(1)} %dynamic-slice_bitcast_fusion), kind=kOutput, calls=%fused_computation.3 | convolution fusion | flops 1611137024 | bytes 4196352 | tf_op jit(solution)/shard_map/kij,kjl->kil/dot_general | solution.py:153
  63.2 0.2 slice_subtract_fusion
  63.4 0.4 sub.36
  64.0 0.6 fusion.14
  64.9 1.4 %collective-permute-start.4 = (f32[4,128,128]{2,1,0:T(8,128)S(1)}, f32[4,128,128]{2,1,0:T(8,128)S(1)}, u32[]{:S(2)}, u32[]{:S(2)}) collective-permute-start(f32[4,128,128]{2,1,0:T(8,128)S(1)} %copy.41), channel_id=1, source_target_pairs={{0,8},{4,12},{8,0},{12,4},{1,9},{5,13},{9,1},{13,5},{2,10},{6,14},... | collective-permute-start | bytes 786440 | tf_op jit(solution)/shard_map/ppermute | solution.py:161
  66.3 2.1 %collective-permute-start.5 = (f32[4,128,128]{2,1,0:T(8,128)S(1)}, f32[4,128,128]{2,1,0:T(8,128)S(1)}, u32[]{:S(2)}, u32[]{:S(2)}) collective-permute-start(f32[4,128,128]{2,1,0:T(8,128)S(1)} %copy.42), channel_id=1, source_target_pairs={{0,12},{4,0},{8,4},{12,8},{1,13},{5,1},{9,5},{13,9},{2,14},{6,2},{... | collective-permute-start | bytes 786440 | tf_op jit(solution)/shard_map/ppermute | solution.py:161
  68.3 1.2 %fusion.4.direct_ref = f32[512,512]{1,0:T(8,128)} fusion(f32[512,512]{1,0:T(8,128)S(1)} %copy-done.4, f32[512,512]{0,1:T(8,128)S(1)} %convolution_subtract_fusion), kind=kLoop, calls=%fused_computation.11 | loop fusion | flops 524288 | bytes 3145728 | tf_op jit(solution)/shard_map/mul | solution.py:165
  69.6 0.7 copy.39.rest_0_
  70.3 1.7 %collective-permute-done.3.rest_1_ = f32[4,128,128]{2,1,0:T(8,128)S(1)} collective-permute-done((f32[4,128,128]{2,1,0:T(8,128)S(1)}, f32[4,128,128]{2,1,0:T(8,128)S(1)}, u32[]{:S(2)}, u32[]{:S(2)}) %collective-permute-start.3) | collective-permute-done | bytes 262176 | tf_op jit(solution)/shard_map/ppermute | solution.py:161
  72.0 17.5 %collective-permute-done.4.rest_2_ = f32[4,128,128]{2,1,0:T(8,128)S(1)} collective-permute-done((f32[4,128,128]{2,1,0:T(8,128)S(1)}, f32[4,128,128]{2,1,0:T(8,128)S(1)}, u32[]{:S(2)}, u32[]{:S(2)}) %collective-permute-start.4) | collective-permute-done | bytes 262176 | tf_op jit(solution)/shard_map/ppermute | solution.py:161
  89.5 0.7 copy-done.7
  90.2 0.7 copy-done.8
  90.9 3.7 %shard_map.83 = f32[512,512]{1,0:T(8,128)} custom-call(s32[16]{0:T(128)} %gather_fusion, f32[512,512]{1,0:T(8,128)} %fusion.4.direct_ref, f32[4,128,128]{2,1,0:T(8,128)} %copy.39.rest_0_, f32[4,128,128]{2,1,0:T(8,128)} %copy-done.6, f32[4,128,128]{2,1,0:T(8,128)} %copy-done.7, f32[4,128,128]{2,1,0:T(8,128)} %copy-done.8), custom_call_target="tpu_custom_call" | custom-call | tf_op jit(solution)/shard_map/pallas_call | solution.py:100
  (48 shorter events, 1.2 us)
Async XLA Ops:
  0.0 11.5 %copy-start = (f32[8,16,16]{2,1,0:T(8,128)S(1)}, f32[8,16,16]{2,1,0:T(8,128)}, u32[]{:S(2)}) copy-start(f32[8,16,16]{2,1,0:T(8,128)} %param.12) | copy-start | bytes 24580
  0.0 7.6 %copy-start.10 = (s32[4,1]{0,1:T(1,128)S(1)}, s32[4,1]{0,1:T(1,128)}, u32[]{:S(2)}) copy-start(s32[4,1]{0,1:T(1,128)} %param.13) | copy-start | bytes 52
  0.0 13.0 %copy-start.3 = (f32[1,1,512,512]{3,2,1,0:T(8,128)S(1)}, f32[1,1,512,512]{3,2,1,0:T(8,128)}, u32[]{:S(2)}) copy-start(f32[1,1,512,512]{3,2,1,0:T(8,128)} %param.9) | copy-start | bytes 3145732
  0.0 13.0 %copy-start.2 = (f32[1,1,512,512]{3,2,1,0:T(8,128)S(1)}, f32[1,1,512,512]{3,2,1,0:T(8,128)}, u32[]{:S(2)}) copy-start(f32[1,1,512,512]{3,2,1,0:T(8,128)} %param.8) | copy-start | bytes 3145732
  0.0 8.9 %copy-start.11 = (s32[4,1]{0,1:T(1,128)S(1)}, s32[4,1]{0,1:T(1,128)}, u32[]{:S(2)}) copy-start(s32[4,1]{0,1:T(1,128)} %param.15) | copy-start | bytes 52
  0.0 13.0 %copy-start.9 = (f32[1,1,512]{2,1,0:T(1,128)S(1)}, f32[1,1,512]{2,1,0:T(1,128)}, u32[]{:S(2)}) copy-start(f32[1,1,512]{2,1,0:T(1,128)} %param.10) | copy-start | bytes 6148
  5.3 14.5 %collective-permute-start = (f32[1028,128]{1,0:T(8,128)}, f32[1028,128]{1,0:T(8,128)}, u32[]{:S(2)}, u32[]{:S(2)}) collective-permute-start(f32[1028,128]{1,0:T(8,128)} %get-tuple-element.10), channel_id=1, source_target_pairs={{0,4},{4,8},{8,12},{12,0},{1,5},{5,9},{9,13},{13,1},{2,6},{6,10},{... | collective-permute-start | bytes 1579016 | tf_op jit(solution)/shard_map/ppermute | solution.py:142
  5.5 47.7 %collective-permute-start.1 = (f32[1028,128]{1,0:T(8,128)}, f32[1028,128]{1,0:T(8,128)}, u32[]{:S(2)}, u32[]{:S(2)}) collective-permute-start(f32[1028,128]{1,0:T(8,128)} %get-tuple-element.11), channel_id=1, source_target_pairs={{0,8},{4,12},{8,0},{12,4},{1,9},{5,13},{9,1},{13,5},{2,10},{6,14},... | collective-permute-start | bytes 1579016 | tf_op jit(solution)/shard_map/ppermute | solution.py:142
  7.2 46.0 %collective-permute-start.2 = (f32[1028,128]{1,0:T(8,128)}, f32[1028,128]{1,0:T(8,128)}, u32[]{:S(2)}, u32[]{:S(2)}) collective-permute-start(f32[1028,128]{1,0:T(8,128)} %get-tuple-element.12), channel_id=1, source_target_pairs={{0,12},{4,0},{8,4},{12,8},{1,13},{5,1},{9,5},{13,9},{2,14},{6,2},{... | collective-permute-start | bytes 1579016 | tf_op jit(solution)/shard_map/ppermute | solution.py:142
  15.1 1.5 %copy-start.1 = (s32[1,1,16]{2,1,0:T(1,128)S(1)}, s32[1,1,16]{2,1,0:T(1,128)}, u32[]{:S(2)}) copy-start(s32[1,1,16]{2,1,0:T(1,128)} %param.14) | copy-start | bytes 196
  15.1 38.1 %copy-start.5 = (f32[1028,128]{1,0:T(8,128)S(1)}, f32[1028,128]{1,0:T(8,128)}, u32[]{:S(2)}) copy-start(f32[1028,128]{1,0:T(8,128)} %get-tuple-element.9) | copy-start | bytes 1579012
  64.6 3.8 %copy-start.4 = (f32[512,512]{1,0:T(8,128)S(1)}, f32[512,512]{1,0:T(8,128)}, u32[]{:S(2)}) copy-start(f32[512,512]{1,0:T(8,128)} %copy.24) | copy-start | bytes 3145732
  64.8 7.2 %collective-permute-start.3 = (f32[4,128,128]{2,1,0:T(8,128)S(1)}, f32[4,128,128]{2,1,0:T(8,128)S(1)}, u32[]{:S(2)}, u32[]{:S(2)}) collective-permute-start(f32[4,128,128]{2,1,0:T(8,128)S(1)} %copy.40), channel_id=1, source_target_pairs={{0,4},{4,8},{8,12},{12,0},{1,5},{5,9},{9,13},{13,1},{2,6},{6,10},{... | collective-permute-start | bytes 786440 | tf_op jit(solution)/shard_map/ppermute | solution.py:161
  64.9 24.6 %collective-permute-start.4 = (f32[4,128,128]{2,1,0:T(8,128)S(1)}, f32[4,128,128]{2,1,0:T(8,128)S(1)}, u32[]{:S(2)}, u32[]{:S(2)}) collective-permute-start(f32[4,128,128]{2,1,0:T(8,128)S(1)} %copy.41), channel_id=1, source_target_pairs={{0,8},{4,12},{8,0},{12,4},{1,9},{5,13},{9,1},{13,5},{2,10},{6,14},... | collective-permute-start | bytes 786440 | tf_op jit(solution)/shard_map/ppermute | solution.py:161
  66.3 23.2 %collective-permute-start.5 = (f32[4,128,128]{2,1,0:T(8,128)S(1)}, f32[4,128,128]{2,1,0:T(8,128)S(1)}, u32[]{:S(2)}, u32[]{:S(2)}) collective-permute-start(f32[4,128,128]{2,1,0:T(8,128)S(1)} %copy.42), channel_id=1, source_target_pairs={{0,12},{4,0},{8,4},{12,8},{1,13},{5,1},{9,5},{13,9},{2,14},{6,2},{... | collective-permute-start | bytes 786440 | tf_op jit(solution)/shard_map/ppermute | solution.py:161
  72.0 17.5 %copy-start.6 = (f32[4,128,128]{2,1,0:T(8,128)}, f32[4,128,128]{2,1,0:T(8,128)S(1)}, u32[]{:S(2)}) copy-start(f32[4,128,128]{2,1,0:T(8,128)S(1)} %collective-permute-done.3.rest_1_) | copy-start | bytes 786436
  89.5 0.7 copy-start.7
  90.2 0.7 copy-start.8

commit v17 on v6

--- a/solution.py
+++ b/solution.py
@@ -153,13 +153,13 @@
     product = bracket(
         from_tiles(generator_mixed, TS), from_tiles(hamilton_mixed, TS), weights_cross
     )
-    mixer_out = mixer[:, (spread_range[None, :] * channels + dest[:, None]).reshape(-1)]
-    back = jnp.einsum("ji,jxy->ixy", mixer_out, to_tiles(product, TS), precision=highest)
-    back = back.reshape(channels, spread, TS, TS)
-    home = [back[0]]
+    back = jnp.einsum("ji,jxy->ixy", mixer, to_tiles(product, TS), precision=highest)
+    back = jnp.swapaxes(back.reshape(spread, channels, TS, TS), 0, 1)
+    home = [lax.dynamic_index_in_dim(back, dest[0], 0, keepdims=False)]
     for shift in range(1, channels):
         pairs = [(c, (c + shift) % channels) for c in range(channels)]
-        home.append(lax.ppermute(back[shift], "chan", pairs))
+        piece = lax.dynamic_index_in_dim(back, dest[shift], 0, keepdims=False)
+        home.append(lax.ppermute(piece, "chan", pairs))
     place = order[(source[:, None] * spread + spread_range[None, :]).reshape(-1)]
 
     direct = bracket(generator[0, 0], hamiltonian[0, 0], pair_weights[0, 0])

time: 93.6 us -> 95 us (1.015)
  between operations: 2.78 us -> 10.3 us
  waiting for transfers between devices: 55.5 us -> 48.8 us
    ppermute x3, waiting for transfers between devices: 36.3 us -> 28.7 us  [body(): got.append(lax.ppermute(sends[shift], 'chan', pairs))]
    another operation x0 -> x1, local copies, waits for them, and re-layouts: none -> 1.67 us
    unnamed x27 -> x23, local copies, waits for them, and re-layouts: 3.65 us -> 2.29 us
  transfers between devices with their start and end apart: 6 -> 6, of which waited for: 4 -> 3; matrix products, arithmetic and copies ran while one was open for 9% -> 8% of each run, Pallas kernels for 0% -> 0%
where the time goes in v17:
time: 95 us; the launch traced here: 94.3 us
  waiting for transfers between devices  48.8 us (51%)
  local copies, waits for them, and re-layouts  10.4 us (11%)
  between operations  10.3 us (11%)
  matrix products  8.66 us (9%)
  Pallas kernels  7.55 us (8%)
  starting transfers between devices  5.72 us (6%)
  other arithmetic  2.92 us (3%)
    ppermute x3, waiting for transfers between devices, body(): got.append(lax.ppermute(sends[shift], 'chan', pairs))  28.7 us
    ppermute x3, waiting for transfers between devices, body(): home.append(lax.ppermute(piece, 'chan', pairs))  20.1 us
    pallas_call x1, Pallas kernels, build_sends(): pl.pallas_call(kernel, grid_spec=pltpu.PrefetchScalarGridSpec(num_scalar_...  3.8 us
    pallas_call x1, Pallas kernels, finish(): pl.pallas_call(kernel, grid_spec=pltpu.PrefetchScalarGridSpec(num_scalar_...  3.75 us
    ppermute x3, starting transfers between devices, body(): home.append(lax.ppermute(piece, 'chan', pairs))  3.36 us
    dot_general x2, matrix products, bracket(): jnp.matmul(right_matrix * scaled, left_matrix, precision=highest)  3.08 us
    ppermute x3, starting transfers between devices, body(): got.append(lax.ppermute(sends[shift], 'chan', pairs))  2.36 us
    unnamed x23, local copies, waits for them, and re-layouts  2.29 us
  transfers between devices with their start and end apart: 6, of which 3 were waited for; matrix products, arithmetic and copies ran while one was open for 8% of the time, Pallas kernels for 0%

profile of v17, /device:TPU:28, one launch (start us, length us, event | category | flops | bytes accessed | tf_op | source)
XLA Modules:
  0.0 94.3 jit_solution(1654328764878769878)
XLA Ops:
  0.0 1.4 %copy.24.weight_ref = f32[1,1,3,512]{3,2,1,0:T(4,128)} copy(f32[1,1,3,512]{3,1,2,0:T(1,128)} %param.11) | data formatting | bytes 12288 | tf_op args[3]
  1.5 3.8 %shard_map.82 = (f32[1028,128]{1,0:T(8,128)}, f32[1028,128]{1,0:T(8,128)}, f32[1028,128]{1,0:T(8,128)}, f32[1028,128]{1,0:T(8,128)}) custom-call(s32[16]{0:T(128)} %bitcast.98, s32[4]{0:T(128)} %bitcast.121, f32[512,512]{1,0:T(8,128)} %bitcast.101, f32[512,512]{1,0:T(8,128)} %bitcast.102, f32[1,1,3,512]{3,2,1,0:T(4,128)} %copy.24.weight_ref), custom_call_target="tpu_custom_call" | custom-call | tf_op jit(solution)/shard_map/pallas_call | solution.py:70
  5.3 0.2 collective-permute-start
  5.5 1.7 %collective-permute-start.1 = (f32[1028,128]{1,0:T(8,128)}, f32[1028,128]{1,0:T(8,128)}, u32[]{:S(2)}, u32[]{:S(2)}) collective-permute-start(f32[1028,128]{1,0:T(8,128)} %get-tuple-element.11), channel_id=1, source_target_pairs={{0,8},{4,12},{8,0},{12,4},{1,9},{5,13},{9,1},{13,5},{2,10},{6,14},... | collective-permute-start | bytes 1579016 | tf_op jit(solution)/shard_map/ppermute | solution.py:142
  7.2 0.4 collective-permute-start.2
  7.7 0.6 constant_dynamic-slice_fusion.4
  9.0 0.7 fusion.26
  14.7 0.6 constant_dynamic-slice_fusion.6
  17.5 0.6 gather_fusion.1
  18.1 1.0 %fusion.13 = f32[512,512]{0,1:T(8,128)S(1)} fusion(f32[1,1,512,512]{3,2,1,0:T(8,128)S(1)} %copy-done.2, f32[512]{0:T(512)S(1)} %bitcast.119, f32[1,1,512,512]{3,2,1,0:T(8,128)S(1)} %copy-done.3), kind=kOutput, calls=%fused_computation.23 | convolution fusion | flops 805568512 | bytes 3147776 | tf_op jit(solution)/shard_map/dot_general | solution.py:34
  19.2 1.1 %convolution_subtract_fusion.1 = f32[512,512]{0,1:T(8,128)S(1)} fusion(f32[512,512]{0,1:T(8,128)S(1)} %fusion.13, f32[1,1,512,512]{3,2,1,0:T(8,128)S(1)} %copy-done.3, f32[512]{0:T(512)S(1)} %bitcast.120, f32[1,1,512,512]{3,2,1,0:T(8,128)S(1)} %copy-done.2), kind=kOutput, calls=%fused_computation.4 | convolution fusion | flops 805830656 | bytes 4196352 | tf_op jit(solution)/shard_map/dot_general | solution.py:35
  20.3 0.3 copy.21
  20.8 1.2 %gather_fusion = s32[16]{0:T(128)} fusion(s32[16]{0:T(128)S(1)} %bitcast.99, s32[1024]{0:T(1024)S(1)} %pad_clamp_fusion.1), kind=kCustom, calls=%fused_computation | custom fusion | bytes 192 | tf_op jit(solution)/shard_map/gather | solution.py:163
  24.5 28.7 %collective-permute-done.1 = f32[1028,128]{1,0:T(8,128)} collective-permute-done((f32[1028,128]{1,0:T(8,128)}, f32[1028,128]{1,0:T(8,128)}, u32[]{:S(2)}, u32[]{:S(2)}) %collective-permute-start.1) | collective-permute-done | bytes 526368 | tf_op jit(solution)/shard_map/ppermute | solution.py:142
  53.2 1.5 %pad_maximum_fusion = f32[4,1028,128]{2,1,0:T(8,128)S(1)} fusion(f32[1,1028,128]{2,1,0:T(8,128)} %bitcast.23, f32[1,1028,128]{2,1,0:T(8,128)} %bitcast.22, f32[1,1028,128]{2,1,0:T(8,128)} %bitcast.21, f32[1,1028,128]{2,1,0:T(8,128)S(1)} %bitcast.112), kind=kLoop, calls=%fused_computation.2 | loop fusion | flops 1579008 | bytes 4210688 | tf_op jit(solution)/shard_map/stack | solution.py:143
  54.7 0.1 slice.32
  54.9 0.2 fusion.25
  55.1 1.2 %fusion.10 = f32[4,4,128,128]{3,1,2,0:T(4,128)S(1)} fusion(f32[4,4,16,1]{2,1,3,0:T(4,128)S(1)} %bitcast.116, f32[16,1,128,128]{3,2,1,0:T(8,128)S(1)} %get-tuple-element.13), kind=kOutput, calls=%fused_computation.17 | convolution fusion | flops 25165824 | bytes 2098176 | tf_op jit(solution)/shard_map/ji,ixy->jxy/dot_general | solution.py:151
  56.3 1.5 %bitcast_multiply_fusion = (f32[4,128,4,128]{3,2,1,0:T(4,128)S(1)}, f32[4,128,4,128]{3,2,1,0:T(4,128)S(1)}, f32[4,4,128,128]{3,1,2,0:T(4,128)S(1)}) fusion(f32[4,128]{1,0:T(4,128)S(1)} %dynamic-slice_bitcast_fusion, f32[4,4,128,128]{3,1,2,0:T(4,128)S(1)} %fusion.10, f32[4,4,16,1]{2,1,3,0:T(4,128)S(1)} %bitcast.117, ...), kind=kOutput, calls=%fused_computation.18 | convolution fusion | flops 25690112 | bytes 5245952 | tf_op jit(solution)/shard_map/ji,ixy->jxy/dot_general | solution.py:152
  57.9 1.0 %fusion.4 = f32[512,512]{1,0:T(8,128)S(1)} fusion(f32[64,8,4,128]{3,2,1,0:T(4,128)S(1)} %bitcast.105, f32[64,8,4,128]{3,2,1,0:T(4,128)S(1)} %bitcast.104), kind=kOutput, calls=%fused_computation.9 | convolution fusion | flops 805306368 | bytes 3145728 | tf_op jit(solution)/shard_map/dot_general | solution.py:34
  58.9 2.0 %convolution_subtract_fusion = f32[512,512]{1,0:T(8,128)} fusion(f32[512,512]{1,0:T(8,128)S(1)} %fusion.4, f32[64,8,4,128]{3,2,1,0:T(4,128)S(1)} %bitcast.100, f32[64,8,4,128]{3,2,1,0:T(4,128)S(1)} %bitcast.106), kind=kOutput, calls=%fused_computation.3 | convolution fusion | flops 805568512 | bytes 4194304 | tf_op jit(solution)/shard_map/dot_general | solution.py:35
  60.9 1.6 %reshape.142 = f32[4,128,4,128]{3,2,1,0:T(4,128)S(1)} reshape(f32[512,512]{1,0:T(8,128)} %convolution_subtract_fusion) | data formatting | bytes 2097152 | tf_op jit(solution)/shard_map/reshape | solution.py:19
  62.5 0.2 copy.27
  62.7 0.7 fusion.27
  63.4 1.7 %constant_dynamic-slice_fusion = (f32[4,1,128,128]{3,1,2,0:T(1,128)S(1)}, f32[4,1,128,128]{3,1,2,0:T(1,128)S(1)}, f32[4,1,128,128]{3,1,2,0:T(1,128)S(1)}, f32[4,1,128,128]{3,1,2,0:T(1,128)}) fusion(f32[4,4,128,128]{3,1,2,0:T(4,128)S(1)} %fusion.27, s32[]{:T(128)S(6)} %select_n.78, s32[]{:T(128)S(6)} %select_n.77, s32[]{:T(128)S(6)} %select_n.76, s32[]{:T(128)S(6)} %select_n.75), kind=kLoop, calls=%fused_computation.39 | loop fusion | bytes 2097168 | tf_op jit(solution)/shard_map/dynamic-slice.4
  65.1 1.3 %collective-permute-start.4 = (f32[4,128,128]{2,1,0:T(8,128)S(1)}, f32[4,128,128]{2,1,0:T(8,128)S(1)}, u32[]{:S(2)}, u32[]{:S(2)}) collective-permute-start(f32[4,128,128]{2,1,0:T(8,128)S(1)} %bitcast.114), channel_id=1, source_target_pairs={{0,8},{4,12},{8,0},{12,4},{1,9},{5,13},{9,1},{13,5},{2,10},{6,14},... | collective-permute-start | bytes 786440 | tf_op jit(solution)/shard_map/ppermute | solution.py:162
  66.4 2.0 %collective-permute-start.5 = (f32[4,128,128]{2,1,0:T(8,128)S(1)}, f32[4,128,128]{2,1,0:T(8,128)S(1)}, u32[]{:S(2)}, u32[]{:S(2)}) collective-permute-start(f32[4,128,128]{2,1,0:T(8,128)S(1)} %bitcast.113), channel_id=1, source_target_pairs={{0,12},{4,0},{8,4},{12,8},{1,13},{5,1},{9,5},{13,9},{2,14},{6,2},{... | collective-permute-start | bytes 786440 | tf_op jit(solution)/shard_map/ppermute | solution.py:162
  68.4 1.2 %fusion.11.direct_ref = f32[512,512]{1,0:T(8,128)} fusion(f32[512,512]{1,0:T(8,128)S(1)} %copy.21, f32[512,512]{0,1:T(8,128)S(1)} %convolution_subtract_fusion.1), kind=kLoop, calls=%fused_computation.21 | loop fusion | flops 524288 | bytes 3145728 | tf_op jit(solution)/shard_map/mul | solution.py:166
  69.6 2.6 %collective-permute-done.3.rest_1_ = f32[4,128,128]{2,1,0:T(8,128)S(1)} collective-permute-done((f32[4,128,128]{2,1,0:T(8,128)S(1)}, f32[4,128,128]{2,1,0:T(8,128)S(1)}, u32[]{:S(2)}, u32[]{:S(2)}) %collective-permute-start.3) | collective-permute-done | bytes 262176 | tf_op jit(solution)/shard_map/ppermute | solution.py:162
  72.2 17.5 %collective-permute-done.4.rest_2_ = f32[4,128,128]{2,1,0:T(8,128)S(1)} collective-permute-done((f32[4,128,128]{2,1,0:T(8,128)S(1)}, f32[4,128,128]{2,1,0:T(8,128)S(1)}, u32[]{:S(2)}, u32[]{:S(2)}) %collective-permute-start.4) | collective-permute-done | bytes 262176 | tf_op jit(solution)/shard_map/ppermute | solution.py:162
  89.7 0.7 copy-done.6
  90.5 3.7 %shard_map.83 = f32[512,512]{1,0:T(8,128)} custom-call(s32[16]{0:T(128)} %gather_fusion, f32[512,512]{1,0:T(8,128)} %fusion.11.direct_ref, f32[4,128,128]{2,1,0:T(8,128)} %bitcast.109, f32[4,128,128]{2,1,0:T(8,128)} %copy-done.5, f32[4,128,128]{2,1,0:T(8,128)} %copy-done.6, f32[4,128,128]{2,1,0:T(8,128)} %copy-done.7), custom_call_target="tpu_custom_call" | custom-call | tf_op jit(solution)/shard_map/pallas_call | solution.py:100
  (40 shorter events, 0.7 us)
Async XLA Ops:
  0.0 17.2 %copy-start = (f32[8,16,16]{2,1,0:T(8,128)S(1)}, f32[8,16,16]{2,1,0:T(8,128)}, u32[]{:S(2)}) copy-start(f32[8,16,16]{2,1,0:T(8,128)} %param.12) | copy-start | bytes 24580
  0.0 7.6 %copy-start.9 = (s32[4,1]{0,1:T(1,128)S(1)}, s32[4,1]{0,1:T(1,128)}, u32[]{:S(2)}) copy-start(s32[4,1]{0,1:T(1,128)} %param.13) | copy-start | bytes 52
  0.0 18.1 %copy-start.3 = (f32[1,1,512,512]{3,2,1,0:T(8,128)S(1)}, f32[1,1,512,512]{3,2,1,0:T(8,128)}, u32[]{:S(2)}) copy-start(f32[1,1,512,512]{3,2,1,0:T(8,128)} %param.9) | copy-start | bytes 3145732
  0.0 18.1 %copy-start.2 = (f32[1,1,512,512]{3,2,1,0:T(8,128)S(1)}, f32[1,1,512,512]{3,2,1,0:T(8,128)}, u32[]{:S(2)}) copy-start(f32[1,1,512,512]{3,2,1,0:T(8,128)} %param.8) | copy-start | bytes 3145732
  0.0 14.6 %copy-start.10 = (s32[4,1]{0,1:T(1,128)S(1)}, s32[4,1]{0,1:T(1,128)}, u32[]{:S(2)}) copy-start(s32[4,1]{0,1:T(1,128)} %param.15) | copy-start | bytes 52
  0.0 18.1 %copy-start.8 = (f32[1,1,512]{2,1,0:T(1,128)S(1)}, f32[1,1,512]{2,1,0:T(1,128)}, u32[]{:S(2)}) copy-start(f32[1,1,512]{2,1,0:T(1,128)} %param.10) | copy-start | bytes 6148
  5.3 19.2 %collective-permute-start = (f32[1028,128]{1,0:T(8,128)}, f32[1028,128]{1,0:T(8,128)}, u32[]{:S(2)}, u32[]{:S(2)}) collective-permute-start(f32[1028,128]{1,0:T(8,128)} %get-tuple-element.10), channel_id=1, source_target_pairs={{0,4},{4,8},{8,12},{12,0},{1,5},{5,9},{9,13},{13,1},{2,6},{6,10},{... | collective-permute-start | bytes 1579016 | tf_op jit(solution)/shard_map/ppermute | solution.py:142
  5.5 47.7 %collective-permute-start.1 = (f32[1028,128]{1,0:T(8,128)}, f32[1028,128]{1,0:T(8,128)}, u32[]{:S(2)}, u32[]{:S(2)}) collective-permute-start(f32[1028,128]{1,0:T(8,128)} %get-tuple-element.11), channel_id=1, source_target_pairs={{0,8},{4,12},{8,0},{12,4},{1,9},{5,13},{9,1},{13,5},{2,10},{6,14},... | collective-permute-start | bytes 1579016 | tf_op jit(solution)/shard_map/ppermute | solution.py:142
  7.2 46.0 %collective-permute-start.2 = (f32[1028,128]{1,0:T(8,128)}, f32[1028,128]{1,0:T(8,128)}, u32[]{:S(2)}, u32[]{:S(2)}) collective-permute-start(f32[1028,128]{1,0:T(8,128)} %get-tuple-element.12), channel_id=1, source_target_pairs={{0,12},{4,0},{8,4},{12,8},{1,13},{5,1},{9,5},{13,9},{2,14},{6,2},{... | collective-permute-start | bytes 1579016 | tf_op jit(solution)/shard_map/ppermute | solution.py:142
  19.2 1.6 %copy-start.1 = (s32[1,1,16]{2,1,0:T(1,128)S(1)}, s32[1,1,16]{2,1,0:T(1,128)}, u32[]{:S(2)}) copy-start(s32[1,1,16]{2,1,0:T(1,128)} %param.14) | copy-start | bytes 196
  20.3 33.0 %copy-start.4 = (f32[1028,128]{1,0:T(8,128)S(1)}, f32[1028,128]{1,0:T(8,128)}, u32[]{:S(2)}) copy-start(f32[1028,128]{1,0:T(8,128)} %get-tuple-element.9) | copy-start | bytes 1579012
  65.1 7.2 %collective-permute-start.3 = (f32[4,128,128]{2,1,0:T(8,128)S(1)}, f32[4,128,128]{2,1,0:T(8,128)S(1)}, u32[]{:S(2)}, u32[]{:S(2)}) collective-permute-start(f32[4,128,128]{2,1,0:T(8,128)S(1)} %bitcast.115), channel_id=1, source_target_pairs={{0,4},{4,8},{8,12},{12,0},{1,5},{5,9},{9,13},{13,1},{2,6},{6,10},{... | collective-permute-start | bytes 786440 | tf_op jit(solution)/shard_map/ppermute | solution.py:162
  65.1 24.7 %collective-permute-start.4 = (f32[4,128,128]{2,1,0:T(8,128)S(1)}, f32[4,128,128]{2,1,0:T(8,128)S(1)}, u32[]{:S(2)}, u32[]{:S(2)}) collective-permute-start(f32[4,128,128]{2,1,0:T(8,128)S(1)} %bitcast.114), channel_id=1, source_target_pairs={{0,8},{4,12},{8,0},{12,4},{1,9},{5,13},{9,1},{13,5},{2,10},{6,14},... | collective-permute-start | bytes 786440 | tf_op jit(solution)/shard_map/ppermute | solution.py:162
  66.4 23.3 %collective-permute-start.5 = (f32[4,128,128]{2,1,0:T(8,128)S(1)}, f32[4,128,128]{2,1,0:T(8,128)S(1)}, u32[]{:S(2)}, u32[]{:S(2)}) collective-permute-start(f32[4,128,128]{2,1,0:T(8,128)S(1)} %bitcast.113), channel_id=1, source_target_pairs={{0,12},{4,0},{8,4},{12,8},{1,13},{5,1},{9,5},{13,9},{2,14},{6,2},{... | collective-permute-start | bytes 786440 | tf_op jit(solution)/shard_map/ppermute | solution.py:162
  72.2 17.5 %copy-start.5 = (f32[4,128,128]{2,1,0:T(8,128)}, f32[4,128,128]{2,1,0:T(8,128)S(1)}, u32[]{:S(2)}) copy-start(f32[4,128,128]{2,1,0:T(8,128)S(1)} %collective-permute-done.3.rest_1_) | copy-start | bytes 786436
  89.7 0.7 copy-start.6
  89.7 0.8 copy-start.7

commit v18 on v6

--- a/solution.py
+++ b/solution.py
@@ -42,8 +42,9 @@
     rows = 2 * spread * TS + length // TS
 
     def kernel(order_ref, owner_ref, gen_ref, ham_ref, weight_ref, *outs):
+        outs = (None,) + outs
         me = lax.axis_index("chan")
-        for s in range(channels):
+        for s in range(1, channels):
             g = (me + s) % channels
             for r in range(spread):
                 tile = order_ref[g * spread + r]
@@ -73,9 +74,9 @@
             num_scalar_prefetch=2,
             grid=(1,),
             in_specs=[whole] * 3,
-            out_specs=[whole] * channels,
+            out_specs=[whole] * (channels - 1),
         ),
-        out_shape=[jax.ShapeDtypeStruct((rows, TS), jnp.float32)] * channels,
+        out_shape=[jax.ShapeDtypeStruct((rows, TS), jnp.float32)] * (channels - 1),
     )(order, owners, generator, hamiltonian, cross_weights)
 
 
@@ -136,10 +137,17 @@
     sends = build_sends(
         order, owners, generator[0, 0], hamiltonian[0, 0], cross_weights, channels, spread
     )
-    got = [sends[0]]
+    got = [None]
     for shift in range(1, channels):
         pairs = [(c, (c + shift) % channels) for c in range(channels)]
-        got.append(lax.ppermute(sends[shift], "chan", pairs))
+        got.append(lax.ppermute(sends[shift - 1], "chan", pairs))
+    earlier = chan_range < me
+    slot = jnp.minimum(jnp.sum(earlier & (owners == owners[me])), capacity - 1)
+    picked = order[me * spread + spread_range]
+    local = jnp.stack(
+        [to_tiles(generator[0, 0], TS)[picked], to_tiles(hamiltonian[0, 0], TS)[picked]], axis=1
+    ).reshape(2 * spread * TS, TS)
+    got[0] = jnp.concatenate([local, cross_weights[0, 0][slot].reshape(-1, TS)], axis=0)
     got = jnp.stack(got)
     tiles_got = got[:, : 2 * spread * TS].reshape(channels, spread, 2, TS, TS)
     weights_cross = got[(me - owners[me]) % channels, 2 * spread * TS :].reshape(-1)

time: 93.6 us -> 91.3 us (0.975)
  waiting for transfers between devices: 55.5 us -> 41.6 us
  local copies, waits for them, and re-layouts: 10.3 us -> 20.6 us
  other arithmetic: 2.94 us -> 4.32 us
  matrix products: 8.43 us -> 7.49 us
    ppermute x3, waiting for transfers between devices: 36.3 us -> 22.4 us  [body(): got.append(lax.ppermute(sends[shift - 1], 'chan', pairs))]
    gather x0 -> x3, local copies, waits for them, and re-layouts: none -> 4.91 us  [the longest x1 2.48 us: body(): to_tiles(hamiltonian[0, 0], TS)[picked]]
    transpose x1 -> x3, local copies, waits for them, and re-layouts: 0.18 us -> 3.62 us  [to_tiles(): shaped = jnp.swapaxes(shaped, -3, -2)]
    another operation x0 -> x3, local copies, waits for them, and re-layouts: none -> 1.7 us  [the longest x2 1.67 us: to_tiles(): shaped = matrix.reshape(leading + (blocks, tile_size, blocks, tile_size))]
    reduce_sum x0 -> x1, other arithmetic: none -> 1.28 us  [body(): slot = jnp.minimum(jnp.sum(earlier & (owners == owners[me])), capacity - 1)]
    reshape x1, local copies, waits for them, and re-layouts: 1.56 us -> 0.36 us  [to_tiles(): shaped = matrix.reshape(leading + (blocks, tile_size, blocks, tile_size))]
    sub x1, local copies, waits for them, and re-layouts: 0.33 us -> 1.31 us  [bracket(): return left_term - right_term]
    dot_general x2, matrix products: 3.03 us -> 2.08 us  [bracket(): jnp.matmul(right_matrix * scaled, left_matrix, precision=highest)]
  transfers between devices with their start and end apart: 6 -> 6, of which waited for: 4 -> 3; matrix products, arithmetic and copies ran while one was open for 9% -> 24% of each run, Pallas kernels for 0% -> 0%
where the time goes in v18:
time: 91.3 us; the launch traced here: 90.9 us
  waiting for transfers between devices  41.6 us (46%)
  local copies, waits for them, and re-layouts  20.6 us (23%)
  matrix products  7.49 us (8%)
  Pallas kernels  7.46 us (8%)
  starting transfers between devices  5.88 us (6%)
  other arithmetic  4.32 us (5%)
  between operations  3.53 us (4%)
    ppermute x3, waiting for transfers between devices, body(): got.append(lax.ppermute(sends[shift - 1], 'chan', pairs))  22.4 us
    ppermute x3, waiting for transfers between devices, body(): home.append(lax.ppermute(back[shift], 'chan', pairs))  19.2 us
    pallas_call x1, Pallas kernels, finish(): pl.pallas_call(kernel, grid_spec=pltpu.PrefetchScalarGridSpec(num_scalar_...  3.75 us
    pallas_call x1, Pallas kernels, build_sends(): pl.pallas_call(kernel, grid_spec=pltpu.PrefetchScalarGridSpec(num_scalar_...  3.71 us
    transpose x3, local copies, waits for them, and re-layouts, to_tiles(): shaped = jnp.swapaxes(shaped, -3, -2)  3.62 us
    unnamed x29, local copies, waits for them, and re-layouts  3.59 us
    ppermute x3, starting transfers between devices, body(): home.append(lax.ppermute(back[shift], 'chan', pairs))  3.52 us
    gather x1, local copies, waits for them, and re-layouts, body(): to_tiles(hamiltonian[0, 0], TS)[picked]  2.48 us
  transfers between devices with their start and end apart: 6, of which 3 were waited for; matrix products, arithmetic and copies ran while one was open for 24% of the time, Pallas kernels for 0%

profile of v18, /device:TPU:28, one launch (start us, length us, event | category | flops | bytes accessed | tf_op | source)
XLA Modules:
  0.0 90.9 jit_solution(10159701639830030271)
XLA Ops:
  0.0 1.4 %copy.45.weight_ref = f32[1,1,3,512]{3,2,1,0:T(4,128)} copy(f32[1,1,3,512]{3,1,2,0:T(1,128)} %param.11) | data formatting | bytes 12288 | tf_op args[3]
  1.4 3.7 %shard_map.82 = (f32[1028,128]{1,0:T(8,128)}, f32[1028,128]{1,0:T(8,128)}, f32[1028,128]{1,0:T(8,128)}) custom-call(s32[16]{0:T(128)} %bitcast.104, s32[4]{0:T(128)} %bitcast.131, f32[512,512]{1,0:T(8,128)} %bitcast.107, f32[512,512]{1,0:T(8,128)} %bitcast.108, f32[1,1,3,512]{3,2,1,0:T(4,128)} %copy.45.weight_ref), custom_call_target="tpu_custom_call" | custom-call | tf_op jit(solution)/shard_map/pallas_call | solution.py:71
  5.3 1.7 %collective-permute-start.1 = (f32[1028,128]{1,0:T(8,128)}, f32[1028,128]{1,0:T(8,128)}, u32[]{:S(2)}, u32[]{:S(2)}) collective-permute-start(f32[1028,128]{1,0:T(8,128)} %get-tuple-element.9), channel_id=1, source_target_pairs={{0,8},{4,12},{8,0},{12,4},{1,9},{5,13},{9,1},{13,5},{2,10},{6,14},... | collective-permute-start | bytes 1579016 | tf_op jit(solution)/shard_map/ppermute | solution.py:143
  7.5 1.3 %reshape_squeeze.9 = f32[4,128,4,128]{3,2,1,0:T(4,128)} reshape(f32[1,1,512,512]{3,2,1,0:T(8,128)S(1)} %copy-done.2) | data formatting | bytes 2097152 | tf_op jit(solution)/shard_map/reshape;squeeze | solution.py:19
  9.2 0.7 constant_dynamic-slice_fusion.1
  9.9 1.3 %fusion.28 = s32[]{:T(128)} fusion(s32[]{:T(128)} %bitcast.28, s32[]{:T(128)S(6)} %axis_index.15, s32[4,1]{0,1:T(1,128)S(1)} %copy-done.10), kind=kLoop, calls=%fused_computation.69 | loop fusion | flops 19 | bytes 28 | tf_op jit(solution)/shard_map/reduce_sum | solution.py:145
  11.2 0.6 gather_fusion.3
  11.8 2.3 %copy.42 = f32[4,4,128,128]{3,2,1,0:T(8,128)} copy(f32[4,4,128,128]{3,1,2,0:T(4,128)} %bitcast.114) | data formatting | bytes 2097152 | tf_op jit(solution)/shard_map/transpose | solution.py:20
  14.2 1.1 %copy.43 = f32[4,4,128,128]{3,2,1,0:T(8,128)} copy(f32[4,4,128,128]{3,1,2,0:T(4,128)S(1)} %bitcast.113) | data formatting | bytes 2097152 | tf_op jit(solution)/shard_map/transpose | solution.py:20
  15.3 1.8 %gather_fusion.4 = f32[4,128,128]{2,1,0:T(8,128)S(1)} fusion(f32[16,128,128]{2,1,0:T(8,128)} %bitcast.122, s32[1024]{0:T(1024)S(1)} %pad_clamp_fusion), kind=kCustom, calls=%fused_computation.4 | custom fusion | bytes 524304 | tf_op jit(solution)/shard_map/gather | solution.py:148
  17.1 2.5 %gather_fusion.5 = f32[4,128,128]{2,1,0:T(8,128)} fusion(f32[16,128,128]{2,1,0:T(8,128)} %bitcast.121, s32[1024]{0:T(1024)S(1)} %pad_clamp_fusion), kind=kCustom, calls=%fused_computation.5 | custom fusion | bytes 524304 | tf_op jit(solution)/shard_map/gather | solution.py:148
  19.5 0.6 constant_dynamic-slice_fusion.3
  21.9 1.1 %fusion.13 = f32[512,512]{0,1:T(8,128)S(1)} fusion(f32[1,1,512,512]{3,2,1,0:T(8,128)S(1)} %copy-done.2, f32[512]{0:T(512)S(1)} %bitcast.129, f32[1,1,512,512]{3,2,1,0:T(8,128)S(1)} %copy-done.3), kind=kOutput, calls=%fused_computation.27 | convolution fusion | flops 805568512 | bytes 3147776 | tf_op jit(solution)/shard_map/dot_general | solution.py:34
  22.9 1.1 %convolution_subtract_fusion.1 = f32[512,512]{0,1:T(8,128)S(1)} fusion(f32[512,512]{0,1:T(8,128)S(1)} %fusion.13, f32[1,1,512,512]{3,2,1,0:T(8,128)S(1)} %copy-done.3, f32[512]{0:T(512)S(1)} %bitcast.130, f32[1,1,512,512]{3,2,1,0:T(8,128)S(1)} %copy-done.2), kind=kOutput, calls=%fused_computation.8 | convolution fusion | flops 805830656 | bytes 4196352 | tf_op jit(solution)/shard_map/dot_general | solution.py:35
  27.4 1.2 %gather_fusion = s32[16]{0:T(128)} fusion(s32[16]{0:T(128)S(1)} %bitcast.106, s32[1024]{0:T(1024)S(1)} %pad_clamp_fusion.4), kind=kCustom, calls=%fused_computation | custom fusion | bytes 192 | tf_op jit(solution)/shard_map/gather | solution.py:171
  28.6 1.3 %copy.39 = f32[512,512]{1,0:T(8,128)} copy(f32[512,512]{0,1:T(8,128)S(1)} %convolution_subtract_fusion.1) | data formatting | bytes 2097152 | tf_op jit(solution)/shard_map/sub | solution.py:36
  29.9 0.7 constant_dynamic-slice_fusion
  30.6 22.4 %collective-permute-done.1 = f32[1028,128]{1,0:T(8,128)} collective-permute-done((f32[1028,128]{1,0:T(8,128)}, f32[1028,128]{1,0:T(8,128)}, u32[]{:S(2)}, u32[]{:S(2)}) %collective-permute-start.1) | collective-permute-done | bytes 526368 | tf_op jit(solution)/shard_map/ppermute | solution.py:143
  53.0 1.5 %pad_maximum_fusion = f32[4,1028,128]{2,1,0:T(8,128)S(1)} fusion(f32[1,1028,128]{2,1,0:T(8,128)} %bitcast.33, f32[1,1028,128]{2,1,0:T(8,128)} %bitcast.32, f32[1,1028,128]{2,1,0:T(8,128)} %bitcast.31, f32[1,1028,128]{2,1,0:T(8,128)S(1)} %maximum_bitcast_fusion), kind=kLoop, calls=%fused_computation.6 | loop fusion | flops 1579008 | bytes 4210688 | tf_op jit(solution)/shard_map/stack | solution.py:151
  54.8 1.2 %fusion.10 = f32[4,4,128,128]{3,1,2,0:T(4,128)S(1)} fusion(f32[4,4,16,1]{2,1,3,0:T(4,128)S(1)} %bitcast.125, f32[16,1,128,128]{3,2,1,0:T(8,128)S(1)} %get-tuple-element.11), kind=kOutput, calls=%fused_computation.21 | convolution fusion | flops 25165824 | bytes 2098176 | tf_op jit(solution)/shard_map/ji,ixy->jxy/dot_general | solution.py:159
  56.1 1.5 %bitcast_multiply_fusion = (f32[4,128,4,128]{3,2,1,0:T(4,128)S(1)}, f32[4,128,4,128]{3,2,1,0:T(4,128)S(1)}, f32[4,4,128,128]{3,1,2,0:T(4,128)S(1)}) fusion(f32[4,128]{1,0:T(4,128)S(1)} %dynamic-slice_bitcast_fusion, f32[4,4,128,128]{3,1,2,0:T(4,128)S(1)} %fusion.10, f32[4,4,16,1]{2,1,3,0:T(4,128)S(1)} %bitcast.126, ...), kind=kOutput, calls=%fused_computation.22 | convolution fusion | flops 25690112 | bytes 5245952 | tf_op jit(solution)/shard_map/ji,ixy->jxy/dot_general | solution.py:160
  57.6 1.0 %fusion.4 = f32[512,512]{1,0:T(8,128)S(1)} fusion(f32[64,8,4,128]{3,2,1,0:T(4,128)S(1)} %bitcast.112, f32[64,8,4,128]{3,2,1,0:T(4,128)S(1)} %bitcast.111), kind=kOutput, calls=%fused_computation.13 | convolution fusion | flops 805306368 | bytes 3145728 | tf_op jit(solution)/shard_map/dot_general | solution.py:34
  58.7 1.0 %convolution_subtract_fusion = f32[512,512]{1,0:T(8,128)S(1)} fusion(f32[512,512]{1,0:T(8,128)S(1)} %fusion.4, f32[64,8,4,128]{3,2,1,0:T(4,128)S(1)} %bitcast.109, f32[64,8,4,128]{3,2,1,0:T(4,128)S(1)} %bitcast.115), kind=kOutput, calls=%fused_computation.7 | convolution fusion | flops 805568512 | bytes 4194304 | tf_op jit(solution)/shard_map/dot_general | solution.py:35
  61.1 1.4 %collective-permute-start.4 = (f32[4,128,128]{2,1,0:T(8,128)S(1)}, f32[4,128,128]{2,1,0:T(8,128)S(1)}, u32[]{:S(2)}, u32[]{:S(2)}) collective-permute-start(f32[4,128,128]{2,1,0:T(8,128)S(1)} %copy.60), channel_id=1, source_target_pairs={{0,8},{4,12},{8,0},{12,4},{1,9},{5,13},{9,1},{13,5},{2,10},{6,14},... | collective-permute-start | bytes 786440 | tf_op jit(solution)/shard_map/ppermute | solution.py:170
  62.5 2.1 %collective-permute-start.5 = (f32[4,128,128]{2,1,0:T(8,128)S(1)}, f32[4,128,128]{2,1,0:T(8,128)S(1)}, u32[]{:S(2)}, u32[]{:S(2)}) collective-permute-start(f32[4,128,128]{2,1,0:T(8,128)S(1)} %copy.61), channel_id=1, source_target_pairs={{0,12},{4,0},{8,4},{12,8},{1,13},{5,1},{9,5},{13,9},{2,14},{6,2},{... | collective-permute-start | bytes 786440 | tf_op jit(solution)/shard_map/ppermute | solution.py:170
  64.6 1.2 %fusion.11.direct_ref = f32[512,512]{1,0:T(8,128)} fusion(f32[512,512]{1,0:T(8,128)S(1)} %copy-done.4, f32[512,512]{0,1:T(8,128)S(1)} %convolution_subtract_fusion.1), kind=kLoop, calls=%fused_computation.25 | loop fusion | flops 524288 | bytes 3145728 | tf_op jit(solution)/shard_map/mul | solution.py:174
  65.8 0.7 copy.58.rest_0_
  66.5 1.7 %collective-permute-done.3.rest_1_ = f32[4,128,128]{2,1,0:T(8,128)S(1)} collective-permute-done((f32[4,128,128]{2,1,0:T(8,128)S(1)}, f32[4,128,128]{2,1,0:T(8,128)S(1)}, u32[]{:S(2)}, u32[]{:S(2)}) %collective-permute-start.3) | collective-permute-done | bytes 262176 | tf_op jit(solution)/shard_map/ppermute | solution.py:170
  68.3 17.5 %collective-permute-done.4.rest_2_ = f32[4,128,128]{2,1,0:T(8,128)S(1)} collective-permute-done((f32[4,128,128]{2,1,0:T(8,128)S(1)}, f32[4,128,128]{2,1,0:T(8,128)S(1)}, u32[]{:S(2)}, u32[]{:S(2)}) %collective-permute-start.4) | collective-permute-done | bytes 262176 | tf_op jit(solution)/shard_map/ppermute | solution.py:170
  85.8 0.7 copy-done.7
  86.5 0.7 copy-done.8
  87.2 3.7 %shard_map.83 = f32[512,512]{1,0:T(8,128)} custom-call(s32[16]{0:T(128)} %gather_fusion, f32[512,512]{1,0:T(8,128)} %fusion.11.direct_ref, f32[4,128,128]{2,1,0:T(8,128)} %copy.58.rest_0_, f32[4,128,128]{2,1,0:T(8,128)} %copy-done.6, f32[4,128,128]{2,1,0:T(8,128)} %copy-done.7, f32[4,128,128]{2,1,0:T(8,128)} %copy-done.8), custom_call_target="tpu_custom_call" | custom-call | tf_op jit(solution)/shard_map/pallas_call | solution.py:101
  (65 shorter events, 4.6 us)
Async XLA Ops:
  0.0 24.7 %copy-start = (f32[8,16,16]{2,1,0:T(8,128)S(1)}, f32[8,16,16]{2,1,0:T(8,128)}, u32[]{:S(2)}) copy-start(f32[8,16,16]{2,1,0:T(8,128)} %param.12) | copy-start | bytes 24580
  0.0 7.5 %copy-start.2 = (f32[1,1,512,512]{3,2,1,0:T(8,128)S(1)}, f32[1,1,512,512]{3,2,1,0:T(8,128)}, u32[]{:S(2)}) copy-start(f32[1,1,512,512]{3,2,1,0:T(8,128)} %param.8) | copy-start | bytes 3145732
  1.4 7.4 %copy-start.3 = (f32[1,1,512,512]{3,2,1,0:T(8,128)S(1)}, f32[1,1,512,512]{3,2,1,0:T(8,128)}, u32[]{:S(2)}) copy-start(f32[1,1,512,512]{3,2,1,0:T(8,128)} %param.9) | copy-start | bytes 3145732
  5.1 4.1 %copy-start.10 = (s32[4,1]{0,1:T(1,128)S(1)}, s32[4,1]{0,1:T(1,128)}, u32[]{:S(2)}) copy-start(s32[4,1]{0,1:T(1,128)} %param.13) | copy-start | bytes 52
  5.1 25.5 %collective-permute-start = (f32[1028,128]{1,0:T(8,128)}, f32[1028,128]{1,0:T(8,128)}, u32[]{:S(2)}, u32[]{:S(2)}) collective-permute-start(f32[1028,128]{1,0:T(8,128)} %get-tuple-element.8), channel_id=1, source_target_pairs={{0,4},{4,8},{8,12},{12,0},{1,5},{5,9},{9,13},{13,1},{2,6},{6,10},{... | collective-permute-start | bytes 1579016 | tf_op jit(solution)/shard_map/ppermute | solution.py:143
  5.3 47.7 %collective-permute-start.1 = (f32[1028,128]{1,0:T(8,128)}, f32[1028,128]{1,0:T(8,128)}, u32[]{:S(2)}, u32[]{:S(2)}) collective-permute-start(f32[1028,128]{1,0:T(8,128)} %get-tuple-element.9), channel_id=1, source_target_pairs={{0,8},{4,12},{8,0},{12,4},{1,9},{5,13},{9,1},{13,5},{2,10},{6,14},... | collective-permute-start | bytes 1579016 | tf_op jit(solution)/shard_map/ppermute | solution.py:143
  7.0 46.0 %collective-permute-start.2 = (f32[1028,128]{1,0:T(8,128)}, f32[1028,128]{1,0:T(8,128)}, u32[]{:S(2)}, u32[]{:S(2)}) collective-permute-start(f32[1028,128]{1,0:T(8,128)} %get-tuple-element.10), channel_id=1, source_target_pairs={{0,12},{4,0},{8,4},{12,8},{1,13},{5,1},{9,5},{13,9},{2,14},{6,2},{... | collective-permute-start | bytes 1579016 | tf_op jit(solution)/shard_map/ppermute | solution.py:143
  7.5 3.7 %copy-start.1 = (s32[1,1,16]{2,1,0:T(1,128)S(1)}, s32[1,1,16]{2,1,0:T(1,128)}, u32[]{:S(2)}) copy-start(s32[1,1,16]{2,1,0:T(1,128)} %param.14) | copy-start | bytes 196
  11.8 7.7 %copy-start.11 = (s32[4,1]{0,1:T(1,128)S(1)}, s32[4,1]{0,1:T(1,128)}, u32[]{:S(2)}) copy-start(s32[4,1]{0,1:T(1,128)} %param.15) | copy-start | bytes 52
  14.2 7.7 %copy-start.9 = (f32[1,1,512]{2,1,0:T(1,128)S(1)}, f32[1,1,512]{2,1,0:T(1,128)}, u32[]{:S(2)}) copy-start(f32[1,1,512]{2,1,0:T(1,128)} %param.10) | copy-start | bytes 6148
  22.9 1.1 %copy-start.5 = (f32[4,128,128]{2,1,0:T(8,128)S(1)}, f32[4,128,128]{2,1,0:T(8,128)}, u32[]{:S(2)}) copy-start(f32[4,128,128]{2,1,0:T(8,128)} %gather_fusion.5) | copy-start | bytes 786436
  60.8 3.8 %copy-start.4 = (f32[512,512]{1,0:T(8,128)S(1)}, f32[512,512]{1,0:T(8,128)}, u32[]{:S(2)}) copy-start(f32[512,512]{1,0:T(8,128)} %copy.39) | copy-start | bytes 3145732
  61.0 7.2 %collective-permute-start.3 = (f32[4,128,128]{2,1,0:T(8,128)S(1)}, f32[4,128,128]{2,1,0:T(8,128)S(1)}, u32[]{:S(2)}, u32[]{:S(2)}) collective-permute-start(f32[4,128,128]{2,1,0:T(8,128)S(1)} %copy.59), channel_id=1, source_target_pairs={{0,4},{4,8},{8,12},{12,0},{1,5},{5,9},{9,13},{13,1},{2,6},{6,10},{... | collective-permute-start | bytes 786440 | tf_op jit(solution)/shard_map/ppermute | solution.py:170
  61.1 24.6 %collective-permute-start.4 = (f32[4,128,128]{2,1,0:T(8,128)S(1)}, f32[4,128,128]{2,1,0:T(8,128)S(1)}, u32[]{:S(2)}, u32[]{:S(2)}) collective-permute-start(f32[4,128,128]{2,1,0:T(8,128)S(1)} %copy.60), channel_id=1, source_target_pairs={{0,8},{4,12},{8,0},{12,4},{1,9},{5,13},{9,1},{13,5},{2,10},{6,14},... | collective-permute-start | bytes 786440 | tf_op jit(solution)/shard_map/ppermute | solution.py:170
  62.5 23.2 %collective-permute-start.5 = (f32[4,128,128]{2,1,0:T(8,128)S(1)}, f32[4,128,128]{2,1,0:T(8,128)S(1)}, u32[]{:S(2)}, u32[]{:S(2)}) collective-permute-start(f32[4,128,128]{2,1,0:T(8,128)S(1)} %copy.61), channel_id=1, source_target_pairs={{0,12},{4,0},{8,4},{12,8},{1,13},{5,1},{9,5},{13,9},{2,14},{6,2},{... | collective-permute-start | bytes 786440 | tf_op jit(solution)/shard_map/ppermute | solution.py:170
  68.3 17.5 %copy-start.6 = (f32[4,128,128]{2,1,0:T(8,128)}, f32[4,128,128]{2,1,0:T(8,128)S(1)}, u32[]{:S(2)}) copy-start(f32[4,128,128]{2,1,0:T(8,128)S(1)} %collective-permute-done.3.rest_1_) | copy-start | bytes 786436
  85.8 0.7 copy-start.7
  86.5 0.7 copy-start.8

commit v19 on v18

--- a/solution.py
+++ b/solution.py
@@ -148,7 +148,10 @@
         [to_tiles(generator[0, 0], TS)[picked], to_tiles(hamiltonian[0, 0], TS)[picked]], axis=1
     ).reshape(2 * spread * TS, TS)
     got[0] = jnp.concatenate([local, cross_weights[0, 0][slot].reshape(-1, TS)], axis=0)
-    got = jnp.stack(got)
+    stacked = jnp.zeros((channels,) + got[0].shape, jnp.float32)
+    for shift, piece in enumerate(got):
+        stacked = stacked.at[shift].set(piece)
+    got = stacked
     tiles_got = got[:, : 2 * spread * TS].reshape(channels, spread, 2, TS, TS)
     weights_cross = got[(me - owners[me]) % channels, 2 * spread * TS :].reshape(-1)
 

time: 91.3 us -> 97.4 us (1.067)
  the two profiles are of different devices: /device:TPU:28 before, /device:TPU:13 now
where the time goes in v19:
time: 97.4 us; the launch traced here: 96.8 us
  waiting for transfers between devices  35.7 us (37%)
  local copies, waits for them, and re-layouts  28.2 us (29%)
  matrix products  10.6 us (11%)
  starting transfers between devices  7.58 us (8%)
  Pallas kernels  7.45 us (8%)
  other arithmetic  3.66 us (4%)
  between operations  3.54 us (4%)
    ppermute x3, waiting for transfers between devices, body(): home.append(lax.ppermute(back[shift], 'chan', pairs))  20.2 us
    ppermute x3, waiting for transfers between devices, body(): got.append(lax.ppermute(sends[shift - 1], 'chan', pairs))  15.5 us
    scatter x4, local copies, waits for them, and re-layouts, body(): stacked = stacked.at[shift].set(piece)  7.15 us
    dot_general x2, matrix products, bracket(): jnp.matmul(right_matrix * scaled, left_matrix, precision=highest)  4.28 us
    ppermute x3, starting transfers between devices, body(): home.append(lax.ppermute(back[shift], 'chan', pairs))  3.8 us
    ppermute x3, starting transfers between devices, body(): got.append(lax.ppermute(sends[shift - 1], 'chan', pairs))  3.77 us
    pallas_call x1, Pallas kernels, finish(): pl.pallas_call(kernel, grid_spec=pltpu.PrefetchScalarGridSpec(num_scalar_...  3.75 us
    pallas_call x1, Pallas kernels, build_sends(): pl.pallas_call(kernel, grid_spec=pltpu.PrefetchScalarGridSpec(num_scalar_...  3.7 us
  transfers between devices with their start and end apart: 6, of which 5 were waited for; matrix products, arithmetic and copies ran while one was open for 29% of the time, Pallas kernels for 0%

profile of v19, /device:TPU:13, one launch (start us, length us, event | category | flops | bytes accessed | tf_op | source)
XLA Modules:
  0.0 96.8 jit_solution(3958741129879708486)
XLA Ops:
  0.0 1.4 %copy.42.weight_ref = f32[1,1,3,512]{3,2,1,0:T(4,128)} copy(f32[1,1,3,512]{3,1,2,0:T(1,128)} %param.19) | data formatting | bytes 12288 | tf_op args[3]
  1.4 3.7 %shard_map.82 = (f32[1028,128]{1,0:T(8,128)}, f32[1028,128]{1,0:T(8,128)}, f32[1028,128]{1,0:T(8,128)}) custom-call(s32[16]{0:T(128)} %bitcast.107, s32[4]{0:T(128)} %bitcast.134, f32[512,512]{1,0:T(8,128)} %bitcast.110, f32[512,512]{1,0:T(8,128)} %bitcast.111, f32[1,1,3,512]{3,2,1,0:T(4,128)} %copy.42.weight_ref), custom_call_target="tpu_custom_call" | custom-call | tf_op jit(solution)/shard_map/pallas_call | solution.py:71
  5.1 1.3 %collective-permute-start = (f32[1028,128]{1,0:T(8,128)}, f32[1028,128]{1,0:T(8,128)}, u32[]{:S(2)}, u32[]{:S(2)}) collective-permute-start(f32[1028,128]{1,0:T(8,128)} %get-tuple-element.56), channel_id=1, source_target_pairs={{0,4},{4,8},{8,12},{12,0},{1,5},{5,9},{9,13},{13,1},{2,6},{6,10},{... | collective-permute-start | bytes 1579016 | tf_op jit(solution)/shard_map/ppermute | solution.py:143
  6.4 1.0 %collective-permute-start.1 = (f32[1028,128]{1,0:T(8,128)}, f32[1028,128]{1,0:T(8,128)}, u32[]{:S(2)}, u32[]{:S(2)}) collective-permute-start(f32[1028,128]{1,0:T(8,128)} %get-tuple-element.57), channel_id=1, source_target_pairs={{0,8},{4,12},{8,0},{12,4},{1,9},{5,13},{9,1},{13,5},{2,10},{6,14},... | collective-permute-start | bytes 1579016 | tf_op jit(solution)/shard_map/ppermute | solution.py:143
  7.4 1.5 %collective-permute-start.2 = (f32[1028,128]{1,0:T(8,128)}, f32[1028,128]{1,0:T(8,128)}, u32[]{:S(2)}, u32[]{:S(2)}) collective-permute-start(f32[1028,128]{1,0:T(8,128)} %get-tuple-element.58), channel_id=1, source_target_pairs={{0,12},{4,0},{8,4},{12,8},{1,13},{5,1},{9,5},{13,9},{2,14},{6,2},{... | collective-permute-start | bytes 1579016 | tf_op jit(solution)/shard_map/ppermute | solution.py:143
  8.9 1.3 %reshape_squeeze.9 = f32[4,128,4,128]{3,2,1,0:T(4,128)} reshape(f32[1,1,512,512]{3,2,1,0:T(8,128)S(1)} %copy-done.2) | data formatting | bytes 2097152 | tf_op jit(solution)/shard_map/reshape;squeeze | solution.py:19
  11.2 1.3 %fusion.28 = s32[]{:T(128)} fusion(s32[]{:T(128)} %bitcast.28, s32[]{:T(128)S(6)} %axis_index.15, s32[4,1]{0,1:T(1,128)S(1)} %copy-done.8), kind=kLoop, calls=%fused_computation.71 | loop fusion | flops 19 | bytes 28 | tf_op jit(solution)/shard_map/reduce_sum | solution.py:145
  14.6 2.3 %copy.39 = f32[4,4,128,128]{3,2,1,0:T(8,128)} copy(f32[4,4,128,128]{3,1,2,0:T(4,128)} %bitcast.117) | data formatting | bytes 2097152 | tf_op jit(solution)/shard_map/transpose | solution.py:20
  17.0 1.1 %copy.40 = f32[4,4,128,128]{3,2,1,0:T(8,128)} copy(f32[4,4,128,128]{3,1,2,0:T(4,128)S(1)} %bitcast.116) | data formatting | bytes 2097152 | tf_op jit(solution)/shard_map/transpose | solution.py:20
  18.1 1.8 %gather_fusion.4 = f32[4,128,128]{2,1,0:T(8,128)S(1)} fusion(f32[16,128,128]{2,1,0:T(8,128)} %bitcast.125, s32[1024]{0:T(1024)S(1)} %pad_clamp_fusion), kind=kCustom, calls=%fused_computation.4 | custom fusion | bytes 524304 | tf_op jit(solution)/shard_map/gather | solution.py:148
  19.9 1.8 %gather_fusion.5 = f32[4,128,128]{2,1,0:T(8,128)S(1)} fusion(f32[16,128,128]{2,1,0:T(8,128)} %bitcast.124, s32[1024]{0:T(1024)S(1)} %pad_clamp_fusion), kind=kCustom, calls=%fused_computation.5 | custom fusion | bytes 524304 | tf_op jit(solution)/shard_map/gather | solution.py:148
  24.1 2.0 %fusion.13 = f32[512,512]{0,1:T(8,128)} fusion(f32[1,1,512,512]{3,2,1,0:T(8,128)S(1)} %copy-done.2, f32[512]{0:T(512)S(1)} %bitcast.132, f32[1,1,512,512]{3,2,1,0:T(8,128)S(1)} %copy-done.3), kind=kOutput, calls=%fused_computation.26 | convolution fusion | flops 805568512 | bytes 3147776 | tf_op jit(solution)/shard_map/dot_general | solution.py:34
  27.6 2.3 %convolution_subtract_fusion.1 = f32[512,512]{0,1:T(8,128)S(1)} fusion(f32[512,512]{0,1:T(8,128)} %fusion.13, f32[1,1,512,512]{3,2,1,0:T(8,128)S(1)} %copy-done.3, f32[512]{0:T(512)S(1)} %bitcast.133, f32[1,1,512,512]{3,2,1,0:T(8,128)S(1)} %copy-done.2), kind=kOutput, calls=%fused_computation.7 | convolution fusion | flops 805830656 | bytes 4196352 | tf_op jit(solution)/shard_map/dot_general | solution.py:35
  31.9 1.2 %gather_fusion = s32[16]{0:T(128)} fusion(s32[16]{0:T(128)S(1)} %bitcast.109, s32[1024]{0:T(1024)S(1)} %pad_clamp_fusion.4), kind=kCustom, calls=%fused_computation | custom fusion | bytes 192 | tf_op jit(solution)/shard_map/gather | solution.py:174
  33.4 1.5 %scatter.14 = f32[4,1028,128]{2,1,0:T(8,128)} pad(f32[1,1028,128]{2,1,0:T(8,128)S(1)} %copy-done.4, f32[]{:T(128)} %constant.156.clone.1), padding=0_3x0_0x0_0 | pad | bytes 2631684 | tf_op jit(solution)/shard_map/scatter | solution.py:153
  34.9 1.9 %bitcast_dynamic-update-slice_fusion.2 = f32[4,1028,128]{2,1,0:T(8,128)} fusion(f32[4,1028,128]{2,1,0:T(8,128)} %scatter.14, f32[1028,128]{1,0:T(8,128)} %collective-permute-done), kind=kLoop, calls=%fused_computation.33 | loop fusion | bytes 1056768 | tf_op jit(solution)/shard_map/scatter | solution.py:153
  36.8 14.6 %collective-permute-done.1 = f32[1028,128]{1,0:T(8,128)} collective-permute-done((f32[1028,128]{1,0:T(8,128)}, f32[1028,128]{1,0:T(8,128)}, u32[]{:S(2)}, u32[]{:S(2)}) %collective-permute-start.1) | collective-permute-done | bytes 526368 | tf_op jit(solution)/shard_map/ppermute | solution.py:143
  51.4 1.9 %bitcast_dynamic-update-slice_fusion.1 = f32[4,1028,128]{2,1,0:T(8,128)} fusion(f32[4,1028,128]{2,1,0:T(8,128)} %bitcast_dynamic-update-slice_fusion.2, f32[1028,128]{1,0:T(8,128)} %collective-permute-done.1), kind=kLoop, calls=%fused_computation.32 | loop fusion | bytes 1056768 | tf_op jit(solution)/shard_map/scatter | solution.py:153
  54.2 1.9 %bitcast_dynamic-update-slice_fusion = f32[4,1028,128]{2,1,0:T(8,128)} fusion(f32[4,1028,128]{2,1,0:T(8,128)} %bitcast_dynamic-update-slice_fusion.1, f32[1028,128]{1,0:T(8,128)} %collective-permute-done.2), kind=kLoop, calls=%fused_computation.31 | loop fusion | bytes 1056768 | tf_op jit(solution)/shard_map/scatter | solution.py:153
  56.1 1.7 %slice.123 = f32[4,1024,128]{2,1,0:T(8,128)S(1)} slice(f32[4,1028,128]{2,1,0:T(8,128)} %bitcast_dynamic-update-slice_fusion), slice={[0:4], [0:1024], [0:128]} | slice | bytes 4194304 | tf_op jit(solution)/shard_map/slice | solution.py:155
  58.7 1.2 %fusion.10 = f32[4,4,128,128]{3,1,2,0:T(4,128)S(1)} fusion(f32[4,4,16,1]{2,1,3,0:T(4,128)S(1)} %bitcast.128, f32[16,1,128,128]{3,2,1,0:T(8,128)S(1)} %get-tuple-element.59), kind=kOutput, calls=%fused_computation.20 | convolution fusion | flops 25165824 | bytes 2098176 | tf_op jit(solution)/shard_map/ji,ixy->jxy/dot_general | solution.py:162
  60.0 1.5 %bitcast_multiply_fusion = (f32[4,128,4,128]{3,2,1,0:T(4,128)S(1)}, f32[4,128,4,128]{3,2,1,0:T(4,128)S(1)}, f32[4,4,128,128]{3,1,2,0:T(4,128)S(1)}) fusion(f32[4,128]{1,0:T(4,128)S(1)} %dynamic-slice_bitcast_fusion, f32[4,4,128,128]{3,1,2,0:T(4,128)S(1)} %fusion.10, f32[4,4,16,1]{2,1,3,0:T(4,128)S(1)} %bitcast.129, ...), kind=kOutput, calls=%fused_computation.21 | convolution fusion | flops 25690112 | bytes 5245952 | tf_op jit(solution)/shard_map/ji,ixy->jxy/dot_general | solution.py:163
  61.5 1.0 %fusion.4 = f32[512,512]{1,0:T(8,128)S(1)} fusion(f32[64,8,4,128]{3,2,1,0:T(4,128)S(1)} %bitcast.115, f32[64,8,4,128]{3,2,1,0:T(4,128)S(1)} %bitcast.114), kind=kOutput, calls=%fused_computation.12 | convolution fusion | flops 805306368 | bytes 3145728 | tf_op jit(solution)/shard_map/dot_general | solution.py:34
  62.5 2.0 %convolution_subtract_fusion = f32[512,512]{1,0:T(8,128)} fusion(f32[512,512]{1,0:T(8,128)S(1)} %fusion.4, f32[64,8,4,128]{3,2,1,0:T(4,128)S(1)} %bitcast.112, f32[64,8,4,128]{3,2,1,0:T(4,128)S(1)} %bitcast.118), kind=kOutput, calls=%fused_computation.6 | convolution fusion | flops 805568512 | bytes 4194304 | tf_op jit(solution)/shard_map/dot_general | solution.py:35
  64.5 1.6 %reshape.354 = f32[4,128,4,128]{3,2,1,0:T(4,128)S(1)} reshape(f32[512,512]{1,0:T(8,128)} %convolution_subtract_fusion) | data formatting | bytes 2097152 | tf_op jit(solution)/shard_map/reshape | solution.py:19
  67.1 2.2 %collective-permute-start.4 = (f32[4,128,128]{2,1,0:T(8,128)S(1)}, f32[4,128,128]{2,1,0:T(8,128)S(1)}, u32[]{:S(2)}, u32[]{:S(2)}) collective-permute-start(f32[4,128,128]{2,1,0:T(8,128)S(1)} %copy.57), channel_id=1, source_target_pairs={{0,8},{4,12},{8,0},{12,4},{1,9},{5,13},{9,1},{13,5},{2,10},{6,14},... | collective-permute-start | bytes 786440 | tf_op jit(solution)/shard_map/ppermute | solution.py:173
  69.4 1.5 %collective-permute-start.5 = (f32[4,128,128]{2,1,0:T(8,128)S(1)}, f32[4,128,128]{2,1,0:T(8,128)}, u32[]{:S(2)}, u32[]{:S(2)}) collective-permute-start(f32[4,128,128]{2,1,0:T(8,128)S(1)} %copy.58), channel_id=1, source_target_pairs={{0,12},{4,0},{8,4},{12,8},{1,13},{5,1},{9,5},{13,9},{2,14},{6,2},{... | collective-permute-start | bytes 786440 | tf_op jit(solution)/shard_map/ppermute | solution.py:173
  70.9 1.2 %fusion.11.direct_ref = f32[512,512]{1,0:T(8,128)} fusion(f32[512,512]{1,0:T(8,128)S(1)} %copy.36, f32[512,512]{0,1:T(8,128)S(1)} %convolution_subtract_fusion.1), kind=kLoop, calls=%fused_computation.24 | loop fusion | flops 524288 | bytes 3145728 | tf_op jit(solution)/shard_map/mul | solution.py:177
  72.8 1.5 %collective-permute-done.3.rest_1_ = f32[4,128,128]{2,1,0:T(8,128)S(1)} collective-permute-done((f32[4,128,128]{2,1,0:T(8,128)S(1)}, f32[4,128,128]{2,1,0:T(8,128)S(1)}, u32[]{:S(2)}, u32[]{:S(2)}) %collective-permute-start.3) | collective-permute-done | bytes 262176 | tf_op jit(solution)/shard_map/ppermute | solution.py:173
  74.3 15.0 %collective-permute-done.4.rest_2_ = f32[4,128,128]{2,1,0:T(8,128)S(1)} collective-permute-done((f32[4,128,128]{2,1,0:T(8,128)S(1)}, f32[4,128,128]{2,1,0:T(8,128)S(1)}, u32[]{:S(2)}, u32[]{:S(2)}) %collective-permute-start.4) | collective-permute-done | bytes 262176 | tf_op jit(solution)/shard_map/ppermute | solution.py:173
  89.3 3.7 %collective-permute-done.5.rest_3_ = f32[4,128,128]{2,1,0:T(8,128)} collective-permute-done((f32[4,128,128]{2,1,0:T(8,128)S(1)}, f32[4,128,128]{2,1,0:T(8,128)}, u32[]{:S(2)}, u32[]{:S(2)}) %collective-permute-start.5) | collective-permute-done | bytes 262176 | tf_op jit(solution)/shard_map/ppermute | solution.py:173
  93.0 3.7 %shard_map.83 = f32[512,512]{1,0:T(8,128)} custom-call(s32[16]{0:T(128)} %gather_fusion, f32[512,512]{1,0:T(8,128)} %fusion.11.direct_ref, f32[4,128,128]{2,1,0:T(8,128)} %copy.55.rest_0_, f32[4,128,128]{2,1,0:T(8,128)} %copy-done.5, f32[4,128,128]{2,1,0:T(8,128)} %copy-done.6, f32[4,128,128]{2,1,0:T(8,128)} %collective-permute-done.5.rest_3_), custom_call_target="tpu_custom_call" | custom-call | tf_op jit(solution)/shard_map/pallas_call | solution.py:101
  (64 shorter events, 9.6 us)
Async XLA Ops:
  0.0 27.6 %copy-start = (f32[8,16,16]{2,1,0:T(8,128)S(1)}, f32[8,16,16]{2,1,0:T(8,128)}, u32[]{:S(2)}) copy-start(f32[8,16,16]{2,1,0:T(8,128)} %param.20) | copy-start | bytes 24580
  0.0 8.9 %copy-start.2 = (f32[1,1,512,512]{3,2,1,0:T(8,128)S(1)}, f32[1,1,512,512]{3,2,1,0:T(8,128)}, u32[]{:S(2)}) copy-start(f32[1,1,512,512]{3,2,1,0:T(8,128)} %param.16) | copy-start | bytes 3145732
  1.4 8.8 %copy-start.3 = (f32[1,1,512,512]{3,2,1,0:T(8,128)S(1)}, f32[1,1,512,512]{3,2,1,0:T(8,128)}, u32[]{:S(2)}) copy-start(f32[1,1,512,512]{3,2,1,0:T(8,128)} %param.17) | copy-start | bytes 3145732
  5.1 5.5 %copy-start.8 = (s32[4,1]{0,1:T(1,128)S(1)}, s32[4,1]{0,1:T(1,128)}, u32[]{:S(2)}) copy-start(s32[4,1]{0,1:T(1,128)} %param.21) | copy-start | bytes 52
  5.1 29.8 %collective-permute-start = (f32[1028,128]{1,0:T(8,128)}, f32[1028,128]{1,0:T(8,128)}, u32[]{:S(2)}, u32[]{:S(2)}) collective-permute-start(f32[1028,128]{1,0:T(8,128)} %get-tuple-element.56), channel_id=1, source_target_pairs={{0,4},{4,8},{8,12},{12,0},{1,5},{5,9},{9,13},{13,1},{2,6},{6,10},{... | collective-permute-start | bytes 1579016 | tf_op jit(solution)/shard_map/ppermute | solution.py:143
  6.4 45.0 %collective-permute-start.1 = (f32[1028,128]{1,0:T(8,128)}, f32[1028,128]{1,0:T(8,128)}, u32[]{:S(2)}, u32[]{:S(2)}) collective-permute-start(f32[1028,128]{1,0:T(8,128)} %get-tuple-element.57), channel_id=1, source_target_pairs={{0,8},{4,12},{8,0},{12,4},{1,9},{5,13},{9,1},{13,5},{2,10},{6,14},... | collective-permute-start | bytes 1579016 | tf_op jit(solution)/shard_map/ppermute | solution.py:143
  7.4 46.8 %collective-permute-start.2 = (f32[1028,128]{1,0:T(8,128)}, f32[1028,128]{1,0:T(8,128)}, u32[]{:S(2)}, u32[]{:S(2)}) collective-permute-start(f32[1028,128]{1,0:T(8,128)} %get-tuple-element.58), channel_id=1, source_target_pairs={{0,12},{4,0},{8,4},{12,8},{1,13},{5,1},{9,5},{13,9},{2,14},{6,2},{... | collective-permute-start | bytes 1579016 | tf_op jit(solution)/shard_map/ppermute | solution.py:143
  8.9 5.1 %copy-start.1 = (s32[1,1,16]{2,1,0:T(1,128)S(1)}, s32[1,1,16]{2,1,0:T(1,128)}, u32[]{:S(2)}) copy-start(s32[1,1,16]{2,1,0:T(1,128)} %param.22) | copy-start | bytes 196
  17.0 4.8 %copy-start.9 = (s32[4,1]{0,1:T(1,128)S(1)}, s32[4,1]{0,1:T(1,128)}, u32[]{:S(2)}) copy-start(s32[4,1]{0,1:T(1,128)} %param.23) | copy-start | bytes 52
  18.1 6.0 %copy-start.7 = (f32[1,1,512]{2,1,0:T(1,128)S(1)}, f32[1,1,512]{2,1,0:T(1,128)}, u32[]{:S(2)}) copy-start(f32[1,1,512]{2,1,0:T(1,128)} %param.18) | copy-start | bytes 6148
  29.9 3.5 %copy-start.4 = (f32[1,1028,128]{2,1,0:T(8,128)S(1)}, f32[1,1028,128]{2,1,0:T(8,128)}, u32[]{:S(2)}) copy-start(f32[1,1028,128]{2,1,0:T(8,128)} %maximum_bitcast_fusion) | copy-start | bytes 1579012
  67.0 7.3 %collective-permute-start.3 = (f32[4,128,128]{2,1,0:T(8,128)S(1)}, f32[4,128,128]{2,1,0:T(8,128)S(1)}, u32[]{:S(2)}, u32[]{:S(2)}) collective-permute-start(f32[4,128,128]{2,1,0:T(8,128)S(1)} %copy.56), channel_id=1, source_target_pairs={{0,4},{4,8},{8,12},{12,0},{1,5},{5,9},{9,13},{13,1},{2,6},{6,10},{... | collective-permute-start | bytes 786440 | tf_op jit(solution)/shard_map/ppermute | solution.py:173
  67.1 22.2 %collective-permute-start.4 = (f32[4,128,128]{2,1,0:T(8,128)S(1)}, f32[4,128,128]{2,1,0:T(8,128)S(1)}, u32[]{:S(2)}, u32[]{:S(2)}) collective-permute-start(f32[4,128,128]{2,1,0:T(8,128)S(1)} %copy.57), channel_id=1, source_target_pairs={{0,8},{4,12},{8,0},{12,4},{1,9},{5,13},{9,1},{13,5},{2,10},{6,14},... | collective-permute-start | bytes 786440 | tf_op jit(solution)/shard_map/ppermute | solution.py:173
  69.4 23.6 %collective-permute-start.5 = (f32[4,128,128]{2,1,0:T(8,128)S(1)}, f32[4,128,128]{2,1,0:T(8,128)}, u32[]{:S(2)}, u32[]{:S(2)}) collective-permute-start(f32[4,128,128]{2,1,0:T(8,128)S(1)} %copy.58), channel_id=1, source_target_pairs={{0,12},{4,0},{8,4},{12,8},{1,13},{5,1},{9,5},{13,9},{2,14},{6,2},{... | collective-permute-start | bytes 786440 | tf_op jit(solution)/shard_map/ppermute | solution.py:173
  74.3 18.7 %copy-start.5 = (f32[4,128,128]{2,1,0:T(8,128)}, f32[4,128,128]{2,1,0:T(8,128)S(1)}, u32[]{:S(2)}) copy-start(f32[4,128,128]{2,1,0:T(8,128)S(1)} %collective-permute-done.3.rest_1_) | copy-start | bytes 786436
  89.3 3.7 %copy-start.6 = (f32[4,128,128]{2,1,0:T(8,128)}, f32[4,128,128]{2,1,0:T(8,128)S(1)}, u32[]{:S(2)}) copy-start(f32[4,128,128]{2,1,0:T(8,128)S(1)} %collective-permute-done.4.rest_2_) | copy-start | bytes 786436

commit v20 on v18

--- a/solution.py
+++ b/solution.py
@@ -164,14 +164,16 @@
     mixer_out = mixer[:, (spread_range[None, :] * channels + dest[:, None]).reshape(-1)]
     back = jnp.einsum("ji,jxy->ixy", mixer_out, to_tiles(product, TS), precision=highest)
     back = back.reshape(channels, spread, TS, TS)
-    home = [back[0]]
+    home = []
     for shift in range(1, channels):
         pairs = [(c, (c + shift) % channels) for c in range(channels)]
         home.append(lax.ppermute(back[shift], "chan", pairs))
     place = order[(source[:, None] * spread + spread_range[None, :]).reshape(-1)]
+    kept = jnp.zeros((tile_count, TS, TS), jnp.float32).at[place[:spread]].set(back[0])
+    kept = from_tiles(kept, TS)
 
     direct = bracket(generator[0, 0], hamiltonian[0, 0], pair_weights[0, 0])
-    return finish(0.5 * (direct + direct.T), home, place)[None, None]
+    return finish(0.5 * (direct + direct.T + kept + kept.T), home, place[spread:])[None, None]
 
 
 def solution(mesh):

time: 91.3 us -> 97.3 us (1.066)
  local copies, waits for them, and re-layouts: 20.6 us -> 23.6 us
  other arithmetic: 4.32 us -> 6.84 us
    add x0 -> x1, other arithmetic: none -> 2.55 us  [body(): direct + direct.T + kept + kept.T]
    add x0 -> x1, local copies, waits for them, and re-layouts: none -> 1.61 us  [body(): direct + direct.T + kept + kept.T]
    reduce_sum x1 -> x0, other arithmetic: 1.28 us -> none  [body(): slot = jnp.minimum(jnp.sum(earlier & (owners == owners[me])), capacity - 1)]
    select_n x0 -> x1, other arithmetic: none -> 1.26 us  [body(): jnp.zeros((tile_count, TS, TS), jnp.float32).at[place[:spread]].set(back[0])]
    unnamed x29 -> x30, local copies, waits for them, and re-layouts: 3.59 us -> 2.86 us
  transfers between devices with their start and end apart: 6 -> 6, of which waited for: 3 -> 3; matrix products, arithmetic and copies ran while one was open for 24% -> 22% of each run, Pallas kernels for 0% -> 0%
where the time goes in v20:
time: 97.3 us; the launch traced here: 96.9 us
  waiting for transfers between devices  42.1 us (43%)
  local copies, waits for them, and re-layouts  23.6 us (24%)
  matrix products  7.51 us (8%)
  Pallas kernels  7.25 us (7%)
  other arithmetic  6.84 us (7%)
  starting transfers between devices  5.88 us (6%)
  between operations  3.67 us (4%)
    ppermute x3, waiting for transfers between devices, body(): got.append(lax.ppermute(sends[shift - 1], 'chan', pairs))  22.2 us
    ppermute x3, waiting for transfers between devices, body(): home.append(lax.ppermute(back[shift], 'chan', pairs))  19.9 us
    pallas_call x1, Pallas kernels, build_sends(): pl.pallas_call(kernel, grid_spec=pltpu.PrefetchScalarGridSpec(num_scalar_...  3.71 us
    transpose x3, local copies, waits for them, and re-layouts, to_tiles(): shaped = jnp.swapaxes(shaped, -3, -2)  3.62 us
    pallas_call x1, Pallas kernels, finish(): pl.pallas_call(kernel, grid_spec=pltpu.PrefetchScalarGridSpec(num_scalar_...  3.54 us
    ppermute x3, starting transfers between devices, body(): home.append(lax.ppermute(back[shift], 'chan', pairs))  3.51 us
    unnamed x30, local copies, waits for them, and re-layouts  2.86 us
    add x1, other arithmetic, body(): direct + direct.T + kept + kept.T  2.55 us
  transfers between devices with their start and end apart: 6, of which 3 were waited for; matrix products, arithmetic and copies ran while one was open for 22% of the time, Pallas kernels for 0%

profile of v20, /device:TPU:28, one launch (start us, length us, event | category | flops | bytes accessed | tf_op | source)
XLA Modules:
  0.0 96.9 jit_solution(3797749575618507299)
XLA Ops:
  0.0 1.4 %copy.41.weight_ref = f32[1,1,3,512]{3,2,1,0:T(4,128)} copy(f32[1,1,3,512]{3,1,2,0:T(1,128)} %param.11) | data formatting | bytes 12288 | tf_op args[3]
  1.4 3.7 %shard_map.82 = (f32[1028,128]{1,0:T(8,128)}, f32[1028,128]{1,0:T(8,128)}, f32[1028,128]{1,0:T(8,128)}) custom-call(s32[16]{0:T(128)} %bitcast.124, s32[4]{0:T(128)} %bitcast.154, f32[512,512]{1,0:T(8,128)} %bitcast.127, f32[512,512]{1,0:T(8,128)} %bitcast.128, f32[1,1,3,512]{3,2,1,0:T(4,128)} %copy.41.weight_ref), custom_call_target="tpu_custom_call" | custom-call | tf_op jit(solution)/shard_map/pallas_call | solution.py:71
  5.3 1.7 %collective-permute-start.1 = (f32[1028,128]{1,0:T(8,128)}, f32[1028,128]{1,0:T(8,128)}, u32[]{:S(2)}, u32[]{:S(2)}) collective-permute-start(f32[1028,128]{1,0:T(8,128)} %get-tuple-element.9), channel_id=1, source_target_pairs={{0,8},{4,12},{8,0},{12,4},{1,9},{5,13},{9,1},{13,5},{2,10},{6,14},... | collective-permute-start | bytes 1579016 | tf_op jit(solution)/shard_map/ppermute | solution.py:143
  7.5 1.3 %reshape_squeeze.9 = f32[4,128,4,128]{3,2,1,0:T(4,128)} reshape(f32[1,1,512,512]{3,2,1,0:T(8,128)S(1)} %copy-done.2) | data formatting | bytes 2097152 | tf_op jit(solution)/shard_map/reshape;squeeze | solution.py:19
  10.0 0.7 gather_fusion
  11.4 2.3 %copy.38 = f32[4,4,128,128]{3,2,1,0:T(8,128)} copy(f32[4,4,128,128]{3,1,2,0:T(4,128)} %bitcast.137) | data formatting | bytes 2097152 | tf_op jit(solution)/shard_map/transpose | solution.py:20
  13.7 1.1 %copy.39 = f32[4,4,128,128]{3,2,1,0:T(8,128)} copy(f32[4,4,128,128]{3,1,2,0:T(4,128)S(1)} %bitcast.136) | data formatting | bytes 2097152 | tf_op jit(solution)/shard_map/transpose | solution.py:20
  14.8 1.8 %gather_fusion.4 = f32[4,128,128]{2,1,0:T(8,128)S(1)} fusion(f32[16,128,128]{2,1,0:T(8,128)} %bitcast.145, s32[1024]{0:T(1024)S(1)} %pad_clamp_fusion), kind=kCustom, calls=%fused_computation.4 | custom fusion | bytes 524304 | tf_op jit(solution)/shard_map/gather | solution.py:148
  16.6 2.5 %gather_fusion.5 = f32[4,128,128]{2,1,0:T(8,128)} fusion(f32[16,128,128]{2,1,0:T(8,128)} %bitcast.144, s32[1024]{0:T(1024)S(1)} %pad_clamp_fusion), kind=kCustom, calls=%fused_computation.5 | custom fusion | bytes 524304 | tf_op jit(solution)/shard_map/gather | solution.py:148
  21.4 1.1 %fusion.14 = f32[512,512]{1,0:T(8,128)S(1)} fusion(f32[1,1,512,512]{3,2,1,0:T(8,128)S(1)} %copy-done.2, f32[512]{0:T(512)S(1)} %bitcast.152, f32[1,1,512,512]{3,2,1,0:T(8,128)S(1)} %copy-done.3), kind=kOutput, calls=%fused_computation.31 | convolution fusion | flops 805568512 | bytes 3147776 | tf_op jit(solution)/shard_map/dot_general | solution.py:34
  22.4 1.1 %convolution_subtract_fusion.1 = f32[512,512]{1,0:T(8,128)S(1)} fusion(f32[512,512]{1,0:T(8,128)S(1)} %fusion.14, f32[1,1,512,512]{3,2,1,0:T(8,128)S(1)} %copy-done.3, f32[512]{0:T(512)S(1)} %bitcast.153, f32[1,1,512,512]{3,2,1,0:T(8,128)S(1)} %copy-done.2), kind=kOutput, calls=%fused_computation.9 | convolution fusion | flops 805830656 | bytes 4196352 | tf_op jit(solution)/shard_map/dot_general | solution.py:35
  23.5 1.3 %compare_select_fusion.4 = (s32[4]{0:T(128)S(1)}, s32[]{:T(128)}) fusion(s32[16]{0:T(128)S(1)} %gather_fusion, s32[]{:T(128)} %bitcast.28, s32[4,1]{0,1:T(1,128)S(1)} %copy-done.11, s32[]{:T(128)S(6)} %axis_index.15), kind=kLoop, calls=%fused_computation.50 | loop fusion | flops 31 | bytes 60 | tf_op jit(solution)/shard_map/select_n | solution.py:172
  28.8 1.3 %copy.35 = f32[512,512]{0,1:T(8,128)} copy(f32[512,512]{1,0:T(8,128)S(1)} %convolution_subtract_fusion.1) | data formatting | bytes 2097152 | tf_op jit(solution)/shard_map/sub | solution.py:36
  30.1 0.7 constant_dynamic-slice_fusion
  30.9 22.1 %collective-permute-done.1 = f32[1028,128]{1,0:T(8,128)} collective-permute-done((f32[1028,128]{1,0:T(8,128)}, f32[1028,128]{1,0:T(8,128)}, u32[]{:S(2)}, u32[]{:S(2)}) %collective-permute-start.1) | collective-permute-done | bytes 526368 | tf_op jit(solution)/shard_map/ppermute | solution.py:143
  53.0 1.5 %pad_maximum_fusion = f32[4,1028,128]{2,1,0:T(8,128)S(1)} fusion(f32[1,1028,128]{2,1,0:T(8,128)} %bitcast.33, f32[1,1028,128]{2,1,0:T(8,128)} %bitcast.32, f32[1,1028,128]{2,1,0:T(8,128)} %bitcast.31, f32[1,1028,128]{2,1,0:T(8,128)S(1)} %maximum_bitcast_fusion), kind=kLoop, calls=%fused_computation.7 | loop fusion | flops 1579008 | bytes 4210688 | tf_op jit(solution)/shard_map/stack | solution.py:151
  54.8 1.2 %fusion.12 = f32[4,4,128,128]{3,1,2,0:T(4,128)S(1)} fusion(f32[4,4,16,1]{2,1,3,0:T(4,128)S(1)} %bitcast.148, f32[16,1,128,128]{3,2,1,0:T(8,128)S(1)} %get-tuple-element.11), kind=kOutput, calls=%fused_computation.26 | convolution fusion | flops 25165824 | bytes 2098176 | tf_op jit(solution)/shard_map/ji,ixy->jxy/dot_general | solution.py:159
  56.1 1.5 %bitcast_multiply_fusion = (f32[4,128,4,128]{3,2,1,0:T(4,128)S(1)}, f32[4,128,4,128]{3,2,1,0:T(4,128)S(1)}, f32[4,4,128,128]{3,1,2,0:T(4,128)S(1)}) fusion(f32[4,128]{1,0:T(4,128)S(1)} %dynamic-slice_bitcast_fusion, f32[4,4,128,128]{3,1,2,0:T(4,128)S(1)} %fusion.12, f32[4,4,16,1]{2,1,3,0:T(4,128)S(1)} %bitcast.149, ...), kind=kOutput, calls=%fused_computation.27 | convolution fusion | flops 25690112 | bytes 5245952 | tf_op jit(solution)/shard_map/ji,ixy->jxy/dot_general | solution.py:160
  57.6 1.0 %fusion.6 = f32[512,512]{1,0:T(8,128)S(1)} fusion(f32[64,8,4,128]{3,2,1,0:T(4,128)S(1)} %bitcast.135, f32[64,8,4,128]{3,2,1,0:T(4,128)S(1)} %bitcast.134), kind=kOutput, calls=%fused_computation.18 | convolution fusion | flops 805306368 | bytes 3145728 | tf_op jit(solution)/shard_map/dot_general | solution.py:34
  58.7 1.0 %convolution_subtract_fusion = f32[512,512]{1,0:T(8,128)S(1)} fusion(f32[512,512]{1,0:T(8,128)S(1)} %fusion.6, f32[64,8,4,128]{3,2,1,0:T(4,128)S(1)} %bitcast.131, f32[64,8,4,128]{3,2,1,0:T(4,128)S(1)} %bitcast.138), kind=kOutput, calls=%fused_computation.8 | convolution fusion | flops 805568512 | bytes 4194304 | tf_op jit(solution)/shard_map/dot_general | solution.py:35
  60.8 1.0 fusion.33
  61.9 0.7 scatter_fusion
  63.0 2.5 %bitcast_add_fusion = f32[512,512]{0,1:T(8,128)} fusion(f32[512,512]{0,1:T(8,128)} %copy.35, f32[512,512]{1,0:T(8,128)S(1)} %convolution_subtract_fusion.1, f32[64,8,4,128]{3,2,1,0:T(4,128)S(1)} %bitcast.129), kind=kLoop, calls=%fused_computation.11 | loop fusion | flops 524288 | bytes 4194304 | tf_op jit(solution)/shard_map/add | solution.py:176
  65.5 1.6 %copy.47 = f32[512,512]{1,0:T(8,128)S(1)} copy(f32[512,512]{0,1:T(8,128)} %bitcast_add_fusion) | data formatting | bytes 2097152 | tf_op jit(solution)/shard_map/add | solution.py:176
  67.3 1.4 %collective-permute-start.4 = (f32[4,128,128]{2,1,0:T(8,128)S(1)}, f32[4,128,128]{2,1,0:T(8,128)S(1)}, u32[]{:S(2)}, u32[]{:S(2)}) collective-permute-start(f32[4,128,128]{2,1,0:T(8,128)S(1)} %copy.55), channel_id=1, source_target_pairs={{0,8},{4,12},{8,0},{12,4},{1,9},{5,13},{9,1},{13,5},{2,10},{6,14},... | collective-permute-start | bytes 786440 | tf_op jit(solution)/shard_map/ppermute | solution.py:170
  68.7 2.1 %collective-permute-start.5 = (f32[4,128,128]{2,1,0:T(8,128)S(1)}, f32[4,128,128]{2,1,0:T(8,128)S(1)}, u32[]{:S(2)}, u32[]{:S(2)}) collective-permute-start(f32[4,128,128]{2,1,0:T(8,128)S(1)} %copy.56), channel_id=1, source_target_pairs={{0,12},{4,0},{8,4},{12,8},{1,13},{5,1},{9,5},{13,9},{2,14},{6,2},{... | collective-permute-start | bytes 786440 | tf_op jit(solution)/shard_map/ppermute | solution.py:170
  70.8 1.2 %fusion.1.direct_ref = f32[512,512]{1,0:T(8,128)} fusion(f32[512,512]{1,0:T(8,128)S(1)} %copy.47, f32[64,8,4,128]{3,2,1,0:T(4,128)S(1)} %bitcast.130), kind=kLoop, calls=%fused_computation.13 | loop fusion | flops 524288 | bytes 3145728 | tf_op jit(solution)/shard_map/mul | solution.py:176
  72.0 2.4 %collective-permute-done.3.rest_0_ = f32[4,128,128]{2,1,0:T(8,128)S(1)} collective-permute-done((f32[4,128,128]{2,1,0:T(8,128)S(1)}, f32[4,128,128]{2,1,0:T(8,128)S(1)}, u32[]{:S(2)}, u32[]{:S(2)}) %collective-permute-start.3) | collective-permute-done | bytes 262176 | tf_op jit(solution)/shard_map/ppermute | solution.py:170
  74.4 17.5 %collective-permute-done.4.rest_1_ = f32[4,128,128]{2,1,0:T(8,128)S(1)} collective-permute-done((f32[4,128,128]{2,1,0:T(8,128)S(1)}, f32[4,128,128]{2,1,0:T(8,128)S(1)}, u32[]{:S(2)}, u32[]{:S(2)}) %collective-permute-start.4) | collective-permute-done | bytes 262176 | tf_op jit(solution)/shard_map/ppermute | solution.py:170
  91.9 0.7 copy-done.8
  92.6 0.7 copy-done.9
  93.3 3.5 %shard_map.83 = f32[512,512]{1,0:T(8,128)} custom-call(s32[12]{0:T(128)} %slice.31.place_ref, f32[512,512]{1,0:T(8,128)} %fusion.1.direct_ref, f32[4,128,128]{2,1,0:T(8,128)} %copy-done.7, f32[4,128,128]{2,1,0:T(8,128)} %copy-done.8, f32[4,128,128]{2,1,0:T(8,128)} %copy-done.9), custom_call_target="tpu_custom_call" | custom-call | tf_op jit(solution)/shard_map/pallas_call | solution.py:101
  (73 shorter events, 7.6 us)
Async XLA Ops:
  0.0 25.5 %copy-start = (f32[8,16,16]{2,1,0:T(8,128)S(1)}, f32[8,16,16]{2,1,0:T(8,128)}, u32[]{:S(2)}) copy-start(f32[8,16,16]{2,1,0:T(8,128)} %param.12) | copy-start | bytes 24580
  0.0 7.5 %copy-start.2 = (f32[1,1,512,512]{3,2,1,0:T(8,128)S(1)}, f32[1,1,512,512]{3,2,1,0:T(8,128)}, u32[]{:S(2)}) copy-start(f32[1,1,512,512]{3,2,1,0:T(8,128)} %param.8) | copy-start | bytes 3145732
  1.4 7.4 %copy-start.3 = (f32[1,1,512,512]{3,2,1,0:T(8,128)S(1)}, f32[1,1,512,512]{3,2,1,0:T(8,128)}, u32[]{:S(2)}) copy-start(f32[1,1,512,512]{3,2,1,0:T(8,128)} %param.9) | copy-start | bytes 3145732
  5.1 4.1 %copy-start.11 = (s32[4,1]{0,1:T(1,128)S(1)}, s32[4,1]{0,1:T(1,128)}, u32[]{:S(2)}) copy-start(s32[4,1]{0,1:T(1,128)} %param.13) | copy-start | bytes 52
  5.1 25.8 %collective-permute-start = (f32[1028,128]{1,0:T(8,128)}, f32[1028,128]{1,0:T(8,128)}, u32[]{:S(2)}, u32[]{:S(2)}) collective-permute-start(f32[1028,128]{1,0:T(8,128)} %get-tuple-element.8), channel_id=1, source_target_pairs={{0,4},{4,8},{8,12},{12,0},{1,5},{5,9},{9,13},{13,1},{2,6},{6,10},{... | collective-permute-start | bytes 1579016 | tf_op jit(solution)/shard_map/ppermute | solution.py:143
  5.3 47.7 %collective-permute-start.1 = (f32[1028,128]{1,0:T(8,128)}, f32[1028,128]{1,0:T(8,128)}, u32[]{:S(2)}, u32[]{:S(2)}) collective-permute-start(f32[1028,128]{1,0:T(8,128)} %get-tuple-element.9), channel_id=1, source_target_pairs={{0,8},{4,12},{8,0},{12,4},{1,9},{5,13},{9,1},{13,5},{2,10},{6,14},... | collective-permute-start | bytes 1579016 | tf_op jit(solution)/shard_map/ppermute | solution.py:143
  7.0 46.0 %collective-permute-start.2 = (f32[1028,128]{1,0:T(8,128)}, f32[1028,128]{1,0:T(8,128)}, u32[]{:S(2)}, u32[]{:S(2)}) collective-permute-start(f32[1028,128]{1,0:T(8,128)} %get-tuple-element.10), channel_id=1, source_target_pairs={{0,12},{4,0},{8,4},{12,8},{1,13},{5,1},{9,5},{13,9},{2,14},{6,2},{... | collective-permute-start | bytes 1579016 | tf_op jit(solution)/shard_map/ppermute | solution.py:143
  7.5 2.6 %copy-start.1 = (s32[1,1,16]{2,1,0:T(1,128)S(1)}, s32[1,1,16]{2,1,0:T(1,128)}, u32[]{:S(2)}) copy-start(s32[1,1,16]{2,1,0:T(1,128)} %param.14) | copy-start | bytes 196
  11.4 7.7 %copy-start.12 = (s32[4,1]{0,1:T(1,128)S(1)}, s32[4,1]{0,1:T(1,128)}, u32[]{:S(2)}) copy-start(s32[4,1]{0,1:T(1,128)} %param.15) | copy-start | bytes 52
  13.7 7.6 %copy-start.10 = (f32[1,1,512]{2,1,0:T(1,128)S(1)}, f32[1,1,512]{2,1,0:T(1,128)}, u32[]{:S(2)}) copy-start(f32[1,1,512]{2,1,0:T(1,128)} %param.10) | copy-start | bytes 6148
  22.4 2.4 %copy-start.4 = (f32[4,128,128]{2,1,0:T(8,128)S(1)}, f32[4,128,128]{2,1,0:T(8,128)}, u32[]{:S(2)}) copy-start(f32[4,128,128]{2,1,0:T(8,128)} %gather_fusion.5) | copy-start | bytes 786436
  65.5 1.6 %copy-start.6 = (f32[4,128,128]{2,0,1:T(4,128)S(1)}, f32[4,128,128]{2,0,1:T(4,128)}, u32[]{:S(2)}) copy-start(f32[4,128,128]{2,0,1:T(4,128)} %get-tuple-element.15) | copy-start | bytes 786436
  65.5 1.7 %copy-start.5 = (f32[4,128,128]{2,0,1:T(4,128)S(1)}, f32[4,128,128]{2,0,1:T(4,128)}, u32[]{:S(2)}) copy-start(f32[4,128,128]{2,0,1:T(4,128)} %get-tuple-element.14) | copy-start | bytes 786436
  67.2 7.2 %collective-permute-start.3 = (f32[4,128,128]{2,1,0:T(8,128)S(1)}, f32[4,128,128]{2,1,0:T(8,128)S(1)}, u32[]{:S(2)}, u32[]{:S(2)}) collective-permute-start(f32[4,128,128]{2,1,0:T(8,128)S(1)} %copy.54), channel_id=1, source_target_pairs={{0,4},{4,8},{8,12},{12,0},{1,5},{5,9},{9,13},{13,1},{2,6},{6,10},{... | collective-permute-start | bytes 786440 | tf_op jit(solution)/shard_map/ppermute | solution.py:170
  67.3 24.6 %collective-permute-start.4 = (f32[4,128,128]{2,1,0:T(8,128)S(1)}, f32[4,128,128]{2,1,0:T(8,128)S(1)}, u32[]{:S(2)}, u32[]{:S(2)}) collective-permute-start(f32[4,128,128]{2,1,0:T(8,128)S(1)} %copy.55), channel_id=1, source_target_pairs={{0,8},{4,12},{8,0},{12,4},{1,9},{5,13},{9,1},{13,5},{2,10},{6,14},... | collective-permute-start | bytes 786440 | tf_op jit(solution)/shard_map/ppermute | solution.py:170
  68.7 23.2 %collective-permute-start.5 = (f32[4,128,128]{2,1,0:T(8,128)S(1)}, f32[4,128,128]{2,1,0:T(8,128)S(1)}, u32[]{:S(2)}, u32[]{:S(2)}) collective-permute-start(f32[4,128,128]{2,1,0:T(8,128)S(1)} %copy.56), channel_id=1, source_target_pairs={{0,12},{4,0},{8,4},{12,8},{1,13},{5,1},{9,5},{13,9},{2,14},{6,2},{... | collective-permute-start | bytes 786440 | tf_op jit(solution)/shard_map/ppermute | solution.py:170
  74.4 17.5 %copy-start.7 = (f32[4,128,128]{2,1,0:T(8,128)}, f32[4,128,128]{2,1,0:T(8,128)S(1)}, u32[]{:S(2)}) copy-start(f32[4,128,128]{2,1,0:T(8,128)S(1)} %collective-permute-done.3.rest_0_) | copy-start | bytes 786436
  91.9 0.7 copy-start.8
  92.6 0.7 copy-start.9
